TPU v7x, 32 devices: a whole 2x2x4 slice. The times are simulated.
32 devices in a mesh: groups: 2 (over y), tm: 4 (over z), chan: 4 (over x, core).
Axes of the slice: x: 2, y: 2, z: 4, core: 2. Of those that a mesh axis runs over, the one named last changes fastest.
Arguments:
- tokens: bfloat16 [1024, 4096], P(('groups', 'tm'), 'chan'), parts along dimension 0, may hold values from -6 to 6
- in_weight: bfloat16 [4096, 8192], P('chan'), may hold values from -0.125 to 0.125
- recur_weight: float32 [2048, 2], P('chan'), may hold values from -0.75 to 0.75
- gate_bias: float32 [2048, 4], P('chan'), may hold values from -2 to 13
- forget_offset: float32 [1024], P(('groups', 'tm')), parts along dimension 0, may hold values from 0 to 14
Outputs:
- hidden_states: float32 [2048, 1024], P('chan', ('groups', 'tm')), parts along dimension 1
There are 2 independent parts, one for each index of `groups`. A program takes and returns all parts, laid end to end along the dimension named above; an argument that names none is the same for every part. Nothing has to cross between parts.
All inputs are finite; a program needn't handle non-finite values.
Results may differ from a plain program's by a relative error of at most 0.0003.
Values may be sent and summed in bfloat16 or wider, within the bound.
No kernel may reach another device: no remote copies, remote signals or barrier semaphores. Data moves between devices by JAX's collectives and lax.ppermute only.
A program may use at most 128 MiB of HBM per device.

v0:
```python
import jax
import jax.numpy as jnp
from jax import lax
from jax.sharding import PartitionSpec as P

ITERS = 2


def passed_along(value, axis, steps):
    count = lax.axis_size(axis)
    leading, last = (max(0, -steps), min(count, count - steps))
    return lax.ppermute(value, axis, [(source, source + steps) for source in range(leading, last)])


def gates(projected, prev_cell, prev_hidden, gate_bias, recur_weight, forget_offset):
    input_gate = jax.nn.sigmoid(projected[:, 0] + gate_bias[:, 0:1])
    forget_gate = jax.nn.sigmoid(
        projected[:, 1]
        + gate_bias[:, 1:2]
        + recur_weight[:, 0:1] * prev_hidden
        - forget_offset[None, :]
    )
    cand_gate = jnp.tanh(projected[:, 2] + gate_bias[:, 2:3])
    output_gate = jax.nn.sigmoid(
        projected[:, 3] + gate_bias[:, 3:4] + recur_weight[:, 1:2] * prev_hidden
    )
    new_cell = forget_gate * prev_cell + input_gate * cand_gate
    squashed = jnp.tanh(new_cell)
    new_hidden = output_gate * squashed
    slope = 1.0 - squashed * squashed
    cell_hidden = prev_cell * forget_gate * (1.0 - forget_gate) * recur_weight[:, 0:1]
    hidden_cell = output_gate * slope * forget_gate
    hidden_hidden = (
        output_gate * (1.0 - output_gate) * recur_weight[:, 1:2] * squashed
        + output_gate * slope * cell_hidden
    )
    offset_cell = new_cell - forget_gate * prev_cell - cell_hidden * prev_hidden
    offset_hidden = new_hidden - hidden_cell * prev_cell - hidden_hidden * prev_hidden
    return (forget_gate, cell_hidden, hidden_cell, hidden_hidden, offset_cell, offset_hidden)


def compose(early, later):
    e_one, e_two, e_three, e_four, e_five, e_six = early
    l_one, l_two, l_three, l_four, l_five, l_six = later
    return (
        l_one * e_one + l_two * e_three,
        l_one * e_two + l_two * e_four,
        l_three * e_one + l_four * e_three,
        l_three * e_two + l_four * e_four,
        l_one * e_five + l_two * e_six + l_five,
        l_three * e_five + l_four * e_six + l_six,
    )


def shards(tokens, in_weight, recur_weight, gate_bias, forget_offset):
    steps_dev = tokens.shape[0]
    channels = recur_weight.shape[0]
    summed = lax.psum_scatter(
        lax.dot_general(
            in_weight, tokens, (((0,), (1,)), ((), ())), preferred_element_type=jnp.float32
        ),
        "chan",
        scatter_dimension=0,
        tiled=True,
    )
    projected = summed.reshape(channels, 4, steps_dev)
    prev_cell = jnp.zeros((channels, steps_dev), jnp.float32)
    prev_hidden = jnp.zeros((channels, steps_dev), jnp.float32)
    hiddens = prev_hidden
    for repeat in range(ITERS):
        terms = gates(projected, prev_cell, prev_hidden, gate_bias, recur_weight, forget_offset)
        prefix = lax.associative_scan(compose, terms, axis=1)
        mats = jnp.stack([part_map[:, -1] for part_map in prefix[:4]])
        vecs = jnp.stack([part_map[:, -1] for part_map in prefix[4:]])
        packed = jnp.concatenate([mats, vecs], axis=0)[None]
        everyone = lax.all_gather(packed, "tm", axis=0, tiled=True)
        running = lax.associative_scan(
            compose, tuple((everyone[:, row] for row in range(6))), axis=0
        )
        position = lax.axis_index("tm")
        before = jnp.maximum(position - 1, 0)
        picked = jnp.stack(
            [
                lax.dynamic_index_in_dim(running[4], before, 0, False),
                lax.dynamic_index_in_dim(running[5], before, 0, False),
            ]
        )
        incoming = jnp.where(position > 0, picked, jnp.zeros_like(picked))
        cells = prefix[0] * incoming[0][:, None] + prefix[1] * incoming[1][:, None] + prefix[4]
        hiddens = prefix[2] * incoming[0][:, None] + prefix[3] * incoming[1][:, None] + prefix[5]
        if repeat + 1 < ITERS:
            last_pair = jnp.stack([cells[:, -1], hiddens[:, -1]])
            before_pair = passed_along(last_pair, "tm", 1)
            prev_cell = jnp.concatenate([before_pair[0][:, None], cells[:, :-1]], axis=1)
            prev_hidden = jnp.concatenate([before_pair[1][:, None], hiddens[:, :-1]], axis=1)
    return hiddens


def solution(mesh):
    placed = (
        P(("groups", "tm"), "chan"),
        P("chan", None),
        P("chan", None),
        P("chan", None),
        P(("groups", "tm")),
    )
    return jax.shard_map(
        shards, mesh=mesh, in_specs=placed, out_specs=P("chan", ("groups", "tm")), check_vma=False
    )
```

profile of v0, /device:TPU:0, one launch (start us, length us, event | category | flops | bytes accessed | tf_op | source)
XLA Modules:
  0.0 185.9 jit_solution(15729941666699118095)
XLA Ops:
  6.6 0.9 copy-done
  7.5 10.2 %fusion.55 = f32[8192,128]{1,0:T(8,128)} fusion(bf16[1024,8192]{1,0:T(8,128)(2,1)} %param.6, bf16[128,1024]{1,0:T(8,128)(2,1)S(1)} %copy-done), kind=kOutput, calls=%fused_computation.480 | convolution fusion | flops 2147483648 | bytes 21233664 | tf_op jit(solution)/shard_map/dot_general | solution.py:59
  17.8 47.3 %reduce-scatter.2.cloned.1.call-done = f32[2048,128]{1,0:T(8,128)} async-done(((f32[8192,128]{1,0:T(8,128)}), f32[2048,128]{1,0:T(8,128)}) %reduce-scatter.2.cloned.1.call-update) | async-done | bytes 1048592 | tf_op jit(solution)/shard_map/reduce_scatter | solution.py:58
  65.1 3.7 %fusion.48 = (f32[512,1,128]{2,1,0:T(1,128)S(1)}, f32[512,1,128]{2,1,0:T(1,128)S(1)}, f32[512,1,128]{2,1,0:T(1,128)S(1)}, f32[512,1,128]{2,1,0:T(1,128)S(1)}) fusion(f32[512,4,128]{2,1,0:T(4,128)} %bitcast.217), kind=kLoop, calls=%fused_computation.473 | loop fusion | bytes 2097152 | tf_op jit(solution)/shard_map/slice | solution.py:16
  73.6 0.7 slice.1645
  76.0 0.7 slice.1769
  78.8 1.3 multiply_add_fusion.13
  103.6 0.7 multiply_add_fusion.9
  104.3 0.7 multiply_add_fusion.8
  105.8 0.7 pad_maximum_fusion.66
  108.6 0.8 add_add_fusion.39
  110.9 0.8 add_add_fusion.31
  113.1 0.8 add_add_fusion.23
  115.3 0.9 add_add_fusion.15
  119.4 0.9 pad_maximum_fusion.2
  121.1 0.9 pad_maximum_fusion.5
  122.8 1.0 pad.623
  123.9 2.4 %pad.593 = f32[512,128]{0,1:T(8,128)} pad(f32[512,64]{0,1:T(8,128)} %add.1550, f32[]{:T(128)} %constant.22.clone.1), padding=0_0_0x1_0_1 | pad | bytes 393220 | tf_op jit(solution)/shard_map/pad | solution.py:72
  126.3 2.4 %pad.621 = f32[512,128]{0,1:T(8,128)} pad(f32[512,64]{0,1:T(8,128)} %add.1552, f32[]{:T(128)} %constant.22.clone.1), padding=0_0_0x1_0_1 | pad | bytes 393220 | tf_op jit(solution)/shard_map/pad | solution.py:72
  128.6 1.4 pad.619
  130.1 0.7 add_bitcast_fusion.8
  130.8 0.7 add_bitcast_fusion.6
  131.6 0.7 add_bitcast_fusion.7
  132.3 13.5 %all-gather.2 = f32[4,6,512]{2,1,0:T(8,128)S(1)} all-gather(f32[1,6,512]{2,1,0:T(8,128)S(1)} %bitcast.223), channel_id=2, replica_groups=mesh['groups'=2,'tm'=4,'chan'=4] {'tm'}, dimensions={0}, use_global_device_ids=true | all-gather | bytes 61440 | tf_op jit(solution)/shard_map/all_gather | solution.py:76
  146.5 1.6 add_add_fusion.1
  148.2 3.4 %collective-permute-start = (f32[2,512]{1,0:T(2,128)S(1)}, f32[2,512]{1,0:T(2,128)S(1)}, u32[]{:S(2)}, u32[]{:S(2)}) collective-permute-start(f32[2,512]{1,0:T(2,128)S(1)} %pad_maximum_fusion.70), channel_id=1, source_target_pairs={{0,4},{4,8},{8,12},{1,5},{5,9},{9,13},{2,6},{6,10},{10,14},{3,7},{... | collective-permute-start | bytes 12296 | tf_op jit(solution)/shard_map/ppermute | solution.py:12
  151.6 1.3 collective-permute-done
  152.9 0.9 multiply_multiply_fusion
  154.3 0.8 multiply_subtract_fusion.1
  155.1 1.0 fusion.5
  163.8 13.5 %all-gather.3 = f32[4,6,512]{2,1,0:T(8,128)S(1)} all-gather(f32[1,6,512]{2,1,0:T(8,128)S(1)} %bitcast.224), channel_id=3, replica_groups=mesh['groups'=2,'tm'=4,'chan'=4] {'tm'}, dimensions={0}, use_global_device_ids=true | all-gather | bytes 61440 | tf_op jit(solution)/shard_map/all_gather | solution.py:76
  178.2 0.8 copy.36
  (714 shorter events, 50.8 us)
Async XLA Ops:
  6.5 1.0 copy-start
  6.5 11.2 %copy-start.15 = (f32[512,2]{0,1:T(2,128)S(1)}, f32[512,2]{0,1:T(2,128)}, u32[]{:S(2)}) copy-start(f32[512,2]{0,1:T(2,128)} %param.7) | copy-start | bytes 12292
  6.5 11.2 %copy-start.14 = (f32[512,4]{0,1:T(4,128)S(1)}, f32[512,4]{0,1:T(4,128)}, u32[]{:S(2)}) copy-start(f32[512,4]{0,1:T(4,128)} %param.8) | copy-start | bytes 24580
  6.5 62.8 %copy-start.16 = (f32[128]{0:T(128)S(1)}, f32[128]{0:T(128)}, u32[]{:S(2)}) copy-start(f32[128]{0:T(128)} %param.9) | copy-start | bytes 1540
  6.5 58.6 %reduce-scatter.2.cloned.1.call-start = ((), (), s32[]{:S(2)}) async-start(), calls=%async_computation.1 | async-start | bytes 5242880 | tf_op jit(solution)/shard_map/reduce_scatter | solution.py:58
  17.7 56.6 %copy-start.10 = (f32[512,1]{0,1:T(1,128)}, f32[512,1]{0,1:T(1,128)S(1)}, u32[]{:S(2)}) copy-start(f32[512,1]{0,1:T(1,128)S(1)} %get-tuple-element.228) | copy-start | bytes 6148
  17.7 56.6 %copy-start.11 = (f32[512,1]{0,1:T(1,128)}, f32[512,1]{0,1:T(1,128)S(1)}, u32[]{:S(2)}) copy-start(f32[512,1]{0,1:T(1,128)S(1)} %get-tuple-element.229) | copy-start | bytes 6148
  17.8 53.9 %copy-start.13 = (f32[512,1]{0,1:T(1,128)}, f32[512,1]{0,1:T(1,128)S(1)}, u32[]{:S(2)}) copy-start(f32[512,1]{0,1:T(1,128)S(1)} %get-tuple-element.203) | copy-start | bytes 6148
  17.8 56.5 %copy-start.12 = (f32[512,1]{0,1:T(1,128)}, f32[512,1]{0,1:T(1,128)S(1)}, u32[]{:S(2)}) copy-start(f32[512,1]{0,1:T(1,128)S(1)} %get-tuple-element.204) | copy-start | bytes 6148
  88.4 10.7 %copy-start.3 = (f32[512,7]{0,1:T(8,128)}, f32[512,7]{0,1:T(8,128)S(1)}, u32[]{:S(2)}) copy-start(f32[512,7]{0,1:T(8,128)S(1)} %slice.1661) | copy-start | bytes 43012
  88.4 10.7 %copy-start.4 = (f32[512,7]{0,1:T(8,128)}, f32[512,7]{0,1:T(8,128)S(1)}, u32[]{:S(2)}) copy-start(f32[512,7]{0,1:T(8,128)S(1)} %slice.1710) | copy-start | bytes 43012
  88.5 10.6 %copy-start.5 = (f32[512,7]{0,1:T(8,128)}, f32[512,7]{0,1:T(8,128)S(1)}, u32[]{:S(2)}) copy-start(f32[512,7]{0,1:T(8,128)S(1)} %slice.1719) | copy-start | bytes 43012
  91.1 7.2 %copy-start.6 = (f32[512,3]{0,1:T(4,128)}, f32[512,3]{0,1:T(4,128)S(1)}, u32[]{:S(2)}) copy-start(f32[512,3]{0,1:T(4,128)S(1)} %slice.1712) | copy-start | bytes 18436
  91.1 7.2 %copy-start.7 = (f32[512,3]{0,1:T(4,128)}, f32[512,3]{0,1:T(4,128)S(1)}, u32[]{:S(2)}) copy-start(f32[512,3]{0,1:T(4,128)S(1)} %slice.1671) | copy-start | bytes 18436
  91.2 7.1 %copy-start.8 = (f32[512,3]{0,1:T(4,128)}, f32[512,3]{0,1:T(4,128)S(1)}, u32[]{:S(2)}) copy-start(f32[512,3]{0,1:T(4,128)S(1)} %slice.1704) | copy-start | bytes 18436
  91.2 7.0 %copy-start.9 = (f32[512,3]{0,1:T(4,128)}, f32[512,3]{0,1:T(4,128)S(1)}, u32[]{:S(2)}) copy-start(f32[512,3]{0,1:T(4,128)S(1)} %slice.1713) | copy-start | bytes 18436
  122.8 23.6 %copy-start.1 = (f32[512,128]{0,1:T(8,128)}, f32[512,128]{0,1:T(8,128)S(1)}, u32[]{:S(2)}) copy-start(f32[512,128]{0,1:T(8,128)S(1)} %pad.620) | copy-start | bytes 786436
  123.9 22.6 %copy-start.2 = (f32[512,128]{0,1:T(8,128)}, f32[512,128]{0,1:T(8,128)S(1)}, u32[]{:S(2)}) copy-start(f32[512,128]{0,1:T(8,128)S(1)} %pad.623) | copy-start | bytes 786436
  148.2 4.7 %collective-permute-start = (f32[2,512]{1,0:T(2,128)S(1)}, f32[2,512]{1,0:T(2,128)S(1)}, u32[]{:S(2)}, u32[]{:S(2)}) collective-permute-start(f32[2,512]{1,0:T(2,128)S(1)} %pad_maximum_fusion.70), channel_id=1, source_target_pairs={{0,4},{4,8},{8,12},{1,5},{5,9},{9,13},{2,6},{6,10},{10,14},{3,7},{... | collective-permute-start | bytes 12296 | tf_op jit(solution)/shard_map/ppermute | solution.py:12
Sparse Core Ops, SparseCore 0:
  17.8 47.2 reduce-scatter.1
where the time goes:
time: 187 us; the launch traced here: 186 us
  waiting for transfers between devices  48.7 us (26%)
  local copies, waits for them, and re-layouts  45.1 us (24%)
  other arithmetic  34.9 us (19%)
  blocking collectives  27 us (14%)
  between operations  16.7 us (9%)
  matrix products  10.2 us (5%)
  starting transfers between devices  3.46 us (2%)
    reduce_scatter x1, waiting for transfers between devices, shards(): lax.psum_scatter(lax.dot_general(in_weight, tokens, (((0,), (1,)), ((), (...  47.3 us
    slice x270, local copies, waits for them, and re-layouts, shards(): prefix = lax.associative_scan(compose, terms, axis=1)  27.2 us
    all_gather x2, blocking collectives, shards(): everyone = lax.all_gather(packed, 'tm', axis=0, tiled=True)  27 us
    concatenate x69, other arithmetic, shards(): prefix = lax.associative_scan(compose, terms, axis=1)  14.6 us
    pad x138, local copies, waits for them, and re-layouts, shards(): prefix = lax.associative_scan(compose, terms, axis=1)  10.7 us
    dot_general x1, matrix products, shards(): lax.dot_general(in_weight, tokens, (((0,), (1,)), ((), ())), preferred_el...  10.2 us
    add x72, other arithmetic, shards(): prefix = lax.associative_scan(compose, terms, axis=1)  3.85 us
  transfers between devices with their start and end apart: 2, of which 2 were waited for; matrix products, arithmetic and copies ran while one was open for 0% of the time, Pallas kernels for 0%

commit v1 on v0

v1 whole, which is shorter than its diff:
```python
import functools

import jax
import jax.numpy as jnp
from jax import lax
from jax.experimental import pallas as pl
from jax.experimental.pallas import tpu as pltpu
from jax.sharding import PartitionSpec as P

LANES = 128
SUB = 8
GATES = 4
GROUP = LANES * GATES
BINADES = 251.0
LOWEST = 125.0
F32 = jnp.float32
BF16 = jnp.bfloat16


def cost(flops, moved):
    return pl.CostEstimate(flops=int(flops), bytes_accessed=int(moved), transcendentals=0)


def vmem(count):
    return [pl.BlockSpec(memory_space=pltpu.VMEM)] * count


def product_kernel(_, x_ref, give_w_ref, keep_w_ref, give_ref, keep_ref):
    x = x_ref[...]
    give_ref[...] = jnp.dot(x, give_w_ref[...], preferred_element_type=F32)
    keep_ref[...] = jnp.dot(x, keep_w_ref[...], preferred_element_type=F32)


def products(owners, tokens, in_weight, first, width, per_owner, tile):
    steps, depth = tokens.shape
    tiles = width // tile

    def column(which):
        return lambda i, who: (0, who[which] * (per_owner // tile) + first // tile + i)

    out = jax.ShapeDtypeStruct((steps, width), F32)
    return pl.pallas_call(
        product_kernel,
        out_shape=(out, out),
        grid_spec=pltpu.PrefetchScalarGridSpec(
            num_scalar_prefetch=1,
            grid=(tiles,),
            in_specs=[
                pl.BlockSpec((steps, depth), lambda i, who: (0, 0)),
                pl.BlockSpec((depth, tile), column(0)),
                pl.BlockSpec((depth, tile), column(1)),
            ],
            out_specs=[pl.BlockSpec((steps, tile), lambda i, who: (0, i))] * 2,
        ),
        compiler_params=pltpu.CompilerParams(dimension_semantics=("arbitrary",)),
        cost_estimate=cost(4 * steps * depth * width, 4 * depth * width + 8 * steps * width),
        name="products",
    )(owners, tokens, in_weight, in_weight)


def encode_kernel(mine_ref, theirs_ref, out_ref, sum_ref):
    steps, width = mine_ref.shape
    blocks = width // LANES
    top = jnp.zeros((steps, LANES), F32)
    for block in range(blocks):
        cols = pl.ds(block * LANES, LANES)
        both = mine_ref[:, cols] + theirs_ref[:, cols]
        sum_ref[:, cols] = both
        top = jnp.maximum(top, jnp.abs(both))
    top = jnp.max(top, axis=0, keepdims=True)
    top = jnp.maximum(top, 1e-30) * 1.0078125
    scale = top.astype(BF16).astype(F32)
    out_ref[pl.ds(blocks * steps, SUB), :] = jnp.broadcast_to(scale, (SUB, LANES)).astype(BF16)
    inverse = 1.0 / scale
    for block in range(blocks):
        value = sum_ref[:, pl.ds(block * LANES, LANES)]
        level = jnp.sqrt(jnp.abs(value) * inverse) * BINADES - LOWEST
        code = jnp.exp2(level)
        out_ref[pl.ds(block * steps, steps), :] = jnp.where(value < 0.0, -code, code).astype(BF16)


def encoded(mine, theirs):
    steps, width = mine.shape
    rows = steps * (width // LANES) + SUB
    return pl.pallas_call(
        encode_kernel,
        out_shape=jax.ShapeDtypeStruct((rows, LANES), BF16),
        in_specs=vmem(2),
        out_specs=pl.BlockSpec(memory_space=pltpu.VMEM),
        scratch_shapes=[pltpu.VMEM((steps, width), F32)],
        cost_estimate=cost(20 * steps * width, 10 * steps * width),
        name="encode",
    )(mine, theirs)


def decoded(code, scale):
    level = (jnp.log2(jnp.abs(code)) + LOWEST) * (1.0 / BINADES)
    size = level * level * scale
    return jnp.where(code < 0.0, -size, size)


def compose(early, later):
    e1, e2, e3, e4, e5, e6 = early
    l1, l2, l3, l4, l5, l6 = later
    return (
        l1 * e1 + l2 * e3,
        l1 * e2 + l2 * e4,
        l3 * e1 + l4 * e3,
        l3 * e2 + l4 * e4,
        l1 * e5 + l2 * e6 + l5,
        l3 * e5 + l4 * e6 + l6,
    )


def compose_lower(early, later):
    e1, e3, e4, e5, e6 = early
    l1, l3, l4, l5, l6 = later
    return (
        l1 * e1,
        l3 * e1 + l4 * e3,
        l4 * e4,
        l1 * e5 + l5,
        l3 * e5 + l4 * e6 + l6,
    )


def sub_blocks(terms, join, identity):
    row = lax.broadcasted_iota(jnp.int32, (SUB, LANES), 0)
    reach = 1
    while reach < SUB:
        moved = tuple(
            jnp.where(row >= reach, pltpu.roll(term, reach, 0), unit)
            for term, unit in zip(terms, identity)
        )
        terms = join(moved, terms)
        reach *= 2
    before = tuple(
        jnp.where(row >= 1, pltpu.roll(term, 1, 0), unit) for term, unit in zip(terms, identity)
    )
    return before, terms


LOWER_UNIT = (1.0, 0.0, 1.0, 0.0, 0.0)
UNIT = (1.0, 0.0, 0.0, 1.0, 0.0, 0.0)


def sigmoid(x):
    return 1.0 / (1.0 + jnp.exp(-x))


def first_kernel(groups, remotes, earlier, *refs):
    refs = list(refs)
    mine_ref, theirs_ref = refs[:2]
    codes = refs[2 : 2 + remotes]
    bias_ref, weight_ref, offset_ref = refs[2 + remotes : 5 + remotes]
    totals_before = refs[5 + remotes : 5 + remotes + earlier]
    kept_ref, prefix_ref, totals_ref, sum_ref = refs[5 + remotes + earlier :]
    steps = mine_ref.shape[0]
    runs = steps // SUB
    blocks = groups * GATES
    done = 0
    for ref in totals_before:
        totals_ref[pl.ds(done, ref.shape[0]), :] = ref[...]
        done += ref.shape[0]
    scales = [
        ref[pl.ds(blocks * steps, SUB), :][0:1, :].astype(F32) for ref in codes
    ]
    lane = lax.broadcasted_iota(jnp.int32, (SUB, LANES), 1)
    quarter = lane // (LANES // GATES)
    inner = lane % (LANES // GATES)
    picks = [inner * GATES + (quarter - q + GATES) % GATES for q in range(GATES)]
    for group in range(groups):
        for q in range(GATES):
            block = group * GATES + q
            cols = pl.ds(block * LANES, LANES)
            value = mine_ref[:, cols] + theirs_ref[:, cols]
            for ref, scale in zip(codes, scales):
                value = value + decoded(ref[pl.ds(block * steps, steps), :].astype(F32), scale)
            sum_ref[q] = value
        channels = pl.ds(group * LANES, LANES)
        biases = [
            jnp.broadcast_to(bias_ref[k : k + 1, channels], (SUB, LANES)) for k in range(GATES)
        ]
        out_weight = jnp.broadcast_to(weight_ref[1:2, channels], (SUB, LANES))
        run = None
        for i in range(runs):
            loaded = [
                jnp.take_along_axis(sum_ref[q, pl.ds(i, SUB, stride=runs), :], picks[q], axis=1)
                for q in range(GATES)
            ]
            pre = []
            for k in range(GATES):
                part = loaded[(0 - k) % GATES]
                for p in range(1, GATES):
                    part = jnp.where(quarter == p, loaded[(p - k) % GATES], part)
                if k:
                    part = pltpu.roll(part, LANES - k * (LANES // GATES), 1)
                pre.append(part + biases[k])
            pre_forget = pre[1] - offset_ref[pl.ds(i * SUB, SUB), :]
            forget = sigmoid(pre_forget)
            output = sigmoid(pre[3])
            cell = sigmoid(pre[0]) * jnp.tanh(pre[2])
            squashed = jnp.tanh(cell)
            hidden_cell = output * (1.0 - squashed * squashed) * forget
            hidden_hidden = output * (1.0 - output) * out_weight * squashed
            term = (forget, hidden_cell, hidden_hidden, cell, output * squashed)
            run = term if run is None else compose_lower(run, term)
            rows = pl.ds(i * SUB, SUB)
            kept_ref[group, 0, rows, :] = pre_forget
            kept_ref[group, 1, rows, :] = pre[3]
            kept_ref[group, 2, rows, :] = cell
        before, total = sub_blocks(run, compose_lower, LOWER_UNIT)
        for index, term in enumerate(before):
            prefix_ref[group, index] = term
        for index, term in enumerate(total):
            totals_ref[pl.ds(done + group * SUB + index, 1), :] = term[SUB - 1 : SUB, :]
        for index in range(len(total), SUB):
            totals_ref[pl.ds(done + group * SUB + index, 1), :] = jnp.zeros((1, LANES), F32)


def first(mine, theirs, codes, bias, weight, offset, earlier):
    steps, width = mine.shape
    groups = width // GROUP
    rows = sum(e.shape[0] for e in earlier) + groups * SUB
    count = 5 + len(codes) + len(earlier)
    return pl.pallas_call(
        functools.partial(first_kernel, groups, len(codes), len(earlier)),
        out_shape=(
            jax.ShapeDtypeStruct((groups, 3, steps, LANES), F32),
            jax.ShapeDtypeStruct((groups, 5, SUB, LANES), F32),
            jax.ShapeDtypeStruct((rows, LANES), F32),
        ),
        in_specs=vmem(count),
        out_specs=vmem(3),
        scratch_shapes=[pltpu.VMEM((GATES, steps, LANES), F32)],
        cost_estimate=cost(60 * steps * width, 20 * steps * width),
        name="first",
    )(mine, theirs, *codes, bias, weight, offset, *earlier)


def in_turn(me, count, own_xor, received):
    for position in range(count - 1):
        picked = received[0]
        for k in range(2, count):
            picked = jnp.where(position == (me ^ k if own_xor else me - k), received[k - 1], picked)
        yield picked, position < me


def arriving(me_ref, count, own_xor, received, group, lower):
    me = me_ref[0]
    rows = [ref[pl.ds(group * SUB, SUB), :] for ref in received]
    cell = jnp.zeros((1, LANES), F32)
    hidden = jnp.zeros((1, LANES), F32)
    for maps, counts in in_turn(me, count, own_xor, rows):
        if lower:
            a, c, d, u, v = (maps[j : j + 1, :] for j in range(5))
            new_cell = a * cell + u
        else:
            a, b, c, d, u, v = (maps[j : j + 1, :] for j in range(6))
            new_cell = a * cell + b * hidden + u
        new_hidden = c * cell + d * hidden + v
        cell = jnp.where(counts, new_cell, cell)
        hidden = jnp.where(counts, new_hidden, hidden)
    return cell, hidden


def second_kernel(count, own_xor, chunks, me_ref, *refs):
    refs = list(refs)
    received = refs[: count - 1]
    kept = refs[count - 1 : count - 1 + chunks]
    prefixes = refs[count - 1 + chunks : count - 1 + 2 * chunks]
    weight_ref = refs[count - 1 + 2 * chunks]
    hidden_ref, prefix_ref, totals_ref = refs[count + 2 * chunks :]
    group = 0
    for kept_ref, before_ref in zip(kept, prefixes):
        groups, _, steps, _ = kept_ref.shape
        for local in range(groups):
            cell, hidden = arriving(me_ref, count, own_xor, received, group, True)
            a, c, d, u, v = (before_ref[local, j] for j in range(5))
            cell, hidden = a * cell + u, c * cell + d * hidden + v
            channels = pl.ds(group * LANES, LANES)
            forget_weight = jnp.broadcast_to(weight_ref[0:1, channels], (SUB, LANES))
            out_weight = jnp.broadcast_to(weight_ref[1:2, channels], (SUB, LANES))
            run = None
            for i in range(steps // SUB):
                rows = pl.ds(i * SUB, SUB)
                pre_forget = kept_ref[local, 0, rows, :]
                pre_output = kept_ref[local, 1, rows, :]
                fresh = kept_ref[local, 2, rows, :]
                forget = sigmoid(pre_forget + forget_weight * hidden)
                output = sigmoid(pre_output + out_weight * hidden)
                kept_cell = forget * cell
                new_cell = kept_cell + fresh
                squashed = jnp.tanh(new_cell)
                slope = output * (1.0 - squashed * squashed)
                cell_hidden = kept_cell * (1.0 - forget) * forget_weight
                hidden_cell = slope * forget
                hidden_hidden = (
                    output * (1.0 - output) * out_weight * squashed + slope * cell_hidden
                )
                offset_cell = new_cell - kept_cell - cell_hidden * hidden
                offset_hidden = output * squashed - hidden_cell * cell - hidden_hidden * hidden
                term = (
                    forget,
                    cell_hidden,
                    hidden_cell,
                    hidden_hidden,
                    offset_cell,
                    offset_hidden,
                )
                run = term if run is None else compose(run, term)
                hidden_ref[group, 0, rows, :] = run[2]
                hidden_ref[group, 1, rows, :] = run[3]
                hidden_ref[group, 2, rows, :] = run[5]
                forget = sigmoid(pre_forget)
                output = sigmoid(pre_output)
                squashed = jnp.tanh(fresh)
                hidden_cell = output * (1.0 - squashed * squashed) * forget
                hidden_hidden = output * (1.0 - output) * out_weight * squashed
                cell, hidden = (
                    forget * cell + fresh,
                    hidden_cell * cell + hidden_hidden * hidden + output * squashed,
                )
            before, total = sub_blocks(run, compose, UNIT)
            for index, term in enumerate(before):
                prefix_ref[group, index] = term
            for index, term in enumerate(total):
                totals_ref[pl.ds(group * SUB + index, 1), :] = term[SUB - 1 : SUB, :]
            for index in range(len(total), SUB):
                totals_ref[pl.ds(group * SUB + index, 1), :] = jnp.zeros((1, LANES), F32)
            group += 1


def second(me, own_xor, received, kept, prefixes, weight):
    count = len(received) + 1
    steps = kept[0].shape[2]
    groups = sum(k.shape[0] for k in kept)
    return pl.pallas_call(
        functools.partial(second_kernel, count, own_xor, len(kept)),
        out_shape=(
            jax.ShapeDtypeStruct((groups, 3, steps, LANES), F32),
            jax.ShapeDtypeStruct((groups, 6, SUB, LANES), F32),
            jax.ShapeDtypeStruct((groups * SUB, LANES), F32),
        ),
        in_specs=[pl.BlockSpec(memory_space=pltpu.SMEM)] + vmem(count - 1 + 2 * len(kept) + 1),
        out_specs=vmem(3),
        cost_estimate=cost(100 * groups * steps * LANES, 24 * groups * steps * LANES),
        name="second",
    )(me, *received, *kept, *prefixes, weight)


def last_kernel(count, own_xor, me_ref, *refs):
    received = refs[: count - 1]
    hidden_ref, prefix_ref, out_ref, turn_ref = refs[count - 1 :]
    groups, _, steps, _ = hidden_ref.shape
    runs = steps // SUB
    for group in range(groups):
        cell, hidden = arriving(me_ref, count, own_xor, received, group, False)
        a, b, c, d, u, v = (prefix_ref[group, j] for j in range(6))
        cell, hidden = a * cell + b * hidden + u, c * cell + d * hidden + v
        for i in range(runs):
            rows = pl.ds(i * SUB, SUB)
            turn_ref[pl.ds(i, SUB, stride=runs), :] = (
                hidden_ref[group, 0, rows, :] * cell
                + hidden_ref[group, 1, rows, :] * hidden
                + hidden_ref[group, 2, rows, :]
            )
        out_ref[pl.ds(group * LANES, LANES), :] = turn_ref[...].T


def last(me, own_xor, received, hiddens, prefix):
    count = len(received) + 1
    groups, _, steps, _ = hiddens.shape
    return pl.pallas_call(
        functools.partial(last_kernel, count, own_xor),
        out_shape=jax.ShapeDtypeStruct((groups * LANES, steps), F32),
        in_specs=[pl.BlockSpec(memory_space=pltpu.SMEM)] + vmem(count + 1),
        out_specs=pl.BlockSpec(memory_space=pltpu.VMEM),
        scratch_shapes=[pltpu.VMEM((steps, LANES), F32)],
        cost_estimate=cost(10 * groups * steps * LANES, 16 * groups * steps * LANES),
        name="last",
    )(me, *received, hiddens, prefix)


def shards(tokens, in_weight, recur_weight, gate_bias, forget_offset):
    steps = tokens.shape[0]
    channels = recur_weight.shape[0]
    groups = channels // LANES
    per_owner = channels * GATES
    owners = lax.axis_size("chan")
    chips = owners // 2
    blocks = lax.axis_size("tm")
    me = lax.axis_index("chan").astype(jnp.int32)
    chip, core = me // 2, me % 2
    when = lax.axis_index("tm").astype(jnp.int32)[None]
    own_xor = blocks & (blocks - 1) == 0

    bias = gate_bias.T
    weight = recur_weight.T
    offset = jnp.broadcast_to(
        forget_offset.reshape(SUB, steps // SUB).T.reshape(steps, 1), (steps, LANES)
    )

    def to_core(value):
        return lax.ppermute(value, "chan", [(i, i ^ 1) for i in range(owners)])

    def to_chip(value, away):
        pairs = [(i, (i + 2 * away) % owners) for i in range(owners)]
        return lax.ppermute(value, "chan", pairs)

    def to_blocks(value):
        if own_xor:
            return [
                lax.ppermute(value, "tm", [(i, i ^ k) for i in range(blocks)])
                for k in range(1, blocks)
            ]
        return [
            lax.ppermute(value, "tm", [(i, i + k) for i in range(blocks - k)])
            for k in range(1, blocks)
        ]

    chunks = [(g * GROUP, GROUP) for g in range(groups)]
    arrived = [[] for _ in chunks]
    for away in range(1, chips):
        target = (chip + away) % chips
        who = jnp.stack([2 * target + 1 - core, 2 * target + core])
        for slot, (start, width) in enumerate(chunks):
            give, keep = products(who, tokens, in_weight, start, width, per_owner, 256)
            code = encoded(keep, to_core(give))
            arrived[slot].append(to_chip(code, away))
    who = jnp.stack([2 * chip + 1 - core, me])
    kept, prefixes, totals = [], [], None
    for slot, (start, width) in enumerate(chunks):
        give, keep = products(who, tokens, in_weight, start, width, per_owner, 256)
        k, p, totals = first(
            keep,
            to_core(give),
            arrived[slot],
            bias[:, start // GATES : (start + width) // GATES],
            weight[:, start // GATES : (start + width) // GATES],
            offset,
            [] if totals is None else [totals],
        )
        kept.append(k)
        prefixes.append(p)
    hiddens, prefix, totals = second(when, own_xor, to_blocks(totals), kept, prefixes, weight)
    return last(when, own_xor, to_blocks(totals), hiddens, prefix)


def solution(mesh):
    placed = (
        P(("groups", "tm"), "chan"),
        P("chan", None),
        P("chan", None),
        P("chan", None),
        P(("groups", "tm")),
    )
    return jax.shard_map(
        shards, mesh=mesh, in_specs=placed, out_specs=P("chan", ("groups", "tm")), check_vma=False
    )
```

time: 187 us -> 81 us (0.43)
  Pallas kernels: 0 us -> 48.7 us
  waiting for transfers between devices: 48.7 us -> 8.71 us
  local copies, waits for them, and re-layouts: 45.1 us -> 5.48 us
  other arithmetic: 34.9 us -> 1.3 us
  blocking collectives: 27 us -> 0 us
  between operations: 16.7 us -> 0.12 us
  starting transfers between devices: 3.46 us -> 16 us
  matrix products: 10.2 us -> 0 us
    pallas_call x0 -> x18, Pallas kernels: none -> 48.7 us  [the longest x8 27.1 us: products(): pl.pallas_call(product_kernel, out_shape=(out, out), grid_spec=pltpu.Pref...]
    reduce_scatter x1 -> x0, waiting for transfers between devices: 47.3 us -> none  [shards(): lax.psum_scatter(lax.dot_general(in_weight, tokens, (((0,), (1,)), ((), (...]
    slice x305 -> x2, local copies, waits for them, and re-layouts: 31.7 us -> 1.18 us  [the longest x1 0.6 us: shards(): bias[:, start // GATES:(start + width) // GATES]]
    all_gather x2 -> x0, blocking collectives: 27 us -> none  [shards(): everyone = lax.all_gather(packed, 'tm', axis=0, tiled=True)]
    add x138 -> x0, other arithmetic: 16 us -> none  [the longest x72 3.85 us: shards(): prefix = lax.associative_scan(compose, terms, axis=1)]
    concatenate x73 -> x0, other arithmetic: 14.6 us -> none  [the longest x69 14.6 us: shards(): prefix = lax.associative_scan(compose, terms, axis=1)]
    ppermute x1 -> x18, starting transfers between devices: 3.42 us -> 16 us  [the longest x6 8.77 us: to_blocks(): lax.ppermute(value, 'tm', [(i, i ^ k) for i in range(blocks)])]
    pad x146 -> x0, local copies, waits for them, and re-layouts: 10.8 us -> none  [the longest x138 10.7 us: shards(): prefix = lax.associative_scan(compose, terms, axis=1)]
  transfers between devices with their start and end apart: 2 -> 18, of which waited for: 2 -> 5; matrix products, arithmetic and copies ran while one was open for 0% -> 3% of each run, Pallas kernels for 0% -> 47%
where the time goes in v1:
time: 81 us; the launch traced here: 80.3 us
  Pallas kernels  48.7 us (60%)
  starting transfers between devices  16 us (20%)
  waiting for transfers between devices  8.71 us (11%)
  local copies, waits for them, and re-layouts  5.48 us (7%)
  other arithmetic  1.3 us (2%)
    pallas_call x8, Pallas kernels, products(): pl.pallas_call(product_kernel, out_shape=(out, out), grid_spec=pltpu.Pref...  27.1 us
    pallas_call x4, Pallas kernels, first(): pl.pallas_call(functools.partial(first_kernel, groups, len(codes), len(ea...  8.93 us
    ppermute x6, starting transfers between devices, to_blocks(): lax.ppermute(value, 'tm', [(i, i ^ k) for i in range(blocks)])  8.77 us
    ppermute x6, waiting for transfers between devices, to_blocks(): lax.ppermute(value, 'tm', [(i, i ^ k) for i in range(blocks)])  7.66 us
    pallas_call x4, Pallas kernels, encoded(): pl.pallas_call(encode_kernel, out_shape=jax.ShapeDtypeStruct((rows, LANES...  7.58 us
    ppermute x4, starting transfers between devices, to_chip(): return lax.ppermute(value, 'chan', pairs)  5 us
    unnamed x44, local copies, waits for them, and re-layouts  3.36 us
    pallas_call x1, Pallas kernels, second(): pl.pallas_call(functools.partial(second_kernel, count, own_xor, len(kept)...  3.03 us
  transfers between devices with their start and end apart: 18, of which 5 were waited for; matrix products, arithmetic and copies ran while one was open for 3% of the time, Pallas kernels for 47%

profile of v1, /device:TPU:0, one launch (start us, length us, event | category | flops | bytes accessed | tf_op | source)
XLA Modules:
  0.0 80.3 jit_solution(9619809565982857790)
XLA Ops:
  0.0 0.7 pad_add_fusion.1._
  0.7 3.3 %products.15 = (f32[128,512]{1,0:T(8,128)}, f32[128,512]{1,0:T(8,128)}) custom-call(s32[2]{0:T(128)} %pad_add_fusion.1._, bf16[128,1024]{1,0:T(8,128)(2,1)} %x_ref.15, bf16[1024,8192]{1,0:T(8,128)(2,1)} %keep_w_ref.15, bf16[1024,8192]{1,0:T(8,128)(2,1)} %keep_w_ref.15), custom_call_target="tpu_custom_call" | custom-call | flops 268435456 | bytes 2621440 | tf_op jit(solution)/shard_map/products/pallas_call | solution.py:42
  4.5 3.4 %products.13 = (f32[128,512]{1,0:T(8,128)}, f32[128,512]{1,0:T(8,128)}) custom-call(s32[2]{0:T(128)} %pad_add_fusion.1._, bf16[128,1024]{1,0:T(8,128)(2,1)} %x_ref.15, bf16[1024,8192]{1,0:T(8,128)(2,1)} %keep_w_ref.15, bf16[1024,8192]{1,0:T(8,128)(2,1)} %keep_w_ref.15), custom_call_target="tpu_custom_call" | custom-call | flops 268435456 | bytes 2621440 | tf_op jit(solution)/shard_map/products/pallas_call | solution.py:42
  7.9 3.4 %products.11 = (f32[128,512]{1,0:T(8,128)}, f32[128,512]{1,0:T(8,128)}) custom-call(s32[2]{0:T(128)} %pad_add_fusion.1._, bf16[128,1024]{1,0:T(8,128)(2,1)} %x_ref.15, bf16[1024,8192]{1,0:T(8,128)(2,1)} %keep_w_ref.15, bf16[1024,8192]{1,0:T(8,128)(2,1)} %keep_w_ref.15), custom_call_target="tpu_custom_call" | custom-call | flops 268435456 | bytes 2621440 | tf_op jit(solution)/shard_map/products/pallas_call | solution.py:42
  11.7 3.4 %products.9 = (f32[128,512]{1,0:T(8,128)}, f32[128,512]{1,0:T(8,128)}) custom-call(s32[2]{0:T(128)} %pad_add_fusion.1._, bf16[128,1024]{1,0:T(8,128)(2,1)} %x_ref.15, bf16[1024,8192]{1,0:T(8,128)(2,1)} %keep_w_ref.15, bf16[1024,8192]{1,0:T(8,128)(2,1)} %keep_w_ref.15), custom_call_target="tpu_custom_call" | custom-call | flops 268435456 | bytes 2621440 | tf_op jit(solution)/shard_map/products/pallas_call | solution.py:42
  15.8 3.3 %products.14 = (f32[128,512]{1,0:T(8,128)}, f32[128,512]{1,0:T(8,128)}) custom-call(s32[2]{0:T(128)} %pad_add_fusion._, bf16[128,1024]{1,0:T(8,128)(2,1)} %x_ref.15, bf16[1024,8192]{1,0:T(8,128)(2,1)} %keep_w_ref.15, bf16[1024,8192]{1,0:T(8,128)(2,1)} %keep_w_ref.15), custom_call_target="tpu_custom_call" | custom-call | flops 268435456 | bytes 2621440 | tf_op jit(solution)/shard_map/products/pallas_call | solution.py:42
  19.6 3.4 %products.12 = (f32[128,512]{1,0:T(8,128)}, f32[128,512]{1,0:T(8,128)}) custom-call(s32[2]{0:T(128)} %pad_add_fusion._, bf16[128,1024]{1,0:T(8,128)(2,1)} %x_ref.15, bf16[1024,8192]{1,0:T(8,128)(2,1)} %keep_w_ref.15, bf16[1024,8192]{1,0:T(8,128)(2,1)} %keep_w_ref.15), custom_call_target="tpu_custom_call" | custom-call | flops 268435456 | bytes 2621440 | tf_op jit(solution)/shard_map/products/pallas_call | solution.py:42
  23.1 3.4 %products.10 = (f32[128,512]{1,0:T(8,128)}, f32[128,512]{1,0:T(8,128)}) custom-call(s32[2]{0:T(128)} %pad_add_fusion._, bf16[128,1024]{1,0:T(8,128)(2,1)} %x_ref.15, bf16[1024,8192]{1,0:T(8,128)(2,1)} %keep_w_ref.15, bf16[1024,8192]{1,0:T(8,128)(2,1)} %keep_w_ref.15), custom_call_target="tpu_custom_call" | custom-call | flops 268435456 | bytes 2621440 | tf_op jit(solution)/shard_map/products/pallas_call | solution.py:42
  26.5 3.5 %products.8 = (f32[128,512]{1,0:T(8,128)}, f32[128,512]{1,0:T(8,128)}) custom-call(s32[2]{0:T(128)} %pad_add_fusion._, bf16[128,1024]{1,0:T(8,128)(2,1)} %x_ref.15, bf16[1024,8192]{1,0:T(8,128)(2,1)} %keep_w_ref.15, bf16[1024,8192]{1,0:T(8,128)(2,1)} %keep_w_ref.15), custom_call_target="tpu_custom_call" | custom-call | flops 268435456 | bytes 2621440 | tf_op jit(solution)/shard_map/products/pallas_call | solution.py:42
  30.0 1.9 %encode.7 = bf16[520,128]{1,0:T(8,128)(2,1)} custom-call(f32[128,512]{1,0:T(8,128)} %get-tuple-element.50.mine_ref, f32[128,512]{1,0:T(8,128)} %copy-done.7), custom_call_target="tpu_custom_call" | custom-call | flops 1310720 | bytes 655360 | tf_op jit(solution)/shard_map/encode/pallas_call | solution.py:85
  32.6 2.9 %collective-permute-start.11 = (bf16[520,128]{1,0:T(8,128)(2,1)}, bf16[520,128]{1,0:T(8,128)(2,1)S(1)}, u32[]{:S(2)}, u32[]{:S(2)}) collective-permute-start(bf16[520,128]{1,0:T(8,128)(2,1)} %encode.7), channel_id=1, source_target_pairs={{0,2},{1,3},{2,0},{3,1},{4,6},{5,7},{6,4},{7,5},{8,10},{9,11},{10,... | collective-permute-start | bytes 399368 | tf_op jit(solution)/shard_map/ppermute | solution.py:409
  36.3 1.9 %encode.6 = bf16[520,128]{1,0:T(8,128)(2,1)} custom-call(f32[128,512]{1,0:T(8,128)} %get-tuple-element.46.mine_ref, f32[128,512]{1,0:T(8,128)} %copy-done.4), custom_call_target="tpu_custom_call" | custom-call | flops 1310720 | bytes 655360 | tf_op jit(solution)/shard_map/encode/pallas_call | solution.py:85
  38.2 1.9 %encode.5 = bf16[520,128]{1,0:T(8,128)(2,1)} custom-call(f32[128,512]{1,0:T(8,128)} %get-tuple-element.42.mine_ref, f32[128,512]{1,0:T(8,128)} %copy-done.5), custom_call_target="tpu_custom_call" | custom-call | flops 1310720 | bytes 655360 | tf_op jit(solution)/shard_map/encode/pallas_call | solution.py:85
  40.1 1.9 %encode.4 = bf16[520,128]{1,0:T(8,128)(2,1)} custom-call(f32[128,512]{1,0:T(8,128)} %get-tuple-element.38.mine_ref, f32[128,512]{1,0:T(8,128)} %copy-done.6), custom_call_target="tpu_custom_call" | custom-call | flops 1310720 | bytes 655360 | tf_op jit(solution)/shard_map/encode/pallas_call | solution.py:85
  42.1 2.0 %collective-permute-start.5 = (bf16[520,128]{1,0:T(8,128)(2,1)}, bf16[520,128]{1,0:T(8,128)(2,1)S(1)}, u32[]{:S(2)}, u32[]{:S(2)}) collective-permute-start(bf16[520,128]{1,0:T(8,128)(2,1)} %encode.5), channel_id=1, source_target_pairs={{0,2},{1,3},{2,0},{3,1},{4,6},{5,7},{6,4},{7,5},{8,10},{9,11},{10,... | collective-permute-start | bytes 399368 | tf_op jit(solution)/shard_map/ppermute | solution.py:409
  44.7 0.7 broadcast_in_dim.12.refs_5_
  45.4 2.2 %first.4 = (f32[1,3,128,128]{3,2,1,0:T(8,128)}, f32[1,5,8,128]{3,2,1,0:T(8,128)}, f32[8,128]{1,0:T(8,128)}) custom-call(f32[128,512]{1,0:T(8,128)} %get-tuple-element.48.refs_0_, f32[128,512]{1,0:T(8,128)} %copy-done.3, bf16[520,128]{1,0:T(8,128)(2,1)} %copy-done.9, f32[4,128]{1,0:T(4,128)} %get-tuple-element.67.refs_3_, ...), custom_call_target="tpu_custom_call" | custom-call | flops 3932160 | bytes 1310720 | tf_op jit(solution)/shard_map/first/pallas_call | solution.py:226
  47.6 1.0 %collective-permute-done.8.refs_2_ = bf16[520,128]{1,0:T(8,128)(2,1)S(1)} collective-permute-done((bf16[520,128]{1,0:T(8,128)(2,1)}, bf16[520,128]{1,0:T(8,128)(2,1)S(1)}, u32[]{:S(2)}, u32[]{:S(2)}) %collective-permute-start.8) | collective-permute-done | bytes 133152 | tf_op jit(solution)/shard_map/ppermute | solution.py:409
  49.3 2.2 %first.5 = (f32[1,3,128,128]{3,2,1,0:T(8,128)}, f32[1,5,8,128]{3,2,1,0:T(8,128)}, f32[16,128]{1,0:T(8,128)}) custom-call(f32[128,512]{1,0:T(8,128)} %get-tuple-element.44.refs_0_, f32[128,512]{1,0:T(8,128)} %copy-done.1, bf16[520,128]{1,0:T(8,128)(2,1)} %copy-done.11, f32[4,128]{1,0:T(4,128)} %get-tuple-element.68.refs_3_, ...), custom_call_target="tpu_custom_call" | custom-call | flops 3932160 | bytes 1310720 | tf_op jit(solution)/shard_map/first/pallas_call | solution.py:226
  51.6 0.7 copy-done.2
  52.3 2.2 %first.6 = (f32[1,3,128,128]{3,2,1,0:T(8,128)}, f32[1,5,8,128]{3,2,1,0:T(8,128)}, f32[24,128]{1,0:T(8,128)}) custom-call(f32[128,512]{1,0:T(8,128)} %get-tuple-element.40.refs_0_, f32[128,512]{1,0:T(8,128)} %copy-done.2, bf16[520,128]{1,0:T(8,128)(2,1)} %copy-done.10, f32[4,128]{1,0:T(4,128)} %get-tuple-element.69.refs_3_, ...), custom_call_target="tpu_custom_call" | custom-call | flops 3932160 | bytes 1310720 | tf_op jit(solution)/shard_map/first/pallas_call | solution.py:226
  54.6 0.7 copy-done
  55.3 2.3 %first.7 = (f32[1,3,128,128]{3,2,1,0:T(8,128)}, f32[1,5,8,128]{3,2,1,0:T(8,128)}, f32[32,128]{1,0:T(8,128)}) custom-call(f32[128,512]{1,0:T(8,128)} %get-tuple-element.36.refs_0_, f32[128,512]{1,0:T(8,128)} %copy-done, bf16[520,128]{1,0:T(8,128)(2,1)} %copy-done.8, f32[4,128]{1,0:T(4,128)} %get-tuple-element.70.refs_3_, f32[2,128]{1,0:T(2,128)} %get-tuple-element.74.refs_4_, ...), custom_call_target="tpu_custom_call" | custom-call | flops 3932160 | bytes 1310720 | tf_op jit(solution)/shard_map/first/pallas_call | solution.py:226
  57.5 1.6 %collective-permute-start.12 = (f32[32,128]{1,0:T(8,128)}, f32[32,128]{1,0:T(8,128)S(1)}, u32[]{:S(2)}, u32[]{:S(2)}) collective-permute-start(f32[32,128]{1,0:T(8,128)} %get-tuple-element.55), channel_id=1, source_target_pairs={{0,4},{4,0},{8,12},{12,8},{1,5},{5,1},{9,13},{13,9},{2,6},{6,2},{1... | collective-permute-start | bytes 49160 | tf_op jit(solution)/shard_map/ppermute | solution.py:414
  59.1 2.6 %collective-permute-start.13 = (f32[32,128]{1,0:T(8,128)}, f32[32,128]{1,0:T(8,128)S(1)}, u32[]{:S(2)}, u32[]{:S(2)}) collective-permute-start(f32[32,128]{1,0:T(8,128)} %get-tuple-element.55), channel_id=1, source_target_pairs={{0,8},{4,12},{8,0},{12,4},{1,9},{5,13},{9,1},{13,5},{2,10},{6,14},... | collective-permute-start | bytes 49160 | tf_op jit(solution)/shard_map/ppermute | solution.py:414
  61.9 2.1 %collective-permute-done.13.refs_1_ = f32[32,128]{1,0:T(8,128)S(1)} collective-permute-done((f32[32,128]{1,0:T(8,128)}, f32[32,128]{1,0:T(8,128)S(1)}, u32[]{:S(2)}, u32[]{:S(2)}) %collective-permute-start.13) | collective-permute-done | bytes 16416 | tf_op jit(solution)/shard_map/ppermute | solution.py:414
  64.0 3.4 %collective-permute-done.14.refs_2_ = f32[32,128]{1,0:T(8,128)S(1)} collective-permute-done((f32[32,128]{1,0:T(8,128)}, f32[32,128]{1,0:T(8,128)S(1)}, u32[]{:S(2)}, u32[]{:S(2)}) %collective-permute-start.14) | collective-permute-done | bytes 16416 | tf_op jit(solution)/shard_map/ppermute | solution.py:414
  68.1 3.0 %second.1 = (f32[4,3,128,128]{3,2,1,0:T(8,128)}, f32[4,6,8,128]{3,2,1,0:T(8,128)}, f32[32,128]{1,0:T(8,128)}) custom-call(s32[1]{0:T(128)} %bitcast.me_ref, f32[32,128]{1,0:T(8,128)} %copy-done.12, f32[32,128]{1,0:T(8,128)} %copy-done.13, f32[32,128]{1,0:T(8,128)} %copy-done.14, f32[1,3,128,128]{3,2,1,0:T(8,128)} %get-tuple-element.56.refs_3_, ...), custom_call_target="tpu_custom_call" | custom-call | flops 6553600 | bytes 1572864 | tf_op jit(solution)/shard_map/second/pallas_call | solution.py:338
  71.1 0.8 collective-permute-start.16
  71.9 3.6 %collective-permute-start.17 = (f32[32,128]{1,0:T(8,128)}, f32[32,128]{1,0:T(8,128)S(1)}, u32[]{:S(2)}, u32[]{:S(2)}) collective-permute-start(f32[32,128]{1,0:T(8,128)} %get-tuple-element.64), channel_id=1, source_target_pairs={{0,12},{4,8},{8,4},{12,0},{1,13},{5,9},{9,5},{13,1},{2,14},{6,10},... | collective-permute-start | bytes 49160 | tf_op jit(solution)/shard_map/ppermute | solution.py:414
  76.0 1.6 %collective-permute-done.17.refs_2_ = f32[32,128]{1,0:T(8,128)S(1)} collective-permute-done((f32[32,128]{1,0:T(8,128)}, f32[32,128]{1,0:T(8,128)S(1)}, u32[]{:S(2)}, u32[]{:S(2)}) %collective-permute-start.17) | collective-permute-done | bytes 16416 | tf_op jit(solution)/shard_map/ppermute | solution.py:414
  78.2 2.1 %last.1 = f32[512,128]{1,0:T(8,128)} custom-call(s32[1]{0:T(128)} %bitcast.me_ref, f32[32,128]{1,0:T(8,128)} %copy-done.15, f32[32,128]{1,0:T(8,128)} %copy-done.16, f32[32,128]{1,0:T(8,128)} %copy-done.17, f32[4,3,128,128]{3,2,1,0:T(8,128)} %get-tuple-element.65.refs_3_, f32[4,6,8,128]{3,2,1,0:T(8,128)} %get-tuple-element.66.refs_4_), custom_call_target="tpu_custom_call" | custom-call | flops 655360 | bytes 1048576 | tf_op jit(solution)/shard_map/last/pallas_call | solution.py:374
  (74 shorter events, 7.2 us)
Async XLA Ops:
  4.0 19.0 %collective-permute-start.10 = (f32[128,512]{1,0:T(8,128)}, f32[128,512]{1,0:T(8,128)S(1)}, u32[]{:S(2)}, u32[]{:S(2)}) collective-permute-start(f32[128,512]{1,0:T(8,128)} %get-tuple-element.51), channel_id=1, source_target_pairs={{0,1},{1,0},{2,3},{3,2},{4,5},{5,4},{6,7},{7,6},{8,9},{9,8},{10,11... | collective-permute-start | bytes 786440 | tf_op jit(solution)/shard_map/ppermute | solution.py:405
  7.8 24.1 %collective-permute-start.7 = (f32[128,512]{1,0:T(8,128)}, f32[128,512]{1,0:T(8,128)S(1)}, u32[]{:S(2)}, u32[]{:S(2)}) collective-permute-start(f32[128,512]{1,0:T(8,128)} %get-tuple-element.47), channel_id=1, source_target_pairs={{0,1},{1,0},{2,3},{3,2},{4,5},{5,4},{6,7},{7,6},{8,9},{9,8},{10,11... | collective-permute-start | bytes 786440 | tf_op jit(solution)/shard_map/ppermute | solution.py:405
  11.2 21.2 %collective-permute-start.4 = (f32[128,512]{1,0:T(8,128)}, f32[128,512]{1,0:T(8,128)S(1)}, u32[]{:S(2)}, u32[]{:S(2)}) collective-permute-start(f32[128,512]{1,0:T(8,128)} %get-tuple-element.43), channel_id=1, source_target_pairs={{0,1},{1,0},{2,3},{3,2},{4,5},{5,4},{6,7},{7,6},{8,9},{9,8},{10,11... | collective-permute-start | bytes 786440 | tf_op jit(solution)/shard_map/ppermute | solution.py:405
  15.1 17.4 %collective-permute-start.1 = (f32[128,512]{1,0:T(8,128)}, f32[128,512]{1,0:T(8,128)S(1)}, u32[]{:S(2)}, u32[]{:S(2)}) collective-permute-start(f32[128,512]{1,0:T(8,128)} %get-tuple-element.39), channel_id=1, source_target_pairs={{0,1},{1,0},{2,3},{3,2},{4,5},{5,4},{6,7},{7,6},{8,9},{9,8},{10,11... | collective-permute-start | bytes 786440 | tf_op jit(solution)/shard_map/ppermute | solution.py:405
  19.1 22.9 %collective-permute-start.9 = (f32[128,512]{1,0:T(8,128)}, f32[128,512]{1,0:T(8,128)S(1)}, u32[]{:S(2)}, u32[]{:S(2)}) collective-permute-start(f32[128,512]{1,0:T(8,128)} %get-tuple-element.49), channel_id=1, source_target_pairs={{0,1},{1,0},{2,3},{3,2},{4,5},{5,4},{6,7},{7,6},{8,9},{9,8},{10,11... | collective-permute-start | bytes 786440 | tf_op jit(solution)/shard_map/ppermute | solution.py:405
  23.0 3.5 %copy-start.7 = (f32[128,512]{1,0:T(8,128)}, f32[128,512]{1,0:T(8,128)S(1)}, u32[]{:S(2)}) copy-start(f32[128,512]{1,0:T(8,128)S(1)} %collective-permute-done.10.theirs_ref) | copy-start | bytes 786436
  23.0 19.1 %collective-permute-start.6 = (f32[128,512]{1,0:T(8,128)}, f32[128,512]{1,0:T(8,128)S(1)}, u32[]{:S(2)}, u32[]{:S(2)}) collective-permute-start(f32[128,512]{1,0:T(8,128)} %get-tuple-element.45), channel_id=1, source_target_pairs={{0,1},{1,0},{2,3},{3,2},{4,5},{5,4},{6,7},{7,6},{8,9},{9,8},{10,11... | collective-permute-start | bytes 786440 | tf_op jit(solution)/shard_map/ppermute | solution.py:405
  26.5 5.4 %copy-start.21 = (f32[128,512]{1,0:T(8,128)S(1)}, f32[128,512]{1,0:T(8,128)}, u32[]{:S(2)}) copy-start(f32[128,512]{1,0:T(8,128)} %get-tuple-element.41) | copy-start | bytes 786436
  26.5 9.0 %copy-start.19 = (f32[512,4]{0,1:T(4,128)S(1)}, f32[512,4]{0,1:T(4,128)}, u32[]{:S(2)}) copy-start(f32[512,4]{0,1:T(4,128)} %param.8) | copy-start | bytes 24580
  26.5 9.6 %copy-start.20 = (f32[128]{0:T(128)S(1)}, f32[128]{0:T(128)}, u32[]{:S(2)}) copy-start(f32[128]{0:T(128)} %param.9) | copy-start | bytes 1540
  26.5 17.6 %copy-start.18 = (f32[512,2]{0,1:T(2,128)S(1)}, f32[512,2]{0,1:T(2,128)}, u32[]{:S(2)}) copy-start(f32[512,2]{0,1:T(2,128)} %param.7) | copy-start | bytes 12292
  31.9 4.4 %copy-start.4 = (f32[128,512]{1,0:T(8,128)}, f32[128,512]{1,0:T(8,128)S(1)}, u32[]{:S(2)}) copy-start(f32[128,512]{1,0:T(8,128)S(1)} %collective-permute-done.7.theirs_ref) | copy-start | bytes 786436
  31.9 19.6 %collective-permute-start.3 = (f32[128,512]{1,0:T(8,128)S(1)}, f32[128,512]{1,0:T(8,128)S(1)}, u32[]{:S(2)}, u32[]{:S(2)}) collective-permute-start(f32[128,512]{1,0:T(8,128)S(1)} %copy-done.21), channel_id=1, source_target_pairs={{0,1},{1,0},{2,3},{3,2},{4,5},{5,4},{6,7},{7,6},{8,9},{9,8},{10,11... | collective-permute-start | bytes 786440 | tf_op jit(solution)/shard_map/ppermute | solution.py:405
  32.5 5.8 %copy-start.5 = (f32[128,512]{1,0:T(8,128)}, f32[128,512]{1,0:T(8,128)S(1)}, u32[]{:S(2)}) copy-start(f32[128,512]{1,0:T(8,128)S(1)} %collective-permute-done.4.theirs_ref) | copy-start | bytes 786436
  32.5 22.1 %collective-permute-start = (f32[128,512]{1,0:T(8,128)}, f32[128,512]{1,0:T(8,128)S(1)}, u32[]{:S(2)}, u32[]{:S(2)}) collective-permute-start(f32[128,512]{1,0:T(8,128)} %get-tuple-element.37), channel_id=1, source_target_pairs={{0,1},{1,0},{2,3},{3,2},{4,5},{5,4},{6,7},{7,6},{8,9},{9,8},{10,11... | collective-permute-start | bytes 786440 | tf_op jit(solution)/shard_map/ppermute | solution.py:405
  32.6 7.6 %copy-start.6 = (f32[128,512]{1,0:T(8,128)}, f32[128,512]{1,0:T(8,128)S(1)}, u32[]{:S(2)}) copy-start(f32[128,512]{1,0:T(8,128)S(1)} %collective-permute-done.1.theirs_ref) | copy-start | bytes 786436
  32.6 11.5 %collective-permute-start.11 = (bf16[520,128]{1,0:T(8,128)(2,1)}, bf16[520,128]{1,0:T(8,128)(2,1)S(1)}, u32[]{:S(2)}, u32[]{:S(2)}) collective-permute-start(bf16[520,128]{1,0:T(8,128)(2,1)} %encode.7), channel_id=1, source_target_pairs={{0,2},{1,3},{2,0},{3,1},{4,6},{5,7},{6,4},{7,5},{8,10},{9,11},{10,... | collective-permute-start | bytes 399368 | tf_op jit(solution)/shard_map/ppermute | solution.py:409
  42.0 3.4 %copy-start.3 = (f32[128,512]{1,0:T(8,128)}, f32[128,512]{1,0:T(8,128)S(1)}, u32[]{:S(2)}) copy-start(f32[128,512]{1,0:T(8,128)S(1)} %collective-permute-done.9.refs_1_) | copy-start | bytes 786436
  42.0 6.6 %collective-permute-start.8 = (bf16[520,128]{1,0:T(8,128)(2,1)}, bf16[520,128]{1,0:T(8,128)(2,1)S(1)}, u32[]{:S(2)}, u32[]{:S(2)}) collective-permute-start(bf16[520,128]{1,0:T(8,128)(2,1)} %encode.6), channel_id=1, source_target_pairs={{0,2},{1,3},{2,0},{3,1},{4,6},{5,7},{6,4},{7,5},{8,10},{9,11},{10,... | collective-permute-start | bytes 399368 | tf_op jit(solution)/shard_map/ppermute | solution.py:409
  42.1 6.6 %copy-start.1 = (f32[128,512]{1,0:T(8,128)}, f32[128,512]{1,0:T(8,128)S(1)}, u32[]{:S(2)}) copy-start(f32[128,512]{1,0:T(8,128)S(1)} %collective-permute-done.6.refs_1_) | copy-start | bytes 786436
  42.1 9.5 %collective-permute-start.5 = (bf16[520,128]{1,0:T(8,128)(2,1)}, bf16[520,128]{1,0:T(8,128)(2,1)S(1)}, u32[]{:S(2)}, u32[]{:S(2)}) collective-permute-start(bf16[520,128]{1,0:T(8,128)(2,1)} %encode.5), channel_id=1, source_target_pairs={{0,2},{1,3},{2,0},{3,1},{4,6},{5,7},{6,4},{7,5},{8,10},{9,11},{10,... | collective-permute-start | bytes 399368 | tf_op jit(solution)/shard_map/ppermute | solution.py:409
  44.1 10.5 %collective-permute-start.2 = (bf16[520,128]{1,0:T(8,128)(2,1)}, bf16[520,128]{1,0:T(8,128)(2,1)S(1)}, u32[]{:S(2)}, u32[]{:S(2)}) collective-permute-start(bf16[520,128]{1,0:T(8,128)(2,1)} %encode.4), channel_id=1, source_target_pairs={{0,2},{1,3},{2,0},{3,1},{4,6},{5,7},{6,4},{7,5},{8,10},{9,11},{10,... | collective-permute-start | bytes 399368 | tf_op jit(solution)/shard_map/ppermute | solution.py:409
  57.5 4.4 %collective-permute-start.12 = (f32[32,128]{1,0:T(8,128)}, f32[32,128]{1,0:T(8,128)S(1)}, u32[]{:S(2)}, u32[]{:S(2)}) collective-permute-start(f32[32,128]{1,0:T(8,128)} %get-tuple-element.55), channel_id=1, source_target_pairs={{0,4},{4,0},{8,12},{12,8},{1,5},{5,1},{9,13},{13,9},{2,6},{6,2},{1... | collective-permute-start | bytes 49160 | tf_op jit(solution)/shard_map/ppermute | solution.py:414
  59.1 4.9 %collective-permute-start.13 = (f32[32,128]{1,0:T(8,128)}, f32[32,128]{1,0:T(8,128)S(1)}, u32[]{:S(2)}, u32[]{:S(2)}) collective-permute-start(f32[32,128]{1,0:T(8,128)} %get-tuple-element.55), channel_id=1, source_target_pairs={{0,8},{4,12},{8,0},{12,4},{1,9},{5,13},{9,1},{13,5},{2,10},{6,14},... | collective-permute-start | bytes 49160 | tf_op jit(solution)/shard_map/ppermute | solution.py:414
  61.7 5.7 %collective-permute-start.14 = (f32[32,128]{1,0:T(8,128)}, f32[32,128]{1,0:T(8,128)S(1)}, u32[]{:S(2)}, u32[]{:S(2)}) collective-permute-start(f32[32,128]{1,0:T(8,128)} %get-tuple-element.55), channel_id=1, source_target_pairs={{0,12},{4,8},{8,4},{12,0},{1,13},{5,9},{9,5},{13,1},{2,14},{6,10},... | collective-permute-start | bytes 49160 | tf_op jit(solution)/shard_map/ppermute | solution.py:414
  61.9 5.5 %copy-start.12 = (f32[32,128]{1,0:T(8,128)}, f32[32,128]{1,0:T(8,128)S(1)}, u32[]{:S(2)}) copy-start(f32[32,128]{1,0:T(8,128)S(1)} %collective-permute-done.12.refs_0_) | copy-start | bytes 49156
  64.0 3.4 %copy-start.13 = (f32[32,128]{1,0:T(8,128)}, f32[32,128]{1,0:T(8,128)S(1)}, u32[]{:S(2)}) copy-start(f32[32,128]{1,0:T(8,128)S(1)} %collective-permute-done.13.refs_1_) | copy-start | bytes 49156
  71.1 4.4 %collective-permute-start.15 = (f32[32,128]{1,0:T(8,128)}, f32[32,128]{1,0:T(8,128)S(1)}, u32[]{:S(2)}, u32[]{:S(2)}) collective-permute-start(f32[32,128]{1,0:T(8,128)} %get-tuple-element.64), channel_id=1, source_target_pairs={{0,4},{4,0},{8,12},{12,8},{1,5},{5,1},{9,13},{13,9},{2,6},{6,2},{1... | collective-permute-start | bytes 49160 | tf_op jit(solution)/shard_map/ppermute | solution.py:414
  71.1 4.9 %collective-permute-start.16 = (f32[32,128]{1,0:T(8,128)}, f32[32,128]{1,0:T(8,128)S(1)}, u32[]{:S(2)}, u32[]{:S(2)}) collective-permute-start(f32[32,128]{1,0:T(8,128)} %get-tuple-element.64), channel_id=1, source_target_pairs={{0,8},{4,12},{8,0},{12,4},{1,9},{5,13},{9,1},{13,5},{2,10},{6,14},... | collective-permute-start | bytes 49160 | tf_op jit(solution)/shard_map/ppermute | solution.py:414
  71.9 5.7 %collective-permute-start.17 = (f32[32,128]{1,0:T(8,128)}, f32[32,128]{1,0:T(8,128)S(1)}, u32[]{:S(2)}, u32[]{:S(2)}) collective-permute-start(f32[32,128]{1,0:T(8,128)} %get-tuple-element.64), channel_id=1, source_target_pairs={{0,12},{4,8},{8,4},{12,0},{1,13},{5,9},{9,5},{13,1},{2,14},{6,10},... | collective-permute-start | bytes 49160 | tf_op jit(solution)/shard_map/ppermute | solution.py:414
  75.5 2.1 %copy-start.15 = (f32[32,128]{1,0:T(8,128)}, f32[32,128]{1,0:T(8,128)S(1)}, u32[]{:S(2)}) copy-start(f32[32,128]{1,0:T(8,128)S(1)} %collective-permute-done.15.refs_0_) | copy-start | bytes 49156
  76.0 1.6 %copy-start.16 = (f32[32,128]{1,0:T(8,128)}, f32[32,128]{1,0:T(8,128)S(1)}, u32[]{:S(2)}) copy-start(f32[32,128]{1,0:T(8,128)S(1)} %collective-permute-done.16.refs_1_) | copy-start | bytes 49156
  (8 other events, 6.1 us)

commit v2 on v1

--- a/solution.py
+++ b/solution.py
@@ -25,37 +25,64 @@
     return [pl.BlockSpec(memory_space=pltpu.VMEM)] * count
 
 
-def product_kernel(_, x_ref, give_w_ref, keep_w_ref, give_ref, keep_ref):
-    x = x_ref[...]
-    give_ref[...] = jnp.dot(x, give_w_ref[...], preferred_element_type=F32)
-    keep_ref[...] = jnp.dot(x, keep_w_ref[...], preferred_element_type=F32)
-
-
-def products(owners, tokens, in_weight, first, width, per_owner, tile):
+def anywhere(count):
+    return [pl.BlockSpec(memory_space=pl.ANY)] * count
+
+
+def on_chip(value):
+    return pltpu.with_memory_space_constraint(value, pltpu.VMEM)
+
+
+PARAMS = pltpu.CompilerParams(vmem_limit_bytes=16 << 20)
+
+
+def product_kernel(chips, away, first, width, per_owner, tile, tokens_ref, weight_ref, *refs):
+    give_ref, keep_ref, x_ref, w_ref, sems = refs[-5:]
+    me = lax.axis_index("chan")
+    chip, core = me // 2, me % 2
+    target = lax.rem(chip + away, chips)
+    tiles = width // tile
+    tokens_copy = pltpu.make_async_copy(tokens_ref, x_ref, sems.at[2 * tiles])
+    tokens_copy.start()
+    copies = []
+    for which, owner in enumerate((2 * target + 1 - core, 2 * target + core)):
+        for i in range(tiles):
+            slot = which * tiles + i
+            column = pl.multiple_of(owner * per_owner + first + i * tile, tile)
+            copies.append(
+                pltpu.make_async_copy(
+                    weight_ref.at[:, pl.ds(column, tile)], w_ref.at[slot], sems.at[slot]
+                )
+            )
+            copies[-1].start()
+    tokens_copy.wait()
+    for slot, copy in enumerate(copies):
+        out_ref = give_ref if slot < tiles else keep_ref
+        copy.wait()
+        out_ref[:, pl.ds(slot % tiles * tile, tile)] = jnp.dot(
+            x_ref[...], w_ref[slot], preferred_element_type=F32
+        )
+
+
+def products(tokens, in_weight, chips, away, first, width, per_owner, after):
     steps, depth = tokens.shape
-    tiles = width // tile
-
-    def column(which):
-        return lambda i, who: (0, who[which] * (per_owner // tile) + first // tile + i)
-
-    out = jax.ShapeDtypeStruct((steps, width), F32)
+    tile = 2 * LANES
+    slots = 2 * width // tile
+    out = pltpu.VMEM((steps, width), F32)
     return pl.pallas_call(
-        product_kernel,
+        functools.partial(product_kernel, chips, away, first, width, per_owner, tile),
         out_shape=(out, out),
-        grid_spec=pltpu.PrefetchScalarGridSpec(
-            num_scalar_prefetch=1,
-            grid=(tiles,),
-            in_specs=[
-                pl.BlockSpec((steps, depth), lambda i, who: (0, 0)),
-                pl.BlockSpec((depth, tile), column(0)),
-                pl.BlockSpec((depth, tile), column(1)),
-            ],
-            out_specs=[pl.BlockSpec((steps, tile), lambda i, who: (0, i))] * 2,
-        ),
-        compiler_params=pltpu.CompilerParams(dimension_semantics=("arbitrary",)),
+        in_specs=anywhere(2 + len(after)),
+        out_specs=vmem(2),
+        scratch_shapes=[
+            pltpu.VMEM((steps, depth), BF16),
+            pltpu.VMEM((slots, depth, tile), BF16),
+            pltpu.SemaphoreType.DMA((slots + 1,)),
+        ],
+        compiler_params=PARAMS,
         cost_estimate=cost(4 * steps * depth * width, 4 * depth * width + 8 * steps * width),
         name="products",
-    )(owners, tokens, in_weight, in_weight)
+    )(tokens, in_weight, *after)
 
 
 def encode_kernel(mine_ref, theirs_ref, out_ref, sum_ref):
@@ -84,10 +111,11 @@
     rows = steps * (width // LANES) + SUB
     return pl.pallas_call(
         encode_kernel,
-        out_shape=jax.ShapeDtypeStruct((rows, LANES), BF16),
+        out_shape=pltpu.VMEM((rows, LANES), BF16),
         in_specs=vmem(2),
         out_specs=pl.BlockSpec(memory_space=pltpu.VMEM),
         scratch_shapes=[pltpu.VMEM((steps, width), F32)],
+        compiler_params=PARAMS,
         cost_estimate=cost(20 * steps * width, 10 * steps * width),
         name="encode",
     )(mine, theirs)
@@ -148,13 +176,13 @@
     return 1.0 / (1.0 + jnp.exp(-x))
 
 
-def first_kernel(groups, remotes, earlier, *refs):
+def first_kernel(start, groups, remotes, earlier, *refs):
     refs = list(refs)
     mine_ref, theirs_ref = refs[:2]
     codes = refs[2 : 2 + remotes]
     bias_ref, weight_ref, offset_ref = refs[2 + remotes : 5 + remotes]
     totals_before = refs[5 + remotes : 5 + remotes + earlier]
-    kept_ref, prefix_ref, totals_ref, sum_ref = refs[5 + remotes + earlier :]
+    kept_ref, prefix_ref, totals_ref, sum_ref, late_ref = refs[5 + remotes + earlier :]
     steps = mine_ref.shape[0]
     runs = steps // SUB
     blocks = groups * GATES
@@ -165,6 +193,7 @@
     scales = [
         ref[pl.ds(blocks * steps, SUB), :][0:1, :].astype(F32) for ref in codes
     ]
+    late_ref[...] = jnp.broadcast_to(offset_ref[...], (LANES, steps)).T
     lane = lax.broadcasted_iota(jnp.int32, (SUB, LANES), 1)
     quarter = lane // (LANES // GATES)
     inner = lane % (LANES // GATES)
@@ -172,12 +201,12 @@
     for group in range(groups):
         for q in range(GATES):
             block = group * GATES + q
-            cols = pl.ds(block * LANES, LANES)
+            cols = pl.ds(start * GROUP + block * LANES, LANES)
             value = mine_ref[:, cols] + theirs_ref[:, cols]
             for ref, scale in zip(codes, scales):
                 value = value + decoded(ref[pl.ds(block * steps, steps), :].astype(F32), scale)
             sum_ref[q] = value
-        channels = pl.ds(group * LANES, LANES)
+        channels = pl.ds((start + group) * LANES, LANES)
         biases = [
             jnp.broadcast_to(bias_ref[k : k + 1, channels], (SUB, LANES)) for k in range(GATES)
         ]
@@ -196,7 +225,7 @@
                 if k:
                     part = pltpu.roll(part, LANES - k * (LANES // GATES), 1)
                 pre.append(part + biases[k])
-            pre_forget = pre[1] - offset_ref[pl.ds(i * SUB, SUB), :]
+            pre_forget = pre[1] - late_ref[pl.ds(i, SUB, stride=runs), :]
             forget = sigmoid(pre_forget)
             output = sigmoid(pre[3])
             cell = sigmoid(pre[0]) * jnp.tanh(pre[2])
@@ -218,22 +247,25 @@
             totals_ref[pl.ds(done + group * SUB + index, 1), :] = jnp.zeros((1, LANES), F32)
 
 
-def first(mine, theirs, codes, bias, weight, offset, earlier):
-    steps, width = mine.shape
-    groups = width // GROUP
+def first(start, groups, mine, theirs, codes, bias, weight, offset, earlier):
+    steps = mine.shape[0]
     rows = sum(e.shape[0] for e in earlier) + groups * SUB
     count = 5 + len(codes) + len(earlier)
     return pl.pallas_call(
-        functools.partial(first_kernel, groups, len(codes), len(earlier)),
+        functools.partial(first_kernel, start, groups, len(codes), len(earlier)),
         out_shape=(
-            jax.ShapeDtypeStruct((groups, 3, steps, LANES), F32),
-            jax.ShapeDtypeStruct((groups, 5, SUB, LANES), F32),
-            jax.ShapeDtypeStruct((rows, LANES), F32),
+            pltpu.VMEM((groups, 3, steps, LANES), F32),
+            pltpu.VMEM((groups, 5, SUB, LANES), F32),
+            pltpu.VMEM((rows, LANES), F32),
         ),
         in_specs=vmem(count),
         out_specs=vmem(3),
-        scratch_shapes=[pltpu.VMEM((GATES, steps, LANES), F32)],
-        cost_estimate=cost(60 * steps * width, 20 * steps * width),
+        scratch_shapes=[
+            pltpu.VMEM((GATES, steps, LANES), F32),
+            pltpu.VMEM((steps, LANES), F32),
+        ],
+        compiler_params=PARAMS,
+        cost_estimate=cost(60 * steps * groups * GROUP, 20 * steps * groups * GROUP),
         name="first",
     )(mine, theirs, *codes, bias, weight, offset, *earlier)
 
@@ -246,8 +278,8 @@
         yield picked, position < me
 
 
-def arriving(me_ref, count, own_xor, received, group, lower):
-    me = me_ref[0]
+def arriving(count, own_xor, received, group, lower):
+    me = lax.axis_index("tm")
     rows = [ref[pl.ds(group * SUB, SUB), :] for ref in received]
     cell = jnp.zeros((1, LANES), F32)
     hidden = jnp.zeros((1, LANES), F32)
@@ -264,7 +296,7 @@
     return cell, hidden
 
 
-def second_kernel(count, own_xor, chunks, me_ref, *refs):
+def second_kernel(count, own_xor, chunks, *refs):
     refs = list(refs)
     received = refs[: count - 1]
     kept = refs[count - 1 : count - 1 + chunks]
@@ -275,7 +307,7 @@
     for kept_ref, before_ref in zip(kept, prefixes):
         groups, _, steps, _ = kept_ref.shape
         for local in range(groups):
-            cell, hidden = arriving(me_ref, count, own_xor, received, group, True)
+            cell, hidden = arriving(count, own_xor, received, group, True)
             a, c, d, u, v = (before_ref[local, j] for j in range(5))
             cell, hidden = a * cell + u, c * cell + d * hidden + v
             channels = pl.ds(group * LANES, LANES)
@@ -331,31 +363,32 @@
             group += 1
 
 
-def second(me, own_xor, received, kept, prefixes, weight):
+def second(own_xor, received, kept, prefixes, weight):
     count = len(received) + 1
     steps = kept[0].shape[2]
     groups = sum(k.shape[0] for k in kept)
     return pl.pallas_call(
         functools.partial(second_kernel, count, own_xor, len(kept)),
         out_shape=(
-            jax.ShapeDtypeStruct((groups, 3, steps, LANES), F32),
-            jax.ShapeDtypeStruct((groups, 6, SUB, LANES), F32),
-            jax.ShapeDtypeStruct((groups * SUB, LANES), F32),
+            pltpu.VMEM((groups, 3, steps, LANES), F32),
+            pltpu.VMEM((groups, 6, SUB, LANES), F32),
+            pltpu.VMEM((groups * SUB, LANES), F32),
         ),
-        in_specs=[pl.BlockSpec(memory_space=pltpu.SMEM)] + vmem(count - 1 + 2 * len(kept) + 1),
+        in_specs=vmem(count - 1 + 2 * len(kept) + 1),
         out_specs=vmem(3),
+        compiler_params=PARAMS,
         cost_estimate=cost(100 * groups * steps * LANES, 24 * groups * steps * LANES),
         name="second",
-    )(me, *received, *kept, *prefixes, weight)
-
-
-def last_kernel(count, own_xor, me_ref, *refs):
+    )(*received, *kept, *prefixes, weight)
+
+
+def last_kernel(count, own_xor, *refs):
     received = refs[: count - 1]
     hidden_ref, prefix_ref, out_ref, turn_ref = refs[count - 1 :]
     groups, _, steps, _ = hidden_ref.shape
     runs = steps // SUB
     for group in range(groups):
-        cell, hidden = arriving(me_ref, count, own_xor, received, group, False)
+        cell, hidden = arriving(count, own_xor, received, group, False)
         a, b, c, d, u, v = (prefix_ref[group, j] for j in range(6))
         cell, hidden = a * cell + b * hidden + u, c * cell + d * hidden + v
         for i in range(runs):
@@ -368,18 +401,19 @@
         out_ref[pl.ds(group * LANES, LANES), :] = turn_ref[...].T
 
 
-def last(me, own_xor, received, hiddens, prefix):
+def last(own_xor, received, hiddens, prefix):
     count = len(received) + 1
     groups, _, steps, _ = hiddens.shape
     return pl.pallas_call(
         functools.partial(last_kernel, count, own_xor),
         out_shape=jax.ShapeDtypeStruct((groups * LANES, steps), F32),
-        in_specs=[pl.BlockSpec(memory_space=pltpu.SMEM)] + vmem(count + 1),
+        in_specs=vmem(count + 1),
+        compiler_params=PARAMS,
         out_specs=pl.BlockSpec(memory_space=pltpu.VMEM),
         scratch_shapes=[pltpu.VMEM((steps, LANES), F32)],
         cost_estimate=cost(10 * groups * steps * LANES, 16 * groups * steps * LANES),
         name="last",
-    )(me, *received, hiddens, prefix)
+    )(*received, hiddens, prefix)
 
 
 def shards(tokens, in_weight, recur_weight, gate_bias, forget_offset):
@@ -390,61 +424,49 @@
     owners = lax.axis_size("chan")
     chips = owners // 2
     blocks = lax.axis_size("tm")
-    me = lax.axis_index("chan").astype(jnp.int32)
-    chip, core = me // 2, me % 2
-    when = lax.axis_index("tm").astype(jnp.int32)[None]
     own_xor = blocks & (blocks - 1) == 0
 
-    bias = gate_bias.T
-    weight = recur_weight.T
-    offset = jnp.broadcast_to(
-        forget_offset.reshape(SUB, steps // SUB).T.reshape(steps, 1), (steps, LANES)
-    )
+    bias = on_chip(gate_bias.T)
+    weight = on_chip(recur_weight.T)
+    offset = on_chip(forget_offset.reshape(1, steps))
 
     def to_core(value):
-        return lax.ppermute(value, "chan", [(i, i ^ 1) for i in range(owners)])
+        return on_chip(lax.ppermute(value, "chan", [(i, i ^ 1) for i in range(owners)]))
 
     def to_chip(value, away):
         pairs = [(i, (i + 2 * away) % owners) for i in range(owners)]
-        return lax.ppermute(value, "chan", pairs)
+        return on_chip(lax.ppermute(value, "chan", pairs))
 
     def to_blocks(value):
         if own_xor:
             return [
-                lax.ppermute(value, "tm", [(i, i ^ k) for i in range(blocks)])
+                on_chip(lax.ppermute(value, "tm", [(i, i ^ k) for i in range(blocks)]))
                 for k in range(1, blocks)
             ]
         return [
-            lax.ppermute(value, "tm", [(i, i + k) for i in range(blocks - k)])
+            on_chip(lax.ppermute(value, "tm", [(i, i + k) for i in range(blocks - k)]))
             for k in range(1, blocks)
         ]
 
-    chunks = [(g * GROUP, GROUP) for g in range(groups)]
-    arrived = [[] for _ in chunks]
+    arrived = [[] for _ in range(groups)]
+    codes = []
     for away in range(1, chips):
-        target = (chip + away) % chips
-        who = jnp.stack([2 * target + 1 - core, 2 * target + core])
-        for slot, (start, width) in enumerate(chunks):
-            give, keep = products(who, tokens, in_weight, start, width, per_owner, 256)
-            code = encoded(keep, to_core(give))
-            arrived[slot].append(to_chip(code, away))
-    who = jnp.stack([2 * chip + 1 - core, me])
-    kept, prefixes, totals = [], [], None
-    for slot, (start, width) in enumerate(chunks):
-        give, keep = products(who, tokens, in_weight, start, width, per_owner, 256)
-        k, p, totals = first(
-            keep,
-            to_core(give),
-            arrived[slot],
-            bias[:, start // GATES : (start + width) // GATES],
-            weight[:, start // GATES : (start + width) // GATES],
-            offset,
-            [] if totals is None else [totals],
-        )
+        for group in range(groups):
+            give, keep = products(
+                tokens, in_weight, chips, away, group * GROUP, GROUP, per_owner, codes[-2:-1]
+            )
+            codes.append(encoded(keep, to_core(give)))
+            arrived[group].append(to_chip(codes[-1], away))
+    give, keep = products(tokens, in_weight, chips, 0, 0, per_owner, per_owner, codes[-1:])
+    given = to_core(give)
+    kept, prefixes, totals = [], [], []
+    for group in range(groups):
+        k, p, total = first(group, 1, keep, given, arrived[group], bias, weight, offset, totals)
+        totals = [total]
         kept.append(k)
         prefixes.append(p)
-    hiddens, prefix, totals = second(when, own_xor, to_blocks(totals), kept, prefixes, weight)
-    return last(when, own_xor, to_blocks(totals), hiddens, prefix)
+    hiddens, prefix, total = second(own_xor, to_blocks(totals[0]), kept, prefixes, weight)
+    return last(own_xor, to_blocks(total), hiddens, prefix)
 
 
 def solution(mesh):

time: 81 us -> 61.6 us (0.76)
  Pallas kernels: 48.7 us -> 16.6 us
  waiting for transfers between devices: 8.71 us -> 19.7 us
  local copies, waits for them, and re-layouts: 5.48 us -> 9.06 us
  other arithmetic: 1.3 us -> 0 us
    pallas_call x16 -> x13, Pallas kernels: 43.6 us -> 14.8 us  [the longest x5 12 us: products(): pl.pallas_call(functools.partial(product_kernel, chips, away, first, widt...]
    ppermute x12 -> x9, waiting for transfers between devices: 1.05 us -> 12.2 us  [the longest x4 8.46 us: to_chip(): return on_chip(lax.ppermute(value, 'chan', pairs))]
    unnamed x44 -> x14, local copies, waits for them, and re-layouts: 3.36 us -> 9.06 us
    pallas_call x1, Pallas kernels: 3.03 us -> 0.8 us  [second(): pl.pallas_call(functools.partial(second_kernel, count, own_xor, len(kept)...]
    another operation x2 -> x0, other arithmetic: 1.3 us -> none  [the longest x1 0.65 us: shards(): who = jnp.stack([2 * target + 1 - core, 2 * target + core])]
    slice x2 -> x0, local copies, waits for them, and re-layouts: 1.18 us -> none  [the longest x1 0.6 us: shards(): bias[:, start // GATES:(start + width) // GATES]]
    pallas_call x1, Pallas kernels: 2.11 us -> 0.95 us  [last(): pl.pallas_call(functools.partial(last_kernel, count, own_xor), out_shape=...]
    ppermute x12 -> x9, starting transfers between devices: 7.23 us -> 6.98 us  [the longest x4 5.02 us: to_chip(): return on_chip(lax.ppermute(value, 'chan', pairs))]
  transfers between devices with their start and end apart: 18 -> 15, of which waited for: 5 -> 11; matrix products, arithmetic and copies ran while one was open for 3% -> 0% of each run, Pallas kernels for 47% -> 8%
where the time goes in v2:
time: 61.6 us; the launch traced here: 61.5 us
  waiting for transfers between devices  19.7 us (32%)
  Pallas kernels  16.6 us (27%)
  starting transfers between devices  15.9 us (26%)
  local copies, waits for them, and re-layouts  9.06 us (15%)
    pallas_call x5, Pallas kernels, products(): pl.pallas_call(functools.partial(product_kernel, chips, away, first, widt...  12 us
    unnamed x14, local copies, waits for them, and re-layouts  9.06 us
    ppermute x6, starting transfers between devices, to_blocks(): lax.ppermute(value, 'tm', [(i, i ^ k) for i in range(blocks)])  8.93 us
    ppermute x4, waiting for transfers between devices, to_chip(): return on_chip(lax.ppermute(value, 'chan', pairs))  8.46 us
    ppermute x6, waiting for transfers between devices, to_blocks(): lax.ppermute(value, 'tm', [(i, i ^ k) for i in range(blocks)])  7.56 us
    ppermute x4, starting transfers between devices, to_chip(): return on_chip(lax.ppermute(value, 'chan', pairs))  5.02 us
    ppermute x5, waiting for transfers between devices, to_core(): lax.ppermute(value, 'chan', [(i, i ^ 1) for i in range(owners)])  3.73 us
    pallas_call x4, Pallas kernels, first(): pl.pallas_call(functools.partial(first_kernel, start, groups, len(codes),...  2.01 us
  transfers between devices with their start and end apart: 15, of which 11 were waited for; matrix products, arithmetic and copies ran while one was open for 0% of the time, Pallas kernels for 8%

profile of v2, /device:TPU:0, one launch (start us, length us, event | category | flops | bytes accessed | tf_op | source)
XLA Modules:
  0.0 61.5 jit_solution(11988579404294118828)
XLA Ops:
  0.0 5.8 %copy-done = bf16[1024,8192]{1,0:T(8,128)(2,1)S(1)} copy-done((bf16[1024,8192]{1,0:T(8,128)(2,1)S(1)}, bf16[1024,8192]{1,0:T(8,128)(2,1)}, u32[]{:S(2)}) %copy-start) | copy-done | bytes 16777240
  5.8 0.9 %copy-done.2 = bf16[128,1024]{1,0:T(8,128)(2,1)S(1)} copy-done((bf16[128,1024]{1,0:T(8,128)(2,1)S(1)}, bf16[128,1024]{1,0:T(8,128)(2,1)}, u32[]{:S(2)}) %copy-start.2) | copy-done | bytes 262168
  6.7 1.5 %products.5 = (f32[128,512]{1,0:T(8,128)S(1)}, f32[128,512]{1,0:T(8,128)S(1)}) custom-call(bf16[128,1024]{1,0:T(8,128)(2,1)S(1)} %copy-done.2, bf16[1024,8192]{1,0:T(8,128)(2,1)S(1)} %copy-done), custom_call_target="tpu_custom_call" | custom-call | flops 268435456 | bytes 2621440 | tf_op jit(solution)/shard_map/products/pallas_call | solution.py:72
  8.2 0.6 collective-permute-start
  8.8 1.2 %collective-permute-done.theirs_ref = f32[128,512]{1,0:T(8,128)S(1)} collective-permute-done((f32[128,512]{1,0:T(8,128)S(1)}, f32[128,512]{1,0:T(8,128)S(1)}, u32[]{:S(2)}, u32[]{:S(2)}) %collective-permute-start) | collective-permute-done | bytes 262176 | tf_op jit(solution)/shard_map/ppermute | solution.py:434
  10.2 2.3 %copy-done.1 = bf16[1024,8192]{1,0:T(8,128)(2,1)S(1)} copy-done((bf16[1024,8192]{1,0:T(8,128)(2,1)S(1)}, bf16[1024,8192]{1,0:T(8,128)(2,1)}, u32[]{:S(2)}) %copy-start.1) | copy-done | bytes 16777240
  12.5 1.5 %products.6 = (f32[128,512]{1,0:T(8,128)S(1)}, f32[128,512]{1,0:T(8,128)S(1)}) custom-call(bf16[128,1024]{1,0:T(8,128)(2,1)S(1)} %copy-done.3, bf16[1024,8192]{1,0:T(8,128)(2,1)S(1)} %copy-done.1, bf16[520,128]{1,0:T(8,128)(2,1)S(1)} %encode.4.refs_0_), custom_call_target="tpu_custom_call" | custom-call | flops 268435456 | bytes 2621440 | tf_op jit(solution)/shard_map/products/pallas_call | solution.py:72
  14.0 0.6 collective-permute-start.1
  14.6 1.2 %collective-permute-done.1.theirs_ref = f32[128,512]{1,0:T(8,128)S(1)} collective-permute-done((f32[128,512]{1,0:T(8,128)S(1)}, f32[128,512]{1,0:T(8,128)S(1)}, u32[]{:S(2)}, u32[]{:S(2)}) %collective-permute-start.1) | collective-permute-done | bytes 262176 | tf_op jit(solution)/shard_map/ppermute | solution.py:434
  15.9 6.0 %products.7 = (f32[128,2048]{1,0:T(8,128)S(1)}, f32[128,2048]{1,0:T(8,128)S(1)}) custom-call(bf16[128,1024]{1,0:T(8,128)(2,1)S(1)} %copy-done.3, bf16[1024,8192]{1,0:T(8,128)(2,1)S(1)} %copy-done.1, bf16[520,128]{1,0:T(8,128)(2,1)S(1)} %encode.5.refs_0_), custom_call_target="tpu_custom_call" | custom-call | flops 1073741824 | bytes 10485760 | tf_op jit(solution)/shard_map/products/pallas_call | solution.py:72
  22.4 1.5 %products.8 = (f32[128,512]{1,0:T(8,128)S(1)}, f32[128,512]{1,0:T(8,128)S(1)}) custom-call(bf16[128,1024]{1,0:T(8,128)(2,1)S(1)} %copy-done.3, bf16[1024,8192]{1,0:T(8,128)(2,1)S(1)} %copy-done.1), custom_call_target="tpu_custom_call" | custom-call | flops 268435456 | bytes 2621440 | tf_op jit(solution)/shard_map/products/pallas_call | solution.py:72
  24.1 1.4 %collective-permute-done.4.theirs_ref = f32[128,512]{1,0:T(8,128)S(1)} collective-permute-done((f32[128,512]{1,0:T(8,128)S(1)}, f32[128,512]{1,0:T(8,128)S(1)}, u32[]{:S(2)}, u32[]{:S(2)}) %collective-permute-start.4) | collective-permute-done | bytes 262176 | tf_op jit(solution)/shard_map/ppermute | solution.py:434
  25.7 1.5 %products.9 = (f32[128,512]{1,0:T(8,128)S(1)}, f32[128,512]{1,0:T(8,128)S(1)}) custom-call(bf16[128,1024]{1,0:T(8,128)(2,1)S(1)} %copy-done.3, bf16[1024,8192]{1,0:T(8,128)(2,1)S(1)} %copy-done.1, bf16[520,128]{1,0:T(8,128)(2,1)S(1)} %encode.6.refs_0_), custom_call_target="tpu_custom_call" | custom-call | flops 268435456 | bytes 2621440 | tf_op jit(solution)/shard_map/products/pallas_call | solution.py:72
  27.4 2.8 %collective-permute-start.8 = (bf16[520,128]{1,0:T(8,128)(2,1)S(1)}, bf16[520,128]{1,0:T(8,128)(2,1)S(1)}, u32[]{:S(2)}, u32[]{:S(2)}) collective-permute-start(bf16[520,128]{1,0:T(8,128)(2,1)S(1)} %encode.6.refs_0_), channel_id=1, source_target_pairs={{0,2},{1,3},{2,0},{3,1},{4,6},{5,7},{6,4},{7,5},{8,10},{9,11},{10,... | collective-permute-start | bytes 399368 | tf_op jit(solution)/shard_map/ppermute | solution.py:438
  30.5 2.1 %collective-permute-start.6 = (bf16[520,128]{1,0:T(8,128)(2,1)S(1)}, bf16[520,128]{1,0:T(8,128)(2,1)S(1)}, u32[]{:S(2)}, u32[]{:S(2)}) collective-permute-start(bf16[520,128]{1,0:T(8,128)(2,1)S(1)} %encode.7), channel_id=1, source_target_pairs={{0,2},{1,3},{2,0},{3,1},{4,6},{5,7},{6,4},{7,5},{8,10},{9,11},{10,... | collective-permute-start | bytes 399368 | tf_op jit(solution)/shard_map/ppermute | solution.py:438
  32.7 2.0 %collective-permute-done.8.refs_2_ = bf16[520,128]{1,0:T(8,128)(2,1)S(1)} collective-permute-done((bf16[520,128]{1,0:T(8,128)(2,1)S(1)}, bf16[520,128]{1,0:T(8,128)(2,1)S(1)}, u32[]{:S(2)}, u32[]{:S(2)}) %collective-permute-start.8) | collective-permute-done | bytes 133152 | tf_op jit(solution)/shard_map/ppermute | solution.py:438
  34.7 0.5 first.4
  35.2 2.3 %collective-permute-done.7.refs_2_ = bf16[520,128]{1,0:T(8,128)(2,1)S(1)} collective-permute-done((bf16[520,128]{1,0:T(8,128)(2,1)S(1)}, bf16[520,128]{1,0:T(8,128)(2,1)S(1)}, u32[]{:S(2)}, u32[]{:S(2)}) %collective-permute-start.7) | collective-permute-done | bytes 133152 | tf_op jit(solution)/shard_map/ppermute | solution.py:438
  37.5 0.5 first.5
  38.0 2.3 %collective-permute-done.6.refs_2_ = bf16[520,128]{1,0:T(8,128)(2,1)S(1)} collective-permute-done((bf16[520,128]{1,0:T(8,128)(2,1)S(1)}, bf16[520,128]{1,0:T(8,128)(2,1)S(1)}, u32[]{:S(2)}, u32[]{:S(2)}) %collective-permute-start.6) | collective-permute-done | bytes 133152 | tf_op jit(solution)/shard_map/ppermute | solution.py:438
  40.4 0.5 first.6
  40.9 1.8 %collective-permute-done.3.refs_2_ = bf16[520,128]{1,0:T(8,128)(2,1)S(1)} collective-permute-done((bf16[520,128]{1,0:T(8,128)(2,1)S(1)}, bf16[520,128]{1,0:T(8,128)(2,1)S(1)}, u32[]{:S(2)}, u32[]{:S(2)}) %collective-permute-start.3) | collective-permute-done | bytes 133152 | tf_op jit(solution)/shard_map/ppermute | solution.py:438
  42.7 0.5 first.7
  43.2 1.9 %collective-permute-start.9 = (f32[32,128]{1,0:T(8,128)S(1)}, f32[32,128]{1,0:T(8,128)S(1)}, u32[]{:S(2)}, u32[]{:S(2)}) collective-permute-start(f32[32,128]{1,0:T(8,128)S(1)} %get-tuple-element.43), channel_id=1, source_target_pairs={{0,4},{4,0},{8,12},{12,8},{1,5},{5,1},{9,13},{13,9},{2,6},{6,2},{1... | collective-permute-start | bytes 49160 | tf_op jit(solution)/shard_map/ppermute | solution.py:443
  45.1 2.6 %collective-permute-start.10 = (f32[32,128]{1,0:T(8,128)S(1)}, f32[32,128]{1,0:T(8,128)S(1)}, u32[]{:S(2)}, u32[]{:S(2)}) collective-permute-start(f32[32,128]{1,0:T(8,128)S(1)} %get-tuple-element.43), channel_id=1, source_target_pairs={{0,8},{4,12},{8,0},{12,4},{1,9},{5,13},{9,1},{13,5},{2,10},{6,14},... | collective-permute-start | bytes 49160 | tf_op jit(solution)/shard_map/ppermute | solution.py:443
  47.7 2.0 %collective-permute-done.10.refs_1_ = f32[32,128]{1,0:T(8,128)S(1)} collective-permute-done((f32[32,128]{1,0:T(8,128)S(1)}, f32[32,128]{1,0:T(8,128)S(1)}, u32[]{:S(2)}, u32[]{:S(2)}) %collective-permute-start.10) | collective-permute-done | bytes 16416 | tf_op jit(solution)/shard_map/ppermute | solution.py:443
  49.7 3.6 %collective-permute-done.11.refs_2_ = f32[32,128]{1,0:T(8,128)S(1)} collective-permute-done((f32[32,128]{1,0:T(8,128)S(1)}, f32[32,128]{1,0:T(8,128)S(1)}, u32[]{:S(2)}, u32[]{:S(2)}) %collective-permute-start.11) | collective-permute-done | bytes 16416 | tf_op jit(solution)/shard_map/ppermute | solution.py:443
  53.4 0.8 %second.1 = (f32[4,3,128,128]{3,2,1,0:T(8,128)S(1)}, f32[4,6,8,128]{3,2,1,0:T(8,128)S(1)}, f32[32,128]{1,0:T(8,128)S(1)}) custom-call(f32[32,128]{1,0:T(8,128)S(1)} %collective-permute-done.9.refs_0_, f32[32,128]{1,0:T(8,128)S(1)} %collective-permute-done.10.refs_1_, f32[32,128]{1,0:T(8,128)S(1)} %collective-permute-done.11.refs_2_, ...), custom_call_target="tpu_custom_call" | custom-call | flops 6553600 | bytes 1572864 | tf_op jit(solution)/shard_map/second/pallas_call | solution.py:370
  54.2 0.6 collective-permute-start.13
  54.8 3.8 %collective-permute-start.14 = (f32[32,128]{1,0:T(8,128)S(1)}, f32[32,128]{1,0:T(8,128)S(1)}, u32[]{:S(2)}, u32[]{:S(2)}) collective-permute-start(f32[32,128]{1,0:T(8,128)S(1)} %get-tuple-element.52), channel_id=1, source_target_pairs={{0,12},{4,8},{8,4},{12,0},{1,13},{5,9},{9,5},{13,1},{2,14},{6,10},... | collective-permute-start | bytes 49160 | tf_op jit(solution)/shard_map/ppermute | solution.py:443
  58.9 1.6 %collective-permute-done.14.refs_2_ = f32[32,128]{1,0:T(8,128)S(1)} collective-permute-done((f32[32,128]{1,0:T(8,128)S(1)}, f32[32,128]{1,0:T(8,128)S(1)}, u32[]{:S(2)}, u32[]{:S(2)}) %collective-permute-start.14) | collective-permute-done | bytes 16416 | tf_op jit(solution)/shard_map/ppermute | solution.py:443
  60.5 0.9 %last.1 = f32[512,128]{1,0:T(8,128)} custom-call(f32[32,128]{1,0:T(8,128)S(1)} %collective-permute-done.12.refs_0_, f32[32,128]{1,0:T(8,128)S(1)} %collective-permute-done.13.refs_1_, f32[32,128]{1,0:T(8,128)S(1)} %collective-permute-done.14.refs_2_, f32[4,3,128,128]{3,2,1,0:T(8,128)S(1)} %get-tuple-element.53.refs_3_, ...), custom_call_target="tpu_custom_call" | custom-call | flops 655360 | bytes 1048576 | tf_op jit(solution)/shard_map/last/pallas_call | solution.py:407
  (27 shorter events, 2.2 us)
Async XLA Ops:
  0.0 5.8 %copy-start = (bf16[1024,8192]{1,0:T(8,128)(2,1)S(1)}, bf16[1024,8192]{1,0:T(8,128)(2,1)}, u32[]{:S(2)}) copy-start(bf16[1024,8192]{1,0:T(8,128)(2,1)} %weight_ref.9) | copy-start | bytes 50331652
  5.8 0.9 %copy-start.2 = (bf16[128,1024]{1,0:T(8,128)(2,1)S(1)}, bf16[128,1024]{1,0:T(8,128)(2,1)}, u32[]{:S(2)}) copy-start(bf16[128,1024]{1,0:T(8,128)(2,1)} %tokens_ref.9) | copy-start | bytes 786436
  6.7 5.8 %copy-start.1 = (bf16[1024,8192]{1,0:T(8,128)(2,1)S(1)}, bf16[1024,8192]{1,0:T(8,128)(2,1)}, u32[]{:S(2)}) copy-start(bf16[1024,8192]{1,0:T(8,128)(2,1)} %weight_ref.9) | copy-start | bytes 50331652
  6.7 5.8 %copy-start.3 = (bf16[128,1024]{1,0:T(8,128)(2,1)S(1)}, bf16[128,1024]{1,0:T(8,128)(2,1)}, u32[]{:S(2)}) copy-start(bf16[128,1024]{1,0:T(8,128)(2,1)} %tokens_ref.9) | copy-start | bytes 786436
  8.2 1.7 %collective-permute-start = (f32[128,512]{1,0:T(8,128)S(1)}, f32[128,512]{1,0:T(8,128)S(1)}, u32[]{:S(2)}, u32[]{:S(2)}) collective-permute-start(f32[128,512]{1,0:T(8,128)S(1)} %get-tuple-element.31), channel_id=1, source_target_pairs={{0,1},{1,0},{2,3},{3,2},{4,5},{5,4},{6,7},{7,6},{8,9},{9,8},{10,11... | collective-permute-start | bytes 786440 | tf_op jit(solution)/shard_map/ppermute | solution.py:434
  14.0 1.7 %collective-permute-start.1 = (f32[128,512]{1,0:T(8,128)S(1)}, f32[128,512]{1,0:T(8,128)S(1)}, u32[]{:S(2)}, u32[]{:S(2)}) collective-permute-start(f32[128,512]{1,0:T(8,128)S(1)} %get-tuple-element.33), channel_id=1, source_target_pairs={{0,1},{1,0},{2,3},{3,2},{4,5},{5,4},{6,7},{7,6},{8,9},{9,8},{10,11... | collective-permute-start | bytes 786440 | tf_op jit(solution)/shard_map/ppermute | solution.py:434
  21.9 12.8 %copy-start.4 = (f32[512,4]{0,1:T(4,128)S(1)}, f32[512,4]{0,1:T(4,128)}, u32[]{:S(2)}) copy-start(f32[512,4]{0,1:T(4,128)} %param.8) | copy-start | bytes 24580
  21.9 12.8 %copy-start.5 = (f32[512,2]{0,1:T(2,128)S(1)}, f32[512,2]{0,1:T(2,128)}, u32[]{:S(2)}) copy-start(f32[512,2]{0,1:T(2,128)} %param.7) | copy-start | bytes 12292
  21.9 12.8 %copy-start.6 = (f32[128]{0:T(128)S(1)}, f32[128]{0:T(128)}, u32[]{:S(2)}) copy-start(f32[128]{0:T(128)} %param.9) | copy-start | bytes 1540
  21.9 12.7 %collective-permute-start.2 = (f32[128,2048]{1,0:T(8,128)S(1)}, f32[128,2048]{1,0:T(8,128)S(1)}, u32[]{:S(2)}, u32[]{:S(2)}) collective-permute-start(f32[128,2048]{1,0:T(8,128)S(1)} %get-tuple-element.35), channel_id=1, source_target_pairs={{0,1},{1,0},{2,3},{3,2},{4,5},{5,4},{6,7},{7,6},{8,9},{9,8},{10,11... | collective-permute-start | bytes 3145736 | tf_op jit(solution)/shard_map/ppermute | solution.py:434
  23.9 1.6 %collective-permute-start.4 = (f32[128,512]{1,0:T(8,128)S(1)}, f32[128,512]{1,0:T(8,128)S(1)}, u32[]{:S(2)}, u32[]{:S(2)}) collective-permute-start(f32[128,512]{1,0:T(8,128)S(1)} %get-tuple-element.37), channel_id=1, source_target_pairs={{0,1},{1,0},{2,3},{3,2},{4,5},{5,4},{6,7},{7,6},{8,9},{9,8},{10,11... | collective-permute-start | bytes 786440 | tf_op jit(solution)/shard_map/ppermute | solution.py:434
  27.2 3.1 %collective-permute-start.5 = (f32[128,512]{1,0:T(8,128)S(1)}, f32[128,512]{1,0:T(8,128)S(1)}, u32[]{:S(2)}, u32[]{:S(2)}) collective-permute-start(f32[128,512]{1,0:T(8,128)S(1)} %get-tuple-element.39), channel_id=1, source_target_pairs={{0,1},{1,0},{2,3},{3,2},{4,5},{5,4},{6,7},{7,6},{8,9},{9,8},{10,11... | collective-permute-start | bytes 786440 | tf_op jit(solution)/shard_map/ppermute | solution.py:434
  27.4 7.2 %collective-permute-start.8 = (bf16[520,128]{1,0:T(8,128)(2,1)S(1)}, bf16[520,128]{1,0:T(8,128)(2,1)S(1)}, u32[]{:S(2)}, u32[]{:S(2)}) collective-permute-start(bf16[520,128]{1,0:T(8,128)(2,1)S(1)} %encode.6.refs_0_), channel_id=1, source_target_pairs={{0,2},{1,3},{2,0},{3,1},{4,6},{5,7},{6,4},{7,5},{8,10},{9,11},{10,... | collective-permute-start | bytes 399368 | tf_op jit(solution)/shard_map/ppermute | solution.py:438
  30.3 7.2 %collective-permute-start.7 = (bf16[520,128]{1,0:T(8,128)(2,1)S(1)}, bf16[520,128]{1,0:T(8,128)(2,1)S(1)}, u32[]{:S(2)}, u32[]{:S(2)}) collective-permute-start(bf16[520,128]{1,0:T(8,128)(2,1)S(1)} %encode.4.refs_0_), channel_id=1, source_target_pairs={{0,2},{1,3},{2,0},{3,1},{4,6},{5,7},{6,4},{7,5},{8,10},{9,11},{10,... | collective-permute-start | bytes 399368 | tf_op jit(solution)/shard_map/ppermute | solution.py:438
  30.5 9.8 %collective-permute-start.6 = (bf16[520,128]{1,0:T(8,128)(2,1)S(1)}, bf16[520,128]{1,0:T(8,128)(2,1)S(1)}, u32[]{:S(2)}, u32[]{:S(2)}) collective-permute-start(bf16[520,128]{1,0:T(8,128)(2,1)S(1)} %encode.7), channel_id=1, source_target_pairs={{0,2},{1,3},{2,0},{3,1},{4,6},{5,7},{6,4},{7,5},{8,10},{9,11},{10,... | collective-permute-start | bytes 399368 | tf_op jit(solution)/shard_map/ppermute | solution.py:438
  32.6 10.1 %collective-permute-start.3 = (bf16[520,128]{1,0:T(8,128)(2,1)S(1)}, bf16[520,128]{1,0:T(8,128)(2,1)S(1)}, u32[]{:S(2)}, u32[]{:S(2)}) collective-permute-start(bf16[520,128]{1,0:T(8,128)(2,1)S(1)} %encode.5.refs_0_), channel_id=1, source_target_pairs={{0,2},{1,3},{2,0},{3,1},{4,6},{5,7},{6,4},{7,5},{8,10},{9,11},{10,... | collective-permute-start | bytes 399368 | tf_op jit(solution)/shard_map/ppermute | solution.py:438
  43.2 4.5 %collective-permute-start.9 = (f32[32,128]{1,0:T(8,128)S(1)}, f32[32,128]{1,0:T(8,128)S(1)}, u32[]{:S(2)}, u32[]{:S(2)}) collective-permute-start(f32[32,128]{1,0:T(8,128)S(1)} %get-tuple-element.43), channel_id=1, source_target_pairs={{0,4},{4,0},{8,12},{12,8},{1,5},{5,1},{9,13},{13,9},{2,6},{6,2},{1... | collective-permute-start | bytes 49160 | tf_op jit(solution)/shard_map/ppermute | solution.py:443
  45.1 4.6 %collective-permute-start.10 = (f32[32,128]{1,0:T(8,128)S(1)}, f32[32,128]{1,0:T(8,128)S(1)}, u32[]{:S(2)}, u32[]{:S(2)}) collective-permute-start(f32[32,128]{1,0:T(8,128)S(1)} %get-tuple-element.43), channel_id=1, source_target_pairs={{0,8},{4,12},{8,0},{12,4},{1,9},{5,13},{9,1},{13,5},{2,10},{6,14},... | collective-permute-start | bytes 49160 | tf_op jit(solution)/shard_map/ppermute | solution.py:443
  47.7 5.7 %collective-permute-start.11 = (f32[32,128]{1,0:T(8,128)S(1)}, f32[32,128]{1,0:T(8,128)S(1)}, u32[]{:S(2)}, u32[]{:S(2)}) collective-permute-start(f32[32,128]{1,0:T(8,128)S(1)} %get-tuple-element.43), channel_id=1, source_target_pairs={{0,12},{4,8},{8,4},{12,0},{1,13},{5,9},{9,5},{13,1},{2,14},{6,10},... | collective-permute-start | bytes 49160 | tf_op jit(solution)/shard_map/ppermute | solution.py:443
  54.2 4.5 %collective-permute-start.12 = (f32[32,128]{1,0:T(8,128)S(1)}, f32[32,128]{1,0:T(8,128)S(1)}, u32[]{:S(2)}, u32[]{:S(2)}) collective-permute-start(f32[32,128]{1,0:T(8,128)S(1)} %get-tuple-element.52), channel_id=1, source_target_pairs={{0,4},{4,0},{8,12},{12,8},{1,5},{5,1},{9,13},{13,9},{2,6},{6,2},{1... | collective-permute-start | bytes 49160 | tf_op jit(solution)/shard_map/ppermute | solution.py:443
  54.2 4.7 %collective-permute-start.13 = (f32[32,128]{1,0:T(8,128)S(1)}, f32[32,128]{1,0:T(8,128)S(1)}, u32[]{:S(2)}, u32[]{:S(2)}) collective-permute-start(f32[32,128]{1,0:T(8,128)S(1)} %get-tuple-element.52), channel_id=1, source_target_pairs={{0,8},{4,12},{8,0},{12,4},{1,9},{5,13},{9,1},{13,5},{2,10},{6,14},... | collective-permute-start | bytes 49160 | tf_op jit(solution)/shard_map/ppermute | solution.py:443
  54.8 5.7 %collective-permute-start.14 = (f32[32,128]{1,0:T(8,128)S(1)}, f32[32,128]{1,0:T(8,128)S(1)}, u32[]{:S(2)}, u32[]{:S(2)}) collective-permute-start(f32[32,128]{1,0:T(8,128)S(1)} %get-tuple-element.52), channel_id=1, source_target_pairs={{0,12},{4,8},{8,4},{12,0},{1,13},{5,9},{9,5},{13,1},{2,14},{6,10},... | collective-permute-start | bytes 49160 | tf_op jit(solution)/shard_map/ppermute | solution.py:443

commit v3 on v2

--- a/solution.py
+++ b/solution.py
@@ -6,6 +6,7 @@
 from jax.experimental import pallas as pl
 from jax.experimental.pallas import tpu as pltpu
 from jax.sharding import PartitionSpec as P
+
 
 LANES = 128
 SUB = 8
@@ -25,8 +26,12 @@
     return [pl.BlockSpec(memory_space=pltpu.VMEM)] * count
 
 
-def anywhere(count):
-    return [pl.BlockSpec(memory_space=pl.ANY)] * count
+def in_hbm(count):
+    return [pl.BlockSpec(memory_space=pltpu.HBM)] * count
+
+
+def off_chip(value):
+    return pltpu.with_memory_space_constraint(value, pltpu.HBM)
 
 
 def on_chip(value):
@@ -72,7 +77,7 @@
     return pl.pallas_call(
         functools.partial(product_kernel, chips, away, first, width, per_owner, tile),
         out_shape=(out, out),
-        in_specs=anywhere(2 + len(after)),
+        in_specs=in_hbm(2) + vmem(len(after)),
         out_specs=vmem(2),
         scratch_shapes=[
             pltpu.VMEM((steps, depth), BF16),
@@ -448,6 +453,7 @@
             for k in range(1, blocks)
         ]
 
+    tokens, in_weight = off_chip(tokens), off_chip(in_weight)
     arrived = [[] for _ in range(groups)]
     codes = []
     for away in range(1, chips):
@@ -455,7 +461,8 @@
             give, keep = products(
                 tokens, in_weight, chips, away, group * GROUP, GROUP, per_owner, codes[-2:-1]
             )
-            codes.append(encoded(keep, to_core(give)))
+            given = to_core(give)
+            codes.append(encoded(keep, given))
             arrived[group].append(to_chip(codes[-1], away))
     give, keep = products(tokens, in_weight, chips, 0, 0, per_owner, per_owner, codes[-1:])
     given = to_core(give)
@@ -477,6 +484,7 @@
         P("chan", None),
         P(("groups", "tm")),
     )
+
     return jax.shard_map(
         shards, mesh=mesh, in_specs=placed, out_specs=P("chan", ("groups", "tm")), check_vma=False
     )

time: 61.6 us -> 55.6 us (0.903)
  local copies, waits for them, and re-layouts: 9.06 us -> 0.02 us
  Pallas kernels: 16.6 us -> 19.7 us
    unnamed x14 -> x6, local copies, waits for them, and re-layouts: 9.06 us -> 0.02 us
    pallas_call x5, Pallas kernels: 12 us -> 15.1 us  [products(): pl.pallas_call(functools.partial(product_kernel, chips, away, first, widt...]
  transfers between devices with their start and end apart: 15 -> 15, of which waited for: 11 -> 11; matrix products, arithmetic and copies ran while one was open for 0% -> 0% of each run, Pallas kernels for 8% -> 12%
where the time goes in v3:
time: 55.6 us; the launch traced here: 55.4 us
  waiting for transfers between devices  19.8 us (36%)
  Pallas kernels  19.7 us (35%)
  starting transfers between devices  15.8 us (28%)
    pallas_call x5, Pallas kernels, products(): pl.pallas_call(functools.partial(product_kernel, chips, away, first, widt...  15.1 us
    ppermute x6, starting transfers between devices, to_blocks(): lax.ppermute(value, 'tm', [(i, i ^ k) for i in range(blocks)])  8.93 us
    ppermute x4, waiting for transfers between devices, to_chip(): return on_chip(lax.ppermute(value, 'chan', pairs))  8.47 us
    ppermute x6, waiting for transfers between devices, to_blocks(): lax.ppermute(value, 'tm', [(i, i ^ k) for i in range(blocks)])  7.57 us
    ppermute x4, starting transfers between devices, to_chip(): return on_chip(lax.ppermute(value, 'chan', pairs))  5.01 us
    ppermute x5, waiting for transfers between devices, to_core(): lax.ppermute(value, 'chan', [(i, i ^ 1) for i in range(owners)])  3.73 us
    pallas_call x4, Pallas kernels, first(): pl.pallas_call(functools.partial(first_kernel, start, groups, len(codes),...  2.01 us
    ppermute x5, starting transfers between devices, to_core(): lax.ppermute(value, 'chan', [(i, i ^ 1) for i in range(owners)])  1.84 us
  transfers between devices with their start and end apart: 15, of which 11 were waited for; matrix products, arithmetic and copies ran while one was open for 0% of the time, Pallas kernels for 12%

profile of v3, /device:TPU:0, one launch (start us, length us, event | category | flops | bytes accessed | tf_op | source)
XLA Modules:
  0.0 55.4 jit_solution(8659604393302564496)
XLA Ops:
  0.0 2.3 %products.5 = (f32[128,512]{1,0:T(8,128)S(1)}, f32[128,512]{1,0:T(8,128)S(1)}) custom-call(bf16[128,1024]{1,0:T(8,128)(2,1)} %tokens_ref.9, bf16[1024,8192]{1,0:T(8,128)(2,1)} %weight_ref.9), custom_call_target="tpu_custom_call" | custom-call | flops 268435456 | bytes 2621440 | tf_op jit(solution)/shard_map/products/pallas_call | solution.py:77
  2.3 0.6 %collective-permute-start = (f32[128,512]{1,0:T(8,128)S(1)}, f32[128,512]{1,0:T(8,128)S(1)}, u32[]{:S(2)}, u32[]{:S(2)}) collective-permute-start(f32[128,512]{1,0:T(8,128)S(1)} %get-tuple-element.31), channel_id=1, source_target_pairs={{0,1},{1,0},{2,3},{3,2},{4,5},{5,4},{6,7},{7,6},{8,9},{9,8},{10,11... | collective-permute-start | bytes 786440 | tf_op jit(solution)/shard_map/ppermute | solution.py:439
  2.9 1.2 %collective-permute-done.theirs_ref = f32[128,512]{1,0:T(8,128)S(1)} collective-permute-done((f32[128,512]{1,0:T(8,128)S(1)}, f32[128,512]{1,0:T(8,128)S(1)}, u32[]{:S(2)}, u32[]{:S(2)}) %collective-permute-start) | collective-permute-done | bytes 262176 | tf_op jit(solution)/shard_map/ppermute | solution.py:439
  4.2 2.3 %products.6 = (f32[128,512]{1,0:T(8,128)S(1)}, f32[128,512]{1,0:T(8,128)S(1)}) custom-call(bf16[128,1024]{1,0:T(8,128)(2,1)} %tokens_ref.9, bf16[1024,8192]{1,0:T(8,128)(2,1)} %weight_ref.9, bf16[520,128]{1,0:T(8,128)(2,1)S(1)} %encode.4.refs_0_), custom_call_target="tpu_custom_call" | custom-call | flops 268435456 | bytes 2621440 | tf_op jit(solution)/shard_map/products/pallas_call | solution.py:77
  6.6 0.4 collective-permute-start.1
  7.0 1.2 %collective-permute-done.1.theirs_ref = f32[128,512]{1,0:T(8,128)S(1)} collective-permute-done((f32[128,512]{1,0:T(8,128)S(1)}, f32[128,512]{1,0:T(8,128)S(1)}, u32[]{:S(2)}, u32[]{:S(2)}) %collective-permute-start.1) | collective-permute-done | bytes 262176 | tf_op jit(solution)/shard_map/ppermute | solution.py:439
  8.4 5.8 %products.7 = (f32[128,2048]{1,0:T(8,128)S(1)}, f32[128,2048]{1,0:T(8,128)S(1)}) custom-call(bf16[128,1024]{1,0:T(8,128)(2,1)} %tokens_ref.9, bf16[1024,8192]{1,0:T(8,128)(2,1)} %weight_ref.9, bf16[520,128]{1,0:T(8,128)(2,1)S(1)} %encode.5.refs_0_), custom_call_target="tpu_custom_call" | custom-call | flops 1073741824 | bytes 10485760 | tf_op jit(solution)/shard_map/products/pallas_call | solution.py:77
  14.3 0.4 collective-permute-start.2
  14.7 2.3 %products.8 = (f32[128,512]{1,0:T(8,128)S(1)}, f32[128,512]{1,0:T(8,128)S(1)}) custom-call(bf16[128,1024]{1,0:T(8,128)(2,1)} %tokens_ref.9, bf16[1024,8192]{1,0:T(8,128)(2,1)} %weight_ref.9), custom_call_target="tpu_custom_call" | custom-call | flops 268435456 | bytes 2621440 | tf_op jit(solution)/shard_map/products/pallas_call | solution.py:77
  17.2 1.4 %collective-permute-done.4.theirs_ref = f32[128,512]{1,0:T(8,128)S(1)} collective-permute-done((f32[128,512]{1,0:T(8,128)S(1)}, f32[128,512]{1,0:T(8,128)S(1)}, u32[]{:S(2)}, u32[]{:S(2)}) %collective-permute-start.4) | collective-permute-done | bytes 262176 | tf_op jit(solution)/shard_map/ppermute | solution.py:439
  18.8 2.3 %products.9 = (f32[128,512]{1,0:T(8,128)S(1)}, f32[128,512]{1,0:T(8,128)S(1)}) custom-call(bf16[128,1024]{1,0:T(8,128)(2,1)} %tokens_ref.9, bf16[1024,8192]{1,0:T(8,128)(2,1)} %weight_ref.9, bf16[520,128]{1,0:T(8,128)(2,1)S(1)} %encode.6.refs_0_), custom_call_target="tpu_custom_call" | custom-call | flops 268435456 | bytes 2621440 | tf_op jit(solution)/shard_map/products/pallas_call | solution.py:77
  21.4 2.8 %collective-permute-start.8 = (bf16[520,128]{1,0:T(8,128)(2,1)S(1)}, bf16[520,128]{1,0:T(8,128)(2,1)S(1)}, u32[]{:S(2)}, u32[]{:S(2)}) collective-permute-start(bf16[520,128]{1,0:T(8,128)(2,1)S(1)} %encode.6.refs_0_), channel_id=1, source_target_pairs={{0,2},{1,3},{2,0},{3,1},{4,6},{5,7},{6,4},{7,5},{8,10},{9,11},{10,... | collective-permute-start | bytes 399368 | tf_op jit(solution)/shard_map/ppermute | solution.py:443
  24.2 0.2 encode.7
  24.4 2.1 %collective-permute-start.6 = (bf16[520,128]{1,0:T(8,128)(2,1)S(1)}, bf16[520,128]{1,0:T(8,128)(2,1)S(1)}, u32[]{:S(2)}, u32[]{:S(2)}) collective-permute-start(bf16[520,128]{1,0:T(8,128)(2,1)S(1)} %encode.7), channel_id=1, source_target_pairs={{0,2},{1,3},{2,0},{3,1},{4,6},{5,7},{6,4},{7,5},{8,10},{9,11},{10,... | collective-permute-start | bytes 399368 | tf_op jit(solution)/shard_map/ppermute | solution.py:443
  26.6 2.0 %collective-permute-done.8.refs_2_ = bf16[520,128]{1,0:T(8,128)(2,1)S(1)} collective-permute-done((bf16[520,128]{1,0:T(8,128)(2,1)S(1)}, bf16[520,128]{1,0:T(8,128)(2,1)S(1)}, u32[]{:S(2)}, u32[]{:S(2)}) %collective-permute-start.8) | collective-permute-done | bytes 133152 | tf_op jit(solution)/shard_map/ppermute | solution.py:443
  28.6 0.5 first.4
  29.1 2.3 %collective-permute-done.7.refs_2_ = bf16[520,128]{1,0:T(8,128)(2,1)S(1)} collective-permute-done((bf16[520,128]{1,0:T(8,128)(2,1)S(1)}, bf16[520,128]{1,0:T(8,128)(2,1)S(1)}, u32[]{:S(2)}, u32[]{:S(2)}) %collective-permute-start.7) | collective-permute-done | bytes 133152 | tf_op jit(solution)/shard_map/ppermute | solution.py:443
  31.4 0.5 first.5
  31.9 2.3 %collective-permute-done.6.refs_2_ = bf16[520,128]{1,0:T(8,128)(2,1)S(1)} collective-permute-done((bf16[520,128]{1,0:T(8,128)(2,1)S(1)}, bf16[520,128]{1,0:T(8,128)(2,1)S(1)}, u32[]{:S(2)}, u32[]{:S(2)}) %collective-permute-start.6) | collective-permute-done | bytes 133152 | tf_op jit(solution)/shard_map/ppermute | solution.py:443
  34.3 0.5 first.6
  34.8 1.8 %collective-permute-done.3.refs_2_ = bf16[520,128]{1,0:T(8,128)(2,1)S(1)} collective-permute-done((bf16[520,128]{1,0:T(8,128)(2,1)S(1)}, bf16[520,128]{1,0:T(8,128)(2,1)S(1)}, u32[]{:S(2)}, u32[]{:S(2)}) %collective-permute-start.3) | collective-permute-done | bytes 133152 | tf_op jit(solution)/shard_map/ppermute | solution.py:443
  36.6 0.5 first.7
  37.1 1.9 %collective-permute-start.9 = (f32[32,128]{1,0:T(8,128)S(1)}, f32[32,128]{1,0:T(8,128)S(1)}, u32[]{:S(2)}, u32[]{:S(2)}) collective-permute-start(f32[32,128]{1,0:T(8,128)S(1)} %get-tuple-element.43), channel_id=1, source_target_pairs={{0,4},{4,0},{8,12},{12,8},{1,5},{5,1},{9,13},{13,9},{2,6},{6,2},{1... | collective-permute-start | bytes 49160 | tf_op jit(solution)/shard_map/ppermute | solution.py:448
  39.0 2.6 %collective-permute-start.10 = (f32[32,128]{1,0:T(8,128)S(1)}, f32[32,128]{1,0:T(8,128)S(1)}, u32[]{:S(2)}, u32[]{:S(2)}) collective-permute-start(f32[32,128]{1,0:T(8,128)S(1)} %get-tuple-element.43), channel_id=1, source_target_pairs={{0,8},{4,12},{8,0},{12,4},{1,9},{5,13},{9,1},{13,5},{2,10},{6,14},... | collective-permute-start | bytes 49160 | tf_op jit(solution)/shard_map/ppermute | solution.py:448
  41.6 2.0 %collective-permute-done.10.refs_1_ = f32[32,128]{1,0:T(8,128)S(1)} collective-permute-done((f32[32,128]{1,0:T(8,128)S(1)}, f32[32,128]{1,0:T(8,128)S(1)}, u32[]{:S(2)}, u32[]{:S(2)}) %collective-permute-start.10) | collective-permute-done | bytes 16416 | tf_op jit(solution)/shard_map/ppermute | solution.py:448
  43.6 3.6 %collective-permute-done.11.refs_2_ = f32[32,128]{1,0:T(8,128)S(1)} collective-permute-done((f32[32,128]{1,0:T(8,128)S(1)}, f32[32,128]{1,0:T(8,128)S(1)}, u32[]{:S(2)}, u32[]{:S(2)}) %collective-permute-start.11) | collective-permute-done | bytes 16416 | tf_op jit(solution)/shard_map/ppermute | solution.py:448
  47.3 0.8 %second.1 = (f32[4,3,128,128]{3,2,1,0:T(8,128)S(1)}, f32[4,6,8,128]{3,2,1,0:T(8,128)S(1)}, f32[32,128]{1,0:T(8,128)S(1)}) custom-call(f32[32,128]{1,0:T(8,128)S(1)} %collective-permute-done.9.refs_0_, f32[32,128]{1,0:T(8,128)S(1)} %collective-permute-done.10.refs_1_, f32[32,128]{1,0:T(8,128)S(1)} %collective-permute-done.11.refs_2_, ...), custom_call_target="tpu_custom_call" | custom-call | flops 6553600 | bytes 1572864 | tf_op jit(solution)/shard_map/second/pallas_call | solution.py:375
  48.2 0.6 %collective-permute-start.13 = (f32[32,128]{1,0:T(8,128)S(1)}, f32[32,128]{1,0:T(8,128)S(1)}, u32[]{:S(2)}, u32[]{:S(2)}) collective-permute-start(f32[32,128]{1,0:T(8,128)S(1)} %get-tuple-element.52), channel_id=1, source_target_pairs={{0,8},{4,12},{8,0},{12,4},{1,9},{5,13},{9,1},{13,5},{2,10},{6,14},... | collective-permute-start | bytes 49160 | tf_op jit(solution)/shard_map/ppermute | solution.py:448
  48.7 3.8 %collective-permute-start.14 = (f32[32,128]{1,0:T(8,128)S(1)}, f32[32,128]{1,0:T(8,128)S(1)}, u32[]{:S(2)}, u32[]{:S(2)}) collective-permute-start(f32[32,128]{1,0:T(8,128)S(1)} %get-tuple-element.52), channel_id=1, source_target_pairs={{0,12},{4,8},{8,4},{12,0},{1,13},{5,9},{9,5},{13,1},{2,14},{6,10},... | collective-permute-start | bytes 49160 | tf_op jit(solution)/shard_map/ppermute | solution.py:448
  52.5 0.3 collective-permute-done.13.refs_1_
  52.9 1.6 %collective-permute-done.14.refs_2_ = f32[32,128]{1,0:T(8,128)S(1)} collective-permute-done((f32[32,128]{1,0:T(8,128)S(1)}, f32[32,128]{1,0:T(8,128)S(1)}, u32[]{:S(2)}, u32[]{:S(2)}) %collective-permute-start.14) | collective-permute-done | bytes 16416 | tf_op jit(solution)/shard_map/ppermute | solution.py:448
  54.4 0.9 %last.1 = f32[512,128]{1,0:T(8,128)} custom-call(f32[32,128]{1,0:T(8,128)S(1)} %collective-permute-done.12.refs_0_, f32[32,128]{1,0:T(8,128)S(1)} %collective-permute-done.13.refs_1_, f32[32,128]{1,0:T(8,128)S(1)} %collective-permute-done.14.refs_2_, f32[4,3,128,128]{3,2,1,0:T(8,128)S(1)} %get-tuple-element.53.refs_3_, ...), custom_call_target="tpu_custom_call" | custom-call | flops 655360 | bytes 1048576 | tf_op jit(solution)/shard_map/last/pallas_call | solution.py:412
  (19 shorter events, 1.2 us)
Async XLA Ops:
  2.3 1.7 %collective-permute-start = (f32[128,512]{1,0:T(8,128)S(1)}, f32[128,512]{1,0:T(8,128)S(1)}, u32[]{:S(2)}, u32[]{:S(2)}) collective-permute-start(f32[128,512]{1,0:T(8,128)S(1)} %get-tuple-element.31), channel_id=1, source_target_pairs={{0,1},{1,0},{2,3},{3,2},{4,5},{5,4},{6,7},{7,6},{8,9},{9,8},{10,11... | collective-permute-start | bytes 786440 | tf_op jit(solution)/shard_map/ppermute | solution.py:439
  6.6 1.6 %collective-permute-start.1 = (f32[128,512]{1,0:T(8,128)S(1)}, f32[128,512]{1,0:T(8,128)S(1)}, u32[]{:S(2)}, u32[]{:S(2)}) collective-permute-start(f32[128,512]{1,0:T(8,128)S(1)} %get-tuple-element.33), channel_id=1, source_target_pairs={{0,1},{1,0},{2,3},{3,2},{4,5},{5,4},{6,7},{7,6},{8,9},{9,8},{10,11... | collective-permute-start | bytes 786440 | tf_op jit(solution)/shard_map/ppermute | solution.py:439
  14.2 14.4 %copy-start = (f32[512,4]{0,1:T(4,128)S(1)}, f32[512,4]{0,1:T(4,128)}, u32[]{:S(2)}) copy-start(f32[512,4]{0,1:T(4,128)} %param.8) | copy-start | bytes 24580
  14.2 14.4 %copy-start.1 = (f32[512,2]{0,1:T(2,128)S(1)}, f32[512,2]{0,1:T(2,128)}, u32[]{:S(2)}) copy-start(f32[512,2]{0,1:T(2,128)} %param.7) | copy-start | bytes 12292
  14.3 14.3 %copy-start.2 = (f32[128]{0:T(128)S(1)}, f32[128]{0:T(128)}, u32[]{:S(2)}) copy-start(f32[128]{0:T(128)} %param.9) | copy-start | bytes 1540
  14.3 14.3 %collective-permute-start.2 = (f32[128,2048]{1,0:T(8,128)S(1)}, f32[128,2048]{1,0:T(8,128)S(1)}, u32[]{:S(2)}, u32[]{:S(2)}) collective-permute-start(f32[128,2048]{1,0:T(8,128)S(1)} %get-tuple-element.35), channel_id=1, source_target_pairs={{0,1},{1,0},{2,3},{3,2},{4,5},{5,4},{6,7},{7,6},{8,9},{9,8},{10,11... | collective-permute-start | bytes 3145736 | tf_op jit(solution)/shard_map/ppermute | solution.py:439
  17.0 1.6 %collective-permute-start.4 = (f32[128,512]{1,0:T(8,128)S(1)}, f32[128,512]{1,0:T(8,128)S(1)}, u32[]{:S(2)}, u32[]{:S(2)}) collective-permute-start(f32[128,512]{1,0:T(8,128)S(1)} %get-tuple-element.37), channel_id=1, source_target_pairs={{0,1},{1,0},{2,3},{3,2},{4,5},{5,4},{6,7},{7,6},{8,9},{9,8},{10,11... | collective-permute-start | bytes 786440 | tf_op jit(solution)/shard_map/ppermute | solution.py:439
  21.2 3.1 %collective-permute-start.5 = (f32[128,512]{1,0:T(8,128)S(1)}, f32[128,512]{1,0:T(8,128)S(1)}, u32[]{:S(2)}, u32[]{:S(2)}) collective-permute-start(f32[128,512]{1,0:T(8,128)S(1)} %get-tuple-element.39), channel_id=1, source_target_pairs={{0,1},{1,0},{2,3},{3,2},{4,5},{5,4},{6,7},{7,6},{8,9},{9,8},{10,11... | collective-permute-start | bytes 786440 | tf_op jit(solution)/shard_map/ppermute | solution.py:439
  21.4 7.2 %collective-permute-start.8 = (bf16[520,128]{1,0:T(8,128)(2,1)S(1)}, bf16[520,128]{1,0:T(8,128)(2,1)S(1)}, u32[]{:S(2)}, u32[]{:S(2)}) collective-permute-start(bf16[520,128]{1,0:T(8,128)(2,1)S(1)} %encode.6.refs_0_), channel_id=1, source_target_pairs={{0,2},{1,3},{2,0},{3,1},{4,6},{5,7},{6,4},{7,5},{8,10},{9,11},{10,... | collective-permute-start | bytes 399368 | tf_op jit(solution)/shard_map/ppermute | solution.py:443
  24.2 7.2 %collective-permute-start.7 = (bf16[520,128]{1,0:T(8,128)(2,1)S(1)}, bf16[520,128]{1,0:T(8,128)(2,1)S(1)}, u32[]{:S(2)}, u32[]{:S(2)}) collective-permute-start(bf16[520,128]{1,0:T(8,128)(2,1)S(1)} %encode.4.refs_0_), channel_id=1, source_target_pairs={{0,2},{1,3},{2,0},{3,1},{4,6},{5,7},{6,4},{7,5},{8,10},{9,11},{10,... | collective-permute-start | bytes 399368 | tf_op jit(solution)/shard_map/ppermute | solution.py:443
  24.4 9.9 %collective-permute-start.6 = (bf16[520,128]{1,0:T(8,128)(2,1)S(1)}, bf16[520,128]{1,0:T(8,128)(2,1)S(1)}, u32[]{:S(2)}, u32[]{:S(2)}) collective-permute-start(bf16[520,128]{1,0:T(8,128)(2,1)S(1)} %encode.7), channel_id=1, source_target_pairs={{0,2},{1,3},{2,0},{3,1},{4,6},{5,7},{6,4},{7,5},{8,10},{9,11},{10,... | collective-permute-start | bytes 399368 | tf_op jit(solution)/shard_map/ppermute | solution.py:443
  26.5 10.1 %collective-permute-start.3 = (bf16[520,128]{1,0:T(8,128)(2,1)S(1)}, bf16[520,128]{1,0:T(8,128)(2,1)S(1)}, u32[]{:S(2)}, u32[]{:S(2)}) collective-permute-start(bf16[520,128]{1,0:T(8,128)(2,1)S(1)} %encode.5.refs_0_), channel_id=1, source_target_pairs={{0,2},{1,3},{2,0},{3,1},{4,6},{5,7},{6,4},{7,5},{8,10},{9,11},{10,... | collective-permute-start | bytes 399368 | tf_op jit(solution)/shard_map/ppermute | solution.py:443
  37.1 4.5 %collective-permute-start.9 = (f32[32,128]{1,0:T(8,128)S(1)}, f32[32,128]{1,0:T(8,128)S(1)}, u32[]{:S(2)}, u32[]{:S(2)}) collective-permute-start(f32[32,128]{1,0:T(8,128)S(1)} %get-tuple-element.43), channel_id=1, source_target_pairs={{0,4},{4,0},{8,12},{12,8},{1,5},{5,1},{9,13},{13,9},{2,6},{6,2},{1... | collective-permute-start | bytes 49160 | tf_op jit(solution)/shard_map/ppermute | solution.py:448
  39.0 4.6 %collective-permute-start.10 = (f32[32,128]{1,0:T(8,128)S(1)}, f32[32,128]{1,0:T(8,128)S(1)}, u32[]{:S(2)}, u32[]{:S(2)}) collective-permute-start(f32[32,128]{1,0:T(8,128)S(1)} %get-tuple-element.43), channel_id=1, source_target_pairs={{0,8},{4,12},{8,0},{12,4},{1,9},{5,13},{9,1},{13,5},{2,10},{6,14},... | collective-permute-start | bytes 49160 | tf_op jit(solution)/shard_map/ppermute | solution.py:448
  41.6 5.7 %collective-permute-start.11 = (f32[32,128]{1,0:T(8,128)S(1)}, f32[32,128]{1,0:T(8,128)S(1)}, u32[]{:S(2)}, u32[]{:S(2)}) collective-permute-start(f32[32,128]{1,0:T(8,128)S(1)} %get-tuple-element.43), channel_id=1, source_target_pairs={{0,12},{4,8},{8,4},{12,0},{1,13},{5,9},{9,5},{13,1},{2,14},{6,10},... | collective-permute-start | bytes 49160 | tf_op jit(solution)/shard_map/ppermute | solution.py:448
  48.1 4.5 %collective-permute-start.12 = (f32[32,128]{1,0:T(8,128)S(1)}, f32[32,128]{1,0:T(8,128)S(1)}, u32[]{:S(2)}, u32[]{:S(2)}) collective-permute-start(f32[32,128]{1,0:T(8,128)S(1)} %get-tuple-element.52), channel_id=1, source_target_pairs={{0,4},{4,0},{8,12},{12,8},{1,5},{5,1},{9,13},{13,9},{2,6},{6,2},{1... | collective-permute-start | bytes 49160 | tf_op jit(solution)/shard_map/ppermute | solution.py:448
  48.2 4.7 %collective-permute-start.13 = (f32[32,128]{1,0:T(8,128)S(1)}, f32[32,128]{1,0:T(8,128)S(1)}, u32[]{:S(2)}, u32[]{:S(2)}) collective-permute-start(f32[32,128]{1,0:T(8,128)S(1)} %get-tuple-element.52), channel_id=1, source_target_pairs={{0,8},{4,12},{8,0},{12,4},{1,9},{5,13},{9,1},{13,5},{2,10},{6,14},... | collective-permute-start | bytes 49160 | tf_op jit(solution)/shard_map/ppermute | solution.py:448
  48.7 5.7 %collective-permute-start.14 = (f32[32,128]{1,0:T(8,128)S(1)}, f32[32,128]{1,0:T(8,128)S(1)}, u32[]{:S(2)}, u32[]{:S(2)}) collective-permute-start(f32[32,128]{1,0:T(8,128)S(1)} %get-tuple-element.52), channel_id=1, source_target_pairs={{0,12},{4,8},{8,4},{12,0},{1,13},{5,9},{9,5},{13,1},{2,14},{6,10},... | collective-permute-start | bytes 49160 | tf_op jit(solution)/shard_map/ppermute | solution.py:448

commit v4 on v3

--- a/solution.py
+++ b/solution.py
@@ -71,7 +71,7 @@
 
 def products(tokens, in_weight, chips, away, first, width, per_owner, after):
     steps, depth = tokens.shape
-    tile = 2 * LANES
+    tile = GROUP
     slots = 2 * width // tile
     out = pltpu.VMEM((steps, width), F32)
     return pl.pallas_call(
@@ -443,15 +443,12 @@
         return on_chip(lax.ppermute(value, "chan", pairs))
 
     def to_blocks(value):
-        if own_xor:
-            return [
-                on_chip(lax.ppermute(value, "tm", [(i, i ^ k) for i in range(blocks)]))
-                for k in range(1, blocks)
-            ]
-        return [
-            on_chip(lax.ppermute(value, "tm", [(i, i + k) for i in range(blocks - k)]))
-            for k in range(1, blocks)
-        ]
+        arriving = []
+        for k in range(1, blocks):
+            pairs = [(i, i ^ k if own_xor else i + k) for i in range(blocks)]
+            sent = lax.ppermute(value, "tm", [pair for pair in pairs if pair[1] < blocks])
+            arriving.append(on_chip(sent))
+        return arriving
 
     tokens, in_weight = off_chip(tokens), off_chip(in_weight)
     arrived = [[] for _ in range(groups)]

time: 55.6 us -> 52.4 us (0.942)
  Pallas kernels: 19.7 us -> 16.5 us
    pallas_call x5, Pallas kernels: 15.1 us -> 11.9 us  [products(): pl.pallas_call(functools.partial(product_kernel, chips, away, first, widt...]
  transfers between devices with their start and end apart: 15 -> 15, of which waited for: 11 -> 11; matrix products, arithmetic and copies ran while one was open for 0% -> 0% of each run, Pallas kernels for 12% -> 11%
where the time goes in v4:
time: 52.4 us; the launch traced here: 52.2 us
  waiting for transfers between devices  19.8 us (38%)
  Pallas kernels  16.5 us (31%)
  starting transfers between devices  15.8 us (30%)
    pallas_call x5, Pallas kernels, products(): pl.pallas_call(functools.partial(product_kernel, chips, away, first, widt...  11.9 us
    ppermute x6, starting transfers between devices, to_blocks(): lax.ppermute(value, 'tm', [pair for pair in pairs if pair[1] < blocks])  8.94 us
    ppermute x4, waiting for transfers between devices, to_chip(): return on_chip(lax.ppermute(value, 'chan', pairs))  8.46 us
    ppermute x6, waiting for transfers between devices, to_blocks(): lax.ppermute(value, 'tm', [pair for pair in pairs if pair[1] < blocks])  7.56 us
    ppermute x4, starting transfers between devices, to_chip(): return on_chip(lax.ppermute(value, 'chan', pairs))  5 us
    ppermute x5, waiting for transfers between devices, to_core(): lax.ppermute(value, 'chan', [(i, i ^ 1) for i in range(owners)])  3.73 us
    pallas_call x4, Pallas kernels, first(): pl.pallas_call(functools.partial(first_kernel, start, groups, len(codes),...  2.01 us
    ppermute x5, starting transfers between devices, to_core(): lax.ppermute(value, 'chan', [(i, i ^ 1) for i in range(owners)])  1.84 us
  transfers between devices with their start and end apart: 15, of which 11 were waited for; matrix products, arithmetic and copies ran while one was open for 0% of the time, Pallas kernels for 11%

profile of v4, /device:TPU:0, one launch (start us, length us, event | category | flops | bytes accessed | tf_op | source)
XLA Modules:
  0.0 52.2 jit_solution(12560864084997810759)
XLA Ops:
  0.0 2.0 %products.5 = (f32[128,512]{1,0:T(8,128)S(1)}, f32[128,512]{1,0:T(8,128)S(1)}) custom-call(bf16[128,1024]{1,0:T(8,128)(2,1)} %tokens_ref.9, bf16[1024,8192]{1,0:T(8,128)(2,1)} %weight_ref.9), custom_call_target="tpu_custom_call" | custom-call | flops 268435456 | bytes 2621440 | tf_op jit(solution)/shard_map/products/pallas_call | solution.py:77
  2.0 0.6 %collective-permute-start = (f32[128,512]{1,0:T(8,128)S(1)}, f32[128,512]{1,0:T(8,128)S(1)}, u32[]{:S(2)}, u32[]{:S(2)}) collective-permute-start(f32[128,512]{1,0:T(8,128)S(1)} %get-tuple-element.31), channel_id=1, source_target_pairs={{0,1},{1,0},{2,3},{3,2},{4,5},{5,4},{6,7},{7,6},{8,9},{9,8},{10,11... | collective-permute-start | bytes 786440 | tf_op jit(solution)/shard_map/ppermute | solution.py:439
  2.5 1.2 %collective-permute-done.theirs_ref = f32[128,512]{1,0:T(8,128)S(1)} collective-permute-done((f32[128,512]{1,0:T(8,128)S(1)}, f32[128,512]{1,0:T(8,128)S(1)}, u32[]{:S(2)}, u32[]{:S(2)}) %collective-permute-start) | collective-permute-done | bytes 262176 | tf_op jit(solution)/shard_map/ppermute | solution.py:439
  3.9 2.0 %products.6 = (f32[128,512]{1,0:T(8,128)S(1)}, f32[128,512]{1,0:T(8,128)S(1)}) custom-call(bf16[128,1024]{1,0:T(8,128)(2,1)} %tokens_ref.9, bf16[1024,8192]{1,0:T(8,128)(2,1)} %weight_ref.9, bf16[520,128]{1,0:T(8,128)(2,1)S(1)} %encode.4.refs_0_), custom_call_target="tpu_custom_call" | custom-call | flops 268435456 | bytes 2621440 | tf_op jit(solution)/shard_map/products/pallas_call | solution.py:77
  5.9 0.4 collective-permute-start.1
  6.4 1.2 %collective-permute-done.1.theirs_ref = f32[128,512]{1,0:T(8,128)S(1)} collective-permute-done((f32[128,512]{1,0:T(8,128)S(1)}, f32[128,512]{1,0:T(8,128)S(1)}, u32[]{:S(2)}, u32[]{:S(2)}) %collective-permute-start.1) | collective-permute-done | bytes 262176 | tf_op jit(solution)/shard_map/ppermute | solution.py:439
  7.7 4.0 %products.7 = (f32[128,2048]{1,0:T(8,128)S(1)}, f32[128,2048]{1,0:T(8,128)S(1)}) custom-call(bf16[128,1024]{1,0:T(8,128)(2,1)} %tokens_ref.9, bf16[1024,8192]{1,0:T(8,128)(2,1)} %weight_ref.9, bf16[520,128]{1,0:T(8,128)(2,1)S(1)} %encode.5.refs_0_), custom_call_target="tpu_custom_call" | custom-call | flops 1073741824 | bytes 10485760 | tf_op jit(solution)/shard_map/products/pallas_call | solution.py:77
  11.7 0.4 collective-permute-start.2
  12.2 2.0 %products.8 = (f32[128,512]{1,0:T(8,128)S(1)}, f32[128,512]{1,0:T(8,128)S(1)}) custom-call(bf16[128,1024]{1,0:T(8,128)(2,1)} %tokens_ref.9, bf16[1024,8192]{1,0:T(8,128)(2,1)} %weight_ref.9), custom_call_target="tpu_custom_call" | custom-call | flops 268435456 | bytes 2621440 | tf_op jit(solution)/shard_map/products/pallas_call | solution.py:77
  14.4 1.4 %collective-permute-done.4.theirs_ref = f32[128,512]{1,0:T(8,128)S(1)} collective-permute-done((f32[128,512]{1,0:T(8,128)S(1)}, f32[128,512]{1,0:T(8,128)S(1)}, u32[]{:S(2)}, u32[]{:S(2)}) %collective-permute-start.4) | collective-permute-done | bytes 262176 | tf_op jit(solution)/shard_map/ppermute | solution.py:439
  16.0 2.0 %products.9 = (f32[128,512]{1,0:T(8,128)S(1)}, f32[128,512]{1,0:T(8,128)S(1)}) custom-call(bf16[128,1024]{1,0:T(8,128)(2,1)} %tokens_ref.9, bf16[1024,8192]{1,0:T(8,128)(2,1)} %weight_ref.9, bf16[520,128]{1,0:T(8,128)(2,1)S(1)} %encode.6.refs_0_), custom_call_target="tpu_custom_call" | custom-call | flops 268435456 | bytes 2621440 | tf_op jit(solution)/shard_map/products/pallas_call | solution.py:77
  18.2 2.8 %collective-permute-start.8 = (bf16[520,128]{1,0:T(8,128)(2,1)S(1)}, bf16[520,128]{1,0:T(8,128)(2,1)S(1)}, u32[]{:S(2)}, u32[]{:S(2)}) collective-permute-start(bf16[520,128]{1,0:T(8,128)(2,1)S(1)} %encode.6.refs_0_), channel_id=1, source_target_pairs={{0,2},{1,3},{2,0},{3,1},{4,6},{5,7},{6,4},{7,5},{8,10},{9,11},{10,... | collective-permute-start | bytes 399368 | tf_op jit(solution)/shard_map/ppermute | solution.py:443
  21.0 0.2 encode.7
  21.3 2.1 %collective-permute-start.6 = (bf16[520,128]{1,0:T(8,128)(2,1)S(1)}, bf16[520,128]{1,0:T(8,128)(2,1)S(1)}, u32[]{:S(2)}, u32[]{:S(2)}) collective-permute-start(bf16[520,128]{1,0:T(8,128)(2,1)S(1)} %encode.7), channel_id=1, source_target_pairs={{0,2},{1,3},{2,0},{3,1},{4,6},{5,7},{6,4},{7,5},{8,10},{9,11},{10,... | collective-permute-start | bytes 399368 | tf_op jit(solution)/shard_map/ppermute | solution.py:443
  23.4 2.0 %collective-permute-done.8.refs_2_ = bf16[520,128]{1,0:T(8,128)(2,1)S(1)} collective-permute-done((bf16[520,128]{1,0:T(8,128)(2,1)S(1)}, bf16[520,128]{1,0:T(8,128)(2,1)S(1)}, u32[]{:S(2)}, u32[]{:S(2)}) %collective-permute-start.8) | collective-permute-done | bytes 133152 | tf_op jit(solution)/shard_map/ppermute | solution.py:443
  25.4 0.5 first.4
  25.9 2.3 %collective-permute-done.7.refs_2_ = bf16[520,128]{1,0:T(8,128)(2,1)S(1)} collective-permute-done((bf16[520,128]{1,0:T(8,128)(2,1)S(1)}, bf16[520,128]{1,0:T(8,128)(2,1)S(1)}, u32[]{:S(2)}, u32[]{:S(2)}) %collective-permute-start.7) | collective-permute-done | bytes 133152 | tf_op jit(solution)/shard_map/ppermute | solution.py:443
  28.3 0.5 first.5
  28.8 2.3 %collective-permute-done.6.refs_2_ = bf16[520,128]{1,0:T(8,128)(2,1)S(1)} collective-permute-done((bf16[520,128]{1,0:T(8,128)(2,1)S(1)}, bf16[520,128]{1,0:T(8,128)(2,1)S(1)}, u32[]{:S(2)}, u32[]{:S(2)}) %collective-permute-start.6) | collective-permute-done | bytes 133152 | tf_op jit(solution)/shard_map/ppermute | solution.py:443
  31.1 0.5 first.6
  31.6 1.8 %collective-permute-done.3.refs_2_ = bf16[520,128]{1,0:T(8,128)(2,1)S(1)} collective-permute-done((bf16[520,128]{1,0:T(8,128)(2,1)S(1)}, bf16[520,128]{1,0:T(8,128)(2,1)S(1)}, u32[]{:S(2)}, u32[]{:S(2)}) %collective-permute-start.3) | collective-permute-done | bytes 133152 | tf_op jit(solution)/shard_map/ppermute | solution.py:443
  33.4 0.5 first.7
  33.9 1.9 %collective-permute-start.9 = (f32[32,128]{1,0:T(8,128)S(1)}, f32[32,128]{1,0:T(8,128)S(1)}, u32[]{:S(2)}, u32[]{:S(2)}) collective-permute-start(f32[32,128]{1,0:T(8,128)S(1)} %get-tuple-element.43), channel_id=1, source_target_pairs={{0,4},{4,0},{8,12},{12,8},{1,5},{5,1},{9,13},{13,9},{2,6},{6,2},{1... | collective-permute-start | bytes 49160 | tf_op jit(solution)/shard_map/ppermute | solution.py:449
  35.8 2.6 %collective-permute-start.10 = (f32[32,128]{1,0:T(8,128)S(1)}, f32[32,128]{1,0:T(8,128)S(1)}, u32[]{:S(2)}, u32[]{:S(2)}) collective-permute-start(f32[32,128]{1,0:T(8,128)S(1)} %get-tuple-element.43), channel_id=1, source_target_pairs={{0,8},{4,12},{8,0},{12,4},{1,9},{5,13},{9,1},{13,5},{2,10},{6,14},... | collective-permute-start | bytes 49160 | tf_op jit(solution)/shard_map/ppermute | solution.py:449
  38.4 2.0 %collective-permute-done.10.refs_1_ = f32[32,128]{1,0:T(8,128)S(1)} collective-permute-done((f32[32,128]{1,0:T(8,128)S(1)}, f32[32,128]{1,0:T(8,128)S(1)}, u32[]{:S(2)}, u32[]{:S(2)}) %collective-permute-start.10) | collective-permute-done | bytes 16416 | tf_op jit(solution)/shard_map/ppermute | solution.py:449
  40.5 3.6 %collective-permute-done.11.refs_2_ = f32[32,128]{1,0:T(8,128)S(1)} collective-permute-done((f32[32,128]{1,0:T(8,128)S(1)}, f32[32,128]{1,0:T(8,128)S(1)}, u32[]{:S(2)}, u32[]{:S(2)}) %collective-permute-start.11) | collective-permute-done | bytes 16416 | tf_op jit(solution)/shard_map/ppermute | solution.py:449
  44.1 0.8 %second.1 = (f32[4,3,128,128]{3,2,1,0:T(8,128)S(1)}, f32[4,6,8,128]{3,2,1,0:T(8,128)S(1)}, f32[32,128]{1,0:T(8,128)S(1)}) custom-call(f32[32,128]{1,0:T(8,128)S(1)} %collective-permute-done.9.refs_0_, f32[32,128]{1,0:T(8,128)S(1)} %collective-permute-done.10.refs_1_, f32[32,128]{1,0:T(8,128)S(1)} %collective-permute-done.11.refs_2_, ...), custom_call_target="tpu_custom_call" | custom-call | flops 6553600 | bytes 1572864 | tf_op jit(solution)/shard_map/second/pallas_call | solution.py:375
  45.0 0.6 %collective-permute-start.13 = (f32[32,128]{1,0:T(8,128)S(1)}, f32[32,128]{1,0:T(8,128)S(1)}, u32[]{:S(2)}, u32[]{:S(2)}) collective-permute-start(f32[32,128]{1,0:T(8,128)S(1)} %get-tuple-element.52), channel_id=1, source_target_pairs={{0,8},{4,12},{8,0},{12,4},{1,9},{5,13},{9,1},{13,5},{2,10},{6,14},... | collective-permute-start | bytes 49160 | tf_op jit(solution)/shard_map/ppermute | solution.py:449
  45.6 3.8 %collective-permute-start.14 = (f32[32,128]{1,0:T(8,128)S(1)}, f32[32,128]{1,0:T(8,128)S(1)}, u32[]{:S(2)}, u32[]{:S(2)}) collective-permute-start(f32[32,128]{1,0:T(8,128)S(1)} %get-tuple-element.52), channel_id=1, source_target_pairs={{0,12},{4,8},{8,4},{12,0},{1,13},{5,9},{9,5},{13,1},{2,14},{6,10},... | collective-permute-start | bytes 49160 | tf_op jit(solution)/shard_map/ppermute | solution.py:449
  49.4 0.3 collective-permute-done.13.refs_1_
  49.7 1.6 %collective-permute-done.14.refs_2_ = f32[32,128]{1,0:T(8,128)S(1)} collective-permute-done((f32[32,128]{1,0:T(8,128)S(1)}, f32[32,128]{1,0:T(8,128)S(1)}, u32[]{:S(2)}, u32[]{:S(2)}) %collective-permute-start.14) | collective-permute-done | bytes 16416 | tf_op jit(solution)/shard_map/ppermute | solution.py:449
  51.2 0.9 %last.1 = f32[512,128]{1,0:T(8,128)} custom-call(f32[32,128]{1,0:T(8,128)S(1)} %collective-permute-done.12.refs_0_, f32[32,128]{1,0:T(8,128)S(1)} %collective-permute-done.13.refs_1_, f32[32,128]{1,0:T(8,128)S(1)} %collective-permute-done.14.refs_2_, f32[4,3,128,128]{3,2,1,0:T(8,128)S(1)} %get-tuple-element.53.refs_3_, ...), custom_call_target="tpu_custom_call" | custom-call | flops 655360 | bytes 1048576 | tf_op jit(solution)/shard_map/last/pallas_call | solution.py:412
  (19 shorter events, 1.2 us)
Async XLA Ops:
  2.0 1.7 %collective-permute-start = (f32[128,512]{1,0:T(8,128)S(1)}, f32[128,512]{1,0:T(8,128)S(1)}, u32[]{:S(2)}, u32[]{:S(2)}) collective-permute-start(f32[128,512]{1,0:T(8,128)S(1)} %get-tuple-element.31), channel_id=1, source_target_pairs={{0,1},{1,0},{2,3},{3,2},{4,5},{5,4},{6,7},{7,6},{8,9},{9,8},{10,11... | collective-permute-start | bytes 786440 | tf_op jit(solution)/shard_map/ppermute | solution.py:439
  5.9 1.6 %collective-permute-start.1 = (f32[128,512]{1,0:T(8,128)S(1)}, f32[128,512]{1,0:T(8,128)S(1)}, u32[]{:S(2)}, u32[]{:S(2)}) collective-permute-start(f32[128,512]{1,0:T(8,128)S(1)} %get-tuple-element.33), channel_id=1, source_target_pairs={{0,1},{1,0},{2,3},{3,2},{4,5},{5,4},{6,7},{7,6},{8,9},{9,8},{10,11... | collective-permute-start | bytes 786440 | tf_op jit(solution)/shard_map/ppermute | solution.py:439
  11.7 13.7 %copy-start = (f32[512,4]{0,1:T(4,128)S(1)}, f32[512,4]{0,1:T(4,128)}, u32[]{:S(2)}) copy-start(f32[512,4]{0,1:T(4,128)} %param.8) | copy-start | bytes 24580
  11.7 13.7 %copy-start.1 = (f32[512,2]{0,1:T(2,128)S(1)}, f32[512,2]{0,1:T(2,128)}, u32[]{:S(2)}) copy-start(f32[512,2]{0,1:T(2,128)} %param.7) | copy-start | bytes 12292
  11.7 13.7 %copy-start.2 = (f32[128]{0:T(128)S(1)}, f32[128]{0:T(128)}, u32[]{:S(2)}) copy-start(f32[128]{0:T(128)} %param.9) | copy-start | bytes 1540
  11.7 13.7 %collective-permute-start.2 = (f32[128,2048]{1,0:T(8,128)S(1)}, f32[128,2048]{1,0:T(8,128)S(1)}, u32[]{:S(2)}, u32[]{:S(2)}) collective-permute-start(f32[128,2048]{1,0:T(8,128)S(1)} %get-tuple-element.35), channel_id=1, source_target_pairs={{0,1},{1,0},{2,3},{3,2},{4,5},{5,4},{6,7},{7,6},{8,9},{9,8},{10,11... | collective-permute-start | bytes 3145736 | tf_op jit(solution)/shard_map/ppermute | solution.py:439
  14.2 1.6 %collective-permute-start.4 = (f32[128,512]{1,0:T(8,128)S(1)}, f32[128,512]{1,0:T(8,128)S(1)}, u32[]{:S(2)}, u32[]{:S(2)}) collective-permute-start(f32[128,512]{1,0:T(8,128)S(1)} %get-tuple-element.37), channel_id=1, source_target_pairs={{0,1},{1,0},{2,3},{3,2},{4,5},{5,4},{6,7},{7,6},{8,9},{9,8},{10,11... | collective-permute-start | bytes 786440 | tf_op jit(solution)/shard_map/ppermute | solution.py:439
  18.0 3.1 %collective-permute-start.5 = (f32[128,512]{1,0:T(8,128)S(1)}, f32[128,512]{1,0:T(8,128)S(1)}, u32[]{:S(2)}, u32[]{:S(2)}) collective-permute-start(f32[128,512]{1,0:T(8,128)S(1)} %get-tuple-element.39), channel_id=1, source_target_pairs={{0,1},{1,0},{2,3},{3,2},{4,5},{5,4},{6,7},{7,6},{8,9},{9,8},{10,11... | collective-permute-start | bytes 786440 | tf_op jit(solution)/shard_map/ppermute | solution.py:439
  18.2 7.2 %collective-permute-start.8 = (bf16[520,128]{1,0:T(8,128)(2,1)S(1)}, bf16[520,128]{1,0:T(8,128)(2,1)S(1)}, u32[]{:S(2)}, u32[]{:S(2)}) collective-permute-start(bf16[520,128]{1,0:T(8,128)(2,1)S(1)} %encode.6.refs_0_), channel_id=1, source_target_pairs={{0,2},{1,3},{2,0},{3,1},{4,6},{5,7},{6,4},{7,5},{8,10},{9,11},{10,... | collective-permute-start | bytes 399368 | tf_op jit(solution)/shard_map/ppermute | solution.py:443
  21.0 7.2 %collective-permute-start.7 = (bf16[520,128]{1,0:T(8,128)(2,1)S(1)}, bf16[520,128]{1,0:T(8,128)(2,1)S(1)}, u32[]{:S(2)}, u32[]{:S(2)}) collective-permute-start(bf16[520,128]{1,0:T(8,128)(2,1)S(1)} %encode.4.refs_0_), channel_id=1, source_target_pairs={{0,2},{1,3},{2,0},{3,1},{4,6},{5,7},{6,4},{7,5},{8,10},{9,11},{10,... | collective-permute-start | bytes 399368 | tf_op jit(solution)/shard_map/ppermute | solution.py:443
  21.3 9.9 %collective-permute-start.6 = (bf16[520,128]{1,0:T(8,128)(2,1)S(1)}, bf16[520,128]{1,0:T(8,128)(2,1)S(1)}, u32[]{:S(2)}, u32[]{:S(2)}) collective-permute-start(bf16[520,128]{1,0:T(8,128)(2,1)S(1)} %encode.7), channel_id=1, source_target_pairs={{0,2},{1,3},{2,0},{3,1},{4,6},{5,7},{6,4},{7,5},{8,10},{9,11},{10,... | collective-permute-start | bytes 399368 | tf_op jit(solution)/shard_map/ppermute | solution.py:443
  23.3 10.1 %collective-permute-start.3 = (bf16[520,128]{1,0:T(8,128)(2,1)S(1)}, bf16[520,128]{1,0:T(8,128)(2,1)S(1)}, u32[]{:S(2)}, u32[]{:S(2)}) collective-permute-start(bf16[520,128]{1,0:T(8,128)(2,1)S(1)} %encode.5.refs_0_), channel_id=1, source_target_pairs={{0,2},{1,3},{2,0},{3,1},{4,6},{5,7},{6,4},{7,5},{8,10},{9,11},{10,... | collective-permute-start | bytes 399368 | tf_op jit(solution)/shard_map/ppermute | solution.py:443
  33.9 4.5 %collective-permute-start.9 = (f32[32,128]{1,0:T(8,128)S(1)}, f32[32,128]{1,0:T(8,128)S(1)}, u32[]{:S(2)}, u32[]{:S(2)}) collective-permute-start(f32[32,128]{1,0:T(8,128)S(1)} %get-tuple-element.43), channel_id=1, source_target_pairs={{0,4},{4,0},{8,12},{12,8},{1,5},{5,1},{9,13},{13,9},{2,6},{6,2},{1... | collective-permute-start | bytes 49160 | tf_op jit(solution)/shard_map/ppermute | solution.py:449
  35.8 4.6 %collective-permute-start.10 = (f32[32,128]{1,0:T(8,128)S(1)}, f32[32,128]{1,0:T(8,128)S(1)}, u32[]{:S(2)}, u32[]{:S(2)}) collective-permute-start(f32[32,128]{1,0:T(8,128)S(1)} %get-tuple-element.43), channel_id=1, source_target_pairs={{0,8},{4,12},{8,0},{12,4},{1,9},{5,13},{9,1},{13,5},{2,10},{6,14},... | collective-permute-start | bytes 49160 | tf_op jit(solution)/shard_map/ppermute | solution.py:449
  38.4 5.7 %collective-permute-start.11 = (f32[32,128]{1,0:T(8,128)S(1)}, f32[32,128]{1,0:T(8,128)S(1)}, u32[]{:S(2)}, u32[]{:S(2)}) collective-permute-start(f32[32,128]{1,0:T(8,128)S(1)} %get-tuple-element.43), channel_id=1, source_target_pairs={{0,12},{4,8},{8,4},{12,0},{1,13},{5,9},{9,5},{13,1},{2,14},{6,10},... | collective-permute-start | bytes 49160 | tf_op jit(solution)/shard_map/ppermute | solution.py:449
  44.9 4.5 %collective-permute-start.12 = (f32[32,128]{1,0:T(8,128)S(1)}, f32[32,128]{1,0:T(8,128)S(1)}, u32[]{:S(2)}, u32[]{:S(2)}) collective-permute-start(f32[32,128]{1,0:T(8,128)S(1)} %get-tuple-element.52), channel_id=1, source_target_pairs={{0,4},{4,0},{8,12},{12,8},{1,5},{5,1},{9,13},{13,9},{2,6},{6,2},{1... | collective-permute-start | bytes 49160 | tf_op jit(solution)/shard_map/ppermute | solution.py:449
  45.0 4.7 %collective-permute-start.13 = (f32[32,128]{1,0:T(8,128)S(1)}, f32[32,128]{1,0:T(8,128)S(1)}, u32[]{:S(2)}, u32[]{:S(2)}) collective-permute-start(f32[32,128]{1,0:T(8,128)S(1)} %get-tuple-element.52), channel_id=1, source_target_pairs={{0,8},{4,12},{8,0},{12,4},{1,9},{5,13},{9,1},{13,5},{2,10},{6,14},... | collective-permute-start | bytes 49160 | tf_op jit(solution)/shard_map/ppermute | solution.py:449
  45.6 5.7 %collective-permute-start.14 = (f32[32,128]{1,0:T(8,128)S(1)}, f32[32,128]{1,0:T(8,128)S(1)}, u32[]{:S(2)}, u32[]{:S(2)}) collective-permute-start(f32[32,128]{1,0:T(8,128)S(1)} %get-tuple-element.52), channel_id=1, source_target_pairs={{0,12},{4,8},{8,4},{12,0},{1,13},{5,9},{9,5},{13,1},{2,14},{6,10},... | collective-permute-start | bytes 49160 | tf_op jit(solution)/shard_map/ppermute | solution.py:449

commit v5 on v4

--- a/solution.py
+++ b/solution.py
@@ -14,6 +14,7 @@
 GROUP = LANES * GATES
 BINADES = 251.0
 LOWEST = 125.0
+GIVE, KEEP = 0, 1
 F32 = jnp.float32
 BF16 = jnp.bfloat16
 
@@ -41,51 +42,49 @@
 PARAMS = pltpu.CompilerParams(vmem_limit_bytes=16 << 20)
 
 
-def product_kernel(chips, away, first, width, per_owner, tile, tokens_ref, weight_ref, *refs):
-    give_ref, keep_ref, x_ref, w_ref, sems = refs[-5:]
+def product_kernel(chips, away, parts, first, per_owner, tile, tokens_ref, weight_ref, *refs):
+    outs, (x_ref, w_ref, sems) = refs[-3 - len(parts) : -3], refs[-3:]
     me = lax.axis_index("chan")
     chip, core = me // 2, me % 2
     target = lax.rem(chip + away, chips)
-    tiles = width // tile
-    tokens_copy = pltpu.make_async_copy(tokens_ref, x_ref, sems.at[2 * tiles])
+    tiles = outs[0].shape[1] // tile
+    slots = len(parts) * tiles
+    tokens_copy = pltpu.make_async_copy(tokens_ref, x_ref, sems.at[slots])
     tokens_copy.start()
     copies = []
-    for which, owner in enumerate((2 * target + 1 - core, 2 * target + core)):
-        for i in range(tiles):
-            slot = which * tiles + i
-            column = pl.multiple_of(owner * per_owner + first + i * tile, tile)
-            copies.append(
-                pltpu.make_async_copy(
-                    weight_ref.at[:, pl.ds(column, tile)], w_ref.at[slot], sems.at[slot]
-                )
+    for slot in range(slots):
+        owner = 2 * target + (core if parts[slot // tiles] == KEEP else 1 - core)
+        column = pl.multiple_of(owner * per_owner + first + slot % tiles * tile, tile)
+        copies.append(
+            pltpu.make_async_copy(
+                weight_ref.at[:, pl.ds(column, tile)], w_ref.at[slot], sems.at[slot]
             )
-            copies[-1].start()
+        )
+        copies[-1].start()
     tokens_copy.wait()
     for slot, copy in enumerate(copies):
-        out_ref = give_ref if slot < tiles else keep_ref
         copy.wait()
-        out_ref[:, pl.ds(slot % tiles * tile, tile)] = jnp.dot(
+        outs[slot // tiles][:, pl.ds(slot % tiles * tile, tile)] = jnp.dot(
             x_ref[...], w_ref[slot], preferred_element_type=F32
         )
 
 
-def products(tokens, in_weight, chips, away, first, width, per_owner, after):
+def products(tokens, in_weight, chips, away, parts, first, width, per_owner, after):
     steps, depth = tokens.shape
     tile = GROUP
-    slots = 2 * width // tile
-    out = pltpu.VMEM((steps, width), F32)
+    slots = len(parts) * width // tile
     return pl.pallas_call(
-        functools.partial(product_kernel, chips, away, first, width, per_owner, tile),
-        out_shape=(out, out),
+        functools.partial(product_kernel, chips, away, parts, first, per_owner, tile),
+        out_shape=[pltpu.VMEM((steps, width), F32)] * len(parts),
         in_specs=in_hbm(2) + vmem(len(after)),
-        out_specs=vmem(2),
+        out_specs=vmem(len(parts)),
         scratch_shapes=[
             pltpu.VMEM((steps, depth), BF16),
             pltpu.VMEM((slots, depth, tile), BF16),
             pltpu.SemaphoreType.DMA((slots + 1,)),
         ],
         compiler_params=PARAMS,
-        cost_estimate=cost(4 * steps * depth * width, 4 * depth * width + 8 * steps * width),
+        cost_estimate=cost(2 * slots * steps * depth * tile, 2 * slots * depth * tile),
         name="products",
     )(tokens, in_weight, *after)
 
@@ -389,9 +388,10 @@
 
 def last_kernel(count, own_xor, *refs):
     received = refs[: count - 1]
-    hidden_ref, prefix_ref, out_ref, turn_ref = refs[count - 1 :]
+    hidden_ref, prefix_ref, out_ref, turn_ref, made_ref, sems = refs[count - 1 :]
     groups, _, steps, _ = hidden_ref.shape
     runs = steps // SUB
+    copies = []
     for group in range(groups):
         cell, hidden = arriving(count, own_xor, received, group, False)
         a, b, c, d, u, v = (prefix_ref[group, j] for j in range(6))
@@ -403,7 +403,12 @@
                 + hidden_ref[group, 1, rows, :] * hidden
                 + hidden_ref[group, 2, rows, :]
             )
-        out_ref[pl.ds(group * LANES, LANES), :] = turn_ref[...].T
+        rows = pl.ds(group * LANES, LANES)
+        made_ref[rows, :] = turn_ref[...].T
+        copies.append(pltpu.make_async_copy(made_ref.at[rows], out_ref.at[rows], sems.at[group]))
+        copies[-1].start()
+    for copy in copies:
+        copy.wait()
 
 
 def last(own_xor, received, hiddens, prefix):
@@ -414,8 +419,12 @@
         out_shape=jax.ShapeDtypeStruct((groups * LANES, steps), F32),
         in_specs=vmem(count + 1),
         compiler_params=PARAMS,
-        out_specs=pl.BlockSpec(memory_space=pltpu.VMEM),
-        scratch_shapes=[pltpu.VMEM((steps, LANES), F32)],
+        out_specs=pl.BlockSpec(memory_space=pltpu.HBM),
+        scratch_shapes=[
+            pltpu.VMEM((steps, LANES), F32),
+            pltpu.VMEM((groups * LANES, steps), F32),
+            pltpu.SemaphoreType.DMA((groups,)),
+        ],
         cost_estimate=cost(10 * groups * steps * LANES, 16 * groups * steps * LANES),
         name="last",
     )(*received, hiddens, prefix)
@@ -456,13 +465,23 @@
     for away in range(1, chips):
         for group in range(groups):
             give, keep = products(
-                tokens, in_weight, chips, away, group * GROUP, GROUP, per_owner, codes[-2:-1]
+                tokens,
+                in_weight,
+                chips,
+                away,
+                (GIVE, KEEP),
+                group * GROUP,
+                GROUP,
+                per_owner,
+                codes[-2:-1],
             )
             given = to_core(give)
             codes.append(encoded(keep, given))
             arrived[group].append(to_chip(codes[-1], away))
-    give, keep = products(tokens, in_weight, chips, 0, 0, per_owner, per_owner, codes[-1:])
+    local = (per_owner, per_owner, codes[-1:])
+    (give,) = products(tokens, in_weight, chips, 0, (GIVE,), 0, *local)
     given = to_core(give)
+    (keep,) = products(tokens, in_weight, chips, 0, (KEEP,), 0, *local)
     kept, prefixes, totals = [], [], []
     for group in range(groups):
         k, p, total = first(group, 1, keep, given, arrived[group], bias, weight, offset, totals)

time: 52.4 us -> 51.1 us (0.975)
  waiting for transfers between devices: 19.8 us -> 17.1 us
  Pallas kernels: 16.5 us -> 17.8 us
    ppermute x4, waiting for transfers between devices: 8.46 us -> 5.8 us  [to_chip(): return on_chip(lax.ppermute(value, 'chan', pairs))]
    pallas_call x5 -> x6, Pallas kernels: 11.9 us -> 13.2 us  [products(): pl.pallas_call(functools.partial(product_kernel, chips, away, parts, firs...]
  transfers between devices with their start and end apart: 15 -> 15, of which waited for: 11 -> 10; matrix products, arithmetic and copies ran while one was open for 0% -> 0% of each run, Pallas kernels for 11% -> 17%
where the time goes in v5:
time: 51.1 us; the launch traced here: 50.8 us
  Pallas kernels  17.8 us (35%)
  waiting for transfers between devices  17.1 us (33%)
  starting transfers between devices  15.8 us (31%)
    pallas_call x6, Pallas kernels, products(): pl.pallas_call(functools.partial(product_kernel, chips, away, parts, firs...  13.2 us
    ppermute x6, starting transfers between devices, to_blocks(): lax.ppermute(value, 'tm', [pair for pair in pairs if pair[1] < blocks])  8.95 us
    ppermute x6, waiting for transfers between devices, to_blocks(): lax.ppermute(value, 'tm', [pair for pair in pairs if pair[1] < blocks])  7.56 us
    ppermute x4, waiting for transfers between devices, to_chip(): return on_chip(lax.ppermute(value, 'chan', pairs))  5.8 us
    ppermute x4, starting transfers between devices, to_chip(): return on_chip(lax.ppermute(value, 'chan', pairs))  5 us
    ppermute x5, waiting for transfers between devices, to_core(): lax.ppermute(value, 'chan', [(i, i ^ 1) for i in range(owners)])  3.73 us
    pallas_call x4, Pallas kernels, first(): pl.pallas_call(functools.partial(first_kernel, start, groups, len(codes),...  2 us
    ppermute x5, starting transfers between devices, to_core(): lax.ppermute(value, 'chan', [(i, i ^ 1) for i in range(owners)])  1.85 us
  transfers between devices with their start and end apart: 15, of which 10 were waited for; matrix products, arithmetic and copies ran while one was open for 0% of the time, Pallas kernels for 17%

profile of v5, /device:TPU:0, one launch (start us, length us, event | category | flops | bytes accessed | tf_op | source)
XLA Modules:
  0.0 50.8 jit_solution(17991500314819873229)
XLA Ops:
  0.0 2.0 %products.6 = (f32[128,512]{1,0:T(8,128)S(1)}, f32[128,512]{1,0:T(8,128)S(1)}) custom-call(bf16[128,1024]{1,0:T(8,128)(2,1)} %tokens_ref.11, bf16[1024,8192]{1,0:T(8,128)(2,1)} %weight_ref.11), custom_call_target="tpu_custom_call" | custom-call | flops 268435456 | bytes 2097152 | tf_op jit(solution)/shard_map/products/pallas_call | solution.py:76
  2.0 0.6 %collective-permute-start = (f32[128,512]{1,0:T(8,128)S(1)}, f32[128,512]{1,0:T(8,128)S(1)}, u32[]{:S(2)}, u32[]{:S(2)}) collective-permute-start(f32[128,512]{1,0:T(8,128)S(1)} %get-tuple-element.29), channel_id=1, source_target_pairs={{0,1},{1,0},{2,3},{3,2},{4,5},{5,4},{6,7},{7,6},{8,9},{9,8},{10,11... | collective-permute-start | bytes 786440 | tf_op jit(solution)/shard_map/ppermute | solution.py:448
  2.5 1.2 %collective-permute-done.theirs_ref = f32[128,512]{1,0:T(8,128)S(1)} collective-permute-done((f32[128,512]{1,0:T(8,128)S(1)}, f32[128,512]{1,0:T(8,128)S(1)}, u32[]{:S(2)}, u32[]{:S(2)}) %collective-permute-start) | collective-permute-done | bytes 262176 | tf_op jit(solution)/shard_map/ppermute | solution.py:448
  3.9 2.0 %products.7 = (f32[128,512]{1,0:T(8,128)S(1)}, f32[128,512]{1,0:T(8,128)S(1)}) custom-call(bf16[128,1024]{1,0:T(8,128)(2,1)} %tokens_ref.11, bf16[1024,8192]{1,0:T(8,128)(2,1)} %weight_ref.11, bf16[520,128]{1,0:T(8,128)(2,1)S(1)} %encode.4.refs_0_), custom_call_target="tpu_custom_call" | custom-call | flops 268435456 | bytes 2097152 | tf_op jit(solution)/shard_map/products/pallas_call | solution.py:76
  5.9 0.4 collective-permute-start.1
  6.4 1.2 %collective-permute-done.1.theirs_ref = f32[128,512]{1,0:T(8,128)S(1)} collective-permute-done((f32[128,512]{1,0:T(8,128)S(1)}, f32[128,512]{1,0:T(8,128)S(1)}, u32[]{:S(2)}, u32[]{:S(2)}) %collective-permute-start.1) | collective-permute-done | bytes 262176 | tf_op jit(solution)/shard_map/ppermute | solution.py:448
  7.7 2.7 %products.9 = f32[128,2048]{1,0:T(8,128)S(1)} custom-call(bf16[128,1024]{1,0:T(8,128)(2,1)} %tokens_ref.11, bf16[1024,8192]{1,0:T(8,128)(2,1)} %weight_ref.11, bf16[520,128]{1,0:T(8,128)(2,1)S(1)} %encode.5.refs_0_), custom_call_target="tpu_custom_call" | custom-call | flops 536870912 | bytes 4194304 | tf_op jit(solution)/shard_map/products/pallas_call | solution.py:76
  10.4 0.4 collective-permute-start.2
  10.8 2.0 %products.10 = (f32[128,512]{1,0:T(8,128)S(1)}, f32[128,512]{1,0:T(8,128)S(1)}) custom-call(bf16[128,1024]{1,0:T(8,128)(2,1)} %tokens_ref.11, bf16[1024,8192]{1,0:T(8,128)(2,1)} %weight_ref.11), custom_call_target="tpu_custom_call" | custom-call | flops 268435456 | bytes 2097152 | tf_op jit(solution)/shard_map/products/pallas_call | solution.py:76
  13.0 1.4 %collective-permute-done.4.theirs_ref = f32[128,512]{1,0:T(8,128)S(1)} collective-permute-done((f32[128,512]{1,0:T(8,128)S(1)}, f32[128,512]{1,0:T(8,128)S(1)}, u32[]{:S(2)}, u32[]{:S(2)}) %collective-permute-start.4) | collective-permute-done | bytes 262176 | tf_op jit(solution)/shard_map/ppermute | solution.py:448
  14.7 2.0 %products.11 = (f32[128,512]{1,0:T(8,128)S(1)}, f32[128,512]{1,0:T(8,128)S(1)}) custom-call(bf16[128,1024]{1,0:T(8,128)(2,1)} %tokens_ref.11, bf16[1024,8192]{1,0:T(8,128)(2,1)} %weight_ref.11, bf16[520,128]{1,0:T(8,128)(2,1)S(1)} %encode.6.refs_0_), custom_call_target="tpu_custom_call" | custom-call | flops 268435456 | bytes 2097152 | tf_op jit(solution)/shard_map/products/pallas_call | solution.py:76
  16.9 2.8 %collective-permute-start.8 = (bf16[520,128]{1,0:T(8,128)(2,1)S(1)}, bf16[520,128]{1,0:T(8,128)(2,1)S(1)}, u32[]{:S(2)}, u32[]{:S(2)}) collective-permute-start(bf16[520,128]{1,0:T(8,128)(2,1)S(1)} %encode.6.refs_0_), channel_id=1, source_target_pairs={{0,2},{1,3},{2,0},{3,1},{4,6},{5,7},{6,4},{7,5},{8,10},{9,11},{10,... | collective-permute-start | bytes 399368 | tf_op jit(solution)/shard_map/ppermute | solution.py:452
  19.7 0.2 encode.7
  19.9 2.1 %collective-permute-start.6 = (bf16[520,128]{1,0:T(8,128)(2,1)S(1)}, bf16[520,128]{1,0:T(8,128)(2,1)S(1)}, u32[]{:S(2)}, u32[]{:S(2)}) collective-permute-start(bf16[520,128]{1,0:T(8,128)(2,1)S(1)} %encode.7), channel_id=1, source_target_pairs={{0,2},{1,3},{2,0},{3,1},{4,6},{5,7},{6,4},{7,5},{8,10},{9,11},{10,... | collective-permute-start | bytes 399368 | tf_op jit(solution)/shard_map/ppermute | solution.py:452
  22.1 2.6 %products.8.refs_0_ = f32[128,2048]{1,0:T(8,128)S(1)} custom-call(bf16[128,1024]{1,0:T(8,128)(2,1)} %tokens_ref.11, bf16[1024,8192]{1,0:T(8,128)(2,1)} %weight_ref.11, bf16[520,128]{1,0:T(8,128)(2,1)S(1)} %encode.5.refs_0_), custom_call_target="tpu_custom_call" | custom-call | flops 536870912 | bytes 4194304 | tf_op jit(solution)/shard_map/products/pallas_call | solution.py:76
  24.8 0.5 first.4
  25.3 1.6 %collective-permute-done.7.refs_2_ = bf16[520,128]{1,0:T(8,128)(2,1)S(1)} collective-permute-done((bf16[520,128]{1,0:T(8,128)(2,1)S(1)}, bf16[520,128]{1,0:T(8,128)(2,1)S(1)}, u32[]{:S(2)}, u32[]{:S(2)}) %collective-permute-start.7) | collective-permute-done | bytes 133152 | tf_op jit(solution)/shard_map/ppermute | solution.py:452
  26.9 0.5 first.5
  27.4 2.3 %collective-permute-done.6.refs_2_ = bf16[520,128]{1,0:T(8,128)(2,1)S(1)} collective-permute-done((bf16[520,128]{1,0:T(8,128)(2,1)S(1)}, bf16[520,128]{1,0:T(8,128)(2,1)S(1)}, u32[]{:S(2)}, u32[]{:S(2)}) %collective-permute-start.6) | collective-permute-done | bytes 133152 | tf_op jit(solution)/shard_map/ppermute | solution.py:452
  29.8 0.5 first.6
  30.3 1.8 %collective-permute-done.3.refs_2_ = bf16[520,128]{1,0:T(8,128)(2,1)S(1)} collective-permute-done((bf16[520,128]{1,0:T(8,128)(2,1)S(1)}, bf16[520,128]{1,0:T(8,128)(2,1)S(1)}, u32[]{:S(2)}, u32[]{:S(2)}) %collective-permute-start.3) | collective-permute-done | bytes 133152 | tf_op jit(solution)/shard_map/ppermute | solution.py:452
  32.1 0.5 first.7
  32.6 1.9 %collective-permute-start.9 = (f32[32,128]{1,0:T(8,128)S(1)}, f32[32,128]{1,0:T(8,128)S(1)}, u32[]{:S(2)}, u32[]{:S(2)}) collective-permute-start(f32[32,128]{1,0:T(8,128)S(1)} %get-tuple-element.39), channel_id=1, source_target_pairs={{0,4},{4,0},{8,12},{12,8},{1,5},{5,1},{9,13},{13,9},{2,6},{6,2},{1... | collective-permute-start | bytes 49160 | tf_op jit(solution)/shard_map/ppermute | solution.py:458
  34.5 2.6 %collective-permute-start.10 = (f32[32,128]{1,0:T(8,128)S(1)}, f32[32,128]{1,0:T(8,128)S(1)}, u32[]{:S(2)}, u32[]{:S(2)}) collective-permute-start(f32[32,128]{1,0:T(8,128)S(1)} %get-tuple-element.39), channel_id=1, source_target_pairs={{0,8},{4,12},{8,0},{12,4},{1,9},{5,13},{9,1},{13,5},{2,10},{6,14},... | collective-permute-start | bytes 49160 | tf_op jit(solution)/shard_map/ppermute | solution.py:458
  37.1 2.0 %collective-permute-done.10.refs_1_ = f32[32,128]{1,0:T(8,128)S(1)} collective-permute-done((f32[32,128]{1,0:T(8,128)S(1)}, f32[32,128]{1,0:T(8,128)S(1)}, u32[]{:S(2)}, u32[]{:S(2)}) %collective-permute-start.10) | collective-permute-done | bytes 16416 | tf_op jit(solution)/shard_map/ppermute | solution.py:458
  39.2 3.6 %collective-permute-done.11.refs_2_ = f32[32,128]{1,0:T(8,128)S(1)} collective-permute-done((f32[32,128]{1,0:T(8,128)S(1)}, f32[32,128]{1,0:T(8,128)S(1)}, u32[]{:S(2)}, u32[]{:S(2)}) %collective-permute-start.11) | collective-permute-done | bytes 16416 | tf_op jit(solution)/shard_map/ppermute | solution.py:458
  42.8 0.8 %second.1 = (f32[4,3,128,128]{3,2,1,0:T(8,128)S(1)}, f32[4,6,8,128]{3,2,1,0:T(8,128)S(1)}, f32[32,128]{1,0:T(8,128)S(1)}) custom-call(f32[32,128]{1,0:T(8,128)S(1)} %collective-permute-done.9.refs_0_, f32[32,128]{1,0:T(8,128)S(1)} %collective-permute-done.10.refs_1_, f32[32,128]{1,0:T(8,128)S(1)} %collective-permute-done.11.refs_2_, ...), custom_call_target="tpu_custom_call" | custom-call | flops 6553600 | bytes 1572864 | tf_op jit(solution)/shard_map/second/pallas_call | solution.py:374
  43.7 0.6 %collective-permute-start.13 = (f32[32,128]{1,0:T(8,128)S(1)}, f32[32,128]{1,0:T(8,128)S(1)}, u32[]{:S(2)}, u32[]{:S(2)}) collective-permute-start(f32[32,128]{1,0:T(8,128)S(1)} %get-tuple-element.48), channel_id=1, source_target_pairs={{0,8},{4,12},{8,0},{12,4},{1,9},{5,13},{9,1},{13,5},{2,10},{6,14},... | collective-permute-start | bytes 49160 | tf_op jit(solution)/shard_map/ppermute | solution.py:458
  44.3 3.8 %collective-permute-start.14 = (f32[32,128]{1,0:T(8,128)S(1)}, f32[32,128]{1,0:T(8,128)S(1)}, u32[]{:S(2)}, u32[]{:S(2)}) collective-permute-start(f32[32,128]{1,0:T(8,128)S(1)} %get-tuple-element.48), channel_id=1, source_target_pairs={{0,12},{4,8},{8,4},{12,0},{1,13},{5,9},{9,5},{13,1},{2,14},{6,10},... | collective-permute-start | bytes 49160 | tf_op jit(solution)/shard_map/ppermute | solution.py:458
  48.1 0.3 collective-permute-done.13.refs_1_
  48.4 1.6 %collective-permute-done.14.refs_2_ = f32[32,128]{1,0:T(8,128)S(1)} collective-permute-done((f32[32,128]{1,0:T(8,128)S(1)}, f32[32,128]{1,0:T(8,128)S(1)}, u32[]{:S(2)}, u32[]{:S(2)}) %collective-permute-start.14) | collective-permute-done | bytes 16416 | tf_op jit(solution)/shard_map/ppermute | solution.py:458
  49.9 0.9 %last.1 = f32[512,128]{1,0:T(8,128)} custom-call(f32[32,128]{1,0:T(8,128)S(1)} %collective-permute-done.12.refs_0_, f32[32,128]{1,0:T(8,128)S(1)} %collective-permute-done.13.refs_1_, f32[32,128]{1,0:T(8,128)S(1)} %collective-permute-done.14.refs_2_, f32[4,3,128,128]{3,2,1,0:T(8,128)S(1)} %get-tuple-element.49.refs_3_, ...), custom_call_target="tpu_custom_call" | custom-call | flops 655360 | bytes 1048576 | tf_op jit(solution)/shard_map/last/pallas_call | solution.py:417
  (20 shorter events, 1.2 us)
Async XLA Ops:
  2.0 1.7 %collective-permute-start = (f32[128,512]{1,0:T(8,128)S(1)}, f32[128,512]{1,0:T(8,128)S(1)}, u32[]{:S(2)}, u32[]{:S(2)}) collective-permute-start(f32[128,512]{1,0:T(8,128)S(1)} %get-tuple-element.29), channel_id=1, source_target_pairs={{0,1},{1,0},{2,3},{3,2},{4,5},{5,4},{6,7},{7,6},{8,9},{9,8},{10,11... | collective-permute-start | bytes 786440 | tf_op jit(solution)/shard_map/ppermute | solution.py:448
  5.9 1.6 %collective-permute-start.1 = (f32[128,512]{1,0:T(8,128)S(1)}, f32[128,512]{1,0:T(8,128)S(1)}, u32[]{:S(2)}, u32[]{:S(2)}) collective-permute-start(f32[128,512]{1,0:T(8,128)S(1)} %get-tuple-element.31), channel_id=1, source_target_pairs={{0,1},{1,0},{2,3},{3,2},{4,5},{5,4},{6,7},{7,6},{8,9},{9,8},{10,11... | collective-permute-start | bytes 786440 | tf_op jit(solution)/shard_map/ppermute | solution.py:448
  10.4 14.4 %collective-permute-start.2 = (f32[128,2048]{1,0:T(8,128)S(1)}, f32[128,2048]{1,0:T(8,128)S(1)}, u32[]{:S(2)}, u32[]{:S(2)}) collective-permute-start(f32[128,2048]{1,0:T(8,128)S(1)} %products.9), channel_id=1, source_target_pairs={{0,1},{1,0},{2,3},{3,2},{4,5},{5,4},{6,7},{7,6},{8,9},{9,8},{10,11... | collective-permute-start | bytes 3145736 | tf_op jit(solution)/shard_map/ppermute | solution.py:448
  12.8 1.6 %collective-permute-start.4 = (f32[128,512]{1,0:T(8,128)S(1)}, f32[128,512]{1,0:T(8,128)S(1)}, u32[]{:S(2)}, u32[]{:S(2)}) collective-permute-start(f32[128,512]{1,0:T(8,128)S(1)} %get-tuple-element.33), channel_id=1, source_target_pairs={{0,1},{1,0},{2,3},{3,2},{4,5},{5,4},{6,7},{7,6},{8,9},{9,8},{10,11... | collective-permute-start | bytes 786440 | tf_op jit(solution)/shard_map/ppermute | solution.py:448
  14.6 10.1 %copy-start = (f32[512,4]{0,1:T(4,128)S(1)}, f32[512,4]{0,1:T(4,128)}, u32[]{:S(2)}) copy-start(f32[512,4]{0,1:T(4,128)} %param.8) | copy-start | bytes 24580
  14.6 10.1 %copy-start.1 = (f32[512,2]{0,1:T(2,128)S(1)}, f32[512,2]{0,1:T(2,128)}, u32[]{:S(2)}) copy-start(f32[512,2]{0,1:T(2,128)} %param.7) | copy-start | bytes 12292
  14.7 10.1 %copy-start.2 = (f32[128]{0:T(128)S(1)}, f32[128]{0:T(128)}, u32[]{:S(2)}) copy-start(f32[128]{0:T(128)} %param.9) | copy-start | bytes 1540
  16.7 3.1 %collective-permute-start.5 = (f32[128,512]{1,0:T(8,128)S(1)}, f32[128,512]{1,0:T(8,128)S(1)}, u32[]{:S(2)}, u32[]{:S(2)}) collective-permute-start(f32[128,512]{1,0:T(8,128)S(1)} %get-tuple-element.35), channel_id=1, source_target_pairs={{0,1},{1,0},{2,3},{3,2},{4,5},{5,4},{6,7},{7,6},{8,9},{9,8},{10,11... | collective-permute-start | bytes 786440 | tf_op jit(solution)/shard_map/ppermute | solution.py:448
  16.9 7.9 %collective-permute-start.8 = (bf16[520,128]{1,0:T(8,128)(2,1)S(1)}, bf16[520,128]{1,0:T(8,128)(2,1)S(1)}, u32[]{:S(2)}, u32[]{:S(2)}) collective-permute-start(bf16[520,128]{1,0:T(8,128)(2,1)S(1)} %encode.6.refs_0_), channel_id=1, source_target_pairs={{0,2},{1,3},{2,0},{3,1},{4,6},{5,7},{6,4},{7,5},{8,10},{9,11},{10,... | collective-permute-start | bytes 399368 | tf_op jit(solution)/shard_map/ppermute | solution.py:452
  19.7 7.2 %collective-permute-start.7 = (bf16[520,128]{1,0:T(8,128)(2,1)S(1)}, bf16[520,128]{1,0:T(8,128)(2,1)S(1)}, u32[]{:S(2)}, u32[]{:S(2)}) collective-permute-start(bf16[520,128]{1,0:T(8,128)(2,1)S(1)} %encode.4.refs_0_), channel_id=1, source_target_pairs={{0,2},{1,3},{2,0},{3,1},{4,6},{5,7},{6,4},{7,5},{8,10},{9,11},{10,... | collective-permute-start | bytes 399368 | tf_op jit(solution)/shard_map/ppermute | solution.py:452
  19.9 9.9 %collective-permute-start.6 = (bf16[520,128]{1,0:T(8,128)(2,1)S(1)}, bf16[520,128]{1,0:T(8,128)(2,1)S(1)}, u32[]{:S(2)}, u32[]{:S(2)}) collective-permute-start(bf16[520,128]{1,0:T(8,128)(2,1)S(1)} %encode.7), channel_id=1, source_target_pairs={{0,2},{1,3},{2,0},{3,1},{4,6},{5,7},{6,4},{7,5},{8,10},{9,11},{10,... | collective-permute-start | bytes 399368 | tf_op jit(solution)/shard_map/ppermute | solution.py:452
  22.0 10.1 %collective-permute-start.3 = (bf16[520,128]{1,0:T(8,128)(2,1)S(1)}, bf16[520,128]{1,0:T(8,128)(2,1)S(1)}, u32[]{:S(2)}, u32[]{:S(2)}) collective-permute-start(bf16[520,128]{1,0:T(8,128)(2,1)S(1)} %encode.5.refs_0_), channel_id=1, source_target_pairs={{0,2},{1,3},{2,0},{3,1},{4,6},{5,7},{6,4},{7,5},{8,10},{9,11},{10,... | collective-permute-start | bytes 399368 | tf_op jit(solution)/shard_map/ppermute | solution.py:452
  32.6 4.5 %collective-permute-start.9 = (f32[32,128]{1,0:T(8,128)S(1)}, f32[32,128]{1,0:T(8,128)S(1)}, u32[]{:S(2)}, u32[]{:S(2)}) collective-permute-start(f32[32,128]{1,0:T(8,128)S(1)} %get-tuple-element.39), channel_id=1, source_target_pairs={{0,4},{4,0},{8,12},{12,8},{1,5},{5,1},{9,13},{13,9},{2,6},{6,2},{1... | collective-permute-start | bytes 49160 | tf_op jit(solution)/shard_map/ppermute | solution.py:458
  34.5 4.6 %collective-permute-start.10 = (f32[32,128]{1,0:T(8,128)S(1)}, f32[32,128]{1,0:T(8,128)S(1)}, u32[]{:S(2)}, u32[]{:S(2)}) collective-permute-start(f32[32,128]{1,0:T(8,128)S(1)} %get-tuple-element.39), channel_id=1, source_target_pairs={{0,8},{4,12},{8,0},{12,4},{1,9},{5,13},{9,1},{13,5},{2,10},{6,14},... | collective-permute-start | bytes 49160 | tf_op jit(solution)/shard_map/ppermute | solution.py:458
  37.1 5.7 %collective-permute-start.11 = (f32[32,128]{1,0:T(8,128)S(1)}, f32[32,128]{1,0:T(8,128)S(1)}, u32[]{:S(2)}, u32[]{:S(2)}) collective-permute-start(f32[32,128]{1,0:T(8,128)S(1)} %get-tuple-element.39), channel_id=1, source_target_pairs={{0,12},{4,8},{8,4},{12,0},{1,13},{5,9},{9,5},{13,1},{2,14},{6,10},... | collective-permute-start | bytes 49160 | tf_op jit(solution)/shard_map/ppermute | solution.py:458
  43.6 4.5 %collective-permute-start.12 = (f32[32,128]{1,0:T(8,128)S(1)}, f32[32,128]{1,0:T(8,128)S(1)}, u32[]{:S(2)}, u32[]{:S(2)}) collective-permute-start(f32[32,128]{1,0:T(8,128)S(1)} %get-tuple-element.48), channel_id=1, source_target_pairs={{0,4},{4,0},{8,12},{12,8},{1,5},{5,1},{9,13},{13,9},{2,6},{6,2},{1... | collective-permute-start | bytes 49160 | tf_op jit(solution)/shard_map/ppermute | solution.py:458
  43.7 4.7 %collective-permute-start.13 = (f32[32,128]{1,0:T(8,128)S(1)}, f32[32,128]{1,0:T(8,128)S(1)}, u32[]{:S(2)}, u32[]{:S(2)}) collective-permute-start(f32[32,128]{1,0:T(8,128)S(1)} %get-tuple-element.48), channel_id=1, source_target_pairs={{0,8},{4,12},{8,0},{12,4},{1,9},{5,13},{9,1},{13,5},{2,10},{6,14},... | collective-permute-start | bytes 49160 | tf_op jit(solution)/shard_map/ppermute | solution.py:458
  44.3 5.7 %collective-permute-start.14 = (f32[32,128]{1,0:T(8,128)S(1)}, f32[32,128]{1,0:T(8,128)S(1)}, u32[]{:S(2)}, u32[]{:S(2)}) collective-permute-start(f32[32,128]{1,0:T(8,128)S(1)} %get-tuple-element.48), channel_id=1, source_target_pairs={{0,12},{4,8},{8,4},{12,0},{1,13},{5,9},{9,5},{13,1},{2,14},{6,10},... | collective-permute-start | bytes 49160 | tf_op jit(solution)/shard_map/ppermute | solution.py:458

commit v6 on v5

--- a/solution.py
+++ b/solution.py
@@ -430,6 +430,11 @@
     )(*received, hiddens, prefix)
 
 
+def chunks_of(groups):
+    half = max(1, groups // 2)
+    return [(0, half)] + [(group, 1) for group in range(half, groups)]
+
+
 def shards(tokens, in_weight, recur_weight, gate_bias, forget_offset):
     steps = tokens.shape[0]
     channels = recur_weight.shape[0]
@@ -460,31 +465,32 @@
         return arriving
 
     tokens, in_weight = off_chip(tokens), off_chip(in_weight)
-    arrived = [[] for _ in range(groups)]
+    chunks = chunks_of(groups)
+    arrived = [[] for _ in chunks]
     codes = []
     for away in range(1, chips):
-        for group in range(groups):
+        for slot, (start, count) in enumerate(chunks):
             give, keep = products(
                 tokens,
                 in_weight,
                 chips,
                 away,
                 (GIVE, KEEP),
-                group * GROUP,
-                GROUP,
+                start * GROUP,
+                count * GROUP,
                 per_owner,
                 codes[-2:-1],
             )
             given = to_core(give)
             codes.append(encoded(keep, given))
-            arrived[group].append(to_chip(codes[-1], away))
+            arrived[slot].append(to_chip(codes[-1], away))
     local = (per_owner, per_owner, codes[-1:])
     (give,) = products(tokens, in_weight, chips, 0, (GIVE,), 0, *local)
     given = to_core(give)
     (keep,) = products(tokens, in_weight, chips, 0, (KEEP,), 0, *local)
     kept, prefixes, totals = [], [], []
-    for group in range(groups):
-        k, p, total = first(group, 1, keep, given, arrived[group], bias, weight, offset, totals)
+    for (start, count), codes in zip(chunks, arrived):
+        k, p, total = first(start, count, keep, given, codes, bias, weight, offset, totals)
         totals = [total]
         kept.append(k)
         prefixes.append(p)

time: 51.1 us -> 48.4 us (0.947)
  waiting for transfers between devices: 17.1 us -> 15.6 us
  Pallas kernels: 17.8 us -> 16.9 us
    pallas_call x6 -> x5, Pallas kernels: 13.2 us -> 11.9 us  [products(): pl.pallas_call(functools.partial(product_kernel, chips, away, parts, firs...]
    ppermute x5 -> x4, waiting for transfers between devices: 3.73 us -> 2.7 us  [to_core(): lax.ppermute(value, 'chan', [(i, i ^ 1) for i in range(owners)])]
    pallas_call x4 -> x3, Pallas kernels: 2 us -> 2.47 us  [first(): pl.pallas_call(functools.partial(first_kernel, start, groups, len(codes),...]
    ppermute x4 -> x3, waiting for transfers between devices: 5.8 us -> 5.38 us  [to_chip(): return on_chip(lax.ppermute(value, 'chan', pairs))]
    ppermute x5 -> x4, starting transfers between devices: 1.85 us -> 1.64 us  [to_core(): lax.ppermute(value, 'chan', [(i, i ^ 1) for i in range(owners)])]
    ppermute x4 -> x3, starting transfers between devices: 5 us -> 4.92 us  [to_chip(): return on_chip(lax.ppermute(value, 'chan', pairs))]
  transfers between devices with their start and end apart: 15 -> 13, of which waited for: 10 -> 9; matrix products, arithmetic and copies ran while one was open for 0% -> 0% of each run, Pallas kernels for 17% -> 14%
where the time goes in v6:
time: 48.4 us; the launch traced here: 48.2 us
  Pallas kernels  16.9 us (35%)
  waiting for transfers between devices  15.6 us (32%)
  starting transfers between devices  15.5 us (32%)
    pallas_call x5, Pallas kernels, products(): pl.pallas_call(functools.partial(product_kernel, chips, away, parts, firs...  11.9 us
    ppermute x6, starting transfers between devices, to_blocks(): lax.ppermute(value, 'tm', [pair for pair in pairs if pair[1] < blocks])  8.95 us
    ppermute x6, waiting for transfers between devices, to_blocks(): lax.ppermute(value, 'tm', [pair for pair in pairs if pair[1] < blocks])  7.56 us
    ppermute x3, waiting for transfers between devices, to_chip(): return on_chip(lax.ppermute(value, 'chan', pairs))  5.38 us
    ppermute x3, starting transfers between devices, to_chip(): return on_chip(lax.ppermute(value, 'chan', pairs))  4.92 us
    ppermute x4, waiting for transfers between devices, to_core(): lax.ppermute(value, 'chan', [(i, i ^ 1) for i in range(owners)])  2.7 us
    pallas_call x3, Pallas kernels, first(): pl.pallas_call(functools.partial(first_kernel, start, groups, len(codes),...  2.47 us
    ppermute x4, starting transfers between devices, to_core(): lax.ppermute(value, 'chan', [(i, i ^ 1) for i in range(owners)])  1.64 us
  transfers between devices with their start and end apart: 13, of which 9 were waited for; matrix products, arithmetic and copies ran while one was open for 0% of the time, Pallas kernels for 14%

profile of v6, /device:TPU:0, one launch (start us, length us, event | category | flops | bytes accessed | tf_op | source)
XLA Modules:
  0.0 48.2 jit_solution(4570718594954203412)
XLA Ops:
  0.0 2.6 %products.5 = (f32[128,1024]{1,0:T(8,128)S(1)}, f32[128,1024]{1,0:T(8,128)S(1)}) custom-call(bf16[128,1024]{1,0:T(8,128)(2,1)} %tokens_ref.9, bf16[1024,8192]{1,0:T(8,128)(2,1)} %weight_ref.9), custom_call_target="tpu_custom_call" | custom-call | flops 536870912 | bytes 4194304 | tf_op jit(solution)/shard_map/products/pallas_call | solution.py:76
  2.6 0.6 %collective-permute-start = (f32[128,1024]{1,0:T(8,128)S(1)}, f32[128,1024]{1,0:T(8,128)S(1)}, u32[]{:S(2)}, u32[]{:S(2)}) collective-permute-start(f32[128,1024]{1,0:T(8,128)S(1)} %get-tuple-element.24), channel_id=1, source_target_pairs={{0,1},{1,0},{2,3},{3,2},{4,5},{5,4},{6,7},{7,6},{8,9},{9,8},{10,11... | collective-permute-start | bytes 1572872 | tf_op jit(solution)/shard_map/ppermute | solution.py:453
  3.2 1.5 %collective-permute-done.theirs_ref = f32[128,1024]{1,0:T(8,128)S(1)} collective-permute-done((f32[128,1024]{1,0:T(8,128)S(1)}, f32[128,1024]{1,0:T(8,128)S(1)}, u32[]{:S(2)}, u32[]{:S(2)}) %collective-permute-start) | collective-permute-done | bytes 524320 | tf_op jit(solution)/shard_map/ppermute | solution.py:453
  4.7 0.4 encode.3.refs_0_
  5.2 2.0 %products.6 = (f32[128,512]{1,0:T(8,128)S(1)}, f32[128,512]{1,0:T(8,128)S(1)}) custom-call(bf16[128,1024]{1,0:T(8,128)(2,1)} %tokens_ref.9, bf16[1024,8192]{1,0:T(8,128)(2,1)} %weight_ref.9, bf16[1032,128]{1,0:T(8,128)(2,1)S(1)} %encode.3.refs_0_), custom_call_target="tpu_custom_call" | custom-call | flops 268435456 | bytes 2097152 | tf_op jit(solution)/shard_map/products/pallas_call | solution.py:76
  7.2 0.4 collective-permute-start.1
  7.6 1.2 %collective-permute-done.1.theirs_ref = f32[128,512]{1,0:T(8,128)S(1)} collective-permute-done((f32[128,512]{1,0:T(8,128)S(1)}, f32[128,512]{1,0:T(8,128)S(1)}, u32[]{:S(2)}, u32[]{:S(2)}) %collective-permute-start.1) | collective-permute-done | bytes 262176 | tf_op jit(solution)/shard_map/ppermute | solution.py:453
  8.8 0.2 encode.4.refs_0_
  9.0 2.6 %products.8 = f32[128,2048]{1,0:T(8,128)S(1)} custom-call(bf16[128,1024]{1,0:T(8,128)(2,1)} %tokens_ref.9, bf16[1024,8192]{1,0:T(8,128)(2,1)} %weight_ref.9, bf16[520,128]{1,0:T(8,128)(2,1)S(1)} %encode.4.refs_0_), custom_call_target="tpu_custom_call" | custom-call | flops 536870912 | bytes 4194304 | tf_op jit(solution)/shard_map/products/pallas_call | solution.py:76
  11.7 0.4 collective-permute-start.2
  12.1 2.0 %products.9 = (f32[128,512]{1,0:T(8,128)S(1)}, f32[128,512]{1,0:T(8,128)S(1)}) custom-call(bf16[128,1024]{1,0:T(8,128)(2,1)} %tokens_ref.9, bf16[1024,8192]{1,0:T(8,128)(2,1)} %weight_ref.9), custom_call_target="tpu_custom_call" | custom-call | flops 268435456 | bytes 2097152 | tf_op jit(solution)/shard_map/products/pallas_call | solution.py:76
  14.3 2.8 %collective-permute-start.6 = (bf16[1032,128]{1,0:T(8,128)(2,1)S(1)}, bf16[1032,128]{1,0:T(8,128)(2,1)S(1)}, u32[]{:S(2)}, u32[]{:S(2)}) collective-permute-start(bf16[1032,128]{1,0:T(8,128)(2,1)S(1)} %encode.3.refs_0_), channel_id=1, source_target_pairs={{0,2},{1,3},{2,0},{3,1},{4,6},{5,7},{6,4},{7,5},{8,10},{9,11},{10,... | collective-permute-start | bytes 792584 | tf_op jit(solution)/shard_map/ppermute | solution.py:457
  17.1 0.2 encode.5
  17.4 1.2 %collective-permute-start.5 = (bf16[520,128]{1,0:T(8,128)(2,1)S(1)}, bf16[520,128]{1,0:T(8,128)(2,1)S(1)}, u32[]{:S(2)}, u32[]{:S(2)}) collective-permute-start(bf16[520,128]{1,0:T(8,128)(2,1)S(1)} %encode.5), channel_id=1, source_target_pairs={{0,2},{1,3},{2,0},{3,1},{4,6},{5,7},{6,4},{7,5},{8,10},{9,11},{10,... | collective-permute-start | bytes 399368 | tf_op jit(solution)/shard_map/ppermute | solution.py:457
  18.6 0.9 %collective-permute-start.3 = (bf16[520,128]{1,0:T(8,128)(2,1)S(1)}, bf16[520,128]{1,0:T(8,128)(2,1)S(1)}, u32[]{:S(2)}, u32[]{:S(2)}) collective-permute-start(bf16[520,128]{1,0:T(8,128)(2,1)S(1)} %encode.4.refs_0_), channel_id=1, source_target_pairs={{0,2},{1,3},{2,0},{3,1},{4,6},{5,7},{6,4},{7,5},{8,10},{9,11},{10,... | collective-permute-start | bytes 399368 | tf_op jit(solution)/shard_map/ppermute | solution.py:457
  19.5 2.6 %products.7.refs_0_ = f32[128,2048]{1,0:T(8,128)S(1)} custom-call(bf16[128,1024]{1,0:T(8,128)(2,1)} %tokens_ref.9, bf16[1024,8192]{1,0:T(8,128)(2,1)} %weight_ref.9, bf16[520,128]{1,0:T(8,128)(2,1)S(1)} %encode.4.refs_0_), custom_call_target="tpu_custom_call" | custom-call | flops 536870912 | bytes 4194304 | tf_op jit(solution)/shard_map/products/pallas_call | solution.py:76
  22.1 2.2 %collective-permute-done.6.refs_2_ = bf16[1032,128]{1,0:T(8,128)(2,1)S(1)} collective-permute-done((bf16[1032,128]{1,0:T(8,128)(2,1)S(1)}, bf16[1032,128]{1,0:T(8,128)(2,1)S(1)}, u32[]{:S(2)}, u32[]{:S(2)}) %collective-permute-start.6) | collective-permute-done | bytes 264224 | tf_op jit(solution)/shard_map/ppermute | solution.py:457
  24.4 1.5 %first.3 = (f32[2,3,128,128]{3,2,1,0:T(8,128)S(1)}, f32[2,5,8,128]{3,2,1,0:T(8,128)S(1)}, f32[16,128]{1,0:T(8,128)S(1)}) custom-call(f32[128,2048]{1,0:T(8,128)S(1)} %products.7.refs_0_, f32[128,2048]{1,0:T(8,128)S(1)} %collective-permute-done.2.refs_1_, bf16[1032,128]{1,0:T(8,128)(2,1)S(1)} %collective-permute-done.6.refs_2_, f32[4,512]{1,0:T(4,128)S(1)} %bitcast.3, ...), custom_call_target="tpu_custom_call" | custom-call | flops 7864320 | bytes 2621440 | tf_op jit(solution)/shard_map/first/pallas_call | solution.py:258
  25.8 1.4 %collective-permute-done.5.refs_2_ = bf16[520,128]{1,0:T(8,128)(2,1)S(1)} collective-permute-done((bf16[520,128]{1,0:T(8,128)(2,1)S(1)}, bf16[520,128]{1,0:T(8,128)(2,1)S(1)}, u32[]{:S(2)}, u32[]{:S(2)}) %collective-permute-start.5) | collective-permute-done | bytes 133152 | tf_op jit(solution)/shard_map/ppermute | solution.py:457
  27.2 0.5 %first.4 = (f32[1,3,128,128]{3,2,1,0:T(8,128)S(1)}, f32[1,5,8,128]{3,2,1,0:T(8,128)S(1)}, f32[24,128]{1,0:T(8,128)S(1)}) custom-call(f32[128,2048]{1,0:T(8,128)S(1)} %products.7.refs_0_, f32[128,2048]{1,0:T(8,128)S(1)} %collective-permute-done.2.refs_1_, bf16[520,128]{1,0:T(8,128)(2,1)S(1)} %collective-permute-done.5.refs_2_, f32[4,512]{1,0:T(4,128)S(1)} %bitcast.4, ...), custom_call_target="tpu_custom_call" | custom-call | flops 3932160 | bytes 1310720 | tf_op jit(solution)/shard_map/first/pallas_call | solution.py:258
  27.7 1.8 %collective-permute-done.3.refs_2_ = bf16[520,128]{1,0:T(8,128)(2,1)S(1)} collective-permute-done((bf16[520,128]{1,0:T(8,128)(2,1)S(1)}, bf16[520,128]{1,0:T(8,128)(2,1)S(1)}, u32[]{:S(2)}, u32[]{:S(2)}) %collective-permute-start.3) | collective-permute-done | bytes 133152 | tf_op jit(solution)/shard_map/ppermute | solution.py:457
  29.5 0.5 %first.5 = (f32[1,3,128,128]{3,2,1,0:T(8,128)S(1)}, f32[1,5,8,128]{3,2,1,0:T(8,128)S(1)}, f32[32,128]{1,0:T(8,128)S(1)}) custom-call(f32[128,2048]{1,0:T(8,128)S(1)} %products.7.refs_0_, f32[128,2048]{1,0:T(8,128)S(1)} %collective-permute-done.2.refs_1_, bf16[520,128]{1,0:T(8,128)(2,1)S(1)} %collective-permute-done.3.refs_2_, f32[4,512]{1,0:T(4,128)S(1)} %bitcast.5, ...), custom_call_target="tpu_custom_call" | custom-call | flops 3932160 | bytes 1310720 | tf_op jit(solution)/shard_map/first/pallas_call | solution.py:258
  30.0 1.9 %collective-permute-start.7 = (f32[32,128]{1,0:T(8,128)S(1)}, f32[32,128]{1,0:T(8,128)S(1)}, u32[]{:S(2)}, u32[]{:S(2)}) collective-permute-start(f32[32,128]{1,0:T(8,128)S(1)} %get-tuple-element.31), channel_id=1, source_target_pairs={{0,4},{4,0},{8,12},{12,8},{1,5},{5,1},{9,13},{13,9},{2,6},{6,2},{1... | collective-permute-start | bytes 49160 | tf_op jit(solution)/shard_map/ppermute | solution.py:463
  31.9 2.6 %collective-permute-start.8 = (f32[32,128]{1,0:T(8,128)S(1)}, f32[32,128]{1,0:T(8,128)S(1)}, u32[]{:S(2)}, u32[]{:S(2)}) collective-permute-start(f32[32,128]{1,0:T(8,128)S(1)} %get-tuple-element.31), channel_id=1, source_target_pairs={{0,8},{4,12},{8,0},{12,4},{1,9},{5,13},{9,1},{13,5},{2,10},{6,14},... | collective-permute-start | bytes 49160 | tf_op jit(solution)/shard_map/ppermute | solution.py:463
  34.5 2.0 %collective-permute-done.8.refs_1_ = f32[32,128]{1,0:T(8,128)S(1)} collective-permute-done((f32[32,128]{1,0:T(8,128)S(1)}, f32[32,128]{1,0:T(8,128)S(1)}, u32[]{:S(2)}, u32[]{:S(2)}) %collective-permute-start.8) | collective-permute-done | bytes 16416 | tf_op jit(solution)/shard_map/ppermute | solution.py:463
  36.5 3.6 %collective-permute-done.9.refs_2_ = f32[32,128]{1,0:T(8,128)S(1)} collective-permute-done((f32[32,128]{1,0:T(8,128)S(1)}, f32[32,128]{1,0:T(8,128)S(1)}, u32[]{:S(2)}, u32[]{:S(2)}) %collective-permute-start.9) | collective-permute-done | bytes 16416 | tf_op jit(solution)/shard_map/ppermute | solution.py:463
  40.2 0.8 %second.1 = (f32[4,3,128,128]{3,2,1,0:T(8,128)S(1)}, f32[4,6,8,128]{3,2,1,0:T(8,128)S(1)}, f32[32,128]{1,0:T(8,128)S(1)}) custom-call(f32[32,128]{1,0:T(8,128)S(1)} %collective-permute-done.7.refs_0_, f32[32,128]{1,0:T(8,128)S(1)} %collective-permute-done.8.refs_1_, f32[32,128]{1,0:T(8,128)S(1)} %collective-permute-done.9.refs_2_, ...), custom_call_target="tpu_custom_call" | custom-call | flops 6553600 | bytes 1572864 | tf_op jit(solution)/shard_map/second/pallas_call | solution.py:374
  41.1 0.6 %collective-permute-start.11 = (f32[32,128]{1,0:T(8,128)S(1)}, f32[32,128]{1,0:T(8,128)S(1)}, u32[]{:S(2)}, u32[]{:S(2)}) collective-permute-start(f32[32,128]{1,0:T(8,128)S(1)} %get-tuple-element.38), channel_id=1, source_target_pairs={{0,8},{4,12},{8,0},{12,4},{1,9},{5,13},{9,1},{13,5},{2,10},{6,14},... | collective-permute-start | bytes 49160 | tf_op jit(solution)/shard_map/ppermute | solution.py:463
  41.6 3.8 %collective-permute-start.12 = (f32[32,128]{1,0:T(8,128)S(1)}, f32[32,128]{1,0:T(8,128)S(1)}, u32[]{:S(2)}, u32[]{:S(2)}) collective-permute-start(f32[32,128]{1,0:T(8,128)S(1)} %get-tuple-element.38), channel_id=1, source_target_pairs={{0,12},{4,8},{8,4},{12,0},{1,13},{5,9},{9,5},{13,1},{2,14},{6,10},... | collective-permute-start | bytes 49160 | tf_op jit(solution)/shard_map/ppermute | solution.py:463
  45.4 0.3 collective-permute-done.11.refs_1_
  45.8 1.6 %collective-permute-done.12.refs_2_ = f32[32,128]{1,0:T(8,128)S(1)} collective-permute-done((f32[32,128]{1,0:T(8,128)S(1)}, f32[32,128]{1,0:T(8,128)S(1)}, u32[]{:S(2)}, u32[]{:S(2)}) %collective-permute-start.12) | collective-permute-done | bytes 16416 | tf_op jit(solution)/shard_map/ppermute | solution.py:463
  47.3 0.9 %last.1 = f32[512,128]{1,0:T(8,128)} custom-call(f32[32,128]{1,0:T(8,128)S(1)} %collective-permute-done.10.refs_0_, f32[32,128]{1,0:T(8,128)S(1)} %collective-permute-done.11.refs_1_, f32[32,128]{1,0:T(8,128)S(1)} %collective-permute-done.12.refs_2_, f32[4,3,128,128]{3,2,1,0:T(8,128)S(1)} %get-tuple-element.39.refs_3_, ...), custom_call_target="tpu_custom_call" | custom-call | flops 655360 | bytes 1048576 | tf_op jit(solution)/shard_map/last/pallas_call | solution.py:417
  (13 shorter events, 0.3 us)
Async XLA Ops:
  2.6 2.1 %collective-permute-start = (f32[128,1024]{1,0:T(8,128)S(1)}, f32[128,1024]{1,0:T(8,128)S(1)}, u32[]{:S(2)}, u32[]{:S(2)}) collective-permute-start(f32[128,1024]{1,0:T(8,128)S(1)} %get-tuple-element.24), channel_id=1, source_target_pairs={{0,1},{1,0},{2,3},{3,2},{4,5},{5,4},{6,7},{7,6},{8,9},{9,8},{10,11... | collective-permute-start | bytes 1572872 | tf_op jit(solution)/shard_map/ppermute | solution.py:453
  7.2 1.6 %collective-permute-start.1 = (f32[128,512]{1,0:T(8,128)S(1)}, f32[128,512]{1,0:T(8,128)S(1)}, u32[]{:S(2)}, u32[]{:S(2)}) collective-permute-start(f32[128,512]{1,0:T(8,128)S(1)} %get-tuple-element.26), channel_id=1, source_target_pairs={{0,1},{1,0},{2,3},{3,2},{4,5},{5,4},{6,7},{7,6},{8,9},{9,8},{10,11... | collective-permute-start | bytes 786440 | tf_op jit(solution)/shard_map/ppermute | solution.py:453
  11.6 12.7 %copy-start = (f32[512,4]{0,1:T(4,128)S(1)}, f32[512,4]{0,1:T(4,128)}, u32[]{:S(2)}) copy-start(f32[512,4]{0,1:T(4,128)} %param.8) | copy-start | bytes 24580
  11.7 12.7 %copy-start.1 = (f32[512,2]{0,1:T(2,128)S(1)}, f32[512,2]{0,1:T(2,128)}, u32[]{:S(2)}) copy-start(f32[512,2]{0,1:T(2,128)} %param.7) | copy-start | bytes 12292
  11.7 12.7 %copy-start.2 = (f32[128]{0:T(128)S(1)}, f32[128]{0:T(128)}, u32[]{:S(2)}) copy-start(f32[128]{0:T(128)} %param.9) | copy-start | bytes 1540
  11.7 12.7 %collective-permute-start.2 = (f32[128,2048]{1,0:T(8,128)S(1)}, f32[128,2048]{1,0:T(8,128)S(1)}, u32[]{:S(2)}, u32[]{:S(2)}) collective-permute-start(f32[128,2048]{1,0:T(8,128)S(1)} %products.8), channel_id=1, source_target_pairs={{0,1},{1,0},{2,3},{3,2},{4,5},{5,4},{6,7},{7,6},{8,9},{9,8},{10,11... | collective-permute-start | bytes 3145736 | tf_op jit(solution)/shard_map/ppermute | solution.py:453
  14.1 3.0 %collective-permute-start.4 = (f32[128,512]{1,0:T(8,128)S(1)}, f32[128,512]{1,0:T(8,128)S(1)}, u32[]{:S(2)}, u32[]{:S(2)}) collective-permute-start(f32[128,512]{1,0:T(8,128)S(1)} %get-tuple-element.28), channel_id=1, source_target_pairs={{0,1},{1,0},{2,3},{3,2},{4,5},{5,4},{6,7},{7,6},{8,9},{9,8},{10,11... | collective-permute-start | bytes 786440 | tf_op jit(solution)/shard_map/ppermute | solution.py:453
  14.3 10.0 %collective-permute-start.6 = (bf16[1032,128]{1,0:T(8,128)(2,1)S(1)}, bf16[1032,128]{1,0:T(8,128)(2,1)S(1)}, u32[]{:S(2)}, u32[]{:S(2)}) collective-permute-start(bf16[1032,128]{1,0:T(8,128)(2,1)S(1)} %encode.3.refs_0_), channel_id=1, source_target_pairs={{0,2},{1,3},{2,0},{3,1},{4,6},{5,7},{6,4},{7,5},{8,10},{9,11},{10,... | collective-permute-start | bytes 792584 | tf_op jit(solution)/shard_map/ppermute | solution.py:457
  17.4 9.8 %collective-permute-start.5 = (bf16[520,128]{1,0:T(8,128)(2,1)S(1)}, bf16[520,128]{1,0:T(8,128)(2,1)S(1)}, u32[]{:S(2)}, u32[]{:S(2)}) collective-permute-start(bf16[520,128]{1,0:T(8,128)(2,1)S(1)} %encode.5), channel_id=1, source_target_pairs={{0,2},{1,3},{2,0},{3,1},{4,6},{5,7},{6,4},{7,5},{8,10},{9,11},{10,... | collective-permute-start | bytes 399368 | tf_op jit(solution)/shard_map/ppermute | solution.py:457
  18.6 10.9 %collective-permute-start.3 = (bf16[520,128]{1,0:T(8,128)(2,1)S(1)}, bf16[520,128]{1,0:T(8,128)(2,1)S(1)}, u32[]{:S(2)}, u32[]{:S(2)}) collective-permute-start(bf16[520,128]{1,0:T(8,128)(2,1)S(1)} %encode.4.refs_0_), channel_id=1, source_target_pairs={{0,2},{1,3},{2,0},{3,1},{4,6},{5,7},{6,4},{7,5},{8,10},{9,11},{10,... | collective-permute-start | bytes 399368 | tf_op jit(solution)/shard_map/ppermute | solution.py:457
  30.0 4.5 %collective-permute-start.7 = (f32[32,128]{1,0:T(8,128)S(1)}, f32[32,128]{1,0:T(8,128)S(1)}, u32[]{:S(2)}, u32[]{:S(2)}) collective-permute-start(f32[32,128]{1,0:T(8,128)S(1)} %get-tuple-element.31), channel_id=1, source_target_pairs={{0,4},{4,0},{8,12},{12,8},{1,5},{5,1},{9,13},{13,9},{2,6},{6,2},{1... | collective-permute-start | bytes 49160 | tf_op jit(solution)/shard_map/ppermute | solution.py:463
  31.9 4.6 %collective-permute-start.8 = (f32[32,128]{1,0:T(8,128)S(1)}, f32[32,128]{1,0:T(8,128)S(1)}, u32[]{:S(2)}, u32[]{:S(2)}) collective-permute-start(f32[32,128]{1,0:T(8,128)S(1)} %get-tuple-element.31), channel_id=1, source_target_pairs={{0,8},{4,12},{8,0},{12,4},{1,9},{5,13},{9,1},{13,5},{2,10},{6,14},... | collective-permute-start | bytes 49160 | tf_op jit(solution)/shard_map/ppermute | solution.py:463
  34.5 5.7 %collective-permute-start.9 = (f32[32,128]{1,0:T(8,128)S(1)}, f32[32,128]{1,0:T(8,128)S(1)}, u32[]{:S(2)}, u32[]{:S(2)}) collective-permute-start(f32[32,128]{1,0:T(8,128)S(1)} %get-tuple-element.31), channel_id=1, source_target_pairs={{0,12},{4,8},{8,4},{12,0},{1,13},{5,9},{9,5},{13,1},{2,14},{6,10},... | collective-permute-start | bytes 49160 | tf_op jit(solution)/shard_map/ppermute | solution.py:463
  41.0 4.5 %collective-permute-start.10 = (f32[32,128]{1,0:T(8,128)S(1)}, f32[32,128]{1,0:T(8,128)S(1)}, u32[]{:S(2)}, u32[]{:S(2)}) collective-permute-start(f32[32,128]{1,0:T(8,128)S(1)} %get-tuple-element.38), channel_id=1, source_target_pairs={{0,4},{4,0},{8,12},{12,8},{1,5},{5,1},{9,13},{13,9},{2,6},{6,2},{1... | collective-permute-start | bytes 49160 | tf_op jit(solution)/shard_map/ppermute | solution.py:463
  41.1 4.7 %collective-permute-start.11 = (f32[32,128]{1,0:T(8,128)S(1)}, f32[32,128]{1,0:T(8,128)S(1)}, u32[]{:S(2)}, u32[]{:S(2)}) collective-permute-start(f32[32,128]{1,0:T(8,128)S(1)} %get-tuple-element.38), channel_id=1, source_target_pairs={{0,8},{4,12},{8,0},{12,4},{1,9},{5,13},{9,1},{13,5},{2,10},{6,14},... | collective-permute-start | bytes 49160 | tf_op jit(solution)/shard_map/ppermute | solution.py:463
  41.6 5.7 %collective-permute-start.12 = (f32[32,128]{1,0:T(8,128)S(1)}, f32[32,128]{1,0:T(8,128)S(1)}, u32[]{:S(2)}, u32[]{:S(2)}) collective-permute-start(f32[32,128]{1,0:T(8,128)S(1)} %get-tuple-element.38), channel_id=1, source_target_pairs={{0,12},{4,8},{8,4},{12,0},{1,13},{5,9},{9,5},{13,1},{2,14},{6,10},... | collective-permute-start | bytes 49160 | tf_op jit(solution)/shard_map/ppermute | solution.py:463

commit v7 on v6

--- a/solution.py
+++ b/solution.py
@@ -15,6 +15,7 @@
 BINADES = 251.0
 LOWEST = 125.0
 GIVE, KEEP = 0, 1
+HALVES = 2
 F32 = jnp.float32
 BF16 = jnp.bfloat16
 
@@ -49,24 +50,31 @@
     target = lax.rem(chip + away, chips)
     tiles = outs[0].shape[1] // tile
     slots = len(parts) * tiles
-    tokens_copy = pltpu.make_async_copy(tokens_ref, x_ref, sems.at[slots])
+    depth = x_ref.shape[1] // HALVES
+    tokens_copy = pltpu.make_async_copy(tokens_ref, x_ref, sems.at[slots * HALVES])
     tokens_copy.start()
     copies = []
     for slot in range(slots):
         owner = 2 * target + (core if parts[slot // tiles] == KEEP else 1 - core)
         column = pl.multiple_of(owner * per_owner + first + slot % tiles * tile, tile)
-        copies.append(
-            pltpu.make_async_copy(
-                weight_ref.at[:, pl.ds(column, tile)], w_ref.at[slot], sems.at[slot]
+        for half in range(HALVES):
+            rows = pl.ds(half * depth, depth)
+            copies.append(
+                pltpu.make_async_copy(
+                    weight_ref.at[rows, pl.ds(column, tile)],
+                    w_ref.at[slot, rows],
+                    sems.at[slot * HALVES + half],
+                )
             )
-        )
-        copies[-1].start()
+            copies[-1].start()
     tokens_copy.wait()
-    for slot, copy in enumerate(copies):
+    for index, copy in enumerate(copies):
+        slot, half = index // HALVES, index % HALVES
+        rows = pl.ds(half * depth, depth)
+        out_ref, cols = outs[slot // tiles], pl.ds(slot % tiles * tile, tile)
         copy.wait()
-        outs[slot // tiles][:, pl.ds(slot % tiles * tile, tile)] = jnp.dot(
-            x_ref[...], w_ref[slot], preferred_element_type=F32
-        )
+        part = jnp.dot(x_ref[:, rows], w_ref[slot, rows, :], preferred_element_type=F32)
+        out_ref[:, cols] = part if half == 0 else out_ref[:, cols] + part
 
 
 def products(tokens, in_weight, chips, away, parts, first, width, per_owner, after):
@@ -81,7 +89,7 @@
         scratch_shapes=[
             pltpu.VMEM((steps, depth), BF16),
             pltpu.VMEM((slots, depth, tile), BF16),
-            pltpu.SemaphoreType.DMA((slots + 1,)),
+            pltpu.SemaphoreType.DMA((slots * HALVES + 1,)),
         ],
         compiler_params=PARAMS,
         cost_estimate=cost(2 * slots * steps * depth * tile, 2 * slots * depth * tile),
@@ -180,7 +188,8 @@
     return 1.0 / (1.0 + jnp.exp(-x))
 
 
-def first_kernel(start, groups, remotes, earlier, *refs):
+def first_kernel(start, place, remotes, earlier, *refs):
+    groups = 1
     refs = list(refs)
     mine_ref, theirs_ref = refs[:2]
     codes = refs[2 : 2 + remotes]
@@ -189,13 +198,12 @@
     kept_ref, prefix_ref, totals_ref, sum_ref, late_ref = refs[5 + remotes + earlier :]
     steps = mine_ref.shape[0]
     runs = steps // SUB
-    blocks = groups * GATES
     done = 0
     for ref in totals_before:
         totals_ref[pl.ds(done, ref.shape[0]), :] = ref[...]
         done += ref.shape[0]
     scales = [
-        ref[pl.ds(blocks * steps, SUB), :][0:1, :].astype(F32) for ref in codes
+        ref[pl.ds(ref.shape[0] - SUB, SUB), :][0:1, :].astype(F32) for ref in codes
     ]
     late_ref[...] = jnp.broadcast_to(offset_ref[...], (LANES, steps)).T
     lane = lax.broadcasted_iota(jnp.int32, (SUB, LANES), 1)
@@ -208,7 +216,8 @@
             cols = pl.ds(start * GROUP + block * LANES, LANES)
             value = mine_ref[:, cols] + theirs_ref[:, cols]
             for ref, scale in zip(codes, scales):
-                value = value + decoded(ref[pl.ds(block * steps, steps), :].astype(F32), scale)
+                rows = pl.ds((place * GATES + block) * steps, steps)
+                value = value + decoded(ref[rows, :].astype(F32), scale)
             sum_ref[q] = value
         channels = pl.ds((start + group) * LANES, LANES)
         biases = [
@@ -251,12 +260,13 @@
             totals_ref[pl.ds(done + group * SUB + index, 1), :] = jnp.zeros((1, LANES), F32)
 
 
-def first(start, groups, mine, theirs, codes, bias, weight, offset, earlier):
+def first(start, place, mine, theirs, codes, bias, weight, offset, earlier):
     steps = mine.shape[0]
+    groups = 1
     rows = sum(e.shape[0] for e in earlier) + groups * SUB
     count = 5 + len(codes) + len(earlier)
     return pl.pallas_call(
-        functools.partial(first_kernel, start, groups, len(codes), len(earlier)),
+        functools.partial(first_kernel, start, place, len(codes), len(earlier)),
         out_shape=(
             pltpu.VMEM((groups, 3, steps, LANES), F32),
             pltpu.VMEM((groups, 5, SUB, LANES), F32),
@@ -431,8 +441,8 @@
 
 
 def chunks_of(groups):
-    half = max(1, groups // 2)
-    return [(0, half)] + [(group, 1) for group in range(half, groups)]
+    middle = [(1, groups - 2)] if groups > 2 else []
+    return [(0, 1)] + middle + [(groups - 1, 1)] * (groups > 1)
 
 
 def shards(tokens, in_weight, recur_weight, gate_bias, forget_offset):
@@ -490,10 +500,13 @@
     (keep,) = products(tokens, in_weight, chips, 0, (KEEP,), 0, *local)
     kept, prefixes, totals = [], [], []
     for (start, count), codes in zip(chunks, arrived):
-        k, p, total = first(start, count, keep, given, codes, bias, weight, offset, totals)
-        totals = [total]
-        kept.append(k)
-        prefixes.append(p)
+        for place in range(count):
+            k, p, total = first(
+                start + place, place, keep, given, codes, bias, weight, offset, totals
+            )
+            totals = [total]
+            kept.append(k)
+            prefixes.append(p)
     hiddens, prefix, total = second(own_xor, to_blocks(totals[0]), kept, prefixes, weight)
     return last(own_xor, to_blocks(total), hiddens, prefix)
 

time: 48.4 us -> 48.4 us (level)
  waiting for transfers between devices: 15.6 us -> 16.3 us
  Pallas kernels: 16.9 us -> 16.4 us
    ppermute x6, waiting for transfers between devices: 7.56 us -> 5.88 us  [to_blocks(): lax.ppermute(value, 'tm', [pair for pair in pairs if pair[1] < blocks])]
    ppermute x4, waiting for transfers between devices: 2.7 us -> 4.1 us  [to_core(): lax.ppermute(value, 'chan', [(i, i ^ 1) for i in range(owners)])]
    ppermute x3, waiting for transfers between devices: 5.38 us -> 6.34 us  [to_chip(): return on_chip(lax.ppermute(value, 'chan', pairs))]
    pallas_call x3 -> x4, Pallas kernels: 2.47 us -> 2.01 us  [first(): pl.pallas_call(functools.partial(first_kernel, start, place, len(codes),...]
  transfers between devices with their start and end apart: 13 -> 13, of which waited for: 9 -> 10; matrix products, arithmetic and copies ran while one was open for 0% -> 0% of each run, Pallas kernels for 14% -> 15%
where the time goes in v7:
time: 48.4 us; the launch traced here: 48.2 us
  Pallas kernels  16.4 us (34%)
  waiting for transfers between devices  16.3 us (34%)
  starting transfers between devices  15.4 us (32%)
    pallas_call x5, Pallas kernels, products(): pl.pallas_call(functools.partial(product_kernel, chips, away, parts, firs...  11.8 us
    ppermute x6, starting transfers between devices, to_blocks(): lax.ppermute(value, 'tm', [pair for pair in pairs if pair[1] < blocks])  9.02 us
    ppermute x3, waiting for transfers between devices, to_chip(): return on_chip(lax.ppermute(value, 'chan', pairs))  6.34 us
    ppermute x6, waiting for transfers between devices, to_blocks(): lax.ppermute(value, 'tm', [pair for pair in pairs if pair[1] < blocks])  5.88 us
    ppermute x3, starting transfers between devices, to_chip(): return on_chip(lax.ppermute(value, 'chan', pairs))  4.69 us
    ppermute x4, waiting for transfers between devices, to_core(): lax.ppermute(value, 'chan', [(i, i ^ 1) for i in range(owners)])  4.1 us
    pallas_call x4, Pallas kernels, first(): pl.pallas_call(functools.partial(first_kernel, start, place, len(codes),...  2.01 us
    ppermute x4, starting transfers between devices, to_core(): lax.ppermute(value, 'chan', [(i, i ^ 1) for i in range(owners)])  1.64 us
  transfers between devices with their start and end apart: 13, of which 10 were waited for; matrix products, arithmetic and copies ran while one was open for 0% of the time, Pallas kernels for 15%

profile of v7, /device:TPU:0, one launch (start us, length us, event | category | flops | bytes accessed | tf_op | source)
XLA Modules:
  0.0 48.2 jit_solution(4627714377596358892)
XLA Ops:
  0.0 1.9 %products.5 = (f32[128,512]{1,0:T(8,128)S(1)}, f32[128,512]{1,0:T(8,128)S(1)}) custom-call(bf16[128,1024]{1,0:T(8,128)(2,1)} %tokens_ref.9, bf16[1024,8192]{1,0:T(8,128)(2,1)} %weight_ref.9), custom_call_target="tpu_custom_call" | custom-call | flops 268435456 | bytes 2097152 | tf_op jit(solution)/shard_map/products/pallas_call | solution.py:84
  1.9 0.6 %collective-permute-start = (f32[128,512]{1,0:T(8,128)S(1)}, f32[128,512]{1,0:T(8,128)S(1)}, u32[]{:S(2)}, u32[]{:S(2)}) collective-permute-start(f32[128,512]{1,0:T(8,128)S(1)} %get-tuple-element.27), channel_id=1, source_target_pairs={{0,1},{1,0},{2,3},{3,2},{4,5},{5,4},{6,7},{7,6},{8,9},{9,8},{10,11... | collective-permute-start | bytes 786440 | tf_op jit(solution)/shard_map/ppermute | solution.py:463
  2.5 1.2 %collective-permute-done.theirs_ref = f32[128,512]{1,0:T(8,128)S(1)} collective-permute-done((f32[128,512]{1,0:T(8,128)S(1)}, f32[128,512]{1,0:T(8,128)S(1)}, u32[]{:S(2)}, u32[]{:S(2)}) %collective-permute-start) | collective-permute-done | bytes 262176 | tf_op jit(solution)/shard_map/ppermute | solution.py:463
  3.6 0.2 encode.3.refs_0_
  3.9 1.9 %products.6 = (f32[128,512]{1,0:T(8,128)S(1)}, f32[128,512]{1,0:T(8,128)S(1)}) custom-call(bf16[128,1024]{1,0:T(8,128)(2,1)} %tokens_ref.9, bf16[1024,8192]{1,0:T(8,128)(2,1)} %weight_ref.9, bf16[520,128]{1,0:T(8,128)(2,1)S(1)} %encode.3.refs_0_), custom_call_target="tpu_custom_call" | custom-call | flops 268435456 | bytes 2097152 | tf_op jit(solution)/shard_map/products/pallas_call | solution.py:84
  5.8 0.4 collective-permute-start.1
  6.2 1.2 %collective-permute-done.1.theirs_ref = f32[128,512]{1,0:T(8,128)S(1)} collective-permute-done((f32[128,512]{1,0:T(8,128)S(1)}, f32[128,512]{1,0:T(8,128)S(1)}, u32[]{:S(2)}, u32[]{:S(2)}) %collective-permute-start.1) | collective-permute-done | bytes 262176 | tf_op jit(solution)/shard_map/ppermute | solution.py:463
  7.6 2.7 %products.8 = f32[128,2048]{1,0:T(8,128)S(1)} custom-call(bf16[128,1024]{1,0:T(8,128)(2,1)} %tokens_ref.9, bf16[1024,8192]{1,0:T(8,128)(2,1)} %weight_ref.9, bf16[520,128]{1,0:T(8,128)(2,1)S(1)} %encode.4.refs_0_), custom_call_target="tpu_custom_call" | custom-call | flops 536870912 | bytes 4194304 | tf_op jit(solution)/shard_map/products/pallas_call | solution.py:84
  10.3 0.4 collective-permute-start.2
  10.8 2.7 %products.9 = (f32[128,1024]{1,0:T(8,128)S(1)}, f32[128,1024]{1,0:T(8,128)S(1)}) custom-call(bf16[128,1024]{1,0:T(8,128)(2,1)} %tokens_ref.9, bf16[1024,8192]{1,0:T(8,128)(2,1)} %weight_ref.9), custom_call_target="tpu_custom_call" | custom-call | flops 536870912 | bytes 4194304 | tf_op jit(solution)/shard_map/products/pallas_call | solution.py:84
  13.6 1.8 %collective-permute-done.4.theirs_ref = f32[128,1024]{1,0:T(8,128)S(1)} collective-permute-done((f32[128,1024]{1,0:T(8,128)S(1)}, f32[128,1024]{1,0:T(8,128)S(1)}, u32[]{:S(2)}, u32[]{:S(2)}) %collective-permute-start.4) | collective-permute-done | bytes 524320 | tf_op jit(solution)/shard_map/ppermute | solution.py:463
  15.4 0.4 encode.5
  15.8 2.7 %collective-permute-start.5 = (bf16[1032,128]{1,0:T(8,128)(2,1)S(1)}, bf16[1032,128]{1,0:T(8,128)(2,1)S(1)}, u32[]{:S(2)}, u32[]{:S(2)}) collective-permute-start(bf16[1032,128]{1,0:T(8,128)(2,1)S(1)} %encode.5), channel_id=1, source_target_pairs={{0,2},{1,3},{2,0},{3,1},{4,6},{5,7},{6,4},{7,5},{8,10},{9,11},{10,... | collective-permute-start | bytes 792584 | tf_op jit(solution)/shard_map/ppermute | solution.py:467
  18.6 1.9 %collective-permute-start.3 = (bf16[520,128]{1,0:T(8,128)(2,1)S(1)}, bf16[520,128]{1,0:T(8,128)(2,1)S(1)}, u32[]{:S(2)}, u32[]{:S(2)}) collective-permute-start(bf16[520,128]{1,0:T(8,128)(2,1)S(1)} %encode.4.refs_0_), channel_id=1, source_target_pairs={{0,2},{1,3},{2,0},{3,1},{4,6},{5,7},{6,4},{7,5},{8,10},{9,11},{10,... | collective-permute-start | bytes 399368 | tf_op jit(solution)/shard_map/ppermute | solution.py:467
  20.5 2.7 %products.7.refs_0_ = f32[128,2048]{1,0:T(8,128)S(1)} custom-call(bf16[128,1024]{1,0:T(8,128)(2,1)} %tokens_ref.9, bf16[1024,8192]{1,0:T(8,128)(2,1)} %weight_ref.9, bf16[520,128]{1,0:T(8,128)(2,1)S(1)} %encode.4.refs_0_), custom_call_target="tpu_custom_call" | custom-call | flops 536870912 | bytes 4194304 | tf_op jit(solution)/shard_map/products/pallas_call | solution.py:84
  23.2 5.4 %collective-permute-done.6.refs_2_ = bf16[520,128]{1,0:T(8,128)(2,1)S(1)} collective-permute-done((bf16[520,128]{1,0:T(8,128)(2,1)S(1)}, bf16[520,128]{1,0:T(8,128)(2,1)S(1)}, u32[]{:S(2)}, u32[]{:S(2)}) %collective-permute-start.6) | collective-permute-done | bytes 133152 | tf_op jit(solution)/shard_map/ppermute | solution.py:467
  28.6 0.5 %first.4 = (f32[1,3,128,128]{3,2,1,0:T(8,128)S(1)}, f32[1,5,8,128]{3,2,1,0:T(8,128)S(1)}, f32[8,128]{1,0:T(8,128)S(1)}) custom-call(f32[128,2048]{1,0:T(8,128)S(1)} %products.7.refs_0_, f32[128,2048]{1,0:T(8,128)S(1)} %collective-permute-done.2.refs_1_, bf16[520,128]{1,0:T(8,128)(2,1)S(1)} %collective-permute-done.6.refs_2_, f32[4,512]{1,0:T(4,128)S(1)} %bitcast.3, ...), custom_call_target="tpu_custom_call" | custom-call | flops 3932160 | bytes 1310720 | tf_op jit(solution)/shard_map/first/pallas_call | solution.py:268
  29.1 0.5 %first.5 = (f32[1,3,128,128]{3,2,1,0:T(8,128)S(1)}, f32[1,5,8,128]{3,2,1,0:T(8,128)S(1)}, f32[16,128]{1,0:T(8,128)S(1)}) custom-call(f32[128,2048]{1,0:T(8,128)S(1)} %products.7.refs_0_, f32[128,2048]{1,0:T(8,128)S(1)} %collective-permute-done.2.refs_1_, bf16[1032,128]{1,0:T(8,128)(2,1)S(1)} %collective-permute-done.5.refs_2_, f32[4,512]{1,0:T(4,128)S(1)} %bitcast.4, ...), custom_call_target="tpu_custom_call" | custom-call | flops 3932160 | bytes 1310720 | tf_op jit(solution)/shard_map/first/pallas_call | solution.py:268
  29.6 0.5 %first.6 = (f32[1,3,128,128]{3,2,1,0:T(8,128)S(1)}, f32[1,5,8,128]{3,2,1,0:T(8,128)S(1)}, f32[24,128]{1,0:T(8,128)S(1)}) custom-call(f32[128,2048]{1,0:T(8,128)S(1)} %products.7.refs_0_, f32[128,2048]{1,0:T(8,128)S(1)} %collective-permute-done.2.refs_1_, bf16[1032,128]{1,0:T(8,128)(2,1)S(1)} %collective-permute-done.5.refs_2_, f32[4,512]{1,0:T(4,128)S(1)} %bitcast.5, ...), custom_call_target="tpu_custom_call" | custom-call | flops 3932160 | bytes 1310720 | tf_op jit(solution)/shard_map/first/pallas_call | solution.py:268
  30.1 1.0 %collective-permute-done.3.refs_2_ = bf16[520,128]{1,0:T(8,128)(2,1)S(1)} collective-permute-done((bf16[520,128]{1,0:T(8,128)(2,1)S(1)}, bf16[520,128]{1,0:T(8,128)(2,1)S(1)}, u32[]{:S(2)}, u32[]{:S(2)}) %collective-permute-start.3) | collective-permute-done | bytes 133152 | tf_op jit(solution)/shard_map/ppermute | solution.py:467
  31.1 0.5 %first.7 = (f32[1,3,128,128]{3,2,1,0:T(8,128)S(1)}, f32[1,5,8,128]{3,2,1,0:T(8,128)S(1)}, f32[32,128]{1,0:T(8,128)S(1)}) custom-call(f32[128,2048]{1,0:T(8,128)S(1)} %products.7.refs_0_, f32[128,2048]{1,0:T(8,128)S(1)} %collective-permute-done.2.refs_1_, bf16[520,128]{1,0:T(8,128)(2,1)S(1)} %collective-permute-done.3.refs_2_, f32[4,512]{1,0:T(4,128)S(1)} %bitcast.6, ...), custom_call_target="tpu_custom_call" | custom-call | flops 3932160 | bytes 1310720 | tf_op jit(solution)/shard_map/first/pallas_call | solution.py:268
  31.6 3.9 %collective-permute-start.9 = (f32[32,128]{1,0:T(8,128)S(1)}, f32[32,128]{1,0:T(8,128)S(1)}, u32[]{:S(2)}, u32[]{:S(2)}) collective-permute-start(f32[32,128]{1,0:T(8,128)S(1)} %get-tuple-element.35), channel_id=1, source_target_pairs={{0,12},{4,8},{8,4},{12,0},{1,13},{5,9},{9,5},{13,1},{2,14},{6,10},... | collective-permute-start | bytes 49160 | tf_op jit(solution)/shard_map/ppermute | solution.py:473
  35.5 0.6 %collective-permute-start.7 = (f32[32,128]{1,0:T(8,128)S(1)}, f32[32,128]{1,0:T(8,128)S(1)}, u32[]{:S(2)}, u32[]{:S(2)}) collective-permute-start(f32[32,128]{1,0:T(8,128)S(1)} %get-tuple-element.35), channel_id=1, source_target_pairs={{0,4},{4,0},{8,12},{12,8},{1,5},{5,1},{9,13},{13,9},{2,6},{6,2},{1... | collective-permute-start | bytes 49160 | tf_op jit(solution)/shard_map/ppermute | solution.py:473
  36.2 1.1 %collective-permute-done.9.refs_2_ = f32[32,128]{1,0:T(8,128)S(1)} collective-permute-done((f32[32,128]{1,0:T(8,128)S(1)}, f32[32,128]{1,0:T(8,128)S(1)}, u32[]{:S(2)}, u32[]{:S(2)}) %collective-permute-start.9) | collective-permute-done | bytes 16416 | tf_op jit(solution)/shard_map/ppermute | solution.py:473
  37.2 2.9 %collective-permute-done.8.refs_1_ = f32[32,128]{1,0:T(8,128)S(1)} collective-permute-done((f32[32,128]{1,0:T(8,128)S(1)}, f32[32,128]{1,0:T(8,128)S(1)}, u32[]{:S(2)}, u32[]{:S(2)}) %collective-permute-start.8) | collective-permute-done | bytes 16416 | tf_op jit(solution)/shard_map/ppermute | solution.py:473
  40.2 0.8 %second.1 = (f32[4,3,128,128]{3,2,1,0:T(8,128)S(1)}, f32[4,6,8,128]{3,2,1,0:T(8,128)S(1)}, f32[32,128]{1,0:T(8,128)S(1)}) custom-call(f32[32,128]{1,0:T(8,128)S(1)} %collective-permute-done.7.refs_0_, f32[32,128]{1,0:T(8,128)S(1)} %collective-permute-done.8.refs_1_, f32[32,128]{1,0:T(8,128)S(1)} %collective-permute-done.9.refs_2_, ...), custom_call_target="tpu_custom_call" | custom-call | flops 6553600 | bytes 1572864 | tf_op jit(solution)/shard_map/second/pallas_call | solution.py:384
  41.0 1.5 %collective-permute-start.12 = (f32[32,128]{1,0:T(8,128)S(1)}, f32[32,128]{1,0:T(8,128)S(1)}, u32[]{:S(2)}, u32[]{:S(2)}) collective-permute-start(f32[32,128]{1,0:T(8,128)S(1)} %get-tuple-element.44), channel_id=1, source_target_pairs={{0,12},{4,8},{8,4},{12,0},{1,13},{5,9},{9,5},{13,1},{2,14},{6,10},... | collective-permute-start | bytes 49160 | tf_op jit(solution)/shard_map/ppermute | solution.py:473
  42.5 0.6 %collective-permute-start.11 = (f32[32,128]{1,0:T(8,128)S(1)}, f32[32,128]{1,0:T(8,128)S(1)}, u32[]{:S(2)}, u32[]{:S(2)}) collective-permute-start(f32[32,128]{1,0:T(8,128)S(1)} %get-tuple-element.44), channel_id=1, source_target_pairs={{0,8},{4,12},{8,0},{12,4},{1,9},{5,13},{9,1},{13,5},{2,10},{6,14},... | collective-permute-start | bytes 49160 | tf_op jit(solution)/shard_map/ppermute | solution.py:473
  43.1 2.3 %collective-permute-start.10 = (f32[32,128]{1,0:T(8,128)S(1)}, f32[32,128]{1,0:T(8,128)S(1)}, u32[]{:S(2)}, u32[]{:S(2)}) collective-permute-start(f32[32,128]{1,0:T(8,128)S(1)} %get-tuple-element.44), channel_id=1, source_target_pairs={{0,4},{4,0},{8,12},{12,8},{1,5},{5,1},{9,13},{13,9},{2,6},{6,2},{1... | collective-permute-start | bytes 49160 | tf_op jit(solution)/shard_map/ppermute | solution.py:473
  45.4 1.1 %collective-permute-done.12.refs_2_ = f32[32,128]{1,0:T(8,128)S(1)} collective-permute-done((f32[32,128]{1,0:T(8,128)S(1)}, f32[32,128]{1,0:T(8,128)S(1)}, u32[]{:S(2)}, u32[]{:S(2)}) %collective-permute-start.12) | collective-permute-done | bytes 16416 | tf_op jit(solution)/shard_map/ppermute | solution.py:473
  46.6 0.6 %collective-permute-done.11.refs_1_ = f32[32,128]{1,0:T(8,128)S(1)} collective-permute-done((f32[32,128]{1,0:T(8,128)S(1)}, f32[32,128]{1,0:T(8,128)S(1)}, u32[]{:S(2)}, u32[]{:S(2)}) %collective-permute-start.11) | collective-permute-done | bytes 16416 | tf_op jit(solution)/shard_map/ppermute | solution.py:473
  47.3 0.9 %last.1 = f32[512,128]{1,0:T(8,128)} custom-call(f32[32,128]{1,0:T(8,128)S(1)} %collective-permute-done.10.refs_0_, f32[32,128]{1,0:T(8,128)S(1)} %collective-permute-done.11.refs_1_, f32[32,128]{1,0:T(8,128)S(1)} %collective-permute-done.12.refs_2_, f32[4,3,128,128]{3,2,1,0:T(8,128)S(1)} %get-tuple-element.45.refs_3_, ...), custom_call_target="tpu_custom_call" | custom-call | flops 655360 | bytes 1048576 | tf_op jit(solution)/shard_map/last/pallas_call | solution.py:427
  (14 shorter events, 0.7 us)
Async XLA Ops:
  1.9 1.7 %collective-permute-start = (f32[128,512]{1,0:T(8,128)S(1)}, f32[128,512]{1,0:T(8,128)S(1)}, u32[]{:S(2)}, u32[]{:S(2)}) collective-permute-start(f32[128,512]{1,0:T(8,128)S(1)} %get-tuple-element.27), channel_id=1, source_target_pairs={{0,1},{1,0},{2,3},{3,2},{4,5},{5,4},{6,7},{7,6},{8,9},{9,8},{10,11... | collective-permute-start | bytes 786440 | tf_op jit(solution)/shard_map/ppermute | solution.py:463
  5.8 1.6 %collective-permute-start.1 = (f32[128,512]{1,0:T(8,128)S(1)}, f32[128,512]{1,0:T(8,128)S(1)}, u32[]{:S(2)}, u32[]{:S(2)}) collective-permute-start(f32[128,512]{1,0:T(8,128)S(1)} %get-tuple-element.29), channel_id=1, source_target_pairs={{0,1},{1,0},{2,3},{3,2},{4,5},{5,4},{6,7},{7,6},{8,9},{9,8},{10,11... | collective-permute-start | bytes 786440 | tf_op jit(solution)/shard_map/ppermute | solution.py:463
  10.3 18.2 %copy-start = (f32[512,4]{0,1:T(4,128)S(1)}, f32[512,4]{0,1:T(4,128)}, u32[]{:S(2)}) copy-start(f32[512,4]{0,1:T(4,128)} %param.8) | copy-start | bytes 24580
  10.3 18.2 %copy-start.1 = (f32[512,2]{0,1:T(2,128)S(1)}, f32[512,2]{0,1:T(2,128)}, u32[]{:S(2)}) copy-start(f32[512,2]{0,1:T(2,128)} %param.7) | copy-start | bytes 12292
  10.3 18.2 %copy-start.2 = (f32[128]{0:T(128)S(1)}, f32[128]{0:T(128)}, u32[]{:S(2)}) copy-start(f32[128]{0:T(128)} %param.9) | copy-start | bytes 1540
  10.3 18.2 %collective-permute-start.2 = (f32[128,2048]{1,0:T(8,128)S(1)}, f32[128,2048]{1,0:T(8,128)S(1)}, u32[]{:S(2)}, u32[]{:S(2)}) collective-permute-start(f32[128,2048]{1,0:T(8,128)S(1)} %products.8), channel_id=1, source_target_pairs={{0,1},{1,0},{2,3},{3,2},{4,5},{5,4},{6,7},{7,6},{8,9},{9,8},{10,11... | collective-permute-start | bytes 3145736 | tf_op jit(solution)/shard_map/ppermute | solution.py:463
  13.4 2.0 %collective-permute-start.4 = (f32[128,1024]{1,0:T(8,128)S(1)}, f32[128,1024]{1,0:T(8,128)S(1)}, u32[]{:S(2)}, u32[]{:S(2)}) collective-permute-start(f32[128,1024]{1,0:T(8,128)S(1)} %get-tuple-element.31), channel_id=1, source_target_pairs={{0,1},{1,0},{2,3},{3,2},{4,5},{5,4},{6,7},{7,6},{8,9},{9,8},{10,11... | collective-permute-start | bytes 1572872 | tf_op jit(solution)/shard_map/ppermute | solution.py:463
  15.8 13.3 %collective-permute-start.5 = (bf16[1032,128]{1,0:T(8,128)(2,1)S(1)}, bf16[1032,128]{1,0:T(8,128)(2,1)S(1)}, u32[]{:S(2)}, u32[]{:S(2)}) collective-permute-start(bf16[1032,128]{1,0:T(8,128)(2,1)S(1)} %encode.5), channel_id=1, source_target_pairs={{0,2},{1,3},{2,0},{3,1},{4,6},{5,7},{6,4},{7,5},{8,10},{9,11},{10,... | collective-permute-start | bytes 792584 | tf_op jit(solution)/shard_map/ppermute | solution.py:467
  18.5 10.1 %collective-permute-start.6 = (bf16[520,128]{1,0:T(8,128)(2,1)S(1)}, bf16[520,128]{1,0:T(8,128)(2,1)S(1)}, u32[]{:S(2)}, u32[]{:S(2)}) collective-permute-start(bf16[520,128]{1,0:T(8,128)(2,1)S(1)} %encode.3.refs_0_), channel_id=1, source_target_pairs={{0,2},{1,3},{2,0},{3,1},{4,6},{5,7},{6,4},{7,5},{8,10},{9,11},{10,... | collective-permute-start | bytes 399368 | tf_op jit(solution)/shard_map/ppermute | solution.py:467
  18.6 12.5 %collective-permute-start.3 = (bf16[520,128]{1,0:T(8,128)(2,1)S(1)}, bf16[520,128]{1,0:T(8,128)(2,1)S(1)}, u32[]{:S(2)}, u32[]{:S(2)}) collective-permute-start(bf16[520,128]{1,0:T(8,128)(2,1)S(1)} %encode.4.refs_0_), channel_id=1, source_target_pairs={{0,2},{1,3},{2,0},{3,1},{4,6},{5,7},{6,4},{7,5},{8,10},{9,11},{10,... | collective-permute-start | bytes 399368 | tf_op jit(solution)/shard_map/ppermute | solution.py:467
  31.6 5.6 %collective-permute-start.9 = (f32[32,128]{1,0:T(8,128)S(1)}, f32[32,128]{1,0:T(8,128)S(1)}, u32[]{:S(2)}, u32[]{:S(2)}) collective-permute-start(f32[32,128]{1,0:T(8,128)S(1)} %get-tuple-element.35), channel_id=1, source_target_pairs={{0,12},{4,8},{8,4},{12,0},{1,13},{5,9},{9,5},{13,1},{2,14},{6,10},... | collective-permute-start | bytes 49160 | tf_op jit(solution)/shard_map/ppermute | solution.py:473
  35.5 4.6 %collective-permute-start.8 = (f32[32,128]{1,0:T(8,128)S(1)}, f32[32,128]{1,0:T(8,128)S(1)}, u32[]{:S(2)}, u32[]{:S(2)}) collective-permute-start(f32[32,128]{1,0:T(8,128)S(1)} %get-tuple-element.35), channel_id=1, source_target_pairs={{0,8},{4,12},{8,0},{12,4},{1,9},{5,13},{9,1},{13,5},{2,10},{6,14},... | collective-permute-start | bytes 49160 | tf_op jit(solution)/shard_map/ppermute | solution.py:473
  35.5 4.6 %collective-permute-start.7 = (f32[32,128]{1,0:T(8,128)S(1)}, f32[32,128]{1,0:T(8,128)S(1)}, u32[]{:S(2)}, u32[]{:S(2)}) collective-permute-start(f32[32,128]{1,0:T(8,128)S(1)} %get-tuple-element.35), channel_id=1, source_target_pairs={{0,4},{4,0},{8,12},{12,8},{1,5},{5,1},{9,13},{13,9},{2,6},{6,2},{1... | collective-permute-start | bytes 49160 | tf_op jit(solution)/shard_map/ppermute | solution.py:473
  41.0 5.6 %collective-permute-start.12 = (f32[32,128]{1,0:T(8,128)S(1)}, f32[32,128]{1,0:T(8,128)S(1)}, u32[]{:S(2)}, u32[]{:S(2)}) collective-permute-start(f32[32,128]{1,0:T(8,128)S(1)} %get-tuple-element.44), channel_id=1, source_target_pairs={{0,12},{4,8},{8,4},{12,0},{1,13},{5,9},{9,5},{13,1},{2,14},{6,10},... | collective-permute-start | bytes 49160 | tf_op jit(solution)/shard_map/ppermute | solution.py:473
  42.5 4.7 %collective-permute-start.11 = (f32[32,128]{1,0:T(8,128)S(1)}, f32[32,128]{1,0:T(8,128)S(1)}, u32[]{:S(2)}, u32[]{:S(2)}) collective-permute-start(f32[32,128]{1,0:T(8,128)S(1)} %get-tuple-element.44), channel_id=1, source_target_pairs={{0,8},{4,12},{8,0},{12,4},{1,9},{5,13},{9,1},{13,5},{2,10},{6,14},... | collective-permute-start | bytes 49160 | tf_op jit(solution)/shard_map/ppermute | solution.py:473
  43.1 4.2 %collective-permute-start.10 = (f32[32,128]{1,0:T(8,128)S(1)}, f32[32,128]{1,0:T(8,128)S(1)}, u32[]{:S(2)}, u32[]{:S(2)}) collective-permute-start(f32[32,128]{1,0:T(8,128)S(1)} %get-tuple-element.44), channel_id=1, source_target_pairs={{0,4},{4,0},{8,12},{12,8},{1,5},{5,1},{9,13},{13,9},{2,6},{6,2},{1... | collective-permute-start | bytes 49160 | tf_op jit(solution)/shard_map/ppermute | solution.py:473

commit v8 on v7

--- a/solution.py
+++ b/solution.py
@@ -15,7 +15,7 @@
 BINADES = 251.0
 LOWEST = 125.0
 GIVE, KEEP = 0, 1
-HALVES = 2
+HALVES = 1
 F32 = jnp.float32
 BF16 = jnp.bfloat16
 
@@ -441,8 +441,8 @@
 
 
 def chunks_of(groups):
-    middle = [(1, groups - 2)] if groups > 2 else []
-    return [(0, 1)] + middle + [(groups - 1, 1)] * (groups > 1)
+    half = max(1, groups // 2)
+    return [(0, half)] + [(group, 1) for group in range(half, groups)]
 
 
 def shards(tokens, in_weight, recur_weight, gate_bias, forget_offset):
@@ -480,17 +480,26 @@
     codes = []
     for away in range(1, chips):
         for slot, (start, count) in enumerate(chunks):
-            give, keep = products(
-                tokens,
-                in_weight,
-                chips,
-                away,
-                (GIVE, KEEP),
-                start * GROUP,
-                count * GROUP,
-                per_owner,
-                codes[-2:-1],
-            )
+            after = codes[-2:][:1]
+
+            def partial(parts):
+                return products(
+                    tokens,
+                    in_weight,
+                    chips,
+                    away,
+                    parts,
+                    start * GROUP,
+                    count * GROUP,
+                    per_owner,
+                    after,
+                )
+
+            if codes:
+                give, keep = partial((GIVE, KEEP))
+            else:
+                (give,) = partial((GIVE,))
+                (keep,) = partial((KEEP,))
             given = to_core(give)
             codes.append(encoded(keep, given))
             arrived[slot].append(to_chip(codes[-1], away))

time: 48.4 us -> 48.1 us (level)
  Pallas kernels: 16.4 us -> 17.8 us
  waiting for transfers between devices: 16.3 us -> 15 us
  starting transfers between devices: 15.4 us -> 14.9 us
    ppermute x4, waiting for transfers between devices: 4.1 us -> 1.52 us  [to_core(): lax.ppermute(value, 'chan', [(i, i ^ 1) for i in range(owners)])]
    ppermute x6, waiting for transfers between devices: 5.88 us -> 7.42 us  [to_blocks(): lax.ppermute(value, 'tm', [pair for pair in pairs if pair[1] < blocks])]
    pallas_call x5 -> x6, Pallas kernels: 11.8 us -> 13.2 us  [products(): pl.pallas_call(functools.partial(product_kernel, chips, away, parts, firs...]
  transfers between devices with their start and end apart: 13 -> 13, of which waited for: 10 -> 8; matrix products, arithmetic and copies ran while one was open for 0% -> 0% of each run, Pallas kernels for 15% -> 17%
where the time goes in v8:
time: 48.1 us; the launch traced here: 47.9 us
  Pallas kernels  17.8 us (37%)
  waiting for transfers between devices  15 us (31%)
  starting transfers between devices  14.9 us (31%)
    pallas_call x6, Pallas kernels, products(): pl.pallas_call(functools.partial(product_kernel, chips, away, parts, firs...  13.2 us
    ppermute x6, starting transfers between devices, to_blocks(): lax.ppermute(value, 'tm', [pair for pair in pairs if pair[1] < blocks])  8.95 us
    ppermute x6, waiting for transfers between devices, to_blocks(): lax.ppermute(value, 'tm', [pair for pair in pairs if pair[1] < blocks])  7.42 us
    ppermute x3, waiting for transfers between devices, to_chip(): return on_chip(lax.ppermute(value, 'chan', pairs))  6.08 us
    ppermute x3, starting transfers between devices, to_chip(): return on_chip(lax.ppermute(value, 'chan', pairs))  4.69 us
    pallas_call x4, Pallas kernels, first(): pl.pallas_call(functools.partial(first_kernel, start, place, len(codes),...  2.01 us
    ppermute x4, waiting for transfers between devices, to_core(): lax.ppermute(value, 'chan', [(i, i ^ 1) for i in range(owners)])  1.52 us
    ppermute x4, starting transfers between devices, to_core(): lax.ppermute(value, 'chan', [(i, i ^ 1) for i in range(owners)])  1.29 us
  transfers between devices with their start and end apart: 13, of which 8 were waited for; matrix products, arithmetic and copies ran while one was open for 0% of the time, Pallas kernels for 17%

profile of v8, /device:TPU:0, one launch (start us, length us, event | category | flops | bytes accessed | tf_op | source)
XLA Modules:
  0.0 47.9 jit_solution(18095570998506208581)
XLA Ops:
  0.0 2.0 %products.7 = f32[128,1024]{1,0:T(8,128)S(1)} custom-call(bf16[128,1024]{1,0:T(8,128)(2,1)} %tokens_ref.11, bf16[1024,8192]{1,0:T(8,128)(2,1)} %weight_ref.11), custom_call_target="tpu_custom_call" | custom-call | flops 268435456 | bytes 2097152 | tf_op jit(solution)/shard_map/products/pallas_call | solution.py:84
  2.0 0.6 %collective-permute-start = (f32[128,1024]{1,0:T(8,128)S(1)}, f32[128,1024]{1,0:T(8,128)S(1)}, u32[]{:S(2)}, u32[]{:S(2)}) collective-permute-start(f32[128,1024]{1,0:T(8,128)S(1)} %products.7), channel_id=1, source_target_pairs={{0,1},{1,0},{2,3},{3,2},{4,5},{5,4},{6,7},{7,6},{8,9},{9,8},{10,11... | collective-permute-start | bytes 1572872 | tf_op jit(solution)/shard_map/ppermute | solution.py:463
  2.5 2.0 %products.6.mine_ref = f32[128,1024]{1,0:T(8,128)S(1)} custom-call(bf16[128,1024]{1,0:T(8,128)(2,1)} %tokens_ref.11, bf16[1024,8192]{1,0:T(8,128)(2,1)} %weight_ref.11), custom_call_target="tpu_custom_call" | custom-call | flops 268435456 | bytes 2097152 | tf_op jit(solution)/shard_map/products/pallas_call | solution.py:84
  4.5 0.4 encode.3.refs_0_
  4.9 2.0 %products.8 = (f32[128,512]{1,0:T(8,128)S(1)}, f32[128,512]{1,0:T(8,128)S(1)}) custom-call(bf16[128,1024]{1,0:T(8,128)(2,1)} %tokens_ref.11, bf16[1024,8192]{1,0:T(8,128)(2,1)} %weight_ref.11, bf16[1032,128]{1,0:T(8,128)(2,1)S(1)} %encode.3.refs_0_), custom_call_target="tpu_custom_call" | custom-call | flops 268435456 | bytes 2097152 | tf_op jit(solution)/shard_map/products/pallas_call | solution.py:84
  7.0 1.5 %collective-permute-done.1.theirs_ref = f32[128,512]{1,0:T(8,128)S(1)} collective-permute-done((f32[128,512]{1,0:T(8,128)S(1)}, f32[128,512]{1,0:T(8,128)S(1)}, u32[]{:S(2)}, u32[]{:S(2)}) %collective-permute-start.1) | collective-permute-done | bytes 262176 | tf_op jit(solution)/shard_map/ppermute | solution.py:463
  8.6 0.2 encode.4.refs_0_
  8.8 2.6 %products.10 = f32[128,2048]{1,0:T(8,128)S(1)} custom-call(bf16[128,1024]{1,0:T(8,128)(2,1)} %tokens_ref.11, bf16[1024,8192]{1,0:T(8,128)(2,1)} %weight_ref.11, bf16[520,128]{1,0:T(8,128)(2,1)S(1)} %encode.4.refs_0_), custom_call_target="tpu_custom_call" | custom-call | flops 536870912 | bytes 4194304 | tf_op jit(solution)/shard_map/products/pallas_call | solution.py:84
  11.7 2.0 %products.11 = (f32[128,512]{1,0:T(8,128)S(1)}, f32[128,512]{1,0:T(8,128)S(1)}) custom-call(bf16[128,1024]{1,0:T(8,128)(2,1)} %tokens_ref.11, bf16[1024,8192]{1,0:T(8,128)(2,1)} %weight_ref.11, bf16[1032,128]{1,0:T(8,128)(2,1)S(1)} %encode.3.refs_0_), custom_call_target="tpu_custom_call" | custom-call | flops 268435456 | bytes 2097152 | tf_op jit(solution)/shard_map/products/pallas_call | solution.py:84
  13.6 0.4 collective-permute-start.4
  14.1 2.6 %collective-permute-start.6 = (bf16[1032,128]{1,0:T(8,128)(2,1)S(1)}, bf16[1032,128]{1,0:T(8,128)(2,1)S(1)}, u32[]{:S(2)}, u32[]{:S(2)}) collective-permute-start(bf16[1032,128]{1,0:T(8,128)(2,1)S(1)} %encode.3.refs_0_), channel_id=1, source_target_pairs={{0,2},{1,3},{2,0},{3,1},{4,6},{5,7},{6,4},{7,5},{8,10},{9,11},{10,... | collective-permute-start | bytes 792584 | tf_op jit(solution)/shard_map/ppermute | solution.py:467
  16.7 0.2 encode.5
  16.9 1.5 %collective-permute-start.5 = (bf16[520,128]{1,0:T(8,128)(2,1)S(1)}, bf16[520,128]{1,0:T(8,128)(2,1)S(1)}, u32[]{:S(2)}, u32[]{:S(2)}) collective-permute-start(bf16[520,128]{1,0:T(8,128)(2,1)S(1)} %encode.5), channel_id=1, source_target_pairs={{0,2},{1,3},{2,0},{3,1},{4,6},{5,7},{6,4},{7,5},{8,10},{9,11},{10,... | collective-permute-start | bytes 399368 | tf_op jit(solution)/shard_map/ppermute | solution.py:467
  18.4 0.6 %collective-permute-start.3 = (bf16[520,128]{1,0:T(8,128)(2,1)S(1)}, bf16[520,128]{1,0:T(8,128)(2,1)S(1)}, u32[]{:S(2)}, u32[]{:S(2)}) collective-permute-start(bf16[520,128]{1,0:T(8,128)(2,1)S(1)} %encode.4.refs_0_), channel_id=1, source_target_pairs={{0,2},{1,3},{2,0},{3,1},{4,6},{5,7},{6,4},{7,5},{8,10},{9,11},{10,... | collective-permute-start | bytes 399368 | tf_op jit(solution)/shard_map/ppermute | solution.py:467
  19.0 2.6 %products.9.refs_0_ = f32[128,2048]{1,0:T(8,128)S(1)} custom-call(bf16[128,1024]{1,0:T(8,128)(2,1)} %tokens_ref.11, bf16[1024,8192]{1,0:T(8,128)(2,1)} %weight_ref.11, bf16[520,128]{1,0:T(8,128)(2,1)S(1)} %encode.4.refs_0_), custom_call_target="tpu_custom_call" | custom-call | flops 536870912 | bytes 4194304 | tf_op jit(solution)/shard_map/products/pallas_call | solution.py:84
  21.6 2.2 %collective-permute-done.6.refs_2_ = bf16[1032,128]{1,0:T(8,128)(2,1)S(1)} collective-permute-done((bf16[1032,128]{1,0:T(8,128)(2,1)S(1)}, bf16[1032,128]{1,0:T(8,128)(2,1)S(1)}, u32[]{:S(2)}, u32[]{:S(2)}) %collective-permute-start.6) | collective-permute-done | bytes 264224 | tf_op jit(solution)/shard_map/ppermute | solution.py:467
  23.9 0.5 %first.4 = (f32[1,3,128,128]{3,2,1,0:T(8,128)S(1)}, f32[1,5,8,128]{3,2,1,0:T(8,128)S(1)}, f32[8,128]{1,0:T(8,128)S(1)}) custom-call(f32[128,2048]{1,0:T(8,128)S(1)} %products.9.refs_0_, f32[128,2048]{1,0:T(8,128)S(1)} %collective-permute-done.2.refs_1_, bf16[1032,128]{1,0:T(8,128)(2,1)S(1)} %collective-permute-done.6.refs_2_, f32[4,512]{1,0:T(4,128)S(1)} %bitcast.3, ...), custom_call_target="tpu_custom_call" | custom-call | flops 3932160 | bytes 1310720 | tf_op jit(solution)/shard_map/first/pallas_call | solution.py:268
  24.4 0.5 %first.5 = (f32[1,3,128,128]{3,2,1,0:T(8,128)S(1)}, f32[1,5,8,128]{3,2,1,0:T(8,128)S(1)}, f32[16,128]{1,0:T(8,128)S(1)}) custom-call(f32[128,2048]{1,0:T(8,128)S(1)} %products.9.refs_0_, f32[128,2048]{1,0:T(8,128)S(1)} %collective-permute-done.2.refs_1_, bf16[1032,128]{1,0:T(8,128)(2,1)S(1)} %collective-permute-done.6.refs_2_, f32[4,512]{1,0:T(4,128)S(1)} %bitcast.4, ...), custom_call_target="tpu_custom_call" | custom-call | flops 3932160 | bytes 1310720 | tf_op jit(solution)/shard_map/first/pallas_call | solution.py:268
  24.9 1.8 %collective-permute-done.5.refs_2_ = bf16[520,128]{1,0:T(8,128)(2,1)S(1)} collective-permute-done((bf16[520,128]{1,0:T(8,128)(2,1)S(1)}, bf16[520,128]{1,0:T(8,128)(2,1)S(1)}, u32[]{:S(2)}, u32[]{:S(2)}) %collective-permute-start.5) | collective-permute-done | bytes 133152 | tf_op jit(solution)/shard_map/ppermute | solution.py:467
  26.7 0.5 %first.6 = (f32[1,3,128,128]{3,2,1,0:T(8,128)S(1)}, f32[1,5,8,128]{3,2,1,0:T(8,128)S(1)}, f32[24,128]{1,0:T(8,128)S(1)}) custom-call(f32[128,2048]{1,0:T(8,128)S(1)} %products.9.refs_0_, f32[128,2048]{1,0:T(8,128)S(1)} %collective-permute-done.2.refs_1_, bf16[520,128]{1,0:T(8,128)(2,1)S(1)} %collective-permute-done.5.refs_2_, f32[4,512]{1,0:T(4,128)S(1)} %bitcast.5, ...), custom_call_target="tpu_custom_call" | custom-call | flops 3932160 | bytes 1310720 | tf_op jit(solution)/shard_map/first/pallas_call | solution.py:268
  27.2 2.0 %collective-permute-done.3.refs_2_ = bf16[520,128]{1,0:T(8,128)(2,1)S(1)} collective-permute-done((bf16[520,128]{1,0:T(8,128)(2,1)S(1)}, bf16[520,128]{1,0:T(8,128)(2,1)S(1)}, u32[]{:S(2)}, u32[]{:S(2)}) %collective-permute-start.3) | collective-permute-done | bytes 133152 | tf_op jit(solution)/shard_map/ppermute | solution.py:467
  29.3 0.5 %first.7 = (f32[1,3,128,128]{3,2,1,0:T(8,128)S(1)}, f32[1,5,8,128]{3,2,1,0:T(8,128)S(1)}, f32[32,128]{1,0:T(8,128)S(1)}) custom-call(f32[128,2048]{1,0:T(8,128)S(1)} %products.9.refs_0_, f32[128,2048]{1,0:T(8,128)S(1)} %collective-permute-done.2.refs_1_, bf16[520,128]{1,0:T(8,128)(2,1)S(1)} %collective-permute-done.3.refs_2_, f32[4,512]{1,0:T(4,128)S(1)} %bitcast.6, ...), custom_call_target="tpu_custom_call" | custom-call | flops 3932160 | bytes 1310720 | tf_op jit(solution)/shard_map/first/pallas_call | solution.py:268
  29.8 1.9 %collective-permute-start.7 = (f32[32,128]{1,0:T(8,128)S(1)}, f32[32,128]{1,0:T(8,128)S(1)}, u32[]{:S(2)}, u32[]{:S(2)}) collective-permute-start(f32[32,128]{1,0:T(8,128)S(1)} %get-tuple-element.31), channel_id=1, source_target_pairs={{0,4},{4,0},{8,12},{12,8},{1,5},{5,1},{9,13},{13,9},{2,6},{6,2},{1... | collective-permute-start | bytes 49160 | tf_op jit(solution)/shard_map/ppermute | solution.py:473
  31.7 2.6 %collective-permute-start.8 = (f32[32,128]{1,0:T(8,128)S(1)}, f32[32,128]{1,0:T(8,128)S(1)}, u32[]{:S(2)}, u32[]{:S(2)}) collective-permute-start(f32[32,128]{1,0:T(8,128)S(1)} %get-tuple-element.31), channel_id=1, source_target_pairs={{0,8},{4,12},{8,0},{12,4},{1,9},{5,13},{9,1},{13,5},{2,10},{6,14},... | collective-permute-start | bytes 49160 | tf_op jit(solution)/shard_map/ppermute | solution.py:473
  34.3 2.0 %collective-permute-done.8.refs_1_ = f32[32,128]{1,0:T(8,128)S(1)} collective-permute-done((f32[32,128]{1,0:T(8,128)S(1)}, f32[32,128]{1,0:T(8,128)S(1)}, u32[]{:S(2)}, u32[]{:S(2)}) %collective-permute-start.8) | collective-permute-done | bytes 16416 | tf_op jit(solution)/shard_map/ppermute | solution.py:473
  36.3 3.5 %collective-permute-done.9.refs_2_ = f32[32,128]{1,0:T(8,128)S(1)} collective-permute-done((f32[32,128]{1,0:T(8,128)S(1)}, f32[32,128]{1,0:T(8,128)S(1)}, u32[]{:S(2)}, u32[]{:S(2)}) %collective-permute-start.9) | collective-permute-done | bytes 16416 | tf_op jit(solution)/shard_map/ppermute | solution.py:473
  39.8 0.8 %second.1 = (f32[4,3,128,128]{3,2,1,0:T(8,128)S(1)}, f32[4,6,8,128]{3,2,1,0:T(8,128)S(1)}, f32[32,128]{1,0:T(8,128)S(1)}) custom-call(f32[32,128]{1,0:T(8,128)S(1)} %collective-permute-done.7.refs_0_, f32[32,128]{1,0:T(8,128)S(1)} %collective-permute-done.8.refs_1_, f32[32,128]{1,0:T(8,128)S(1)} %collective-permute-done.9.refs_2_, ...), custom_call_target="tpu_custom_call" | custom-call | flops 6553600 | bytes 1572864 | tf_op jit(solution)/shard_map/second/pallas_call | solution.py:384
  40.7 0.7 %collective-permute-start.11 = (f32[32,128]{1,0:T(8,128)S(1)}, f32[32,128]{1,0:T(8,128)S(1)}, u32[]{:S(2)}, u32[]{:S(2)}) collective-permute-start(f32[32,128]{1,0:T(8,128)S(1)} %get-tuple-element.40), channel_id=1, source_target_pairs={{0,8},{4,12},{8,0},{12,4},{1,9},{5,13},{9,1},{13,5},{2,10},{6,14},... | collective-permute-start | bytes 49160 | tf_op jit(solution)/shard_map/ppermute | solution.py:473
  41.4 3.6 %collective-permute-start.12 = (f32[32,128]{1,0:T(8,128)S(1)}, f32[32,128]{1,0:T(8,128)S(1)}, u32[]{:S(2)}, u32[]{:S(2)}) collective-permute-start(f32[32,128]{1,0:T(8,128)S(1)} %get-tuple-element.40), channel_id=1, source_target_pairs={{0,12},{4,8},{8,4},{12,0},{1,13},{5,9},{9,5},{13,1},{2,14},{6,10},... | collective-permute-start | bytes 49160 | tf_op jit(solution)/shard_map/ppermute | solution.py:473
  45.1 0.3 collective-permute-done.11.refs_1_
  45.4 1.6 %collective-permute-done.12.refs_2_ = f32[32,128]{1,0:T(8,128)S(1)} collective-permute-done((f32[32,128]{1,0:T(8,128)S(1)}, f32[32,128]{1,0:T(8,128)S(1)}, u32[]{:S(2)}, u32[]{:S(2)}) %collective-permute-start.12) | collective-permute-done | bytes 16416 | tf_op jit(solution)/shard_map/ppermute | solution.py:473
  47.0 0.9 %last.1 = f32[512,128]{1,0:T(8,128)} custom-call(f32[32,128]{1,0:T(8,128)S(1)} %collective-permute-done.10.refs_0_, f32[32,128]{1,0:T(8,128)S(1)} %collective-permute-done.11.refs_1_, f32[32,128]{1,0:T(8,128)S(1)} %collective-permute-done.12.refs_2_, f32[4,3,128,128]{3,2,1,0:T(8,128)S(1)} %get-tuple-element.41.refs_3_, ...), custom_call_target="tpu_custom_call" | custom-call | flops 655360 | bytes 1048576 | tf_op jit(solution)/shard_map/last/pallas_call | solution.py:427
  (15 shorter events, 0.4 us)
Async XLA Ops:
  2.0 2.5 %collective-permute-start = (f32[128,1024]{1,0:T(8,128)S(1)}, f32[128,1024]{1,0:T(8,128)S(1)}, u32[]{:S(2)}, u32[]{:S(2)}) collective-permute-start(f32[128,1024]{1,0:T(8,128)S(1)} %products.7), channel_id=1, source_target_pairs={{0,1},{1,0},{2,3},{3,2},{4,5},{5,4},{6,7},{7,6},{8,9},{9,8},{10,11... | collective-permute-start | bytes 1572872 | tf_op jit(solution)/shard_map/ppermute | solution.py:463
  7.0 1.6 %collective-permute-start.1 = (f32[128,512]{1,0:T(8,128)S(1)}, f32[128,512]{1,0:T(8,128)S(1)}, u32[]{:S(2)}, u32[]{:S(2)}) collective-permute-start(f32[128,512]{1,0:T(8,128)S(1)} %get-tuple-element.25), channel_id=1, source_target_pairs={{0,1},{1,0},{2,3},{3,2},{4,5},{5,4},{6,7},{7,6},{8,9},{9,8},{10,11... | collective-permute-start | bytes 786440 | tf_op jit(solution)/shard_map/ppermute | solution.py:463
  11.4 12.5 %copy-start = (f32[512,4]{0,1:T(4,128)S(1)}, f32[512,4]{0,1:T(4,128)}, u32[]{:S(2)}) copy-start(f32[512,4]{0,1:T(4,128)} %param.8) | copy-start | bytes 24580
  11.4 12.5 %copy-start.1 = (f32[512,2]{0,1:T(2,128)S(1)}, f32[512,2]{0,1:T(2,128)}, u32[]{:S(2)}) copy-start(f32[512,2]{0,1:T(2,128)} %param.7) | copy-start | bytes 12292
  11.4 12.4 %copy-start.2 = (f32[128]{0:T(128)S(1)}, f32[128]{0:T(128)}, u32[]{:S(2)}) copy-start(f32[128]{0:T(128)} %param.9) | copy-start | bytes 1540
  11.5 12.4 %collective-permute-start.2 = (f32[128,2048]{1,0:T(8,128)S(1)}, f32[128,2048]{1,0:T(8,128)S(1)}, u32[]{:S(2)}, u32[]{:S(2)}) collective-permute-start(f32[128,2048]{1,0:T(8,128)S(1)} %products.10), channel_id=1, source_target_pairs={{0,1},{1,0},{2,3},{3,2},{4,5},{5,4},{6,7},{7,6},{8,9},{9,8},{10,11... | collective-permute-start | bytes 3145736 | tf_op jit(solution)/shard_map/ppermute | solution.py:463
  13.6 3.0 %collective-permute-start.4 = (f32[128,512]{1,0:T(8,128)S(1)}, f32[128,512]{1,0:T(8,128)S(1)}, u32[]{:S(2)}, u32[]{:S(2)}) collective-permute-start(f32[128,512]{1,0:T(8,128)S(1)} %get-tuple-element.27), channel_id=1, source_target_pairs={{0,1},{1,0},{2,3},{3,2},{4,5},{5,4},{6,7},{7,6},{8,9},{9,8},{10,11... | collective-permute-start | bytes 786440 | tf_op jit(solution)/shard_map/ppermute | solution.py:463
  14.1 9.8 %collective-permute-start.6 = (bf16[1032,128]{1,0:T(8,128)(2,1)S(1)}, bf16[1032,128]{1,0:T(8,128)(2,1)S(1)}, u32[]{:S(2)}, u32[]{:S(2)}) collective-permute-start(bf16[1032,128]{1,0:T(8,128)(2,1)S(1)} %encode.3.refs_0_), channel_id=1, source_target_pairs={{0,2},{1,3},{2,0},{3,1},{4,6},{5,7},{6,4},{7,5},{8,10},{9,11},{10,... | collective-permute-start | bytes 792584 | tf_op jit(solution)/shard_map/ppermute | solution.py:467
  16.9 9.8 %collective-permute-start.5 = (bf16[520,128]{1,0:T(8,128)(2,1)S(1)}, bf16[520,128]{1,0:T(8,128)(2,1)S(1)}, u32[]{:S(2)}, u32[]{:S(2)}) collective-permute-start(bf16[520,128]{1,0:T(8,128)(2,1)S(1)} %encode.5), channel_id=1, source_target_pairs={{0,2},{1,3},{2,0},{3,1},{4,6},{5,7},{6,4},{7,5},{8,10},{9,11},{10,... | collective-permute-start | bytes 399368 | tf_op jit(solution)/shard_map/ppermute | solution.py:467
  18.4 10.9 %collective-permute-start.3 = (bf16[520,128]{1,0:T(8,128)(2,1)S(1)}, bf16[520,128]{1,0:T(8,128)(2,1)S(1)}, u32[]{:S(2)}, u32[]{:S(2)}) collective-permute-start(bf16[520,128]{1,0:T(8,128)(2,1)S(1)} %encode.4.refs_0_), channel_id=1, source_target_pairs={{0,2},{1,3},{2,0},{3,1},{4,6},{5,7},{6,4},{7,5},{8,10},{9,11},{10,... | collective-permute-start | bytes 399368 | tf_op jit(solution)/shard_map/ppermute | solution.py:467
  29.8 4.5 %collective-permute-start.7 = (f32[32,128]{1,0:T(8,128)S(1)}, f32[32,128]{1,0:T(8,128)S(1)}, u32[]{:S(2)}, u32[]{:S(2)}) collective-permute-start(f32[32,128]{1,0:T(8,128)S(1)} %get-tuple-element.31), channel_id=1, source_target_pairs={{0,4},{4,0},{8,12},{12,8},{1,5},{5,1},{9,13},{13,9},{2,6},{6,2},{1... | collective-permute-start | bytes 49160 | tf_op jit(solution)/shard_map/ppermute | solution.py:473
  31.7 4.6 %collective-permute-start.8 = (f32[32,128]{1,0:T(8,128)S(1)}, f32[32,128]{1,0:T(8,128)S(1)}, u32[]{:S(2)}, u32[]{:S(2)}) collective-permute-start(f32[32,128]{1,0:T(8,128)S(1)} %get-tuple-element.31), channel_id=1, source_target_pairs={{0,8},{4,12},{8,0},{12,4},{1,9},{5,13},{9,1},{13,5},{2,10},{6,14},... | collective-permute-start | bytes 49160 | tf_op jit(solution)/shard_map/ppermute | solution.py:473
  34.3 5.5 %collective-permute-start.9 = (f32[32,128]{1,0:T(8,128)S(1)}, f32[32,128]{1,0:T(8,128)S(1)}, u32[]{:S(2)}, u32[]{:S(2)}) collective-permute-start(f32[32,128]{1,0:T(8,128)S(1)} %get-tuple-element.31), channel_id=1, source_target_pairs={{0,12},{4,8},{8,4},{12,0},{1,13},{5,9},{9,5},{13,1},{2,14},{6,10},... | collective-permute-start | bytes 49160 | tf_op jit(solution)/shard_map/ppermute | solution.py:473
  40.6 4.5 %collective-permute-start.10 = (f32[32,128]{1,0:T(8,128)S(1)}, f32[32,128]{1,0:T(8,128)S(1)}, u32[]{:S(2)}, u32[]{:S(2)}) collective-permute-start(f32[32,128]{1,0:T(8,128)S(1)} %get-tuple-element.40), channel_id=1, source_target_pairs={{0,4},{4,0},{8,12},{12,8},{1,5},{5,1},{9,13},{13,9},{2,6},{6,2},{1... | collective-permute-start | bytes 49160 | tf_op jit(solution)/shard_map/ppermute | solution.py:473
  40.7 4.7 %collective-permute-start.11 = (f32[32,128]{1,0:T(8,128)S(1)}, f32[32,128]{1,0:T(8,128)S(1)}, u32[]{:S(2)}, u32[]{:S(2)}) collective-permute-start(f32[32,128]{1,0:T(8,128)S(1)} %get-tuple-element.40), channel_id=1, source_target_pairs={{0,8},{4,12},{8,0},{12,4},{1,9},{5,13},{9,1},{13,5},{2,10},{6,14},... | collective-permute-start | bytes 49160 | tf_op jit(solution)/shard_map/ppermute | solution.py:473
  41.4 5.5 %collective-permute-start.12 = (f32[32,128]{1,0:T(8,128)S(1)}, f32[32,128]{1,0:T(8,128)S(1)}, u32[]{:S(2)}, u32[]{:S(2)}) collective-permute-start(f32[32,128]{1,0:T(8,128)S(1)} %get-tuple-element.40), channel_id=1, source_target_pairs={{0,12},{4,8},{8,4},{12,0},{1,13},{5,9},{9,5},{13,1},{2,14},{6,10},... | collective-permute-start | bytes 49160 | tf_op jit(solution)/shard_map/ppermute | solution.py:473

commit v9 on v5

--- a/solution.py
+++ b/solution.py
@@ -42,61 +42,58 @@
 PARAMS = pltpu.CompilerParams(vmem_limit_bytes=16 << 20)
 
 
-def product_kernel(chips, away, parts, first, per_owner, tile, tokens_ref, weight_ref, *refs):
+def product_kernel(chips, parts, per_owner, tokens_ref, weight_ref, *refs):
     outs, (x_ref, w_ref, sems) = refs[-3 - len(parts) : -3], refs[-3:]
     me = lax.axis_index("chan")
     chip, core = me // 2, me % 2
-    target = lax.rem(chip + away, chips)
-    tiles = outs[0].shape[1] // tile
-    slots = len(parts) * tiles
-    tokens_copy = pltpu.make_async_copy(tokens_ref, x_ref, sems.at[slots])
+    tokens_copy = pltpu.make_async_copy(tokens_ref, x_ref, sems.at[w_ref.shape[0]])
     tokens_copy.start()
     copies = []
-    for slot in range(slots):
-        owner = 2 * target + (core if parts[slot // tiles] == KEEP else 1 - core)
-        column = pl.multiple_of(owner * per_owner + first + slot % tiles * tile, tile)
-        copies.append(
-            pltpu.make_async_copy(
-                weight_ref.at[:, pl.ds(column, tile)], w_ref.at[slot], sems.at[slot]
+    for (away, which, first, width), out_ref in zip(parts, outs):
+        owner = 2 * lax.rem(chip + away, chips) + (core if which == KEEP else 1 - core)
+        for start in range(0, width, GROUP):
+            slot = len(copies)
+            column = pl.multiple_of(owner * per_owner + first + start, GROUP)
+            copy = pltpu.make_async_copy(
+                weight_ref.at[:, pl.ds(column, GROUP)], w_ref.at[slot], sems.at[slot]
             )
-        )
-        copies[-1].start()
+            copy.start()
+            copies.append((copy, out_ref, start))
     tokens_copy.wait()
-    for slot, copy in enumerate(copies):
+    for slot, (copy, out_ref, start) in enumerate(copies):
         copy.wait()
-        outs[slot // tiles][:, pl.ds(slot % tiles * tile, tile)] = jnp.dot(
+        out_ref[:, pl.ds(start, GROUP)] = jnp.dot(
             x_ref[...], w_ref[slot], preferred_element_type=F32
         )
 
 
-def products(tokens, in_weight, chips, away, parts, first, width, per_owner, after):
+def products(tokens, in_weight, chips, per_owner, parts, after):
     steps, depth = tokens.shape
-    tile = GROUP
-    slots = len(parts) * width // tile
+    slots = sum(width for _, _, _, width in parts) // GROUP
     return pl.pallas_call(
-        functools.partial(product_kernel, chips, away, parts, first, per_owner, tile),
-        out_shape=[pltpu.VMEM((steps, width), F32)] * len(parts),
+        functools.partial(product_kernel, chips, parts, per_owner),
+        out_shape=[pltpu.VMEM((steps, width), F32) for _, _, _, width in parts],
         in_specs=in_hbm(2) + vmem(len(after)),
         out_specs=vmem(len(parts)),
         scratch_shapes=[
             pltpu.VMEM((steps, depth), BF16),
-            pltpu.VMEM((slots, depth, tile), BF16),
+            pltpu.VMEM((slots, depth, GROUP), BF16),
             pltpu.SemaphoreType.DMA((slots + 1,)),
         ],
         compiler_params=PARAMS,
-        cost_estimate=cost(2 * slots * steps * depth * tile, 2 * slots * depth * tile),
+        cost_estimate=cost(2 * slots * steps * depth * GROUP, 2 * slots * depth * GROUP),
         name="products",
     )(tokens, in_weight, *after)
 
 
-def encode_kernel(mine_ref, theirs_ref, out_ref, sum_ref):
-    steps, width = mine_ref.shape
+def encode_kernel(first, mine_ref, theirs_ref, out_ref, sum_ref):
+    steps, width = sum_ref.shape
     blocks = width // LANES
     top = jnp.zeros((steps, LANES), F32)
     for block in range(blocks):
-        cols = pl.ds(block * LANES, LANES)
+        cols = pl.ds(first + block * LANES, LANES)
         both = mine_ref[:, cols] + theirs_ref[:, cols]
-        sum_ref[:, cols] = both
+        sum_ref[:, pl.ds(block * LANES, LANES)] = both
         top = jnp.maximum(top, jnp.abs(both))
     top = jnp.max(top, axis=0, keepdims=True)
     top = jnp.maximum(top, 1e-30) * 1.0078125
@@ -110,11 +107,11 @@
         out_ref[pl.ds(block * steps, steps), :] = jnp.where(value < 0.0, -code, code).astype(BF16)
 
 
-def encoded(mine, theirs):
-    steps, width = mine.shape
+def encoded(mine, theirs, first, width):
+    steps = mine.shape[0]
     rows = steps * (width // LANES) + SUB
     return pl.pallas_call(
-        encode_kernel,
+        functools.partial(encode_kernel, first),
         out_shape=pltpu.VMEM((rows, LANES), BF16),
         in_specs=vmem(2),
         out_specs=pl.BlockSpec(memory_space=pltpu.VMEM),
@@ -180,7 +177,8 @@
     return 1.0 / (1.0 + jnp.exp(-x))
 
 
-def first_kernel(start, groups, remotes, earlier, *refs):
+def first_kernel(start, places, earlier, *refs):
+    groups, remotes = 1, len(places)
     refs = list(refs)
     mine_ref, theirs_ref = refs[:2]
     codes = refs[2 : 2 + remotes]
@@ -189,13 +187,12 @@
     kept_ref, prefix_ref, totals_ref, sum_ref, late_ref = refs[5 + remotes + earlier :]
     steps = mine_ref.shape[0]
     runs = steps // SUB
-    blocks = groups * GATES
     done = 0
     for ref in totals_before:
         totals_ref[pl.ds(done, ref.shape[0]), :] = ref[...]
         done += ref.shape[0]
     scales = [
-        ref[pl.ds(blocks * steps, SUB), :][0:1, :].astype(F32) for ref in codes
+        ref[pl.ds(ref.shape[0] - SUB, SUB), :][0:1, :].astype(F32) for ref in codes
     ]
     late_ref[...] = jnp.broadcast_to(offset_ref[...], (LANES, steps)).T
     lane = lax.broadcasted_iota(jnp.int32, (SUB, LANES), 1)
@@ -207,8 +204,9 @@
             block = group * GATES + q
             cols = pl.ds(start * GROUP + block * LANES, LANES)
             value = mine_ref[:, cols] + theirs_ref[:, cols]
-            for ref, scale in zip(codes, scales):
-                value = value + decoded(ref[pl.ds(block * steps, steps), :].astype(F32), scale)
+            for ref, scale, place in zip(codes, scales, places):
+                rows = pl.ds((place * GATES + block) * steps, steps)
+                value = value + decoded(ref[rows, :].astype(F32), scale)
             sum_ref[q] = value
         channels = pl.ds((start + group) * LANES, LANES)
         biases = [
@@ -251,12 +249,13 @@
             totals_ref[pl.ds(done + group * SUB + index, 1), :] = jnp.zeros((1, LANES), F32)
 
 
-def first(start, groups, mine, theirs, codes, bias, weight, offset, earlier):
+def first(start, places, mine, theirs, codes, bias, weight, offset, earlier):
     steps = mine.shape[0]
+    groups = 1
     rows = sum(e.shape[0] for e in earlier) + groups * SUB
     count = 5 + len(codes) + len(earlier)
     return pl.pallas_call(
-        functools.partial(first_kernel, start, groups, len(codes), len(earlier)),
+        functools.partial(first_kernel, start, places, len(earlier)),
         out_shape=(
             pltpu.VMEM((groups, 3, steps, LANES), F32),
             pltpu.VMEM((groups, 5, SUB, LANES), F32),
@@ -430,6 +429,13 @@
     )(*received, hiddens, prefix)
 
 
+def pieces_of(groups, chips):
+    half = max(1, groups // 2)
+    pieces = [(1, 0, half), (1, half, groups - half)]
+    pieces += [(away, 0, groups) for away in range(2, chips)]
+    return [piece for piece in pieces if piece[2]]
+
+
 def shards(tokens, in_weight, recur_weight, gate_bias, forget_offset):
     steps = tokens.shape[0]
     channels = recur_weight.shape[0]
@@ -460,31 +466,46 @@
         return arriving
 
     tokens, in_weight = off_chip(tokens), off_chip(in_weight)
-    arrived = [[] for _ in range(groups)]
+
+    def product(parts, after):
+        return products(tokens, in_weight, chips, per_owner, parts, after)
+
+    coded = [[] for _ in range(groups)]
+
+    def send(away, start, count, mine, theirs, inside):
+        code = encoded(mine, theirs, inside, count * GROUP)
+        arrived = to_chip(code, away)
+        for place in range(count):
+            coded[start + place].append((arrived, place))
+        return code
+
+    local_give, local_keep = ((0, which, 0, per_owner) for which in (GIVE, KEEP))
+    given = None
     codes = []
-    for away in range(1, chips):
-        for group in range(groups):
-            give, keep = products(
-                tokens,
-                in_weight,
-                chips,
-                away,
-                (GIVE, KEEP),
-                group * GROUP,
-                GROUP,
-                per_owner,
-                codes[-2:-1],
-            )
-            given = to_core(give)
-            codes.append(encoded(keep, given))
-            arrived[group].append(to_chip(codes[-1], away))
-    local = (per_owner, per_owner, codes[-1:])
-    (give,) = products(tokens, in_weight, chips, 0, (GIVE,), 0, *local)
-    given = to_core(give)
-    (keep,) = products(tokens, in_weight, chips, 0, (KEEP,), 0, *local)
+    for index, (away, start, count) in enumerate(pieces_of(groups, chips)):
+        last_piece = index == len(pieces_of(groups, chips)) - 1
+        parts = tuple((away, which, start * GROUP, count * GROUP) for which in (GIVE, KEEP))
+        if index == 0:
+            (give,) = product(parts[:1], [])
+            theirs = to_core(give)
+            keep, *more = product(parts[1:] + (local_give,) * last_piece, [])
+        else:
+            give, keep, *more = product(parts + (local_give,) * last_piece, codes[-1:])
+            theirs = to_core(give)
+        if last_piece:
+            given = to_core(more[0])
+        if index == 0:
+            codes.append(send(away, start, count, keep, theirs, 0))
+        else:
+            for group in range(start, start + count):
+                codes.append(send(away, group, 1, keep, theirs, (group - start) * GROUP))
+    (keep,) = product((local_keep,), codes[-1:])
     kept, prefixes, totals = [], [], []
     for group in range(groups):
-        k, p, total = first(group, 1, keep, given, arrived[group], bias, weight, offset, totals)
+        arrived, places = zip(*coded[group]) if coded[group] else ((), ())
+        k, p, total = first(
+            group, places, keep, given, list(arrived), bias, weight, offset, totals
+        )
         totals = [total]
         kept.append(k)
         prefixes.append(p)

time: 51.1 us -> 42 us (0.82)
  waiting for transfers between devices: 17.1 us -> 11.1 us
  Pallas kernels: 17.8 us -> 15.1 us
    ppermute x5 -> x3, waiting for transfers between devices: 3.73 us -> 0.35 us  [to_core(): lax.ppermute(value, 'chan', [(i, i ^ 1) for i in range(owners)])]
    pallas_call x14 -> x11, Pallas kernels: 16.1 us -> 13.4 us  [the longest x4 10.6 us: products(): pl.pallas_call(functools.partial(product_kernel, chips, parts, per_owner)...]
    ppermute x6, waiting for transfers between devices: 7.56 us -> 5.88 us  [to_blocks(): lax.ppermute(value, 'tm', [pair for pair in pairs if pair[1] < blocks])]
    ppermute x4 -> x3, waiting for transfers between devices: 5.8 us -> 4.91 us  [to_chip(): return on_chip(lax.ppermute(value, 'chan', pairs))]
    ppermute x5 -> x3, starting transfers between devices: 1.85 us -> 1.14 us  [to_core(): lax.ppermute(value, 'chan', [(i, i ^ 1) for i in range(owners)])]
    ppermute x4 -> x3, starting transfers between devices: 5 us -> 5.31 us  [to_chip(): return on_chip(lax.ppermute(value, 'chan', pairs))]
  transfers between devices with their start and end apart: 15 -> 12, of which waited for: 10 -> 9; matrix products, arithmetic and copies ran while one was open for 0% -> 0% of each run, Pallas kernels for 17% -> 16%
where the time goes in v9:
time: 42 us; the launch traced here: 41.9 us
  starting transfers between devices  15.5 us (37%)
  Pallas kernels  15.1 us (36%)
  waiting for transfers between devices  11.1 us (26%)
    pallas_call x4, Pallas kernels, products(): pl.pallas_call(functools.partial(product_kernel, chips, parts, per_owner)...  10.6 us
    ppermute x6, starting transfers between devices, to_blocks(): lax.ppermute(value, 'tm', [pair for pair in pairs if pair[1] < blocks])  9.01 us
    ppermute x6, waiting for transfers between devices, to_blocks(): lax.ppermute(value, 'tm', [pair for pair in pairs if pair[1] < blocks])  5.88 us
    ppermute x3, starting transfers between devices, to_chip(): return on_chip(lax.ppermute(value, 'chan', pairs))  5.31 us
    ppermute x3, waiting for transfers between devices, to_chip(): return on_chip(lax.ppermute(value, 'chan', pairs))  4.91 us
    pallas_call x4, Pallas kernels, first(): pl.pallas_call(functools.partial(first_kernel, start, places, len(earlier...  2.01 us
    ppermute x3, starting transfers between devices, to_core(): lax.ppermute(value, 'chan', [(i, i ^ 1) for i in range(owners)])  1.14 us
    pallas_call x1, Pallas kernels, last(): pl.pallas_call(functools.partial(last_kernel, count, own_xor), out_shape=...  0.91 us
  transfers between devices with their start and end apart: 12, of which 9 were waited for; matrix products, arithmetic and copies ran while one was open for 0% of the time, Pallas kernels for 16%

profile of v9, /device:TPU:0, one launch (start us, length us, event | category | flops | bytes accessed | tf_op | source)
XLA Modules:
  0.0 41.9 jit_solution(13282998264806433314)
XLA Ops:
  0.0 2.0 %products.5 = f32[128,1024]{1,0:T(8,128)S(1)} custom-call(bf16[128,1024]{1,0:T(8,128)(2,1)} %tokens_ref.7, bf16[1024,8192]{1,0:T(8,128)(2,1)} %weight_ref.7), custom_call_target="tpu_custom_call" | custom-call | flops 268435456 | bytes 2097152 | tf_op jit(solution)/shard_map/products/pallas_call | solution.py:73
  2.0 0.6 %collective-permute-start = (f32[128,1024]{1,0:T(8,128)S(1)}, f32[128,1024]{1,0:T(8,128)S(1)}, u32[]{:S(2)}, u32[]{:S(2)}) collective-permute-start(f32[128,1024]{1,0:T(8,128)S(1)} %products.5), channel_id=1, source_target_pairs={{0,1},{1,0},{2,3},{3,2},{4,5},{5,4},{6,7},{7,6},{8,9},{9,8},{10,11... | collective-permute-start | bytes 1572872 | tf_op jit(solution)/shard_map/ppermute | solution.py:454
  2.5 2.0 %products.4.mine_ref = f32[128,1024]{1,0:T(8,128)S(1)} custom-call(bf16[128,1024]{1,0:T(8,128)(2,1)} %tokens_ref.7, bf16[1024,8192]{1,0:T(8,128)(2,1)} %weight_ref.7), custom_call_target="tpu_custom_call" | custom-call | flops 268435456 | bytes 2097152 | tf_op jit(solution)/shard_map/products/pallas_call | solution.py:73
  4.5 0.4 encode.3.refs_0_
  5.0 4.0 %products.6 = (f32[128,1024]{1,0:T(8,128)S(1)}, f32[128,1024]{1,0:T(8,128)S(1)}, f32[128,2048]{1,0:T(8,128)S(1)}) custom-call(bf16[128,1024]{1,0:T(8,128)(2,1)} %tokens_ref.7, bf16[1024,8192]{1,0:T(8,128)(2,1)} %weight_ref.7, bf16[1032,128]{1,0:T(8,128)(2,1)S(1)} %encode.3.refs_0_), custom_call_target="tpu_custom_call" | custom-call | flops 1073741824 | bytes 8388608 | tf_op jit(solution)/shard_map/products/pallas_call | solution.py:73
  9.0 0.1 collective-permute-start.2
  9.0 0.5 %collective-permute-start.1 = (f32[128,1024]{1,0:T(8,128)S(1)}, f32[128,1024]{1,0:T(8,128)S(1)}, u32[]{:S(2)}, u32[]{:S(2)}) collective-permute-start(f32[128,1024]{1,0:T(8,128)S(1)} %get-tuple-element.24), channel_id=1, source_target_pairs={{0,1},{1,0},{2,3},{3,2},{4,5},{5,4},{6,7},{7,6},{8,9},{9,8},{10,11... | collective-permute-start | bytes 1572872 | tf_op jit(solution)/shard_map/ppermute | solution.py:454
  9.5 2.6 %collective-permute-start.5 = (bf16[1032,128]{1,0:T(8,128)(2,1)S(1)}, bf16[1032,128]{1,0:T(8,128)(2,1)S(1)}, u32[]{:S(2)}, u32[]{:S(2)}) collective-permute-start(bf16[1032,128]{1,0:T(8,128)(2,1)S(1)} %encode.3.refs_0_), channel_id=1, source_target_pairs={{0,2},{1,3},{2,0},{3,1},{4,6},{5,7},{6,4},{7,5},{8,10},{9,11},{10,... | collective-permute-start | bytes 792584 | tf_op jit(solution)/shard_map/ppermute | solution.py:458
  12.1 0.3 collective-permute-done.1.theirs_ref
  12.4 0.2 encode.5
  12.6 2.7 %collective-permute-start.4 = (bf16[520,128]{1,0:T(8,128)(2,1)S(1)}, bf16[520,128]{1,0:T(8,128)(2,1)S(1)}, u32[]{:S(2)}, u32[]{:S(2)}) collective-permute-start(bf16[520,128]{1,0:T(8,128)(2,1)S(1)} %encode.5), channel_id=1, source_target_pairs={{0,2},{1,3},{2,0},{3,1},{4,6},{5,7},{6,4},{7,5},{8,10},{9,11},{10,... | collective-permute-start | bytes 399368 | tf_op jit(solution)/shard_map/ppermute | solution.py:458
  15.3 0.2 encode.4.refs_0_
  15.6 2.6 %products.7.refs_0_ = f32[128,2048]{1,0:T(8,128)S(1)} custom-call(bf16[128,1024]{1,0:T(8,128)(2,1)} %tokens_ref.7, bf16[1024,8192]{1,0:T(8,128)(2,1)} %weight_ref.7, bf16[520,128]{1,0:T(8,128)(2,1)S(1)} %encode.4.refs_0_), custom_call_target="tpu_custom_call" | custom-call | flops 536870912 | bytes 4194304 | tf_op jit(solution)/shard_map/products/pallas_call | solution.py:73
  18.3 1.0 %collective-permute-done.5.refs_2_ = bf16[1032,128]{1,0:T(8,128)(2,1)S(1)} collective-permute-done((bf16[1032,128]{1,0:T(8,128)(2,1)S(1)}, bf16[1032,128]{1,0:T(8,128)(2,1)S(1)}, u32[]{:S(2)}, u32[]{:S(2)}) %collective-permute-start.5) | collective-permute-done | bytes 264224 | tf_op jit(solution)/shard_map/ppermute | solution.py:458
  19.3 0.5 %first.4 = (f32[1,3,128,128]{3,2,1,0:T(8,128)S(1)}, f32[1,5,8,128]{3,2,1,0:T(8,128)S(1)}, f32[8,128]{1,0:T(8,128)S(1)}) custom-call(f32[128,2048]{1,0:T(8,128)S(1)} %products.7.refs_0_, f32[128,2048]{1,0:T(8,128)S(1)} %collective-permute-done.2.refs_1_, bf16[1032,128]{1,0:T(8,128)(2,1)S(1)} %collective-permute-done.5.refs_2_, f32[4,512]{1,0:T(4,128)S(1)} %bitcast.3, ...), custom_call_target="tpu_custom_call" | custom-call | flops 3932160 | bytes 1310720 | tf_op jit(solution)/shard_map/first/pallas_call | solution.py:257
  19.8 0.5 %first.5 = (f32[1,3,128,128]{3,2,1,0:T(8,128)S(1)}, f32[1,5,8,128]{3,2,1,0:T(8,128)S(1)}, f32[16,128]{1,0:T(8,128)S(1)}) custom-call(f32[128,2048]{1,0:T(8,128)S(1)} %products.7.refs_0_, f32[128,2048]{1,0:T(8,128)S(1)} %collective-permute-done.2.refs_1_, bf16[1032,128]{1,0:T(8,128)(2,1)S(1)} %collective-permute-done.5.refs_2_, f32[4,512]{1,0:T(4,128)S(1)} %bitcast.4, ...), custom_call_target="tpu_custom_call" | custom-call | flops 3932160 | bytes 1310720 | tf_op jit(solution)/shard_map/first/pallas_call | solution.py:257
  20.3 1.8 %collective-permute-done.4.refs_2_ = bf16[520,128]{1,0:T(8,128)(2,1)S(1)} collective-permute-done((bf16[520,128]{1,0:T(8,128)(2,1)S(1)}, bf16[520,128]{1,0:T(8,128)(2,1)S(1)}, u32[]{:S(2)}, u32[]{:S(2)}) %collective-permute-start.4) | collective-permute-done | bytes 133152 | tf_op jit(solution)/shard_map/ppermute | solution.py:458
  22.1 0.5 %first.6 = (f32[1,3,128,128]{3,2,1,0:T(8,128)S(1)}, f32[1,5,8,128]{3,2,1,0:T(8,128)S(1)}, f32[24,128]{1,0:T(8,128)S(1)}) custom-call(f32[128,2048]{1,0:T(8,128)S(1)} %products.7.refs_0_, f32[128,2048]{1,0:T(8,128)S(1)} %collective-permute-done.2.refs_1_, bf16[520,128]{1,0:T(8,128)(2,1)S(1)} %collective-permute-done.4.refs_2_, f32[4,512]{1,0:T(4,128)S(1)} %bitcast.5, ...), custom_call_target="tpu_custom_call" | custom-call | flops 3932160 | bytes 1310720 | tf_op jit(solution)/shard_map/first/pallas_call | solution.py:257
  22.6 2.1 %collective-permute-done.3.refs_2_ = bf16[520,128]{1,0:T(8,128)(2,1)S(1)} collective-permute-done((bf16[520,128]{1,0:T(8,128)(2,1)S(1)}, bf16[520,128]{1,0:T(8,128)(2,1)S(1)}, u32[]{:S(2)}, u32[]{:S(2)}) %collective-permute-start.3) | collective-permute-done | bytes 133152 | tf_op jit(solution)/shard_map/ppermute | solution.py:458
  24.7 0.5 %first.7 = (f32[1,3,128,128]{3,2,1,0:T(8,128)S(1)}, f32[1,5,8,128]{3,2,1,0:T(8,128)S(1)}, f32[32,128]{1,0:T(8,128)S(1)}) custom-call(f32[128,2048]{1,0:T(8,128)S(1)} %products.7.refs_0_, f32[128,2048]{1,0:T(8,128)S(1)} %collective-permute-done.2.refs_1_, bf16[520,128]{1,0:T(8,128)(2,1)S(1)} %collective-permute-done.3.refs_2_, f32[4,512]{1,0:T(4,128)S(1)} %bitcast.6, ...), custom_call_target="tpu_custom_call" | custom-call | flops 3932160 | bytes 1310720 | tf_op jit(solution)/shard_map/first/pallas_call | solution.py:257
  25.2 3.9 %collective-permute-start.8 = (f32[32,128]{1,0:T(8,128)S(1)}, f32[32,128]{1,0:T(8,128)S(1)}, u32[]{:S(2)}, u32[]{:S(2)}) collective-permute-start(f32[32,128]{1,0:T(8,128)S(1)} %get-tuple-element.29), channel_id=1, source_target_pairs={{0,12},{4,8},{8,4},{12,0},{1,13},{5,9},{9,5},{13,1},{2,14},{6,10},... | collective-permute-start | bytes 49160 | tf_op jit(solution)/shard_map/ppermute | solution.py:464
  29.2 0.6 %collective-permute-start.6 = (f32[32,128]{1,0:T(8,128)S(1)}, f32[32,128]{1,0:T(8,128)S(1)}, u32[]{:S(2)}, u32[]{:S(2)}) collective-permute-start(f32[32,128]{1,0:T(8,128)S(1)} %get-tuple-element.29), channel_id=1, source_target_pairs={{0,4},{4,0},{8,12},{12,8},{1,5},{5,1},{9,13},{13,9},{2,6},{6,2},{1... | collective-permute-start | bytes 49160 | tf_op jit(solution)/shard_map/ppermute | solution.py:464
  29.8 1.1 %collective-permute-done.8.refs_2_ = f32[32,128]{1,0:T(8,128)S(1)} collective-permute-done((f32[32,128]{1,0:T(8,128)S(1)}, f32[32,128]{1,0:T(8,128)S(1)}, u32[]{:S(2)}, u32[]{:S(2)}) %collective-permute-start.8) | collective-permute-done | bytes 16416 | tf_op jit(solution)/shard_map/ppermute | solution.py:464
  30.9 2.9 %collective-permute-done.7.refs_1_ = f32[32,128]{1,0:T(8,128)S(1)} collective-permute-done((f32[32,128]{1,0:T(8,128)S(1)}, f32[32,128]{1,0:T(8,128)S(1)}, u32[]{:S(2)}, u32[]{:S(2)}) %collective-permute-start.7) | collective-permute-done | bytes 16416 | tf_op jit(solution)/shard_map/ppermute | solution.py:464
  33.8 0.8 %second.1 = (f32[4,3,128,128]{3,2,1,0:T(8,128)S(1)}, f32[4,6,8,128]{3,2,1,0:T(8,128)S(1)}, f32[32,128]{1,0:T(8,128)S(1)}) custom-call(f32[32,128]{1,0:T(8,128)S(1)} %collective-permute-done.6.refs_0_, f32[32,128]{1,0:T(8,128)S(1)} %collective-permute-done.7.refs_1_, f32[32,128]{1,0:T(8,128)S(1)} %collective-permute-done.8.refs_2_, ...), custom_call_target="tpu_custom_call" | custom-call | flops 6553600 | bytes 1572864 | tf_op jit(solution)/shard_map/second/pallas_call | solution.py:373
  34.6 1.5 %collective-permute-start.11 = (f32[32,128]{1,0:T(8,128)S(1)}, f32[32,128]{1,0:T(8,128)S(1)}, u32[]{:S(2)}, u32[]{:S(2)}) collective-permute-start(f32[32,128]{1,0:T(8,128)S(1)} %get-tuple-element.38), channel_id=1, source_target_pairs={{0,12},{4,8},{8,4},{12,0},{1,13},{5,9},{9,5},{13,1},{2,14},{6,10},... | collective-permute-start | bytes 49160 | tf_op jit(solution)/shard_map/ppermute | solution.py:464
  36.1 0.6 %collective-permute-start.10 = (f32[32,128]{1,0:T(8,128)S(1)}, f32[32,128]{1,0:T(8,128)S(1)}, u32[]{:S(2)}, u32[]{:S(2)}) collective-permute-start(f32[32,128]{1,0:T(8,128)S(1)} %get-tuple-element.38), channel_id=1, source_target_pairs={{0,8},{4,12},{8,0},{12,4},{1,9},{5,13},{9,1},{13,5},{2,10},{6,14},... | collective-permute-start | bytes 49160 | tf_op jit(solution)/shard_map/ppermute | solution.py:464
  36.8 2.3 %collective-permute-start.9 = (f32[32,128]{1,0:T(8,128)S(1)}, f32[32,128]{1,0:T(8,128)S(1)}, u32[]{:S(2)}, u32[]{:S(2)}) collective-permute-start(f32[32,128]{1,0:T(8,128)S(1)} %get-tuple-element.38), channel_id=1, source_target_pairs={{0,4},{4,0},{8,12},{12,8},{1,5},{5,1},{9,13},{13,9},{2,6},{6,2},{1... | collective-permute-start | bytes 49160 | tf_op jit(solution)/shard_map/ppermute | solution.py:464
  39.1 1.1 %collective-permute-done.11.refs_2_ = f32[32,128]{1,0:T(8,128)S(1)} collective-permute-done((f32[32,128]{1,0:T(8,128)S(1)}, f32[32,128]{1,0:T(8,128)S(1)}, u32[]{:S(2)}, u32[]{:S(2)}) %collective-permute-start.11) | collective-permute-done | bytes 16416 | tf_op jit(solution)/shard_map/ppermute | solution.py:464
  40.2 0.6 %collective-permute-done.10.refs_1_ = f32[32,128]{1,0:T(8,128)S(1)} collective-permute-done((f32[32,128]{1,0:T(8,128)S(1)}, f32[32,128]{1,0:T(8,128)S(1)}, u32[]{:S(2)}, u32[]{:S(2)}) %collective-permute-start.10) | collective-permute-done | bytes 16416 | tf_op jit(solution)/shard_map/ppermute | solution.py:464
  40.8 0.2 collective-permute-done.9.refs_0_
  40.9 0.9 %last.1 = f32[512,128]{1,0:T(8,128)} custom-call(f32[32,128]{1,0:T(8,128)S(1)} %collective-permute-done.9.refs_0_, f32[32,128]{1,0:T(8,128)S(1)} %collective-permute-done.10.refs_1_, f32[32,128]{1,0:T(8,128)S(1)} %collective-permute-done.11.refs_2_, f32[4,3,128,128]{3,2,1,0:T(8,128)S(1)} %get-tuple-element.39.refs_3_, ...), custom_call_target="tpu_custom_call" | custom-call | flops 655360 | bytes 1048576 | tf_op jit(solution)/shard_map/last/pallas_call | solution.py:416
  (11 shorter events, 0.1 us)
Async XLA Ops:
  2.0 2.5 %collective-permute-start = (f32[128,1024]{1,0:T(8,128)S(1)}, f32[128,1024]{1,0:T(8,128)S(1)}, u32[]{:S(2)}, u32[]{:S(2)}) collective-permute-start(f32[128,1024]{1,0:T(8,128)S(1)} %products.5), channel_id=1, source_target_pairs={{0,1},{1,0},{2,3},{3,2},{4,5},{5,4},{6,7},{7,6},{8,9},{9,8},{10,11... | collective-permute-start | bytes 1572872 | tf_op jit(solution)/shard_map/ppermute | solution.py:454
  4.9 14.4 %copy-start = (f32[512,4]{0,1:T(4,128)S(1)}, f32[512,4]{0,1:T(4,128)}, u32[]{:S(2)}) copy-start(f32[512,4]{0,1:T(4,128)} %param.8) | copy-start | bytes 24580
  5.0 14.3 %copy-start.1 = (f32[512,2]{0,1:T(2,128)S(1)}, f32[512,2]{0,1:T(2,128)}, u32[]{:S(2)}) copy-start(f32[512,2]{0,1:T(2,128)} %param.7) | copy-start | bytes 12292
  5.0 14.3 %copy-start.2 = (f32[128]{0:T(128)S(1)}, f32[128]{0:T(128)}, u32[]{:S(2)}) copy-start(f32[128]{0:T(128)} %param.9) | copy-start | bytes 1540
  9.0 10.3 %collective-permute-start.2 = (f32[128,2048]{1,0:T(8,128)S(1)}, f32[128,2048]{1,0:T(8,128)S(1)}, u32[]{:S(2)}, u32[]{:S(2)}) collective-permute-start(f32[128,2048]{1,0:T(8,128)S(1)} %get-tuple-element.25), channel_id=1, source_target_pairs={{0,1},{1,0},{2,3},{3,2},{4,5},{5,4},{6,7},{7,6},{8,9},{9,8},{10,11... | collective-permute-start | bytes 3145736 | tf_op jit(solution)/shard_map/ppermute | solution.py:454
  9.0 3.4 %collective-permute-start.1 = (f32[128,1024]{1,0:T(8,128)S(1)}, f32[128,1024]{1,0:T(8,128)S(1)}, u32[]{:S(2)}, u32[]{:S(2)}) collective-permute-start(f32[128,1024]{1,0:T(8,128)S(1)} %get-tuple-element.24), channel_id=1, source_target_pairs={{0,1},{1,0},{2,3},{3,2},{4,5},{5,4},{6,7},{7,6},{8,9},{9,8},{10,11... | collective-permute-start | bytes 1572872 | tf_op jit(solution)/shard_map/ppermute | solution.py:454
  9.5 9.8 %collective-permute-start.5 = (bf16[1032,128]{1,0:T(8,128)(2,1)S(1)}, bf16[1032,128]{1,0:T(8,128)(2,1)S(1)}, u32[]{:S(2)}, u32[]{:S(2)}) collective-permute-start(bf16[1032,128]{1,0:T(8,128)(2,1)S(1)} %encode.3.refs_0_), channel_id=1, source_target_pairs={{0,2},{1,3},{2,0},{3,1},{4,6},{5,7},{6,4},{7,5},{8,10},{9,11},{10,... | collective-permute-start | bytes 792584 | tf_op jit(solution)/shard_map/ppermute | solution.py:458
  12.6 9.5 %collective-permute-start.4 = (bf16[520,128]{1,0:T(8,128)(2,1)S(1)}, bf16[520,128]{1,0:T(8,128)(2,1)S(1)}, u32[]{:S(2)}, u32[]{:S(2)}) collective-permute-start(bf16[520,128]{1,0:T(8,128)(2,1)S(1)} %encode.5), channel_id=1, source_target_pairs={{0,2},{1,3},{2,0},{3,1},{4,6},{5,7},{6,4},{7,5},{8,10},{9,11},{10,... | collective-permute-start | bytes 399368 | tf_op jit(solution)/shard_map/ppermute | solution.py:458
  15.5 9.2 %collective-permute-start.3 = (bf16[520,128]{1,0:T(8,128)(2,1)S(1)}, bf16[520,128]{1,0:T(8,128)(2,1)S(1)}, u32[]{:S(2)}, u32[]{:S(2)}) collective-permute-start(bf16[520,128]{1,0:T(8,128)(2,1)S(1)} %encode.4.refs_0_), channel_id=1, source_target_pairs={{0,2},{1,3},{2,0},{3,1},{4,6},{5,7},{6,4},{7,5},{8,10},{9,11},{10,... | collective-permute-start | bytes 399368 | tf_op jit(solution)/shard_map/ppermute | solution.py:458
  25.2 5.6 %collective-permute-start.8 = (f32[32,128]{1,0:T(8,128)S(1)}, f32[32,128]{1,0:T(8,128)S(1)}, u32[]{:S(2)}, u32[]{:S(2)}) collective-permute-start(f32[32,128]{1,0:T(8,128)S(1)} %get-tuple-element.29), channel_id=1, source_target_pairs={{0,12},{4,8},{8,4},{12,0},{1,13},{5,9},{9,5},{13,1},{2,14},{6,10},... | collective-permute-start | bytes 49160 | tf_op jit(solution)/shard_map/ppermute | solution.py:464
  29.2 4.6 %collective-permute-start.7 = (f32[32,128]{1,0:T(8,128)S(1)}, f32[32,128]{1,0:T(8,128)S(1)}, u32[]{:S(2)}, u32[]{:S(2)}) collective-permute-start(f32[32,128]{1,0:T(8,128)S(1)} %get-tuple-element.29), channel_id=1, source_target_pairs={{0,8},{4,12},{8,0},{12,4},{1,9},{5,13},{9,1},{13,5},{2,10},{6,14},... | collective-permute-start | bytes 49160 | tf_op jit(solution)/shard_map/ppermute | solution.py:464
  29.2 4.6 %collective-permute-start.6 = (f32[32,128]{1,0:T(8,128)S(1)}, f32[32,128]{1,0:T(8,128)S(1)}, u32[]{:S(2)}, u32[]{:S(2)}) collective-permute-start(f32[32,128]{1,0:T(8,128)S(1)} %get-tuple-element.29), channel_id=1, source_target_pairs={{0,4},{4,0},{8,12},{12,8},{1,5},{5,1},{9,13},{13,9},{2,6},{6,2},{1... | collective-permute-start | bytes 49160 | tf_op jit(solution)/shard_map/ppermute | solution.py:464
  34.6 5.6 %collective-permute-start.11 = (f32[32,128]{1,0:T(8,128)S(1)}, f32[32,128]{1,0:T(8,128)S(1)}, u32[]{:S(2)}, u32[]{:S(2)}) collective-permute-start(f32[32,128]{1,0:T(8,128)S(1)} %get-tuple-element.38), channel_id=1, source_target_pairs={{0,12},{4,8},{8,4},{12,0},{1,13},{5,9},{9,5},{13,1},{2,14},{6,10},... | collective-permute-start | bytes 49160 | tf_op jit(solution)/shard_map/ppermute | solution.py:464
  36.1 4.7 %collective-permute-start.10 = (f32[32,128]{1,0:T(8,128)S(1)}, f32[32,128]{1,0:T(8,128)S(1)}, u32[]{:S(2)}, u32[]{:S(2)}) collective-permute-start(f32[32,128]{1,0:T(8,128)S(1)} %get-tuple-element.38), channel_id=1, source_target_pairs={{0,8},{4,12},{8,0},{12,4},{1,9},{5,13},{9,1},{13,5},{2,10},{6,14},... | collective-permute-start | bytes 49160 | tf_op jit(solution)/shard_map/ppermute | solution.py:464
  36.8 4.2 %collective-permute-start.9 = (f32[32,128]{1,0:T(8,128)S(1)}, f32[32,128]{1,0:T(8,128)S(1)}, u32[]{:S(2)}, u32[]{:S(2)}) collective-permute-start(f32[32,128]{1,0:T(8,128)S(1)} %get-tuple-element.38), channel_id=1, source_target_pairs={{0,4},{4,0},{8,12},{12,8},{1,5},{5,1},{9,13},{13,9},{2,6},{6,2},{1... | collective-permute-start | bytes 49160 | tf_op jit(solution)/shard_map/ppermute | solution.py:464

commit v10 on v9

--- a/solution.py
+++ b/solution.py
@@ -431,9 +431,8 @@
 
 def pieces_of(groups, chips):
     half = max(1, groups // 2)
-    pieces = [(1, 0, half), (1, half, groups - half)]
-    pieces += [(away, 0, groups) for away in range(2, chips)]
-    return [piece for piece in pieces if piece[2]]
+    pieces = [(1, 0, half)] + [(1, group, 1) for group in range(half, groups)]
+    return pieces + [(away, 0, groups) for away in range(2, chips)]
 
 
 def shards(tokens, in_weight, recur_weight, gate_bias, forget_offset):
@@ -490,7 +489,7 @@
             theirs = to_core(give)
             keep, *more = product(parts[1:] + (local_give,) * last_piece, [])
         else:
-            give, keep, *more = product(parts + (local_give,) * last_piece, codes[-1:])
+            give, keep, *more = product(parts + (local_give,) * last_piece, codes[-2:][:1])
             theirs = to_core(give)
         if last_piece:
             given = to_core(more[0])

time: 42 us -> 45.1 us (1.074)
  waiting for transfers between devices: 11.1 us -> 13.1 us
  Pallas kernels: 15.1 us -> 16.4 us
    ppermute x6, waiting for transfers between devices: 5.88 us -> 7.57 us  [to_blocks(): lax.ppermute(value, 'tm', [pair for pair in pairs if pair[1] < blocks])]
    pallas_call x4 -> x5, Pallas kernels: 10.6 us -> 11.9 us  [products(): pl.pallas_call(functools.partial(product_kernel, chips, parts, per_owner)...]
    ppermute x3, waiting for transfers between devices: 4.91 us -> 5.51 us  [to_chip(): return on_chip(lax.ppermute(value, 'chan', pairs))]
    ppermute x3 -> x4, starting transfers between devices: 1.14 us -> 1.28 us  [to_core(): lax.ppermute(value, 'chan', [(i, i ^ 1) for i in range(owners)])]
  transfers between devices with their start and end apart: 12 -> 13, of which waited for: 9 -> 7; matrix products, arithmetic and copies ran while one was open for 0% -> 0% of each run, Pallas kernels for 16% -> 19%
where the time goes in v10:
time: 45.1 us; the launch traced here: 44.9 us
  Pallas kernels  16.4 us (36%)
  starting transfers between devices  15.3 us (34%)
  waiting for transfers between devices  13.1 us (29%)
    pallas_call x5, Pallas kernels, products(): pl.pallas_call(functools.partial(product_kernel, chips, parts, per_owner)...  11.9 us
    ppermute x6, starting transfers between devices, to_blocks(): lax.ppermute(value, 'tm', [pair for pair in pairs if pair[1] < blocks])  8.93 us
    ppermute x6, waiting for transfers between devices, to_blocks(): lax.ppermute(value, 'tm', [pair for pair in pairs if pair[1] < blocks])  7.57 us
    ppermute x3, waiting for transfers between devices, to_chip(): return on_chip(lax.ppermute(value, 'chan', pairs))  5.51 us
    ppermute x3, starting transfers between devices, to_chip(): return on_chip(lax.ppermute(value, 'chan', pairs))  5.06 us
    pallas_call x4, Pallas kernels, first(): pl.pallas_call(functools.partial(first_kernel, start, places, len(earlier...  2 us
    ppermute x4, starting transfers between devices, to_core(): lax.ppermute(value, 'chan', [(i, i ^ 1) for i in range(owners)])  1.28 us
    pallas_call x1, Pallas kernels, last(): pl.pallas_call(functools.partial(last_kernel, count, own_xor), out_shape=...  0.91 us
  transfers between devices with their start and end apart: 13, of which 7 were waited for; matrix products, arithmetic and copies ran while one was open for 0% of the time, Pallas kernels for 19%

profile of v10, /device:TPU:0, one launch (start us, length us, event | category | flops | bytes accessed | tf_op | source)
XLA Modules:
  0.0 44.9 jit_solution(9849973206318039894)
XLA Ops:
  0.0 2.0 %products.6 = f32[128,1024]{1,0:T(8,128)S(1)} custom-call(bf16[128,1024]{1,0:T(8,128)(2,1)} %tokens_ref.9, bf16[1024,8192]{1,0:T(8,128)(2,1)} %weight_ref.9), custom_call_target="tpu_custom_call" | custom-call | flops 268435456 | bytes 2097152 | tf_op jit(solution)/shard_map/products/pallas_call | solution.py:73
  2.0 0.6 %collective-permute-start = (f32[128,1024]{1,0:T(8,128)S(1)}, f32[128,1024]{1,0:T(8,128)S(1)}, u32[]{:S(2)}, u32[]{:S(2)}) collective-permute-start(f32[128,1024]{1,0:T(8,128)S(1)} %products.6), channel_id=1, source_target_pairs={{0,1},{1,0},{2,3},{3,2},{4,5},{5,4},{6,7},{7,6},{8,9},{9,8},{10,11... | collective-permute-start | bytes 1572872 | tf_op jit(solution)/shard_map/ppermute | solution.py:453
  2.5 2.0 %products.5.mine_ref = f32[128,1024]{1,0:T(8,128)S(1)} custom-call(bf16[128,1024]{1,0:T(8,128)(2,1)} %tokens_ref.9, bf16[1024,8192]{1,0:T(8,128)(2,1)} %weight_ref.9), custom_call_target="tpu_custom_call" | custom-call | flops 268435456 | bytes 2097152 | tf_op jit(solution)/shard_map/products/pallas_call | solution.py:73
  4.5 0.4 encode.3.refs_0_
  4.9 3.3 %products.7 = (f32[128,512]{1,0:T(8,128)S(1)}, f32[128,512]{1,0:T(8,128)S(1)}, f32[128,2048]{1,0:T(8,128)S(1)}) custom-call(bf16[128,1024]{1,0:T(8,128)(2,1)} %tokens_ref.9, bf16[1024,8192]{1,0:T(8,128)(2,1)} %weight_ref.9, bf16[1032,128]{1,0:T(8,128)(2,1)S(1)} %encode.3.refs_0_), custom_call_target="tpu_custom_call" | custom-call | flops 805306368 | bytes 6291456 | tf_op jit(solution)/shard_map/products/pallas_call | solution.py:73
  8.3 0.1 collective-permute-start.2
  8.4 2.0 %products.9 = (f32[128,512]{1,0:T(8,128)S(1)}, f32[128,512]{1,0:T(8,128)S(1)}) custom-call(bf16[128,1024]{1,0:T(8,128)(2,1)} %tokens_ref.9, bf16[1024,8192]{1,0:T(8,128)(2,1)} %weight_ref.9, bf16[1032,128]{1,0:T(8,128)(2,1)S(1)} %encode.3.refs_0_), custom_call_target="tpu_custom_call" | custom-call | flops 268435456 | bytes 2097152 | tf_op jit(solution)/shard_map/products/pallas_call | solution.py:73
  10.4 0.6 %collective-permute-start.4 = (f32[128,512]{1,0:T(8,128)S(1)}, f32[128,512]{1,0:T(8,128)S(1)}, u32[]{:S(2)}, u32[]{:S(2)}) collective-permute-start(f32[128,512]{1,0:T(8,128)S(1)} %get-tuple-element.29), channel_id=1, source_target_pairs={{0,1},{1,0},{2,3},{3,2},{4,5},{5,4},{6,7},{7,6},{8,9},{9,8},{10,11... | collective-permute-start | bytes 786440 | tf_op jit(solution)/shard_map/ppermute | solution.py:453
  10.9 0.1 collective-permute-start.1
  11.0 2.9 %collective-permute-start.6 = (bf16[1032,128]{1,0:T(8,128)(2,1)S(1)}, bf16[1032,128]{1,0:T(8,128)(2,1)S(1)}, u32[]{:S(2)}, u32[]{:S(2)}) collective-permute-start(bf16[1032,128]{1,0:T(8,128)(2,1)S(1)} %encode.3.refs_0_), channel_id=1, source_target_pairs={{0,2},{1,3},{2,0},{3,1},{4,6},{5,7},{6,4},{7,5},{8,10},{9,11},{10,... | collective-permute-start | bytes 792584 | tf_op jit(solution)/shard_map/ppermute | solution.py:457
  13.9 0.2 encode.5
  14.1 1.1 %collective-permute-start.5 = (bf16[520,128]{1,0:T(8,128)(2,1)S(1)}, bf16[520,128]{1,0:T(8,128)(2,1)S(1)}, u32[]{:S(2)}, u32[]{:S(2)}) collective-permute-start(bf16[520,128]{1,0:T(8,128)(2,1)S(1)} %encode.5), channel_id=1, source_target_pairs={{0,2},{1,3},{2,0},{3,1},{4,6},{5,7},{6,4},{7,5},{8,10},{9,11},{10,... | collective-permute-start | bytes 399368 | tf_op jit(solution)/shard_map/ppermute | solution.py:457
  15.2 0.2 encode.4.refs_0_
  15.4 1.1 %collective-permute-start.3 = (bf16[520,128]{1,0:T(8,128)(2,1)S(1)}, bf16[520,128]{1,0:T(8,128)(2,1)S(1)}, u32[]{:S(2)}, u32[]{:S(2)}) collective-permute-start(bf16[520,128]{1,0:T(8,128)(2,1)S(1)} %encode.4.refs_0_), channel_id=1, source_target_pairs={{0,2},{1,3},{2,0},{3,1},{4,6},{5,7},{6,4},{7,5},{8,10},{9,11},{10,... | collective-permute-start | bytes 399368 | tf_op jit(solution)/shard_map/ppermute | solution.py:457
  16.5 2.6 %products.8.refs_0_ = f32[128,2048]{1,0:T(8,128)S(1)} custom-call(bf16[128,1024]{1,0:T(8,128)(2,1)} %tokens_ref.9, bf16[1024,8192]{1,0:T(8,128)(2,1)} %weight_ref.9, bf16[520,128]{1,0:T(8,128)(2,1)S(1)} %encode.4.refs_0_), custom_call_target="tpu_custom_call" | custom-call | flops 536870912 | bytes 4194304 | tf_op jit(solution)/shard_map/products/pallas_call | solution.py:73
  19.1 2.0 %collective-permute-done.6.refs_2_ = bf16[1032,128]{1,0:T(8,128)(2,1)S(1)} collective-permute-done((bf16[1032,128]{1,0:T(8,128)(2,1)S(1)}, bf16[1032,128]{1,0:T(8,128)(2,1)S(1)}, u32[]{:S(2)}, u32[]{:S(2)}) %collective-permute-start.6) | collective-permute-done | bytes 264224 | tf_op jit(solution)/shard_map/ppermute | solution.py:457
  21.1 0.5 %first.4 = (f32[1,3,128,128]{3,2,1,0:T(8,128)S(1)}, f32[1,5,8,128]{3,2,1,0:T(8,128)S(1)}, f32[8,128]{1,0:T(8,128)S(1)}) custom-call(f32[128,2048]{1,0:T(8,128)S(1)} %products.8.refs_0_, f32[128,2048]{1,0:T(8,128)S(1)} %collective-permute-done.2.refs_1_, bf16[1032,128]{1,0:T(8,128)(2,1)S(1)} %collective-permute-done.6.refs_2_, f32[4,512]{1,0:T(4,128)S(1)} %bitcast.3, ...), custom_call_target="tpu_custom_call" | custom-call | flops 3932160 | bytes 1310720 | tf_op jit(solution)/shard_map/first/pallas_call | solution.py:257
  21.6 0.5 %first.5 = (f32[1,3,128,128]{3,2,1,0:T(8,128)S(1)}, f32[1,5,8,128]{3,2,1,0:T(8,128)S(1)}, f32[16,128]{1,0:T(8,128)S(1)}) custom-call(f32[128,2048]{1,0:T(8,128)S(1)} %products.8.refs_0_, f32[128,2048]{1,0:T(8,128)S(1)} %collective-permute-done.2.refs_1_, bf16[1032,128]{1,0:T(8,128)(2,1)S(1)} %collective-permute-done.6.refs_2_, f32[4,512]{1,0:T(4,128)S(1)} %bitcast.4, ...), custom_call_target="tpu_custom_call" | custom-call | flops 3932160 | bytes 1310720 | tf_op jit(solution)/shard_map/first/pallas_call | solution.py:257
  22.1 1.8 %collective-permute-done.5.refs_2_ = bf16[520,128]{1,0:T(8,128)(2,1)S(1)} collective-permute-done((bf16[520,128]{1,0:T(8,128)(2,1)S(1)}, bf16[520,128]{1,0:T(8,128)(2,1)S(1)}, u32[]{:S(2)}, u32[]{:S(2)}) %collective-permute-start.5) | collective-permute-done | bytes 133152 | tf_op jit(solution)/shard_map/ppermute | solution.py:457
  24.0 0.5 %first.6 = (f32[1,3,128,128]{3,2,1,0:T(8,128)S(1)}, f32[1,5,8,128]{3,2,1,0:T(8,128)S(1)}, f32[24,128]{1,0:T(8,128)S(1)}) custom-call(f32[128,2048]{1,0:T(8,128)S(1)} %products.8.refs_0_, f32[128,2048]{1,0:T(8,128)S(1)} %collective-permute-done.2.refs_1_, bf16[520,128]{1,0:T(8,128)(2,1)S(1)} %collective-permute-done.5.refs_2_, f32[4,512]{1,0:T(4,128)S(1)} %bitcast.5, ...), custom_call_target="tpu_custom_call" | custom-call | flops 3932160 | bytes 1310720 | tf_op jit(solution)/shard_map/first/pallas_call | solution.py:257
  24.5 1.7 %collective-permute-done.3.refs_2_ = bf16[520,128]{1,0:T(8,128)(2,1)S(1)} collective-permute-done((bf16[520,128]{1,0:T(8,128)(2,1)S(1)}, bf16[520,128]{1,0:T(8,128)(2,1)S(1)}, u32[]{:S(2)}, u32[]{:S(2)}) %collective-permute-start.3) | collective-permute-done | bytes 133152 | tf_op jit(solution)/shard_map/ppermute | solution.py:457
  26.2 0.5 %first.7 = (f32[1,3,128,128]{3,2,1,0:T(8,128)S(1)}, f32[1,5,8,128]{3,2,1,0:T(8,128)S(1)}, f32[32,128]{1,0:T(8,128)S(1)}) custom-call(f32[128,2048]{1,0:T(8,128)S(1)} %products.8.refs_0_, f32[128,2048]{1,0:T(8,128)S(1)} %collective-permute-done.2.refs_1_, bf16[520,128]{1,0:T(8,128)(2,1)S(1)} %collective-permute-done.3.refs_2_, f32[4,512]{1,0:T(4,128)S(1)} %bitcast.6, ...), custom_call_target="tpu_custom_call" | custom-call | flops 3932160 | bytes 1310720 | tf_op jit(solution)/shard_map/first/pallas_call | solution.py:257
  26.7 1.9 %collective-permute-start.7 = (f32[32,128]{1,0:T(8,128)S(1)}, f32[32,128]{1,0:T(8,128)S(1)}, u32[]{:S(2)}, u32[]{:S(2)}) collective-permute-start(f32[32,128]{1,0:T(8,128)S(1)} %get-tuple-element.33), channel_id=1, source_target_pairs={{0,4},{4,0},{8,12},{12,8},{1,5},{5,1},{9,13},{13,9},{2,6},{6,2},{1... | collective-permute-start | bytes 49160 | tf_op jit(solution)/shard_map/ppermute | solution.py:463
  28.6 2.6 %collective-permute-start.8 = (f32[32,128]{1,0:T(8,128)S(1)}, f32[32,128]{1,0:T(8,128)S(1)}, u32[]{:S(2)}, u32[]{:S(2)}) collective-permute-start(f32[32,128]{1,0:T(8,128)S(1)} %get-tuple-element.33), channel_id=1, source_target_pairs={{0,8},{4,12},{8,0},{12,4},{1,9},{5,13},{9,1},{13,5},{2,10},{6,14},... | collective-permute-start | bytes 49160 | tf_op jit(solution)/shard_map/ppermute | solution.py:463
  31.2 2.0 %collective-permute-done.8.refs_1_ = f32[32,128]{1,0:T(8,128)S(1)} collective-permute-done((f32[32,128]{1,0:T(8,128)S(1)}, f32[32,128]{1,0:T(8,128)S(1)}, u32[]{:S(2)}, u32[]{:S(2)}) %collective-permute-start.8) | collective-permute-done | bytes 16416 | tf_op jit(solution)/shard_map/ppermute | solution.py:463
  33.2 3.6 %collective-permute-done.9.refs_2_ = f32[32,128]{1,0:T(8,128)S(1)} collective-permute-done((f32[32,128]{1,0:T(8,128)S(1)}, f32[32,128]{1,0:T(8,128)S(1)}, u32[]{:S(2)}, u32[]{:S(2)}) %collective-permute-start.9) | collective-permute-done | bytes 16416 | tf_op jit(solution)/shard_map/ppermute | solution.py:463
  36.9 0.8 %second.1 = (f32[4,3,128,128]{3,2,1,0:T(8,128)S(1)}, f32[4,6,8,128]{3,2,1,0:T(8,128)S(1)}, f32[32,128]{1,0:T(8,128)S(1)}) custom-call(f32[32,128]{1,0:T(8,128)S(1)} %collective-permute-done.7.refs_0_, f32[32,128]{1,0:T(8,128)S(1)} %collective-permute-done.8.refs_1_, f32[32,128]{1,0:T(8,128)S(1)} %collective-permute-done.9.refs_2_, ...), custom_call_target="tpu_custom_call" | custom-call | flops 6553600 | bytes 1572864 | tf_op jit(solution)/shard_map/second/pallas_call | solution.py:373
  37.8 0.6 %collective-permute-start.11 = (f32[32,128]{1,0:T(8,128)S(1)}, f32[32,128]{1,0:T(8,128)S(1)}, u32[]{:S(2)}, u32[]{:S(2)}) collective-permute-start(f32[32,128]{1,0:T(8,128)S(1)} %get-tuple-element.42), channel_id=1, source_target_pairs={{0,8},{4,12},{8,0},{12,4},{1,9},{5,13},{9,1},{13,5},{2,10},{6,14},... | collective-permute-start | bytes 49160 | tf_op jit(solution)/shard_map/ppermute | solution.py:463
  38.3 3.8 %collective-permute-start.12 = (f32[32,128]{1,0:T(8,128)S(1)}, f32[32,128]{1,0:T(8,128)S(1)}, u32[]{:S(2)}, u32[]{:S(2)}) collective-permute-start(f32[32,128]{1,0:T(8,128)S(1)} %get-tuple-element.42), channel_id=1, source_target_pairs={{0,12},{4,8},{8,4},{12,0},{1,13},{5,9},{9,5},{13,1},{2,14},{6,10},... | collective-permute-start | bytes 49160 | tf_op jit(solution)/shard_map/ppermute | solution.py:463
  42.1 0.3 collective-permute-done.11.refs_1_
  42.5 1.6 %collective-permute-done.12.refs_2_ = f32[32,128]{1,0:T(8,128)S(1)} collective-permute-done((f32[32,128]{1,0:T(8,128)S(1)}, f32[32,128]{1,0:T(8,128)S(1)}, u32[]{:S(2)}, u32[]{:S(2)}) %collective-permute-start.12) | collective-permute-done | bytes 16416 | tf_op jit(solution)/shard_map/ppermute | solution.py:463
  44.0 0.9 %last.1 = f32[512,128]{1,0:T(8,128)} custom-call(f32[32,128]{1,0:T(8,128)S(1)} %collective-permute-done.10.refs_0_, f32[32,128]{1,0:T(8,128)S(1)} %collective-permute-done.11.refs_1_, f32[32,128]{1,0:T(8,128)S(1)} %collective-permute-done.12.refs_2_, f32[4,3,128,128]{3,2,1,0:T(8,128)S(1)} %get-tuple-element.43.refs_3_, ...), custom_call_target="tpu_custom_call" | custom-call | flops 655360 | bytes 1048576 | tf_op jit(solution)/shard_map/last/pallas_call | solution.py:416
  (14 shorter events, 0.1 us)
Async XLA Ops:
  2.0 2.5 %collective-permute-start = (f32[128,1024]{1,0:T(8,128)S(1)}, f32[128,1024]{1,0:T(8,128)S(1)}, u32[]{:S(2)}, u32[]{:S(2)}) collective-permute-start(f32[128,1024]{1,0:T(8,128)S(1)} %products.6), channel_id=1, source_target_pairs={{0,1},{1,0},{2,3},{3,2},{4,5},{5,4},{6,7},{7,6},{8,9},{9,8},{10,11... | collective-permute-start | bytes 1572872 | tf_op jit(solution)/shard_map/ppermute | solution.py:453
  8.3 12.8 %copy-start = (f32[512,4]{0,1:T(4,128)S(1)}, f32[512,4]{0,1:T(4,128)}, u32[]{:S(2)}) copy-start(f32[512,4]{0,1:T(4,128)} %param.8) | copy-start | bytes 24580
  8.3 12.8 %copy-start.1 = (f32[512,2]{0,1:T(2,128)S(1)}, f32[512,2]{0,1:T(2,128)}, u32[]{:S(2)}) copy-start(f32[512,2]{0,1:T(2,128)} %param.7) | copy-start | bytes 12292
  8.3 12.8 %copy-start.2 = (f32[128]{0:T(128)S(1)}, f32[128]{0:T(128)}, u32[]{:S(2)}) copy-start(f32[128]{0:T(128)} %param.9) | copy-start | bytes 1540
  8.3 12.8 %collective-permute-start.2 = (f32[128,2048]{1,0:T(8,128)S(1)}, f32[128,2048]{1,0:T(8,128)S(1)}, u32[]{:S(2)}, u32[]{:S(2)}) collective-permute-start(f32[128,2048]{1,0:T(8,128)S(1)} %get-tuple-element.27), channel_id=1, source_target_pairs={{0,1},{1,0},{2,3},{3,2},{4,5},{5,4},{6,7},{7,6},{8,9},{9,8},{10,11... | collective-permute-start | bytes 3145736 | tf_op jit(solution)/shard_map/ppermute | solution.py:453
  10.4 3.5 %collective-permute-start.4 = (f32[128,512]{1,0:T(8,128)S(1)}, f32[128,512]{1,0:T(8,128)S(1)}, u32[]{:S(2)}, u32[]{:S(2)}) collective-permute-start(f32[128,512]{1,0:T(8,128)S(1)} %get-tuple-element.29), channel_id=1, source_target_pairs={{0,1},{1,0},{2,3},{3,2},{4,5},{5,4},{6,7},{7,6},{8,9},{9,8},{10,11... | collective-permute-start | bytes 786440 | tf_op jit(solution)/shard_map/ppermute | solution.py:453
  10.9 4.3 %collective-permute-start.1 = (f32[128,512]{1,0:T(8,128)S(1)}, f32[128,512]{1,0:T(8,128)S(1)}, u32[]{:S(2)}, u32[]{:S(2)}) collective-permute-start(f32[128,512]{1,0:T(8,128)S(1)} %get-tuple-element.26), channel_id=1, source_target_pairs={{0,1},{1,0},{2,3},{3,2},{4,5},{5,4},{6,7},{7,6},{8,9},{9,8},{10,11... | collective-permute-start | bytes 786440 | tf_op jit(solution)/shard_map/ppermute | solution.py:453
  11.0 10.1 %collective-permute-start.6 = (bf16[1032,128]{1,0:T(8,128)(2,1)S(1)}, bf16[1032,128]{1,0:T(8,128)(2,1)S(1)}, u32[]{:S(2)}, u32[]{:S(2)}) collective-permute-start(bf16[1032,128]{1,0:T(8,128)(2,1)S(1)} %encode.3.refs_0_), channel_id=1, source_target_pairs={{0,2},{1,3},{2,0},{3,1},{4,6},{5,7},{6,4},{7,5},{8,10},{9,11},{10,... | collective-permute-start | bytes 792584 | tf_op jit(solution)/shard_map/ppermute | solution.py:457
  14.1 9.8 %collective-permute-start.5 = (bf16[520,128]{1,0:T(8,128)(2,1)S(1)}, bf16[520,128]{1,0:T(8,128)(2,1)S(1)}, u32[]{:S(2)}, u32[]{:S(2)}) collective-permute-start(bf16[520,128]{1,0:T(8,128)(2,1)S(1)} %encode.5), channel_id=1, source_target_pairs={{0,2},{1,3},{2,0},{3,1},{4,6},{5,7},{6,4},{7,5},{8,10},{9,11},{10,... | collective-permute-start | bytes 399368 | tf_op jit(solution)/shard_map/ppermute | solution.py:457
  15.4 10.8 %collective-permute-start.3 = (bf16[520,128]{1,0:T(8,128)(2,1)S(1)}, bf16[520,128]{1,0:T(8,128)(2,1)S(1)}, u32[]{:S(2)}, u32[]{:S(2)}) collective-permute-start(bf16[520,128]{1,0:T(8,128)(2,1)S(1)} %encode.4.refs_0_), channel_id=1, source_target_pairs={{0,2},{1,3},{2,0},{3,1},{4,6},{5,7},{6,4},{7,5},{8,10},{9,11},{10,... | collective-permute-start | bytes 399368 | tf_op jit(solution)/shard_map/ppermute | solution.py:457
  26.7 4.5 %collective-permute-start.7 = (f32[32,128]{1,0:T(8,128)S(1)}, f32[32,128]{1,0:T(8,128)S(1)}, u32[]{:S(2)}, u32[]{:S(2)}) collective-permute-start(f32[32,128]{1,0:T(8,128)S(1)} %get-tuple-element.33), channel_id=1, source_target_pairs={{0,4},{4,0},{8,12},{12,8},{1,5},{5,1},{9,13},{13,9},{2,6},{6,2},{1... | collective-permute-start | bytes 49160 | tf_op jit(solution)/shard_map/ppermute | solution.py:463
  28.6 4.6 %collective-permute-start.8 = (f32[32,128]{1,0:T(8,128)S(1)}, f32[32,128]{1,0:T(8,128)S(1)}, u32[]{:S(2)}, u32[]{:S(2)}) collective-permute-start(f32[32,128]{1,0:T(8,128)S(1)} %get-tuple-element.33), channel_id=1, source_target_pairs={{0,8},{4,12},{8,0},{12,4},{1,9},{5,13},{9,1},{13,5},{2,10},{6,14},... | collective-permute-start | bytes 49160 | tf_op jit(solution)/shard_map/ppermute | solution.py:463
  31.2 5.7 %collective-permute-start.9 = (f32[32,128]{1,0:T(8,128)S(1)}, f32[32,128]{1,0:T(8,128)S(1)}, u32[]{:S(2)}, u32[]{:S(2)}) collective-permute-start(f32[32,128]{1,0:T(8,128)S(1)} %get-tuple-element.33), channel_id=1, source_target_pairs={{0,12},{4,8},{8,4},{12,0},{1,13},{5,9},{9,5},{13,1},{2,14},{6,10},... | collective-permute-start | bytes 49160 | tf_op jit(solution)/shard_map/ppermute | solution.py:463
  37.7 4.5 %collective-permute-start.10 = (f32[32,128]{1,0:T(8,128)S(1)}, f32[32,128]{1,0:T(8,128)S(1)}, u32[]{:S(2)}, u32[]{:S(2)}) collective-permute-start(f32[32,128]{1,0:T(8,128)S(1)} %get-tuple-element.42), channel_id=1, source_target_pairs={{0,4},{4,0},{8,12},{12,8},{1,5},{5,1},{9,13},{13,9},{2,6},{6,2},{1... | collective-permute-start | bytes 49160 | tf_op jit(solution)/shard_map/ppermute | solution.py:463
  37.8 4.7 %collective-permute-start.11 = (f32[32,128]{1,0:T(8,128)S(1)}, f32[32,128]{1,0:T(8,128)S(1)}, u32[]{:S(2)}, u32[]{:S(2)}) collective-permute-start(f32[32,128]{1,0:T(8,128)S(1)} %get-tuple-element.42), channel_id=1, source_target_pairs={{0,8},{4,12},{8,0},{12,4},{1,9},{5,13},{9,1},{13,5},{2,10},{6,14},... | collective-permute-start | bytes 49160 | tf_op jit(solution)/shard_map/ppermute | solution.py:463
  38.3 5.7 %collective-permute-start.12 = (f32[32,128]{1,0:T(8,128)S(1)}, f32[32,128]{1,0:T(8,128)S(1)}, u32[]{:S(2)}, u32[]{:S(2)}) collective-permute-start(f32[32,128]{1,0:T(8,128)S(1)} %get-tuple-element.42), channel_id=1, source_target_pairs={{0,12},{4,8},{8,4},{12,0},{1,13},{5,9},{9,5},{13,1},{2,14},{6,10},... | collective-permute-start | bytes 49160 | tf_op jit(solution)/shard_map/ppermute | solution.py:463

commit v11 on v9

--- a/solution.py
+++ b/solution.py
@@ -480,25 +480,21 @@
         return code
 
     local_give, local_keep = ((0, which, 0, per_owner) for which in (GIVE, KEEP))
-    given = None
     codes = []
     for index, (away, start, count) in enumerate(pieces_of(groups, chips)):
-        last_piece = index == len(pieces_of(groups, chips)) - 1
         parts = tuple((away, which, start * GROUP, count * GROUP) for which in (GIVE, KEEP))
         if index == 0:
             (give,) = product(parts[:1], [])
             theirs = to_core(give)
-            keep, *more = product(parts[1:] + (local_give,) * last_piece, [])
-        else:
-            give, keep, *more = product(parts + (local_give,) * last_piece, codes[-1:])
-            theirs = to_core(give)
-        if last_piece:
-            given = to_core(more[0])
-        if index == 0:
+            (keep,) = product(parts[1:], [])
             codes.append(send(away, start, count, keep, theirs, 0))
         else:
+            give, keep = product(parts, codes[-1:])
+            theirs = to_core(give)
             for group in range(start, start + count):
                 codes.append(send(away, group, 1, keep, theirs, (group - start) * GROUP))
+    (give,) = product((local_give,), codes[-1:])
+    given = to_core(give)
     (keep,) = product((local_keep,), codes[-1:])
     kept, prefixes, totals = [], [], []
     for group in range(groups):

time: 42 us -> 45.2 us (1.076)
  waiting for transfers between devices: 11.1 us -> 13.6 us
  Pallas kernels: 15.1 us -> 16.4 us
  starting transfers between devices: 15.5 us -> 14.8 us
    ppermute x3, waiting for transfers between devices: 0.35 us -> 1.89 us  [to_core(): lax.ppermute(value, 'chan', [(i, i ^ 1) for i in range(owners)])]
    pallas_call x4 -> x5, Pallas kernels: 10.6 us -> 11.9 us  [products(): pl.pallas_call(functools.partial(product_kernel, chips, parts, per_owner)...]
    ppermute x3, waiting for transfers between devices: 4.91 us -> 5.86 us  [to_chip(): return on_chip(lax.ppermute(value, 'chan', pairs))]
  transfers between devices with their start and end apart: 12 -> 12, of which waited for: 9 -> 9; matrix products, arithmetic and copies ran while one was open for 0% -> 0% of each run, Pallas kernels for 16% -> 14%
where the time goes in v11:
time: 45.2 us; the launch traced here: 45 us
  Pallas kernels  16.4 us (36%)
  starting transfers between devices  14.8 us (33%)
  waiting for transfers between devices  13.6 us (30%)
    pallas_call x5, Pallas kernels, products(): pl.pallas_call(functools.partial(product_kernel, chips, parts, per_owner)...  11.9 us
    ppermute x6, starting transfers between devices, to_blocks(): lax.ppermute(value, 'tm', [pair for pair in pairs if pair[1] < blocks])  9.01 us
    ppermute x6, waiting for transfers between devices, to_blocks(): lax.ppermute(value, 'tm', [pair for pair in pairs if pair[1] < blocks])  5.88 us
    ppermute x3, waiting for transfers between devices, to_chip(): return on_chip(lax.ppermute(value, 'chan', pairs))  5.86 us
    ppermute x3, starting transfers between devices, to_chip(): return on_chip(lax.ppermute(value, 'chan', pairs))  4.94 us
    pallas_call x4, Pallas kernels, first(): pl.pallas_call(functools.partial(first_kernel, start, places, len(earlier...  2.01 us
    ppermute x3, waiting for transfers between devices, to_core(): lax.ppermute(value, 'chan', [(i, i ^ 1) for i in range(owners)])  1.89 us
  transfers between devices with their start and end apart: 12, of which 9 were waited for; matrix products, arithmetic and copies ran while one was open for 0% of the time, Pallas kernels for 14%

profile of v11, /device:TPU:0, one launch (start us, length us, event | category | flops | bytes accessed | tf_op | source)
XLA Modules:
  0.0 45.0 jit_solution(13443870476828883567)
XLA Ops:
  0.0 2.0 %products.6 = f32[128,1024]{1,0:T(8,128)S(1)} custom-call(bf16[128,1024]{1,0:T(8,128)(2,1)} %tokens_ref.9, bf16[1024,8192]{1,0:T(8,128)(2,1)} %weight_ref.9), custom_call_target="tpu_custom_call" | custom-call | flops 268435456 | bytes 2097152 | tf_op jit(solution)/shard_map/products/pallas_call | solution.py:73
  2.0 0.6 %collective-permute-start = (f32[128,1024]{1,0:T(8,128)S(1)}, f32[128,1024]{1,0:T(8,128)S(1)}, u32[]{:S(2)}, u32[]{:S(2)}) collective-permute-start(f32[128,1024]{1,0:T(8,128)S(1)} %products.6), channel_id=1, source_target_pairs={{0,1},{1,0},{2,3},{3,2},{4,5},{5,4},{6,7},{7,6},{8,9},{9,8},{10,11... | collective-permute-start | bytes 1572872 | tf_op jit(solution)/shard_map/ppermute | solution.py:454
  2.5 2.0 %products.5.mine_ref = f32[128,1024]{1,0:T(8,128)S(1)} custom-call(bf16[128,1024]{1,0:T(8,128)(2,1)} %tokens_ref.9, bf16[1024,8192]{1,0:T(8,128)(2,1)} %weight_ref.9), custom_call_target="tpu_custom_call" | custom-call | flops 268435456 | bytes 2097152 | tf_op jit(solution)/shard_map/products/pallas_call | solution.py:73
  4.5 0.4 encode.3.refs_0_
  4.9 2.6 %products.7 = (f32[128,1024]{1,0:T(8,128)S(1)}, f32[128,1024]{1,0:T(8,128)S(1)}) custom-call(bf16[128,1024]{1,0:T(8,128)(2,1)} %tokens_ref.9, bf16[1024,8192]{1,0:T(8,128)(2,1)} %weight_ref.9, bf16[1032,128]{1,0:T(8,128)(2,1)S(1)} %encode.3.refs_0_), custom_call_target="tpu_custom_call" | custom-call | flops 536870912 | bytes 4194304 | tf_op jit(solution)/shard_map/products/pallas_call | solution.py:73
  7.7 1.9 %collective-permute-done.1.theirs_ref = f32[128,1024]{1,0:T(8,128)S(1)} collective-permute-done((f32[128,1024]{1,0:T(8,128)S(1)}, f32[128,1024]{1,0:T(8,128)S(1)}, u32[]{:S(2)}, u32[]{:S(2)}) %collective-permute-start.1) | collective-permute-done | bytes 524320 | tf_op jit(solution)/shard_map/ppermute | solution.py:454
  9.6 0.2 encode.4.refs_0_
  9.8 2.7 %products.9 = f32[128,2048]{1,0:T(8,128)S(1)} custom-call(bf16[128,1024]{1,0:T(8,128)(2,1)} %tokens_ref.9, bf16[1024,8192]{1,0:T(8,128)(2,1)} %weight_ref.9, bf16[520,128]{1,0:T(8,128)(2,1)S(1)} %encode.4.refs_0_), custom_call_target="tpu_custom_call" | custom-call | flops 536870912 | bytes 4194304 | tf_op jit(solution)/shard_map/products/pallas_call | solution.py:73
  12.5 0.2 collective-permute-start.2
  12.7 2.9 %collective-permute-start.5 = (bf16[1032,128]{1,0:T(8,128)(2,1)S(1)}, bf16[1032,128]{1,0:T(8,128)(2,1)S(1)}, u32[]{:S(2)}, u32[]{:S(2)}) collective-permute-start(bf16[1032,128]{1,0:T(8,128)(2,1)S(1)} %encode.3.refs_0_), channel_id=1, source_target_pairs={{0,2},{1,3},{2,0},{3,1},{4,6},{5,7},{6,4},{7,5},{8,10},{9,11},{10,... | collective-permute-start | bytes 792584 | tf_op jit(solution)/shard_map/ppermute | solution.py:458
  15.5 0.2 encode.5
  15.8 2.0 %collective-permute-start.3 = (bf16[520,128]{1,0:T(8,128)(2,1)S(1)}, bf16[520,128]{1,0:T(8,128)(2,1)S(1)}, u32[]{:S(2)}, u32[]{:S(2)}) collective-permute-start(bf16[520,128]{1,0:T(8,128)(2,1)S(1)} %encode.4.refs_0_), channel_id=1, source_target_pairs={{0,2},{1,3},{2,0},{3,1},{4,6},{5,7},{6,4},{7,5},{8,10},{9,11},{10,... | collective-permute-start | bytes 399368 | tf_op jit(solution)/shard_map/ppermute | solution.py:458
  17.8 2.6 %products.8.refs_0_ = f32[128,2048]{1,0:T(8,128)S(1)} custom-call(bf16[128,1024]{1,0:T(8,128)(2,1)} %tokens_ref.9, bf16[1024,8192]{1,0:T(8,128)(2,1)} %weight_ref.9, bf16[520,128]{1,0:T(8,128)(2,1)S(1)} %encode.4.refs_0_), custom_call_target="tpu_custom_call" | custom-call | flops 536870912 | bytes 4194304 | tf_op jit(solution)/shard_map/products/pallas_call | solution.py:73
  20.5 2.2 %collective-permute-done.5.refs_2_ = bf16[1032,128]{1,0:T(8,128)(2,1)S(1)} collective-permute-done((bf16[1032,128]{1,0:T(8,128)(2,1)S(1)}, bf16[1032,128]{1,0:T(8,128)(2,1)S(1)}, u32[]{:S(2)}, u32[]{:S(2)}) %collective-permute-start.5) | collective-permute-done | bytes 264224 | tf_op jit(solution)/shard_map/ppermute | solution.py:458
  22.8 0.5 %first.4 = (f32[1,3,128,128]{3,2,1,0:T(8,128)S(1)}, f32[1,5,8,128]{3,2,1,0:T(8,128)S(1)}, f32[8,128]{1,0:T(8,128)S(1)}) custom-call(f32[128,2048]{1,0:T(8,128)S(1)} %products.8.refs_0_, f32[128,2048]{1,0:T(8,128)S(1)} %collective-permute-done.2.refs_1_, bf16[1032,128]{1,0:T(8,128)(2,1)S(1)} %collective-permute-done.5.refs_2_, f32[4,512]{1,0:T(4,128)S(1)} %bitcast.3, ...), custom_call_target="tpu_custom_call" | custom-call | flops 3932160 | bytes 1310720 | tf_op jit(solution)/shard_map/first/pallas_call | solution.py:257
  23.3 0.5 %first.5 = (f32[1,3,128,128]{3,2,1,0:T(8,128)S(1)}, f32[1,5,8,128]{3,2,1,0:T(8,128)S(1)}, f32[16,128]{1,0:T(8,128)S(1)}) custom-call(f32[128,2048]{1,0:T(8,128)S(1)} %products.8.refs_0_, f32[128,2048]{1,0:T(8,128)S(1)} %collective-permute-done.2.refs_1_, bf16[1032,128]{1,0:T(8,128)(2,1)S(1)} %collective-permute-done.5.refs_2_, f32[4,512]{1,0:T(4,128)S(1)} %bitcast.4, ...), custom_call_target="tpu_custom_call" | custom-call | flops 3932160 | bytes 1310720 | tf_op jit(solution)/shard_map/first/pallas_call | solution.py:257
  23.8 1.8 %collective-permute-done.4.refs_2_ = bf16[520,128]{1,0:T(8,128)(2,1)S(1)} collective-permute-done((bf16[520,128]{1,0:T(8,128)(2,1)S(1)}, bf16[520,128]{1,0:T(8,128)(2,1)S(1)}, u32[]{:S(2)}, u32[]{:S(2)}) %collective-permute-start.4) | collective-permute-done | bytes 133152 | tf_op jit(solution)/shard_map/ppermute | solution.py:458
  25.6 0.5 %first.6 = (f32[1,3,128,128]{3,2,1,0:T(8,128)S(1)}, f32[1,5,8,128]{3,2,1,0:T(8,128)S(1)}, f32[24,128]{1,0:T(8,128)S(1)}) custom-call(f32[128,2048]{1,0:T(8,128)S(1)} %products.8.refs_0_, f32[128,2048]{1,0:T(8,128)S(1)} %collective-permute-done.2.refs_1_, bf16[520,128]{1,0:T(8,128)(2,1)S(1)} %collective-permute-done.4.refs_2_, f32[4,512]{1,0:T(4,128)S(1)} %bitcast.5, ...), custom_call_target="tpu_custom_call" | custom-call | flops 3932160 | bytes 1310720 | tf_op jit(solution)/shard_map/first/pallas_call | solution.py:257
  26.1 1.8 %collective-permute-done.3.refs_2_ = bf16[520,128]{1,0:T(8,128)(2,1)S(1)} collective-permute-done((bf16[520,128]{1,0:T(8,128)(2,1)S(1)}, bf16[520,128]{1,0:T(8,128)(2,1)S(1)}, u32[]{:S(2)}, u32[]{:S(2)}) %collective-permute-start.3) | collective-permute-done | bytes 133152 | tf_op jit(solution)/shard_map/ppermute | solution.py:458
  27.9 0.5 %first.7 = (f32[1,3,128,128]{3,2,1,0:T(8,128)S(1)}, f32[1,5,8,128]{3,2,1,0:T(8,128)S(1)}, f32[32,128]{1,0:T(8,128)S(1)}) custom-call(f32[128,2048]{1,0:T(8,128)S(1)} %products.8.refs_0_, f32[128,2048]{1,0:T(8,128)S(1)} %collective-permute-done.2.refs_1_, bf16[520,128]{1,0:T(8,128)(2,1)S(1)} %collective-permute-done.3.refs_2_, f32[4,512]{1,0:T(4,128)S(1)} %bitcast.6, ...), custom_call_target="tpu_custom_call" | custom-call | flops 3932160 | bytes 1310720 | tf_op jit(solution)/shard_map/first/pallas_call | solution.py:257
  28.4 3.9 %collective-permute-start.8 = (f32[32,128]{1,0:T(8,128)S(1)}, f32[32,128]{1,0:T(8,128)S(1)}, u32[]{:S(2)}, u32[]{:S(2)}) collective-permute-start(f32[32,128]{1,0:T(8,128)S(1)} %get-tuple-element.27), channel_id=1, source_target_pairs={{0,12},{4,8},{8,4},{12,0},{1,13},{5,9},{9,5},{13,1},{2,14},{6,10},... | collective-permute-start | bytes 49160 | tf_op jit(solution)/shard_map/ppermute | solution.py:464
  32.3 0.6 %collective-permute-start.6 = (f32[32,128]{1,0:T(8,128)S(1)}, f32[32,128]{1,0:T(8,128)S(1)}, u32[]{:S(2)}, u32[]{:S(2)}) collective-permute-start(f32[32,128]{1,0:T(8,128)S(1)} %get-tuple-element.27), channel_id=1, source_target_pairs={{0,4},{4,0},{8,12},{12,8},{1,5},{5,1},{9,13},{13,9},{2,6},{6,2},{1... | collective-permute-start | bytes 49160 | tf_op jit(solution)/shard_map/ppermute | solution.py:464
  33.0 1.3 %collective-permute-done.8.refs_2_ = f32[32,128]{1,0:T(8,128)S(1)} collective-permute-done((f32[32,128]{1,0:T(8,128)S(1)}, f32[32,128]{1,0:T(8,128)S(1)}, u32[]{:S(2)}, u32[]{:S(2)}) %collective-permute-start.8) | collective-permute-done | bytes 16416 | tf_op jit(solution)/shard_map/ppermute | solution.py:464
  34.2 2.7 %collective-permute-done.7.refs_1_ = f32[32,128]{1,0:T(8,128)S(1)} collective-permute-done((f32[32,128]{1,0:T(8,128)S(1)}, f32[32,128]{1,0:T(8,128)S(1)}, u32[]{:S(2)}, u32[]{:S(2)}) %collective-permute-start.7) | collective-permute-done | bytes 16416 | tf_op jit(solution)/shard_map/ppermute | solution.py:464
  37.0 0.8 %second.1 = (f32[4,3,128,128]{3,2,1,0:T(8,128)S(1)}, f32[4,6,8,128]{3,2,1,0:T(8,128)S(1)}, f32[32,128]{1,0:T(8,128)S(1)}) custom-call(f32[32,128]{1,0:T(8,128)S(1)} %collective-permute-done.6.refs_0_, f32[32,128]{1,0:T(8,128)S(1)} %collective-permute-done.7.refs_1_, f32[32,128]{1,0:T(8,128)S(1)} %collective-permute-done.8.refs_2_, ...), custom_call_target="tpu_custom_call" | custom-call | flops 6553600 | bytes 1572864 | tf_op jit(solution)/shard_map/second/pallas_call | solution.py:373
  37.8 1.5 %collective-permute-start.11 = (f32[32,128]{1,0:T(8,128)S(1)}, f32[32,128]{1,0:T(8,128)S(1)}, u32[]{:S(2)}, u32[]{:S(2)}) collective-permute-start(f32[32,128]{1,0:T(8,128)S(1)} %get-tuple-element.36), channel_id=1, source_target_pairs={{0,12},{4,8},{8,4},{12,0},{1,13},{5,9},{9,5},{13,1},{2,14},{6,10},... | collective-permute-start | bytes 49160 | tf_op jit(solution)/shard_map/ppermute | solution.py:464
  39.3 0.6 %collective-permute-start.10 = (f32[32,128]{1,0:T(8,128)S(1)}, f32[32,128]{1,0:T(8,128)S(1)}, u32[]{:S(2)}, u32[]{:S(2)}) collective-permute-start(f32[32,128]{1,0:T(8,128)S(1)} %get-tuple-element.36), channel_id=1, source_target_pairs={{0,8},{4,12},{8,0},{12,4},{1,9},{5,13},{9,1},{13,5},{2,10},{6,14},... | collective-permute-start | bytes 49160 | tf_op jit(solution)/shard_map/ppermute | solution.py:464
  39.9 2.3 %collective-permute-start.9 = (f32[32,128]{1,0:T(8,128)S(1)}, f32[32,128]{1,0:T(8,128)S(1)}, u32[]{:S(2)}, u32[]{:S(2)}) collective-permute-start(f32[32,128]{1,0:T(8,128)S(1)} %get-tuple-element.36), channel_id=1, source_target_pairs={{0,4},{4,0},{8,12},{12,8},{1,5},{5,1},{9,13},{13,9},{2,6},{6,2},{1... | collective-permute-start | bytes 49160 | tf_op jit(solution)/shard_map/ppermute | solution.py:464
  42.2 1.1 %collective-permute-done.11.refs_2_ = f32[32,128]{1,0:T(8,128)S(1)} collective-permute-done((f32[32,128]{1,0:T(8,128)S(1)}, f32[32,128]{1,0:T(8,128)S(1)}, u32[]{:S(2)}, u32[]{:S(2)}) %collective-permute-start.11) | collective-permute-done | bytes 16416 | tf_op jit(solution)/shard_map/ppermute | solution.py:464
  43.4 0.6 %collective-permute-done.10.refs_1_ = f32[32,128]{1,0:T(8,128)S(1)} collective-permute-done((f32[32,128]{1,0:T(8,128)S(1)}, f32[32,128]{1,0:T(8,128)S(1)}, u32[]{:S(2)}, u32[]{:S(2)}) %collective-permute-start.10) | collective-permute-done | bytes 16416 | tf_op jit(solution)/shard_map/ppermute | solution.py:464
  43.9 0.2 collective-permute-done.9.refs_0_
  44.1 0.9 %last.1 = f32[512,128]{1,0:T(8,128)} custom-call(f32[32,128]{1,0:T(8,128)S(1)} %collective-permute-done.9.refs_0_, f32[32,128]{1,0:T(8,128)S(1)} %collective-permute-done.10.refs_1_, f32[32,128]{1,0:T(8,128)S(1)} %collective-permute-done.11.refs_2_, f32[4,3,128,128]{3,2,1,0:T(8,128)S(1)} %get-tuple-element.37.refs_3_, ...), custom_call_target="tpu_custom_call" | custom-call | flops 655360 | bytes 1048576 | tf_op jit(solution)/shard_map/last/pallas_call | solution.py:416
  (12 shorter events, 0.2 us)
Async XLA Ops:
  2.0 2.5 %collective-permute-start = (f32[128,1024]{1,0:T(8,128)S(1)}, f32[128,1024]{1,0:T(8,128)S(1)}, u32[]{:S(2)}, u32[]{:S(2)}) collective-permute-start(f32[128,1024]{1,0:T(8,128)S(1)} %products.6), channel_id=1, source_target_pairs={{0,1},{1,0},{2,3},{3,2},{4,5},{5,4},{6,7},{7,6},{8,9},{9,8},{10,11... | collective-permute-start | bytes 1572872 | tf_op jit(solution)/shard_map/ppermute | solution.py:454
  7.6 2.0 %collective-permute-start.1 = (f32[128,1024]{1,0:T(8,128)S(1)}, f32[128,1024]{1,0:T(8,128)S(1)}, u32[]{:S(2)}, u32[]{:S(2)}) collective-permute-start(f32[128,1024]{1,0:T(8,128)S(1)} %get-tuple-element.23), channel_id=1, source_target_pairs={{0,1},{1,0},{2,3},{3,2},{4,5},{5,4},{6,7},{7,6},{8,9},{9,8},{10,11... | collective-permute-start | bytes 1572872 | tf_op jit(solution)/shard_map/ppermute | solution.py:454
  9.8 13.0 %copy-start = (f32[512,4]{0,1:T(4,128)S(1)}, f32[512,4]{0,1:T(4,128)}, u32[]{:S(2)}) copy-start(f32[512,4]{0,1:T(4,128)} %param.8) | copy-start | bytes 24580
  9.8 12.9 %copy-start.1 = (f32[512,2]{0,1:T(2,128)S(1)}, f32[512,2]{0,1:T(2,128)}, u32[]{:S(2)}) copy-start(f32[512,2]{0,1:T(2,128)} %param.7) | copy-start | bytes 12292
  9.8 12.9 %copy-start.2 = (f32[128]{0:T(128)S(1)}, f32[128]{0:T(128)}, u32[]{:S(2)}) copy-start(f32[128]{0:T(128)} %param.9) | copy-start | bytes 1540
  12.5 10.3 %collective-permute-start.2 = (f32[128,2048]{1,0:T(8,128)S(1)}, f32[128,2048]{1,0:T(8,128)S(1)}, u32[]{:S(2)}, u32[]{:S(2)}) collective-permute-start(f32[128,2048]{1,0:T(8,128)S(1)} %products.9), channel_id=1, source_target_pairs={{0,1},{1,0},{2,3},{3,2},{4,5},{5,4},{6,7},{7,6},{8,9},{9,8},{10,11... | collective-permute-start | bytes 3145736 | tf_op jit(solution)/shard_map/ppermute | solution.py:454
  12.7 10.0 %collective-permute-start.5 = (bf16[1032,128]{1,0:T(8,128)(2,1)S(1)}, bf16[1032,128]{1,0:T(8,128)(2,1)S(1)}, u32[]{:S(2)}, u32[]{:S(2)}) collective-permute-start(bf16[1032,128]{1,0:T(8,128)(2,1)S(1)} %encode.3.refs_0_), channel_id=1, source_target_pairs={{0,2},{1,3},{2,0},{3,1},{4,6},{5,7},{6,4},{7,5},{8,10},{9,11},{10,... | collective-permute-start | bytes 792584 | tf_op jit(solution)/shard_map/ppermute | solution.py:458
  15.8 9.8 %collective-permute-start.4 = (bf16[520,128]{1,0:T(8,128)(2,1)S(1)}, bf16[520,128]{1,0:T(8,128)(2,1)S(1)}, u32[]{:S(2)}, u32[]{:S(2)}) collective-permute-start(bf16[520,128]{1,0:T(8,128)(2,1)S(1)} %encode.5), channel_id=1, source_target_pairs={{0,2},{1,3},{2,0},{3,1},{4,6},{5,7},{6,4},{7,5},{8,10},{9,11},{10,... | collective-permute-start | bytes 399368 | tf_op jit(solution)/shard_map/ppermute | solution.py:458
  15.8 12.1 %collective-permute-start.3 = (bf16[520,128]{1,0:T(8,128)(2,1)S(1)}, bf16[520,128]{1,0:T(8,128)(2,1)S(1)}, u32[]{:S(2)}, u32[]{:S(2)}) collective-permute-start(bf16[520,128]{1,0:T(8,128)(2,1)S(1)} %encode.4.refs_0_), channel_id=1, source_target_pairs={{0,2},{1,3},{2,0},{3,1},{4,6},{5,7},{6,4},{7,5},{8,10},{9,11},{10,... | collective-permute-start | bytes 399368 | tf_op jit(solution)/shard_map/ppermute | solution.py:458
  28.4 5.8 %collective-permute-start.8 = (f32[32,128]{1,0:T(8,128)S(1)}, f32[32,128]{1,0:T(8,128)S(1)}, u32[]{:S(2)}, u32[]{:S(2)}) collective-permute-start(f32[32,128]{1,0:T(8,128)S(1)} %get-tuple-element.27), channel_id=1, source_target_pairs={{0,12},{4,8},{8,4},{12,0},{1,13},{5,9},{9,5},{13,1},{2,14},{6,10},... | collective-permute-start | bytes 49160 | tf_op jit(solution)/shard_map/ppermute | solution.py:464
  32.3 4.6 %collective-permute-start.7 = (f32[32,128]{1,0:T(8,128)S(1)}, f32[32,128]{1,0:T(8,128)S(1)}, u32[]{:S(2)}, u32[]{:S(2)}) collective-permute-start(f32[32,128]{1,0:T(8,128)S(1)} %get-tuple-element.27), channel_id=1, source_target_pairs={{0,8},{4,12},{8,0},{12,4},{1,9},{5,13},{9,1},{13,5},{2,10},{6,14},... | collective-permute-start | bytes 49160 | tf_op jit(solution)/shard_map/ppermute | solution.py:464
  32.3 4.6 %collective-permute-start.6 = (f32[32,128]{1,0:T(8,128)S(1)}, f32[32,128]{1,0:T(8,128)S(1)}, u32[]{:S(2)}, u32[]{:S(2)}) collective-permute-start(f32[32,128]{1,0:T(8,128)S(1)} %get-tuple-element.27), channel_id=1, source_target_pairs={{0,4},{4,0},{8,12},{12,8},{1,5},{5,1},{9,13},{13,9},{2,6},{6,2},{1... | collective-permute-start | bytes 49160 | tf_op jit(solution)/shard_map/ppermute | solution.py:464
  37.8 5.6 %collective-permute-start.11 = (f32[32,128]{1,0:T(8,128)S(1)}, f32[32,128]{1,0:T(8,128)S(1)}, u32[]{:S(2)}, u32[]{:S(2)}) collective-permute-start(f32[32,128]{1,0:T(8,128)S(1)} %get-tuple-element.36), channel_id=1, source_target_pairs={{0,12},{4,8},{8,4},{12,0},{1,13},{5,9},{9,5},{13,1},{2,14},{6,10},... | collective-permute-start | bytes 49160 | tf_op jit(solution)/shard_map/ppermute | solution.py:464
  39.3 4.7 %collective-permute-start.10 = (f32[32,128]{1,0:T(8,128)S(1)}, f32[32,128]{1,0:T(8,128)S(1)}, u32[]{:S(2)}, u32[]{:S(2)}) collective-permute-start(f32[32,128]{1,0:T(8,128)S(1)} %get-tuple-element.36), channel_id=1, source_target_pairs={{0,8},{4,12},{8,0},{12,4},{1,9},{5,13},{9,1},{13,5},{2,10},{6,14},... | collective-permute-start | bytes 49160 | tf_op jit(solution)/shard_map/ppermute | solution.py:464
  39.9 4.2 %collective-permute-start.9 = (f32[32,128]{1,0:T(8,128)S(1)}, f32[32,128]{1,0:T(8,128)S(1)}, u32[]{:S(2)}, u32[]{:S(2)}) collective-permute-start(f32[32,128]{1,0:T(8,128)S(1)} %get-tuple-element.36), channel_id=1, source_target_pairs={{0,4},{4,0},{8,12},{12,8},{1,5},{5,1},{9,13},{13,9},{2,6},{6,2},{1... | collective-permute-start | bytes 49160 | tf_op jit(solution)/shard_map/ppermute | solution.py:464

commit v12 on v11

--- a/solution.py
+++ b/solution.py
@@ -184,7 +184,7 @@
     codes = refs[2 : 2 + remotes]
     bias_ref, weight_ref, offset_ref = refs[2 + remotes : 5 + remotes]
     totals_before = refs[5 + remotes : 5 + remotes + earlier]
-    kept_ref, prefix_ref, totals_ref, sum_ref, late_ref = refs[5 + remotes + earlier :]
+    kept_ref, run_ref, prefix_ref, totals_ref, sum_ref, late_ref = refs[5 + remotes + earlier :]
     steps = mine_ref.shape[0]
     runs = steps // SUB
     done = 0
@@ -240,6 +240,8 @@
             kept_ref[group, 0, rows, :] = pre_forget
             kept_ref[group, 1, rows, :] = pre[3]
             kept_ref[group, 2, rows, :] = cell
+            for index, part in enumerate(run):
+                run_ref[group, index, rows, :] = part
         before, total = sub_blocks(run, compose_lower, LOWER_UNIT)
         for index, term in enumerate(before):
             prefix_ref[group, index] = term
@@ -258,11 +260,12 @@
         functools.partial(first_kernel, start, places, len(earlier)),
         out_shape=(
             pltpu.VMEM((groups, 3, steps, LANES), F32),
+            pltpu.VMEM((groups, 5, steps, LANES), F32),
             pltpu.VMEM((groups, 5, SUB, LANES), F32),
             pltpu.VMEM((rows, LANES), F32),
         ),
         in_specs=vmem(count),
-        out_specs=vmem(3),
+        out_specs=vmem(4),
         scratch_shapes=[
             pltpu.VMEM((GATES, steps, LANES), F32),
             pltpu.VMEM((steps, LANES), F32),
@@ -299,138 +302,155 @@
     return cell, hidden
 
 
-def second_kernel(count, own_xor, chunks, *refs):
-    refs = list(refs)
-    received = refs[: count - 1]
-    kept = refs[count - 1 : count - 1 + chunks]
-    prefixes = refs[count - 1 + chunks : count - 1 + 2 * chunks]
-    weight_ref = refs[count - 1 + 2 * chunks]
-    hidden_ref, prefix_ref, totals_ref = refs[count + 2 * chunks :]
-    group = 0
-    for kept_ref, before_ref in zip(kept, prefixes):
-        groups, _, steps, _ = kept_ref.shape
-        for local in range(groups):
-            cell, hidden = arriving(count, own_xor, received, group, True)
-            a, c, d, u, v = (before_ref[local, j] for j in range(5))
-            cell, hidden = a * cell + u, c * cell + d * hidden + v
-            channels = pl.ds(group * LANES, LANES)
-            forget_weight = jnp.broadcast_to(weight_ref[0:1, channels], (SUB, LANES))
-            out_weight = jnp.broadcast_to(weight_ref[1:2, channels], (SUB, LANES))
-            run = None
-            for i in range(steps // SUB):
-                rows = pl.ds(i * SUB, SUB)
-                pre_forget = kept_ref[local, 0, rows, :]
-                pre_output = kept_ref[local, 1, rows, :]
-                fresh = kept_ref[local, 2, rows, :]
-                forget = sigmoid(pre_forget + forget_weight * hidden)
-                output = sigmoid(pre_output + out_weight * hidden)
-                kept_cell = forget * cell
-                new_cell = kept_cell + fresh
-                squashed = jnp.tanh(new_cell)
-                slope = output * (1.0 - squashed * squashed)
-                cell_hidden = kept_cell * (1.0 - forget) * forget_weight
-                hidden_cell = slope * forget
-                hidden_hidden = (
-                    output * (1.0 - output) * out_weight * squashed + slope * cell_hidden
-                )
-                offset_cell = new_cell - kept_cell - cell_hidden * hidden
-                offset_hidden = output * squashed - hidden_cell * cell - hidden_hidden * hidden
-                term = (
-                    forget,
-                    cell_hidden,
-                    hidden_cell,
-                    hidden_hidden,
-                    offset_cell,
-                    offset_hidden,
-                )
-                run = term if run is None else compose(run, term)
-                hidden_ref[group, 0, rows, :] = run[2]
-                hidden_ref[group, 1, rows, :] = run[3]
-                hidden_ref[group, 2, rows, :] = run[5]
-                forget = sigmoid(pre_forget)
-                output = sigmoid(pre_output)
-                squashed = jnp.tanh(fresh)
-                hidden_cell = output * (1.0 - squashed * squashed) * forget
-                hidden_hidden = output * (1.0 - output) * out_weight * squashed
-                cell, hidden = (
-                    forget * cell + fresh,
-                    hidden_cell * cell + hidden_hidden * hidden + output * squashed,
-                )
-            before, total = sub_blocks(run, compose, UNIT)
-            for index, term in enumerate(before):
-                prefix_ref[group, index] = term
-            for index, term in enumerate(total):
-                totals_ref[pl.ds(group * SUB + index, 1), :] = term[SUB - 1 : SUB, :]
-            for index in range(len(total), SUB):
-                totals_ref[pl.ds(group * SUB + index, 1), :] = jnp.zeros((1, LANES), F32)
-            group += 1
-
-
-def second(own_xor, received, kept, prefixes, weight):
+def lead_kernel(groups, *refs):
+    runs, befores, lead_ref = refs[:groups], refs[groups : 2 * groups], refs[-1]
+    steps = lead_ref.shape[2]
+    for group in range(groups):
+        before = tuple(befores[group][0, j] for j in range(5))
+        for i in range(steps // SUB):
+            terms = before
+            if i:
+                rows = pl.ds((i - 1) * SUB, SUB)
+                terms = compose_lower(before, tuple(runs[group][0, j, rows, :] for j in range(5)))
+            for index, term in enumerate(terms):
+                lead_ref[group, index, pl.ds(i * SUB, SUB), :] = term
+
+
+def leads(runs, befores):
+    groups, steps = len(runs), runs[0].shape[2]
+    return pl.pallas_call(
+        functools.partial(lead_kernel, groups),
+        out_shape=pltpu.VMEM((groups, 5, steps, LANES), F32),
+        in_specs=vmem(2 * groups),
+        out_specs=pl.BlockSpec(memory_space=pltpu.VMEM),
+        compiler_params=PARAMS,
+        cost_estimate=cost(12 * groups * steps * LANES, 40 * groups * steps * LANES),
+        name="leads",
+    )(*runs, *befores)
+
+
+def second_kernel(count, own_xor, groups, *refs):
+    received, kept = refs[: count - 1], refs[count - 1 : count - 1 + groups]
+    lead_ref, weight_ref, hidden_ref, prefix_ref, totals_ref = refs[count - 1 + groups :]
+    steps = lead_ref.shape[2]
+    for group, kept_ref in enumerate(kept):
+        first_cell, first_hidden = arriving(count, own_xor, received, group, True)
+        first_cell = jnp.broadcast_to(first_cell, (SUB, LANES))
+        first_hidden = jnp.broadcast_to(first_hidden, (SUB, LANES))
+        channels = pl.ds(group * LANES, LANES)
+        forget_weight = jnp.broadcast_to(weight_ref[0:1, channels], (SUB, LANES))
+        out_weight = jnp.broadcast_to(weight_ref[1:2, channels], (SUB, LANES))
+        run = None
+        for i in range(steps // SUB):
+            rows = pl.ds(i * SUB, SUB)
+            a, c, d, u, v = (lead_ref[group, j, rows, :] for j in range(5))
+            cell = a * first_cell + u
+            hidden = c * first_cell + d * first_hidden + v
+            forget = sigmoid(kept_ref[0, 0, rows, :] + forget_weight * hidden)
+            output = sigmoid(kept_ref[0, 1, rows, :] + out_weight * hidden)
+            kept_cell = forget * cell
+            new_cell = kept_cell + kept_ref[0, 2, rows, :]
+            squashed = jnp.tanh(new_cell)
+            slope = output * (1.0 - squashed * squashed)
+            cell_hidden = kept_cell * (1.0 - forget) * forget_weight
+            hidden_cell = slope * forget
+            hidden_hidden = output * (1.0 - output) * out_weight * squashed + slope * cell_hidden
+            offset_cell = new_cell - kept_cell - cell_hidden * hidden
+            offset_hidden = output * squashed - hidden_cell * cell - hidden_hidden * hidden
+            term = (forget, cell_hidden, hidden_cell, hidden_hidden, offset_cell, offset_hidden)
+            run = term if run is None else compose(run, term)
+            hidden_ref[group, 0, rows, :] = run[2]
+            hidden_ref[group, 1, rows, :] = run[3]
+            hidden_ref[group, 2, rows, :] = run[5]
+        before, total = sub_blocks(run, compose, UNIT)
+        for index, term in enumerate(before):
+            prefix_ref[group, index] = term
+        for index, term in enumerate(total):
+            totals_ref[pl.ds(group * SUB + index, 1), :] = term[SUB - 1 : SUB, :]
+        for index in range(len(total), SUB):
+            totals_ref[pl.ds(group * SUB + index, 1), :] = jnp.zeros((1, LANES), F32)
+
+
+def second(own_xor, received, kept, lead, weight):
     count = len(received) + 1
-    steps = kept[0].shape[2]
-    groups = sum(k.shape[0] for k in kept)
-    return pl.pallas_call(
-        functools.partial(second_kernel, count, own_xor, len(kept)),
+    groups, steps = len(kept), lead.shape[2]
+    return pl.pallas_call(
+        functools.partial(second_kernel, count, own_xor, groups),
         out_shape=(
             pltpu.VMEM((groups, 3, steps, LANES), F32),
             pltpu.VMEM((groups, 6, SUB, LANES), F32),
             pltpu.VMEM((groups * SUB, LANES), F32),
         ),
-        in_specs=vmem(count - 1 + 2 * len(kept) + 1),
+        in_specs=vmem(count - 1 + groups + 2),
         out_specs=vmem(3),
         compiler_params=PARAMS,
-        cost_estimate=cost(100 * groups * steps * LANES, 24 * groups * steps * LANES),
+        cost_estimate=cost(80 * groups * steps * LANES, 24 * groups * steps * LANES),
         name="second",
-    )(*received, *kept, *prefixes, weight)
+    )(*received, *kept, lead, weight)
+
+
+def ordered_kernel(hidden_ref, prefix_ref, out_ref):
+    groups, _, steps, _ = hidden_ref.shape
+    runs = steps // SUB
+    for group in range(groups):
+        a, b, c, d, u, v = (prefix_ref[group, j] for j in range(6))
+        for i in range(runs):
+            rows, times = pl.ds(i * SUB, SUB), pl.ds(i, SUB, stride=runs)
+            by_cell, by_hidden, offset = (hidden_ref[group, j, rows, :] for j in range(3))
+            out_ref[3 * group, times, :] = by_cell * a + by_hidden * c
+            out_ref[3 * group + 1, times, :] = by_cell * b + by_hidden * d
+            out_ref[3 * group + 2, times, :] = by_cell * u + by_hidden * v + offset
+
+
+def ordered(hiddens, prefix):
+    groups, _, steps, _ = hiddens.shape
+    return pl.pallas_call(
+        ordered_kernel,
+        out_shape=pltpu.VMEM((3 * groups, steps, LANES), F32),
+        in_specs=vmem(2),
+        out_specs=pl.BlockSpec(memory_space=pltpu.VMEM),
+        compiler_params=PARAMS,
+        cost_estimate=cost(10 * groups * steps * LANES, 24 * groups * steps * LANES),
+        name="ordered",
+    )(hiddens, prefix)
 
 
 def last_kernel(count, own_xor, *refs):
     received = refs[: count - 1]
-    hidden_ref, prefix_ref, out_ref, turn_ref, made_ref, sems = refs[count - 1 :]
-    groups, _, steps, _ = hidden_ref.shape
-    runs = steps // SUB
+    maps_ref, out_ref, made_ref, sems = refs[count - 1 :]
+    groups = maps_ref.shape[0] // 3
     copies = []
     for group in range(groups):
         cell, hidden = arriving(count, own_xor, received, group, False)
-        a, b, c, d, u, v = (prefix_ref[group, j] for j in range(6))
-        cell, hidden = a * cell + b * hidden + u, c * cell + d * hidden + v
-        for i in range(runs):
-            rows = pl.ds(i * SUB, SUB)
-            turn_ref[pl.ds(i, SUB, stride=runs), :] = (
-                hidden_ref[group, 0, rows, :] * cell
-                + hidden_ref[group, 1, rows, :] * hidden
-                + hidden_ref[group, 2, rows, :]
-            )
+        made = maps_ref[3 * group] * cell + maps_ref[3 * group + 1] * hidden
         rows = pl.ds(group * LANES, LANES)
-        made_ref[rows, :] = turn_ref[...].T
+        made_ref[rows, :] = (made + maps_ref[3 * group + 2]).T
         copies.append(pltpu.make_async_copy(made_ref.at[rows], out_ref.at[rows], sems.at[group]))
         copies[-1].start()
     for copy in copies:
         copy.wait()
 
 
-def last(own_xor, received, hiddens, prefix):
+def last(own_xor, received, maps):
     count = len(received) + 1
-    groups, _, steps, _ = hiddens.shape
+    groups, steps = maps.shape[0] // 3, maps.shape[1]
     return pl.pallas_call(
         functools.partial(last_kernel, count, own_xor),
         out_shape=jax.ShapeDtypeStruct((groups * LANES, steps), F32),
-        in_specs=vmem(count + 1),
-        compiler_params=PARAMS,
+        in_specs=vmem(count),
         out_specs=pl.BlockSpec(memory_space=pltpu.HBM),
         scratch_shapes=[
-            pltpu.VMEM((steps, LANES), F32),
             pltpu.VMEM((groups * LANES, steps), F32),
             pltpu.SemaphoreType.DMA((groups,)),
         ],
+        compiler_params=PARAMS,
         cost_estimate=cost(10 * groups * steps * LANES, 16 * groups * steps * LANES),
         name="last",
-    )(*received, hiddens, prefix)
+    )(*received, maps)
 
 
 def pieces_of(groups, chips):
-    half = max(1, groups // 2)
+    half = max(1, groups - 1)
     pieces = [(1, 0, half), (1, half, groups - half)]
     pieces += [(away, 0, groups) for away in range(2, chips)]
     return [piece for piece in pieces if piece[2]]
@@ -491,22 +511,26 @@
         else:
             give, keep = product(parts, codes[-1:])
             theirs = to_core(give)
-            for group in range(start, start + count):
-                codes.append(send(away, group, 1, keep, theirs, (group - start) * GROUP))
+            codes.append(send(away, start, count, keep, theirs, 0))
     (give,) = product((local_give,), codes[-1:])
     given = to_core(give)
     (keep,) = product((local_keep,), codes[-1:])
-    kept, prefixes, totals = [], [], []
+    kept, runs, prefixes, totals = [], [], [], []
     for group in range(groups):
         arrived, places = zip(*coded[group]) if coded[group] else ((), ())
-        k, p, total = first(
+        k, r, p, total = first(
             group, places, keep, given, list(arrived), bias, weight, offset, totals
         )
         totals = [total]
         kept.append(k)
+        runs.append(r)
         prefixes.append(p)
-    hiddens, prefix, total = second(own_xor, to_blocks(totals[0]), kept, prefixes, weight)
-    return last(own_xor, to_blocks(total), hiddens, prefix)
+    received = to_blocks(totals[0])
+    lead = leads(runs, prefixes)
+    hiddens, prefix, total = second(own_xor, received, kept, lead, weight)
+    received = to_blocks(total)
+    maps = ordered(hiddens, prefix)
+    return last(own_xor, received, maps)
 
 
 def solution(mesh):

time: 45.2 us -> 44.8 us (level)
  starting transfers between devices: 14.8 us -> 12.7 us
  waiting for transfers between devices: 13.6 us -> 15.1 us
    ppermute x3 -> x2, waiting for transfers between devices: 5.86 us -> 8.09 us  [to_chip(): return on_chip(lax.ppermute(value, 'chan', pairs))]
    ppermute x3 -> x2, starting transfers between devices: 4.94 us -> 2.85 us  [to_chip(): return on_chip(lax.ppermute(value, 'chan', pairs))]
    pallas_call x1 -> x3, Pallas kernels: 0.8 us -> 1 us  [the longest x1 0.65 us: second(): pl.pallas_call(functools.partial(second_kernel, count, own_xor, groups),...]
  transfers between devices with their start and end apart: 12 -> 11, of which waited for: 9 -> 8; matrix products, arithmetic and copies ran while one was open for 0% -> 0% of each run, Pallas kernels for 14% -> 15%
where the time goes in v12:
time: 44.8 us; the launch traced here: 44.6 us
  Pallas kernels  16.6 us (37%)
  waiting for transfers between devices  15.1 us (34%)
  starting transfers between devices  12.7 us (28%)
    pallas_call x5, Pallas kernels, products(): pl.pallas_call(functools.partial(product_kernel, chips, parts, per_owner)...  11.9 us
    ppermute x6, starting transfers between devices, to_blocks(): lax.ppermute(value, 'tm', [pair for pair in pairs if pair[1] < blocks])  9.02 us
    ppermute x2, waiting for transfers between devices, to_chip(): return on_chip(lax.ppermute(value, 'chan', pairs))  8.09 us
    ppermute x6, waiting for transfers between devices, to_blocks(): lax.ppermute(value, 'tm', [pair for pair in pairs if pair[1] < blocks])  5.51 us
    ppermute x2, starting transfers between devices, to_chip(): return on_chip(lax.ppermute(value, 'chan', pairs))  2.85 us
    pallas_call x4, Pallas kernels, first(): pl.pallas_call(functools.partial(first_kernel, start, places, len(earlier...  2.01 us
    ppermute x3, waiting for transfers between devices, to_core(): lax.ppermute(value, 'chan', [(i, i ^ 1) for i in range(owners)])  1.52 us
  transfers between devices with their start and end apart: 11, of which 8 were waited for; matrix products, arithmetic and copies ran while one was open for 0% of the time, Pallas kernels for 15%

profile of v12, /device:TPU:0, one launch (start us, length us, event | category | flops | bytes accessed | tf_op | source)
XLA Modules:
  0.0 44.6 jit_solution(10926002584023361240)
XLA Ops:
  0.0 2.3 %products.6 = f32[128,1536]{1,0:T(8,128)S(1)} custom-call(bf16[128,1024]{1,0:T(8,128)(2,1)} %tokens_ref.9, bf16[1024,8192]{1,0:T(8,128)(2,1)} %weight_ref.9), custom_call_target="tpu_custom_call" | custom-call | flops 402653184 | bytes 3145728 | tf_op jit(solution)/shard_map/products/pallas_call | solution.py:73
  2.3 0.6 %collective-permute-start = (f32[128,1536]{1,0:T(8,128)S(1)}, f32[128,1536]{1,0:T(8,128)S(1)}, u32[]{:S(2)}, u32[]{:S(2)}) collective-permute-start(f32[128,1536]{1,0:T(8,128)S(1)} %products.6), channel_id=1, source_target_pairs={{0,1},{1,0},{2,3},{3,2},{4,5},{5,4},{6,7},{7,6},{8,9},{9,8},{10,11... | collective-permute-start | bytes 2359304 | tf_op jit(solution)/shard_map/ppermute | solution.py:474
  2.9 2.3 %products.5.mine_ref = f32[128,1536]{1,0:T(8,128)S(1)} custom-call(bf16[128,1024]{1,0:T(8,128)(2,1)} %tokens_ref.9, bf16[1024,8192]{1,0:T(8,128)(2,1)} %weight_ref.9), custom_call_target="tpu_custom_call" | custom-call | flops 402653184 | bytes 3145728 | tf_op jit(solution)/shard_map/products/pallas_call | solution.py:73
  5.2 0.6 %encode.2.refs_0_ = bf16[1544,128]{1,0:T(8,128)(2,1)S(1)} custom-call(f32[128,1536]{1,0:T(8,128)S(1)} %products.5.mine_ref, f32[128,1536]{1,0:T(8,128)S(1)} %collective-permute-done.theirs_ref), custom_call_target="tpu_custom_call" | custom-call | flops 3932160 | bytes 1966080 | tf_op jit(solution)/shard_map/encode/pallas_call | solution.py:113
  5.8 2.0 %products.7 = (f32[128,512]{1,0:T(8,128)S(1)}, f32[128,512]{1,0:T(8,128)S(1)}) custom-call(bf16[128,1024]{1,0:T(8,128)(2,1)} %tokens_ref.9, bf16[1024,8192]{1,0:T(8,128)(2,1)} %weight_ref.9, bf16[1544,128]{1,0:T(8,128)(2,1)S(1)} %encode.2.refs_0_), custom_call_target="tpu_custom_call" | custom-call | flops 268435456 | bytes 2097152 | tf_op jit(solution)/shard_map/products/pallas_call | solution.py:73
  7.8 0.1 collective-permute-start.1
  7.9 1.5 %collective-permute-done.1.theirs_ref = f32[128,512]{1,0:T(8,128)S(1)} collective-permute-done((f32[128,512]{1,0:T(8,128)S(1)}, f32[128,512]{1,0:T(8,128)S(1)}, u32[]{:S(2)}, u32[]{:S(2)}) %collective-permute-start.1) | collective-permute-done | bytes 262176 | tf_op jit(solution)/shard_map/ppermute | solution.py:474
  9.4 0.2 encode.3.refs_0_
  9.7 2.7 %products.9 = f32[128,2048]{1,0:T(8,128)S(1)} custom-call(bf16[128,1024]{1,0:T(8,128)(2,1)} %tokens_ref.9, bf16[1024,8192]{1,0:T(8,128)(2,1)} %weight_ref.9, bf16[520,128]{1,0:T(8,128)(2,1)S(1)} %encode.3.refs_0_), custom_call_target="tpu_custom_call" | custom-call | flops 536870912 | bytes 4194304 | tf_op jit(solution)/shard_map/products/pallas_call | solution.py:73
  12.3 0.2 collective-permute-start.2
  12.5 2.8 %collective-permute-start.4 = (bf16[1544,128]{1,0:T(8,128)(2,1)S(1)}, bf16[1544,128]{1,0:T(8,128)(2,1)S(1)}, u32[]{:S(2)}, u32[]{:S(2)}) collective-permute-start(bf16[1544,128]{1,0:T(8,128)(2,1)S(1)} %encode.2.refs_0_), channel_id=1, source_target_pairs={{0,2},{1,3},{2,0},{3,1},{4,6},{5,7},{6,4},{7,5},{8,10},{9,11},{10,... | collective-permute-start | bytes 1185800 | tf_op jit(solution)/shard_map/ppermute | solution.py:478
  15.4 2.6 %products.8.refs_0_ = f32[128,2048]{1,0:T(8,128)S(1)} custom-call(bf16[128,1024]{1,0:T(8,128)(2,1)} %tokens_ref.9, bf16[1024,8192]{1,0:T(8,128)(2,1)} %weight_ref.9, bf16[520,128]{1,0:T(8,128)(2,1)S(1)} %encode.3.refs_0_), custom_call_target="tpu_custom_call" | custom-call | flops 536870912 | bytes 4194304 | tf_op jit(solution)/shard_map/products/pallas_call | solution.py:73
  18.0 7.3 %collective-permute-done.4.refs_2_ = bf16[1544,128]{1,0:T(8,128)(2,1)S(1)} collective-permute-done((bf16[1544,128]{1,0:T(8,128)(2,1)S(1)}, bf16[1544,128]{1,0:T(8,128)(2,1)S(1)}, u32[]{:S(2)}, u32[]{:S(2)}) %collective-permute-start.4) | collective-permute-done | bytes 395296 | tf_op jit(solution)/shard_map/ppermute | solution.py:478
  25.4 0.5 %first.4 = (f32[1,3,128,128]{3,2,1,0:T(8,128)S(1)}, f32[1,5,128,128]{3,2,1,0:T(8,128)S(1)}, f32[1,5,8,128]{3,2,1,0:T(8,128)S(1)}, f32[8,128]{1,0:T(8,128)S(1)}) custom-call(f32[128,2048]{1,0:T(8,128)S(1)} %products.8.refs_0_, f32[128,2048]{1,0:T(8,128)S(1)} %collective-permute-done.2.refs_1_, bf16[1544,128]{1,0:T(8,128)(2,1)S(1)} %collective-permute-done.4.refs_2_, ...), custom_call_target="tpu_custom_call" | custom-call | flops 3932160 | bytes 1310720 | tf_op jit(solution)/shard_map/first/pallas_call | solution.py:259
  25.9 0.5 %first.5 = (f32[1,3,128,128]{3,2,1,0:T(8,128)S(1)}, f32[1,5,128,128]{3,2,1,0:T(8,128)S(1)}, f32[1,5,8,128]{3,2,1,0:T(8,128)S(1)}, f32[16,128]{1,0:T(8,128)S(1)}) custom-call(f32[128,2048]{1,0:T(8,128)S(1)} %products.8.refs_0_, f32[128,2048]{1,0:T(8,128)S(1)} %collective-permute-done.2.refs_1_, bf16[1544,128]{1,0:T(8,128)(2,1)S(1)} %collective-permute-done.4.refs_2_, ...), custom_call_target="tpu_custom_call" | custom-call | flops 3932160 | bytes 1310720 | tf_op jit(solution)/shard_map/first/pallas_call | solution.py:259
  26.4 0.5 %first.6 = (f32[1,3,128,128]{3,2,1,0:T(8,128)S(1)}, f32[1,5,128,128]{3,2,1,0:T(8,128)S(1)}, f32[1,5,8,128]{3,2,1,0:T(8,128)S(1)}, f32[24,128]{1,0:T(8,128)S(1)}) custom-call(f32[128,2048]{1,0:T(8,128)S(1)} %products.8.refs_0_, f32[128,2048]{1,0:T(8,128)S(1)} %collective-permute-done.2.refs_1_, bf16[1544,128]{1,0:T(8,128)(2,1)S(1)} %collective-permute-done.4.refs_2_, ...), custom_call_target="tpu_custom_call" | custom-call | flops 3932160 | bytes 1310720 | tf_op jit(solution)/shard_map/first/pallas_call | solution.py:259
  26.9 0.8 %collective-permute-done.3.refs_2_ = bf16[520,128]{1,0:T(8,128)(2,1)S(1)} collective-permute-done((bf16[520,128]{1,0:T(8,128)(2,1)S(1)}, bf16[520,128]{1,0:T(8,128)(2,1)S(1)}, u32[]{:S(2)}, u32[]{:S(2)}) %collective-permute-start.3) | collective-permute-done | bytes 133152 | tf_op jit(solution)/shard_map/ppermute | solution.py:478
  27.7 0.5 %first.7 = (f32[1,3,128,128]{3,2,1,0:T(8,128)S(1)}, f32[1,5,128,128]{3,2,1,0:T(8,128)S(1)}, f32[1,5,8,128]{3,2,1,0:T(8,128)S(1)}, f32[32,128]{1,0:T(8,128)S(1)}) custom-call(f32[128,2048]{1,0:T(8,128)S(1)} %products.8.refs_0_, f32[128,2048]{1,0:T(8,128)S(1)} %collective-permute-done.2.refs_1_, bf16[520,128]{1,0:T(8,128)(2,1)S(1)} %collective-permute-done.3.refs_2_, ...), custom_call_target="tpu_custom_call" | custom-call | flops 3932160 | bytes 1310720 | tf_op jit(solution)/shard_map/first/pallas_call | solution.py:259
  28.2 3.9 %collective-permute-start.7 = (f32[32,128]{1,0:T(8,128)S(1)}, f32[32,128]{1,0:T(8,128)S(1)}, u32[]{:S(2)}, u32[]{:S(2)}) collective-permute-start(f32[32,128]{1,0:T(8,128)S(1)} %get-tuple-element.31), channel_id=1, source_target_pairs={{0,12},{4,8},{8,4},{12,0},{1,13},{5,9},{9,5},{13,1},{2,14},{6,10},... | collective-permute-start | bytes 49160 | tf_op jit(solution)/shard_map/ppermute | solution.py:484
  32.1 0.6 %collective-permute-start.5 = (f32[32,128]{1,0:T(8,128)S(1)}, f32[32,128]{1,0:T(8,128)S(1)}, u32[]{:S(2)}, u32[]{:S(2)}) collective-permute-start(f32[32,128]{1,0:T(8,128)S(1)} %get-tuple-element.31), channel_id=1, source_target_pairs={{0,4},{4,0},{8,12},{12,8},{1,5},{5,1},{9,13},{13,9},{2,6},{6,2},{1... | collective-permute-start | bytes 49160 | tf_op jit(solution)/shard_map/ppermute | solution.py:484
  32.8 0.1 leads.1.refs_7_
  32.9 1.2 %collective-permute-done.7.refs_2_ = f32[32,128]{1,0:T(8,128)S(1)} collective-permute-done((f32[32,128]{1,0:T(8,128)S(1)}, f32[32,128]{1,0:T(8,128)S(1)}, u32[]{:S(2)}, u32[]{:S(2)}) %collective-permute-start.7) | collective-permute-done | bytes 16416 | tf_op jit(solution)/shard_map/ppermute | solution.py:484
  34.0 2.7 %collective-permute-done.6.refs_1_ = f32[32,128]{1,0:T(8,128)S(1)} collective-permute-done((f32[32,128]{1,0:T(8,128)S(1)}, f32[32,128]{1,0:T(8,128)S(1)}, u32[]{:S(2)}, u32[]{:S(2)}) %collective-permute-start.6) | collective-permute-done | bytes 16416 | tf_op jit(solution)/shard_map/ppermute | solution.py:484
  36.8 0.6 %second.1 = (f32[4,3,128,128]{3,2,1,0:T(8,128)S(1)}, f32[4,6,8,128]{3,2,1,0:T(8,128)S(1)}, f32[32,128]{1,0:T(8,128)S(1)}) custom-call(f32[32,128]{1,0:T(8,128)S(1)} %collective-permute-done.5.refs_0_, f32[32,128]{1,0:T(8,128)S(1)} %collective-permute-done.6.refs_1_, f32[32,128]{1,0:T(8,128)S(1)} %collective-permute-done.7.refs_2_, ...), custom_call_target="tpu_custom_call" | custom-call | flops 5242880 | bytes 1572864 | tf_op jit(solution)/shard_map/second/pallas_call | solution.py:377
  37.4 1.5 %collective-permute-start.10 = (f32[32,128]{1,0:T(8,128)S(1)}, f32[32,128]{1,0:T(8,128)S(1)}, u32[]{:S(2)}, u32[]{:S(2)}) collective-permute-start(f32[32,128]{1,0:T(8,128)S(1)} %get-tuple-element.44), channel_id=1, source_target_pairs={{0,12},{4,8},{8,4},{12,0},{1,13},{5,9},{9,5},{13,1},{2,14},{6,10},... | collective-permute-start | bytes 49160 | tf_op jit(solution)/shard_map/ppermute | solution.py:484
  38.9 0.6 %collective-permute-start.9 = (f32[32,128]{1,0:T(8,128)S(1)}, f32[32,128]{1,0:T(8,128)S(1)}, u32[]{:S(2)}, u32[]{:S(2)}) collective-permute-start(f32[32,128]{1,0:T(8,128)S(1)} %get-tuple-element.44), channel_id=1, source_target_pairs={{0,8},{4,12},{8,0},{12,4},{1,9},{5,13},{9,1},{13,5},{2,10},{6,14},... | collective-permute-start | bytes 49160 | tf_op jit(solution)/shard_map/ppermute | solution.py:484
  39.6 2.3 %collective-permute-start.8 = (f32[32,128]{1,0:T(8,128)S(1)}, f32[32,128]{1,0:T(8,128)S(1)}, u32[]{:S(2)}, u32[]{:S(2)}) collective-permute-start(f32[32,128]{1,0:T(8,128)S(1)} %get-tuple-element.44), channel_id=1, source_target_pairs={{0,4},{4,0},{8,12},{12,8},{1,5},{5,1},{9,13},{13,9},{2,6},{6,2},{1... | collective-permute-start | bytes 49160 | tf_op jit(solution)/shard_map/ppermute | solution.py:484
  41.9 0.2 ordered.1.refs_3_
  42.1 0.9 %collective-permute-done.10.refs_2_ = f32[32,128]{1,0:T(8,128)S(1)} collective-permute-done((f32[32,128]{1,0:T(8,128)S(1)}, f32[32,128]{1,0:T(8,128)S(1)}, u32[]{:S(2)}, u32[]{:S(2)}) %collective-permute-start.10) | collective-permute-done | bytes 16416 | tf_op jit(solution)/shard_map/ppermute | solution.py:484
  43.0 0.6 %collective-permute-done.9.refs_1_ = f32[32,128]{1,0:T(8,128)S(1)} collective-permute-done((f32[32,128]{1,0:T(8,128)S(1)}, f32[32,128]{1,0:T(8,128)S(1)}, u32[]{:S(2)}, u32[]{:S(2)}) %collective-permute-start.9) | collective-permute-done | bytes 16416 | tf_op jit(solution)/shard_map/ppermute | solution.py:484
  43.6 0.2 collective-permute-done.8.refs_0_
  43.7 0.9 %last.1 = f32[512,128]{1,0:T(8,128)} custom-call(f32[32,128]{1,0:T(8,128)S(1)} %collective-permute-done.8.refs_0_, f32[32,128]{1,0:T(8,128)S(1)} %collective-permute-done.9.refs_1_, f32[32,128]{1,0:T(8,128)S(1)} %collective-permute-done.10.refs_2_, f32[12,128,128]{2,1,0:T(8,128)S(1)} %ordered.1.refs_3_), custom_call_target="tpu_custom_call" | custom-call | flops 655360 | bytes 1048576 | tf_op jit(solution)/shard_map/last/pallas_call | solution.py:437
  (11 shorter events, 0.1 us)
Async XLA Ops:
  2.3 2.9 %collective-permute-start = (f32[128,1536]{1,0:T(8,128)S(1)}, f32[128,1536]{1,0:T(8,128)S(1)}, u32[]{:S(2)}, u32[]{:S(2)}) collective-permute-start(f32[128,1536]{1,0:T(8,128)S(1)} %products.6), channel_id=1, source_target_pairs={{0,1},{1,0},{2,3},{3,2},{4,5},{5,4},{6,7},{7,6},{8,9},{9,8},{10,11... | collective-permute-start | bytes 2359304 | tf_op jit(solution)/shard_map/ppermute | solution.py:474
  7.8 1.6 %collective-permute-start.1 = (f32[128,512]{1,0:T(8,128)S(1)}, f32[128,512]{1,0:T(8,128)S(1)}, u32[]{:S(2)}, u32[]{:S(2)}) collective-permute-start(f32[128,512]{1,0:T(8,128)S(1)} %get-tuple-element.27), channel_id=1, source_target_pairs={{0,1},{1,0},{2,3},{3,2},{4,5},{5,4},{6,7},{7,6},{8,9},{9,8},{10,11... | collective-permute-start | bytes 786440 | tf_op jit(solution)/shard_map/ppermute | solution.py:474
  9.6 15.7 %copy-start = (f32[512,4]{0,1:T(4,128)S(1)}, f32[512,4]{0,1:T(4,128)}, u32[]{:S(2)}) copy-start(f32[512,4]{0,1:T(4,128)} %param.8) | copy-start | bytes 24580
  9.6 15.7 %copy-start.1 = (f32[512,2]{0,1:T(2,128)S(1)}, f32[512,2]{0,1:T(2,128)}, u32[]{:S(2)}) copy-start(f32[512,2]{0,1:T(2,128)} %param.7) | copy-start | bytes 12292
  9.7 15.7 %copy-start.2 = (f32[128]{0:T(128)S(1)}, f32[128]{0:T(128)}, u32[]{:S(2)}) copy-start(f32[128]{0:T(128)} %param.9) | copy-start | bytes 1540
  12.3 13.0 %collective-permute-start.2 = (f32[128,2048]{1,0:T(8,128)S(1)}, f32[128,2048]{1,0:T(8,128)S(1)}, u32[]{:S(2)}, u32[]{:S(2)}) collective-permute-start(f32[128,2048]{1,0:T(8,128)S(1)} %products.9), channel_id=1, source_target_pairs={{0,1},{1,0},{2,3},{3,2},{4,5},{5,4},{6,7},{7,6},{8,9},{9,8},{10,11... | collective-permute-start | bytes 3145736 | tf_op jit(solution)/shard_map/ppermute | solution.py:474
  12.5 12.8 %collective-permute-start.4 = (bf16[1544,128]{1,0:T(8,128)(2,1)S(1)}, bf16[1544,128]{1,0:T(8,128)(2,1)S(1)}, u32[]{:S(2)}, u32[]{:S(2)}) collective-permute-start(bf16[1544,128]{1,0:T(8,128)(2,1)S(1)} %encode.2.refs_0_), channel_id=1, source_target_pairs={{0,2},{1,3},{2,0},{3,1},{4,6},{5,7},{6,4},{7,5},{8,10},{9,11},{10,... | collective-permute-start | bytes 1185800 | tf_op jit(solution)/shard_map/ppermute | solution.py:478
  15.4 12.3 %collective-permute-start.3 = (bf16[520,128]{1,0:T(8,128)(2,1)S(1)}, bf16[520,128]{1,0:T(8,128)(2,1)S(1)}, u32[]{:S(2)}, u32[]{:S(2)}) collective-permute-start(bf16[520,128]{1,0:T(8,128)(2,1)S(1)} %encode.3.refs_0_), channel_id=1, source_target_pairs={{0,2},{1,3},{2,0},{3,1},{4,6},{5,7},{6,4},{7,5},{8,10},{9,11},{10,... | collective-permute-start | bytes 399368 | tf_op jit(solution)/shard_map/ppermute | solution.py:478
  28.2 5.8 %collective-permute-start.7 = (f32[32,128]{1,0:T(8,128)S(1)}, f32[32,128]{1,0:T(8,128)S(1)}, u32[]{:S(2)}, u32[]{:S(2)}) collective-permute-start(f32[32,128]{1,0:T(8,128)S(1)} %get-tuple-element.31), channel_id=1, source_target_pairs={{0,12},{4,8},{8,4},{12,0},{1,13},{5,9},{9,5},{13,1},{2,14},{6,10},... | collective-permute-start | bytes 49160 | tf_op jit(solution)/shard_map/ppermute | solution.py:484
  32.1 4.6 %collective-permute-start.6 = (f32[32,128]{1,0:T(8,128)S(1)}, f32[32,128]{1,0:T(8,128)S(1)}, u32[]{:S(2)}, u32[]{:S(2)}) collective-permute-start(f32[32,128]{1,0:T(8,128)S(1)} %get-tuple-element.31), channel_id=1, source_target_pairs={{0,8},{4,12},{8,0},{12,4},{1,9},{5,13},{9,1},{13,5},{2,10},{6,14},... | collective-permute-start | bytes 49160 | tf_op jit(solution)/shard_map/ppermute | solution.py:484
  32.1 4.6 %collective-permute-start.5 = (f32[32,128]{1,0:T(8,128)S(1)}, f32[32,128]{1,0:T(8,128)S(1)}, u32[]{:S(2)}, u32[]{:S(2)}) collective-permute-start(f32[32,128]{1,0:T(8,128)S(1)} %get-tuple-element.31), channel_id=1, source_target_pairs={{0,4},{4,0},{8,12},{12,8},{1,5},{5,1},{9,13},{13,9},{2,6},{6,2},{1... | collective-permute-start | bytes 49160 | tf_op jit(solution)/shard_map/ppermute | solution.py:484
  37.4 5.6 %collective-permute-start.10 = (f32[32,128]{1,0:T(8,128)S(1)}, f32[32,128]{1,0:T(8,128)S(1)}, u32[]{:S(2)}, u32[]{:S(2)}) collective-permute-start(f32[32,128]{1,0:T(8,128)S(1)} %get-tuple-element.44), channel_id=1, source_target_pairs={{0,12},{4,8},{8,4},{12,0},{1,13},{5,9},{9,5},{13,1},{2,14},{6,10},... | collective-permute-start | bytes 49160 | tf_op jit(solution)/shard_map/ppermute | solution.py:484
  38.9 4.7 %collective-permute-start.9 = (f32[32,128]{1,0:T(8,128)S(1)}, f32[32,128]{1,0:T(8,128)S(1)}, u32[]{:S(2)}, u32[]{:S(2)}) collective-permute-start(f32[32,128]{1,0:T(8,128)S(1)} %get-tuple-element.44), channel_id=1, source_target_pairs={{0,8},{4,12},{8,0},{12,4},{1,9},{5,13},{9,1},{13,5},{2,10},{6,14},... | collective-permute-start | bytes 49160 | tf_op jit(solution)/shard_map/ppermute | solution.py:484
  39.6 4.2 %collective-permute-start.8 = (f32[32,128]{1,0:T(8,128)S(1)}, f32[32,128]{1,0:T(8,128)S(1)}, u32[]{:S(2)}, u32[]{:S(2)}) collective-permute-start(f32[32,128]{1,0:T(8,128)S(1)} %get-tuple-element.44), channel_id=1, source_target_pairs={{0,4},{4,0},{8,12},{12,8},{1,5},{5,1},{9,13},{13,9},{2,6},{6,2},{1... | collective-permute-start | bytes 49160 | tf_op jit(solution)/shard_map/ppermute | solution.py:484

commit v13 on v12

--- a/solution.py
+++ b/solution.py
@@ -450,10 +450,9 @@
 
 
 def pieces_of(groups, chips):
-    half = max(1, groups - 1)
-    pieces = [(1, 0, half), (1, half, groups - half)]
-    pieces += [(away, 0, groups) for away in range(2, chips)]
-    return [piece for piece in pieces if piece[2]]
+    half = max(1, groups // 2)
+    pieces = [(1, 0, half)] + [(1, group, 1) for group in range(half, groups)]
+    return pieces + [(away, 0, groups) for away in range(2, chips)]
 
 
 def shards(tokens, in_weight, recur_weight, gate_bias, forget_offset):
@@ -504,12 +503,11 @@
     for index, (away, start, count) in enumerate(pieces_of(groups, chips)):
         parts = tuple((away, which, start * GROUP, count * GROUP) for which in (GIVE, KEEP))
         if index == 0:
-            (give,) = product(parts[:1], [])
+            give, keep = product(parts, [])
             theirs = to_core(give)
-            (keep,) = product(parts[1:], [])
             codes.append(send(away, start, count, keep, theirs, 0))
         else:
-            give, keep = product(parts, codes[-1:])
+            give, keep = product(parts, codes[-2:-1])
             theirs = to_core(give)
             codes.append(send(away, start, count, keep, theirs, 0))
     (give,) = product((local_give,), codes[-1:])

time: 44.8 us -> 46.6 us (1.040)
  starting transfers between devices: 12.7 us -> 15.6 us
  waiting for transfers between devices: 15.1 us -> 14.1 us
    ppermute x2 -> x3, waiting for transfers between devices: 8.09 us -> 5.85 us  [to_chip(): return on_chip(lax.ppermute(value, 'chan', pairs))]
    ppermute x2 -> x3, starting transfers between devices: 2.85 us -> 4.92 us  [to_chip(): return on_chip(lax.ppermute(value, 'chan', pairs))]
    ppermute x3 -> x4, waiting for transfers between devices: 1.52 us -> 2.7 us  [to_core(): lax.ppermute(value, 'chan', [(i, i ^ 1) for i in range(owners)])]
    ppermute x3 -> x4, starting transfers between devices: 0.85 us -> 1.64 us  [to_core(): lax.ppermute(value, 'chan', [(i, i ^ 1) for i in range(owners)])]
  transfers between devices with their start and end apart: 11 -> 13, of which waited for: 8 -> 10; matrix products, arithmetic and copies ran while one was open for 0% -> 0% of each run, Pallas kernels for 15% -> 14%
where the time goes in v13:
time: 46.6 us; the launch traced here: 46.4 us
  Pallas kernels  16.6 us (36%)
  starting transfers between devices  15.6 us (33%)
  waiting for transfers between devices  14.1 us (30%)
    pallas_call x5, Pallas kernels, products(): pl.pallas_call(functools.partial(product_kernel, chips, parts, per_owner)...  11.9 us
    ppermute x6, starting transfers between devices, to_blocks(): lax.ppermute(value, 'tm', [pair for pair in pairs if pair[1] < blocks])  9.04 us
    ppermute x3, waiting for transfers between devices, to_chip(): return on_chip(lax.ppermute(value, 'chan', pairs))  5.85 us
    ppermute x6, waiting for transfers between devices, to_blocks(): lax.ppermute(value, 'tm', [pair for pair in pairs if pair[1] < blocks])  5.51 us
    ppermute x3, starting transfers between devices, to_chip(): return on_chip(lax.ppermute(value, 'chan', pairs))  4.92 us
    ppermute x4, waiting for transfers between devices, to_core(): lax.ppermute(value, 'chan', [(i, i ^ 1) for i in range(owners)])  2.7 us
    pallas_call x4, Pallas kernels, first(): pl.pallas_call(functools.partial(first_kernel, start, places, len(earlier...  2 us
    ppermute x4, starting transfers between devices, to_core(): lax.ppermute(value, 'chan', [(i, i ^ 1) for i in range(owners)])  1.64 us
  transfers between devices with their start and end apart: 13, of which 10 were waited for; matrix products, arithmetic and copies ran while one was open for 0% of the time, Pallas kernels for 14%

profile of v13, /device:TPU:0, one launch (start us, length us, event | category | flops | bytes accessed | tf_op | source)
XLA Modules:
  0.0 46.4 jit_solution(6284661764854033405)
XLA Ops:
  0.0 2.6 %products.5 = (f32[128,1024]{1,0:T(8,128)S(1)}, f32[128,1024]{1,0:T(8,128)S(1)}) custom-call(bf16[128,1024]{1,0:T(8,128)(2,1)} %tokens_ref.9, bf16[1024,8192]{1,0:T(8,128)(2,1)} %weight_ref.9), custom_call_target="tpu_custom_call" | custom-call | flops 536870912 | bytes 4194304 | tf_op jit(solution)/shard_map/products/pallas_call | solution.py:73
  2.6 0.6 %collective-permute-start = (f32[128,1024]{1,0:T(8,128)S(1)}, f32[128,1024]{1,0:T(8,128)S(1)}, u32[]{:S(2)}, u32[]{:S(2)}) collective-permute-start(f32[128,1024]{1,0:T(8,128)S(1)} %get-tuple-element.31), channel_id=1, source_target_pairs={{0,1},{1,0},{2,3},{3,2},{4,5},{5,4},{6,7},{7,6},{8,9},{9,8},{10,11... | collective-permute-start | bytes 1572872 | tf_op jit(solution)/shard_map/ppermute | solution.py:473
  3.2 1.5 %collective-permute-done.theirs_ref = f32[128,1024]{1,0:T(8,128)S(1)} collective-permute-done((f32[128,1024]{1,0:T(8,128)S(1)}, f32[128,1024]{1,0:T(8,128)S(1)}, u32[]{:S(2)}, u32[]{:S(2)}) %collective-permute-start) | collective-permute-done | bytes 524320 | tf_op jit(solution)/shard_map/ppermute | solution.py:473
  4.7 0.4 encode.3.refs_0_
  5.2 2.0 %products.6 = (f32[128,512]{1,0:T(8,128)S(1)}, f32[128,512]{1,0:T(8,128)S(1)}) custom-call(bf16[128,1024]{1,0:T(8,128)(2,1)} %tokens_ref.9, bf16[1024,8192]{1,0:T(8,128)(2,1)} %weight_ref.9, bf16[1032,128]{1,0:T(8,128)(2,1)S(1)} %encode.3.refs_0_), custom_call_target="tpu_custom_call" | custom-call | flops 268435456 | bytes 2097152 | tf_op jit(solution)/shard_map/products/pallas_call | solution.py:73
  7.2 0.4 collective-permute-start.1
  7.6 1.2 %collective-permute-done.1.theirs_ref = f32[128,512]{1,0:T(8,128)S(1)} collective-permute-done((f32[128,512]{1,0:T(8,128)S(1)}, f32[128,512]{1,0:T(8,128)S(1)}, u32[]{:S(2)}, u32[]{:S(2)}) %collective-permute-start.1) | collective-permute-done | bytes 262176 | tf_op jit(solution)/shard_map/ppermute | solution.py:473
  9.0 2.6 %products.8 = f32[128,2048]{1,0:T(8,128)S(1)} custom-call(bf16[128,1024]{1,0:T(8,128)(2,1)} %tokens_ref.9, bf16[1024,8192]{1,0:T(8,128)(2,1)} %weight_ref.9, bf16[520,128]{1,0:T(8,128)(2,1)S(1)} %encode.4.refs_0_), custom_call_target="tpu_custom_call" | custom-call | flops 536870912 | bytes 4194304 | tf_op jit(solution)/shard_map/products/pallas_call | solution.py:73
  11.7 0.4 collective-permute-start.2
  12.1 2.0 %products.9 = (f32[128,512]{1,0:T(8,128)S(1)}, f32[128,512]{1,0:T(8,128)S(1)}) custom-call(bf16[128,1024]{1,0:T(8,128)(2,1)} %tokens_ref.9, bf16[1024,8192]{1,0:T(8,128)(2,1)} %weight_ref.9), custom_call_target="tpu_custom_call" | custom-call | flops 268435456 | bytes 2097152 | tf_op jit(solution)/shard_map/products/pallas_call | solution.py:73
  14.3 2.8 %collective-permute-start.6 = (bf16[1032,128]{1,0:T(8,128)(2,1)S(1)}, bf16[1032,128]{1,0:T(8,128)(2,1)S(1)}, u32[]{:S(2)}, u32[]{:S(2)}) collective-permute-start(bf16[1032,128]{1,0:T(8,128)(2,1)S(1)} %encode.3.refs_0_), channel_id=1, source_target_pairs={{0,2},{1,3},{2,0},{3,1},{4,6},{5,7},{6,4},{7,5},{8,10},{9,11},{10,... | collective-permute-start | bytes 792584 | tf_op jit(solution)/shard_map/ppermute | solution.py:477
  17.4 1.2 %collective-permute-start.5 = (bf16[520,128]{1,0:T(8,128)(2,1)S(1)}, bf16[520,128]{1,0:T(8,128)(2,1)S(1)}, u32[]{:S(2)}, u32[]{:S(2)}) collective-permute-start(bf16[520,128]{1,0:T(8,128)(2,1)S(1)} %encode.5), channel_id=1, source_target_pairs={{0,2},{1,3},{2,0},{3,1},{4,6},{5,7},{6,4},{7,5},{8,10},{9,11},{10,... | collective-permute-start | bytes 399368 | tf_op jit(solution)/shard_map/ppermute | solution.py:477
  18.6 0.9 %collective-permute-start.3 = (bf16[520,128]{1,0:T(8,128)(2,1)S(1)}, bf16[520,128]{1,0:T(8,128)(2,1)S(1)}, u32[]{:S(2)}, u32[]{:S(2)}) collective-permute-start(bf16[520,128]{1,0:T(8,128)(2,1)S(1)} %encode.4.refs_0_), channel_id=1, source_target_pairs={{0,2},{1,3},{2,0},{3,1},{4,6},{5,7},{6,4},{7,5},{8,10},{9,11},{10,... | collective-permute-start | bytes 399368 | tf_op jit(solution)/shard_map/ppermute | solution.py:477
  19.4 2.6 %products.7.refs_0_ = f32[128,2048]{1,0:T(8,128)S(1)} custom-call(bf16[128,1024]{1,0:T(8,128)(2,1)} %tokens_ref.9, bf16[1024,8192]{1,0:T(8,128)(2,1)} %weight_ref.9, bf16[520,128]{1,0:T(8,128)(2,1)S(1)} %encode.4.refs_0_), custom_call_target="tpu_custom_call" | custom-call | flops 536870912 | bytes 4194304 | tf_op jit(solution)/shard_map/products/pallas_call | solution.py:73
  22.1 2.2 %collective-permute-done.6.refs_2_ = bf16[1032,128]{1,0:T(8,128)(2,1)S(1)} collective-permute-done((bf16[1032,128]{1,0:T(8,128)(2,1)S(1)}, bf16[1032,128]{1,0:T(8,128)(2,1)S(1)}, u32[]{:S(2)}, u32[]{:S(2)}) %collective-permute-start.6) | collective-permute-done | bytes 264224 | tf_op jit(solution)/shard_map/ppermute | solution.py:477
  24.4 0.5 %first.4 = (f32[1,3,128,128]{3,2,1,0:T(8,128)S(1)}, f32[1,5,128,128]{3,2,1,0:T(8,128)S(1)}, f32[1,5,8,128]{3,2,1,0:T(8,128)S(1)}, f32[8,128]{1,0:T(8,128)S(1)}) custom-call(f32[128,2048]{1,0:T(8,128)S(1)} %products.7.refs_0_, f32[128,2048]{1,0:T(8,128)S(1)} %collective-permute-done.2.refs_1_, bf16[1032,128]{1,0:T(8,128)(2,1)S(1)} %collective-permute-done.6.refs_2_, ...), custom_call_target="tpu_custom_call" | custom-call | flops 3932160 | bytes 1310720 | tf_op jit(solution)/shard_map/first/pallas_call | solution.py:259
  24.9 0.5 %first.5 = (f32[1,3,128,128]{3,2,1,0:T(8,128)S(1)}, f32[1,5,128,128]{3,2,1,0:T(8,128)S(1)}, f32[1,5,8,128]{3,2,1,0:T(8,128)S(1)}, f32[16,128]{1,0:T(8,128)S(1)}) custom-call(f32[128,2048]{1,0:T(8,128)S(1)} %products.7.refs_0_, f32[128,2048]{1,0:T(8,128)S(1)} %collective-permute-done.2.refs_1_, bf16[1032,128]{1,0:T(8,128)(2,1)S(1)} %collective-permute-done.6.refs_2_, ...), custom_call_target="tpu_custom_call" | custom-call | flops 3932160 | bytes 1310720 | tf_op jit(solution)/shard_map/first/pallas_call | solution.py:259
  25.4 1.8 %collective-permute-done.5.refs_2_ = bf16[520,128]{1,0:T(8,128)(2,1)S(1)} collective-permute-done((bf16[520,128]{1,0:T(8,128)(2,1)S(1)}, bf16[520,128]{1,0:T(8,128)(2,1)S(1)}, u32[]{:S(2)}, u32[]{:S(2)}) %collective-permute-start.5) | collective-permute-done | bytes 133152 | tf_op jit(solution)/shard_map/ppermute | solution.py:477
  27.2 0.5 %first.6 = (f32[1,3,128,128]{3,2,1,0:T(8,128)S(1)}, f32[1,5,128,128]{3,2,1,0:T(8,128)S(1)}, f32[1,5,8,128]{3,2,1,0:T(8,128)S(1)}, f32[24,128]{1,0:T(8,128)S(1)}) custom-call(f32[128,2048]{1,0:T(8,128)S(1)} %products.7.refs_0_, f32[128,2048]{1,0:T(8,128)S(1)} %collective-permute-done.2.refs_1_, bf16[520,128]{1,0:T(8,128)(2,1)S(1)} %collective-permute-done.5.refs_2_, ...), custom_call_target="tpu_custom_call" | custom-call | flops 3932160 | bytes 1310720 | tf_op jit(solution)/shard_map/first/pallas_call | solution.py:259
  27.7 1.8 %collective-permute-done.3.refs_2_ = bf16[520,128]{1,0:T(8,128)(2,1)S(1)} collective-permute-done((bf16[520,128]{1,0:T(8,128)(2,1)S(1)}, bf16[520,128]{1,0:T(8,128)(2,1)S(1)}, u32[]{:S(2)}, u32[]{:S(2)}) %collective-permute-start.3) | collective-permute-done | bytes 133152 | tf_op jit(solution)/shard_map/ppermute | solution.py:477
  29.5 0.5 %first.7 = (f32[1,3,128,128]{3,2,1,0:T(8,128)S(1)}, f32[1,5,128,128]{3,2,1,0:T(8,128)S(1)}, f32[1,5,8,128]{3,2,1,0:T(8,128)S(1)}, f32[32,128]{1,0:T(8,128)S(1)}) custom-call(f32[128,2048]{1,0:T(8,128)S(1)} %products.7.refs_0_, f32[128,2048]{1,0:T(8,128)S(1)} %collective-permute-done.2.refs_1_, bf16[520,128]{1,0:T(8,128)(2,1)S(1)} %collective-permute-done.3.refs_2_, ...), custom_call_target="tpu_custom_call" | custom-call | flops 3932160 | bytes 1310720 | tf_op jit(solution)/shard_map/first/pallas_call | solution.py:259
  30.0 3.9 %collective-permute-start.9 = (f32[32,128]{1,0:T(8,128)S(1)}, f32[32,128]{1,0:T(8,128)S(1)}, u32[]{:S(2)}, u32[]{:S(2)}) collective-permute-start(f32[32,128]{1,0:T(8,128)S(1)} %get-tuple-element.39), channel_id=1, source_target_pairs={{0,12},{4,8},{8,4},{12,0},{1,13},{5,9},{9,5},{13,1},{2,14},{6,10},... | collective-permute-start | bytes 49160 | tf_op jit(solution)/shard_map/ppermute | solution.py:483
  33.9 0.6 %collective-permute-start.7 = (f32[32,128]{1,0:T(8,128)S(1)}, f32[32,128]{1,0:T(8,128)S(1)}, u32[]{:S(2)}, u32[]{:S(2)}) collective-permute-start(f32[32,128]{1,0:T(8,128)S(1)} %get-tuple-element.39), channel_id=1, source_target_pairs={{0,4},{4,0},{8,12},{12,8},{1,5},{5,1},{9,13},{13,9},{2,6},{6,2},{1... | collective-permute-start | bytes 49160 | tf_op jit(solution)/shard_map/ppermute | solution.py:483
  34.7 1.2 %collective-permute-done.9.refs_2_ = f32[32,128]{1,0:T(8,128)S(1)} collective-permute-done((f32[32,128]{1,0:T(8,128)S(1)}, f32[32,128]{1,0:T(8,128)S(1)}, u32[]{:S(2)}, u32[]{:S(2)}) %collective-permute-start.9) | collective-permute-done | bytes 16416 | tf_op jit(solution)/shard_map/ppermute | solution.py:483
  35.9 2.7 %collective-permute-done.8.refs_1_ = f32[32,128]{1,0:T(8,128)S(1)} collective-permute-done((f32[32,128]{1,0:T(8,128)S(1)}, f32[32,128]{1,0:T(8,128)S(1)}, u32[]{:S(2)}, u32[]{:S(2)}) %collective-permute-start.8) | collective-permute-done | bytes 16416 | tf_op jit(solution)/shard_map/ppermute | solution.py:483
  38.6 0.6 %second.1 = (f32[4,3,128,128]{3,2,1,0:T(8,128)S(1)}, f32[4,6,8,128]{3,2,1,0:T(8,128)S(1)}, f32[32,128]{1,0:T(8,128)S(1)}) custom-call(f32[32,128]{1,0:T(8,128)S(1)} %collective-permute-done.7.refs_0_, f32[32,128]{1,0:T(8,128)S(1)} %collective-permute-done.8.refs_1_, f32[32,128]{1,0:T(8,128)S(1)} %collective-permute-done.9.refs_2_, ...), custom_call_target="tpu_custom_call" | custom-call | flops 5242880 | bytes 1572864 | tf_op jit(solution)/shard_map/second/pallas_call | solution.py:377
  39.2 1.5 %collective-permute-start.12 = (f32[32,128]{1,0:T(8,128)S(1)}, f32[32,128]{1,0:T(8,128)S(1)}, u32[]{:S(2)}, u32[]{:S(2)}) collective-permute-start(f32[32,128]{1,0:T(8,128)S(1)} %get-tuple-element.52), channel_id=1, source_target_pairs={{0,12},{4,8},{8,4},{12,0},{1,13},{5,9},{9,5},{13,1},{2,14},{6,10},... | collective-permute-start | bytes 49160 | tf_op jit(solution)/shard_map/ppermute | solution.py:483
  40.7 0.6 %collective-permute-start.11 = (f32[32,128]{1,0:T(8,128)S(1)}, f32[32,128]{1,0:T(8,128)S(1)}, u32[]{:S(2)}, u32[]{:S(2)}) collective-permute-start(f32[32,128]{1,0:T(8,128)S(1)} %get-tuple-element.52), channel_id=1, source_target_pairs={{0,8},{4,12},{8,0},{12,4},{1,9},{5,13},{9,1},{13,5},{2,10},{6,14},... | collective-permute-start | bytes 49160 | tf_op jit(solution)/shard_map/ppermute | solution.py:483
  41.4 2.3 %collective-permute-start.10 = (f32[32,128]{1,0:T(8,128)S(1)}, f32[32,128]{1,0:T(8,128)S(1)}, u32[]{:S(2)}, u32[]{:S(2)}) collective-permute-start(f32[32,128]{1,0:T(8,128)S(1)} %get-tuple-element.52), channel_id=1, source_target_pairs={{0,4},{4,0},{8,12},{12,8},{1,5},{5,1},{9,13},{13,9},{2,6},{6,2},{1... | collective-permute-start | bytes 49160 | tf_op jit(solution)/shard_map/ppermute | solution.py:483
  43.9 0.9 %collective-permute-done.12.refs_2_ = f32[32,128]{1,0:T(8,128)S(1)} collective-permute-done((f32[32,128]{1,0:T(8,128)S(1)}, f32[32,128]{1,0:T(8,128)S(1)}, u32[]{:S(2)}, u32[]{:S(2)}) %collective-permute-start.12) | collective-permute-done | bytes 16416 | tf_op jit(solution)/shard_map/ppermute | solution.py:483
  44.8 0.6 %collective-permute-done.11.refs_1_ = f32[32,128]{1,0:T(8,128)S(1)} collective-permute-done((f32[32,128]{1,0:T(8,128)S(1)}, f32[32,128]{1,0:T(8,128)S(1)}, u32[]{:S(2)}, u32[]{:S(2)}) %collective-permute-start.11) | collective-permute-done | bytes 16416 | tf_op jit(solution)/shard_map/ppermute | solution.py:483
  45.6 0.9 %last.1 = f32[512,128]{1,0:T(8,128)} custom-call(f32[32,128]{1,0:T(8,128)S(1)} %collective-permute-done.10.refs_0_, f32[32,128]{1,0:T(8,128)S(1)} %collective-permute-done.11.refs_1_, f32[32,128]{1,0:T(8,128)S(1)} %collective-permute-done.12.refs_2_, f32[12,128,128]{2,1,0:T(8,128)S(1)} %ordered.1.refs_3_), custom_call_target="tpu_custom_call" | custom-call | flops 655360 | bytes 1048576 | tf_op jit(solution)/shard_map/last/pallas_call | solution.py:437
  (16 shorter events, 1.2 us)
Async XLA Ops:
  2.6 2.1 %collective-permute-start = (f32[128,1024]{1,0:T(8,128)S(1)}, f32[128,1024]{1,0:T(8,128)S(1)}, u32[]{:S(2)}, u32[]{:S(2)}) collective-permute-start(f32[128,1024]{1,0:T(8,128)S(1)} %get-tuple-element.31), channel_id=1, source_target_pairs={{0,1},{1,0},{2,3},{3,2},{4,5},{5,4},{6,7},{7,6},{8,9},{9,8},{10,11... | collective-permute-start | bytes 1572872 | tf_op jit(solution)/shard_map/ppermute | solution.py:473
  7.2 1.6 %collective-permute-start.1 = (f32[128,512]{1,0:T(8,128)S(1)}, f32[128,512]{1,0:T(8,128)S(1)}, u32[]{:S(2)}, u32[]{:S(2)}) collective-permute-start(f32[128,512]{1,0:T(8,128)S(1)} %get-tuple-element.33), channel_id=1, source_target_pairs={{0,1},{1,0},{2,3},{3,2},{4,5},{5,4},{6,7},{7,6},{8,9},{9,8},{10,11... | collective-permute-start | bytes 786440 | tf_op jit(solution)/shard_map/ppermute | solution.py:473
  11.6 12.7 %copy-start = (f32[512,4]{0,1:T(4,128)S(1)}, f32[512,4]{0,1:T(4,128)}, u32[]{:S(2)}) copy-start(f32[512,4]{0,1:T(4,128)} %param.8) | copy-start | bytes 24580
  11.7 12.7 %copy-start.1 = (f32[512,2]{0,1:T(2,128)S(1)}, f32[512,2]{0,1:T(2,128)}, u32[]{:S(2)}) copy-start(f32[512,2]{0,1:T(2,128)} %param.7) | copy-start | bytes 12292
  11.7 12.7 %copy-start.2 = (f32[128]{0:T(128)S(1)}, f32[128]{0:T(128)}, u32[]{:S(2)}) copy-start(f32[128]{0:T(128)} %param.9) | copy-start | bytes 1540
  11.7 12.7 %collective-permute-start.2 = (f32[128,2048]{1,0:T(8,128)S(1)}, f32[128,2048]{1,0:T(8,128)S(1)}, u32[]{:S(2)}, u32[]{:S(2)}) collective-permute-start(f32[128,2048]{1,0:T(8,128)S(1)} %products.8), channel_id=1, source_target_pairs={{0,1},{1,0},{2,3},{3,2},{4,5},{5,4},{6,7},{7,6},{8,9},{9,8},{10,11... | collective-permute-start | bytes 3145736 | tf_op jit(solution)/shard_map/ppermute | solution.py:473
  14.1 3.0 %collective-permute-start.4 = (f32[128,512]{1,0:T(8,128)S(1)}, f32[128,512]{1,0:T(8,128)S(1)}, u32[]{:S(2)}, u32[]{:S(2)}) collective-permute-start(f32[128,512]{1,0:T(8,128)S(1)} %get-tuple-element.35), channel_id=1, source_target_pairs={{0,1},{1,0},{2,3},{3,2},{4,5},{5,4},{6,7},{7,6},{8,9},{9,8},{10,11... | collective-permute-start | bytes 786440 | tf_op jit(solution)/shard_map/ppermute | solution.py:473
  14.3 10.0 %collective-permute-start.6 = (bf16[1032,128]{1,0:T(8,128)(2,1)S(1)}, bf16[1032,128]{1,0:T(8,128)(2,1)S(1)}, u32[]{:S(2)}, u32[]{:S(2)}) collective-permute-start(bf16[1032,128]{1,0:T(8,128)(2,1)S(1)} %encode.3.refs_0_), channel_id=1, source_target_pairs={{0,2},{1,3},{2,0},{3,1},{4,6},{5,7},{6,4},{7,5},{8,10},{9,11},{10,... | collective-permute-start | bytes 792584 | tf_op jit(solution)/shard_map/ppermute | solution.py:477
  17.4 9.8 %collective-permute-start.5 = (bf16[520,128]{1,0:T(8,128)(2,1)S(1)}, bf16[520,128]{1,0:T(8,128)(2,1)S(1)}, u32[]{:S(2)}, u32[]{:S(2)}) collective-permute-start(bf16[520,128]{1,0:T(8,128)(2,1)S(1)} %encode.5), channel_id=1, source_target_pairs={{0,2},{1,3},{2,0},{3,1},{4,6},{5,7},{6,4},{7,5},{8,10},{9,11},{10,... | collective-permute-start | bytes 399368 | tf_op jit(solution)/shard_map/ppermute | solution.py:477
  18.6 10.9 %collective-permute-start.3 = (bf16[520,128]{1,0:T(8,128)(2,1)S(1)}, bf16[520,128]{1,0:T(8,128)(2,1)S(1)}, u32[]{:S(2)}, u32[]{:S(2)}) collective-permute-start(bf16[520,128]{1,0:T(8,128)(2,1)S(1)} %encode.4.refs_0_), channel_id=1, source_target_pairs={{0,2},{1,3},{2,0},{3,1},{4,6},{5,7},{6,4},{7,5},{8,10},{9,11},{10,... | collective-permute-start | bytes 399368 | tf_op jit(solution)/shard_map/ppermute | solution.py:477
  30.0 5.9 %collective-permute-start.9 = (f32[32,128]{1,0:T(8,128)S(1)}, f32[32,128]{1,0:T(8,128)S(1)}, u32[]{:S(2)}, u32[]{:S(2)}) collective-permute-start(f32[32,128]{1,0:T(8,128)S(1)} %get-tuple-element.39), channel_id=1, source_target_pairs={{0,12},{4,8},{8,4},{12,0},{1,13},{5,9},{9,5},{13,1},{2,14},{6,10},... | collective-permute-start | bytes 49160 | tf_op jit(solution)/shard_map/ppermute | solution.py:483
  33.9 4.6 %collective-permute-start.8 = (f32[32,128]{1,0:T(8,128)S(1)}, f32[32,128]{1,0:T(8,128)S(1)}, u32[]{:S(2)}, u32[]{:S(2)}) collective-permute-start(f32[32,128]{1,0:T(8,128)S(1)} %get-tuple-element.39), channel_id=1, source_target_pairs={{0,8},{4,12},{8,0},{12,4},{1,9},{5,13},{9,1},{13,5},{2,10},{6,14},... | collective-permute-start | bytes 49160 | tf_op jit(solution)/shard_map/ppermute | solution.py:483
  33.9 4.6 %collective-permute-start.7 = (f32[32,128]{1,0:T(8,128)S(1)}, f32[32,128]{1,0:T(8,128)S(1)}, u32[]{:S(2)}, u32[]{:S(2)}) collective-permute-start(f32[32,128]{1,0:T(8,128)S(1)} %get-tuple-element.39), channel_id=1, source_target_pairs={{0,4},{4,0},{8,12},{12,8},{1,5},{5,1},{9,13},{13,9},{2,6},{6,2},{1... | collective-permute-start | bytes 49160 | tf_op jit(solution)/shard_map/ppermute | solution.py:483
  39.2 5.6 %collective-permute-start.12 = (f32[32,128]{1,0:T(8,128)S(1)}, f32[32,128]{1,0:T(8,128)S(1)}, u32[]{:S(2)}, u32[]{:S(2)}) collective-permute-start(f32[32,128]{1,0:T(8,128)S(1)} %get-tuple-element.52), channel_id=1, source_target_pairs={{0,12},{4,8},{8,4},{12,0},{1,13},{5,9},{9,5},{13,1},{2,14},{6,10},... | collective-permute-start | bytes 49160 | tf_op jit(solution)/shard_map/ppermute | solution.py:483
  40.7 4.7 %collective-permute-start.11 = (f32[32,128]{1,0:T(8,128)S(1)}, f32[32,128]{1,0:T(8,128)S(1)}, u32[]{:S(2)}, u32[]{:S(2)}) collective-permute-start(f32[32,128]{1,0:T(8,128)S(1)} %get-tuple-element.52), channel_id=1, source_target_pairs={{0,8},{4,12},{8,0},{12,4},{1,9},{5,13},{9,1},{13,5},{2,10},{6,14},... | collective-permute-start | bytes 49160 | tf_op jit(solution)/shard_map/ppermute | solution.py:483
  41.4 4.2 %collective-permute-start.10 = (f32[32,128]{1,0:T(8,128)S(1)}, f32[32,128]{1,0:T(8,128)S(1)}, u32[]{:S(2)}, u32[]{:S(2)}) collective-permute-start(f32[32,128]{1,0:T(8,128)S(1)} %get-tuple-element.52), channel_id=1, source_target_pairs={{0,4},{4,0},{8,12},{12,8},{1,5},{5,1},{9,13},{13,9},{2,6},{6,2},{1... | collective-permute-start | bytes 49160 | tf_op jit(solution)/shard_map/ppermute | solution.py:483

commit v14 on v13

--- a/solution.py
+++ b/solution.py
@@ -102,7 +102,8 @@
     inverse = 1.0 / scale
     for block in range(blocks):
         value = sum_ref[:, pl.ds(block * LANES, LANES)]
-        level = jnp.sqrt(jnp.abs(value) * inverse) * BINADES - LOWEST
+        share = jnp.abs(value) * inverse
+        level = share * lax.rsqrt(jnp.maximum(share, 1e-30)) * BINADES - LOWEST
         code = jnp.exp2(level)
         out_ref[pl.ds(block * steps, steps), :] = jnp.where(value < 0.0, -code, code).astype(BF16)
 
@@ -500,16 +501,28 @@
 
     local_give, local_keep = ((0, which, 0, per_owner) for which in (GIVE, KEEP))
     codes = []
-    for index, (away, start, count) in enumerate(pieces_of(groups, chips)):
+    pieces = pieces_of(groups, chips)
+    owed = None
+    for index, (away, start, count) in enumerate(pieces):
         parts = tuple((away, which, start * GROUP, count * GROUP) for which in (GIVE, KEEP))
         if index == 0:
             give, keep = product(parts, [])
+            codes.append(send(away, start, count, keep, to_core(give), 0))
+        elif index == 1 and len(pieces) > 2:
+            (give,) = product(parts[:1], [])
+            owed = (away, start, count, to_core(give), parts[1:])
+        else:
+            before = () if owed is None else owed[4]
+            *rest, give, keep = product(before + parts, codes[:1])
             theirs = to_core(give)
-            codes.append(send(away, start, count, keep, theirs, 0))
-        else:
-            give, keep = product(parts, codes[-2:-1])
-            theirs = to_core(give)
-            codes.append(send(away, start, count, keep, theirs, 0))
+            ready = [(away, start, count, keep, theirs)]
+            if owed is not None:
+                ready.insert(0, (*owed[:3], rest[0], owed[3]))
+                owed = None
+            for away_, start_, count_, keep_, theirs_ in ready:
+                for group in range(start_, start_ + count_):
+                    inside = (group - start_) * GROUP
+                    codes.append(send(away_, group, 1, keep_, theirs_, inside))
     (give,) = product((local_give,), codes[-1:])
     given = to_core(give)
     (keep,) = product((local_keep,), codes[-1:])

time: 46.6 us -> 46.4 us (level)
  no operation moved by 1% of the time
where the time goes in v14:
time: 46.4 us; the launch traced here: 46.3 us
  Pallas kernels  16.4 us (35%)
  starting transfers between devices  15.6 us (34%)
  waiting for transfers between devices  14.1 us (30%)
    pallas_call x5, Pallas kernels, products(): pl.pallas_call(functools.partial(product_kernel, chips, parts, per_owner)...  11.9 us
    ppermute x6, starting transfers between devices, to_blocks(): lax.ppermute(value, 'tm', [pair for pair in pairs if pair[1] < blocks])  9.02 us
    ppermute x3, waiting for transfers between devices, to_chip(): return on_chip(lax.ppermute(value, 'chan', pairs))  5.88 us
    ppermute x6, waiting for transfers between devices, to_blocks(): lax.ppermute(value, 'tm', [pair for pair in pairs if pair[1] < blocks])  5.51 us
    ppermute x3, starting transfers between devices, to_chip(): return on_chip(lax.ppermute(value, 'chan', pairs))  4.94 us
    ppermute x4, waiting for transfers between devices, to_core(): lax.ppermute(value, 'chan', [(i, i ^ 1) for i in range(owners)])  2.7 us
    pallas_call x4, Pallas kernels, first(): pl.pallas_call(functools.partial(first_kernel, start, places, len(earlier...  2 us
    ppermute x4, starting transfers between devices, to_core(): lax.ppermute(value, 'chan', [(i, i ^ 1) for i in range(owners)])  1.64 us
  transfers between devices with their start and end apart: 13, of which 10 were waited for; matrix products, arithmetic and copies ran while one was open for 0% of the time, Pallas kernels for 14%

profile of v14, /device:TPU:0, one launch (start us, length us, event | category | flops | bytes accessed | tf_op | source)
XLA Modules:
  0.0 46.3 jit_solution(1907809167322493087)
XLA Ops:
  0.0 2.6 %products.5 = (f32[128,1024]{1,0:T(8,128)S(1)}, f32[128,1024]{1,0:T(8,128)S(1)}) custom-call(bf16[128,1024]{1,0:T(8,128)(2,1)} %tokens_ref.9, bf16[1024,8192]{1,0:T(8,128)(2,1)} %weight_ref.9), custom_call_target="tpu_custom_call" | custom-call | flops 536870912 | bytes 4194304 | tf_op jit(solution)/shard_map/products/pallas_call | solution.py:73
  2.6 0.6 %collective-permute-start = (f32[128,1024]{1,0:T(8,128)S(1)}, f32[128,1024]{1,0:T(8,128)S(1)}, u32[]{:S(2)}, u32[]{:S(2)}) collective-permute-start(f32[128,1024]{1,0:T(8,128)S(1)} %get-tuple-element.30), channel_id=1, source_target_pairs={{0,1},{1,0},{2,3},{3,2},{4,5},{5,4},{6,7},{7,6},{8,9},{9,8},{10,11... | collective-permute-start | bytes 1572872 | tf_op jit(solution)/shard_map/ppermute | solution.py:474
  3.2 1.5 %collective-permute-done.theirs_ref = f32[128,1024]{1,0:T(8,128)S(1)} collective-permute-done((f32[128,1024]{1,0:T(8,128)S(1)}, f32[128,1024]{1,0:T(8,128)S(1)}, u32[]{:S(2)}, u32[]{:S(2)}) %collective-permute-start) | collective-permute-done | bytes 524320 | tf_op jit(solution)/shard_map/ppermute | solution.py:474
  4.7 0.3 encode.3.refs_0_
  5.1 2.3 %products.6 = (f32[128,512]{1,0:T(8,128)S(1)}, f32[128,512]{1,0:T(8,128)S(1)}, f32[128,512]{1,0:T(8,128)S(1)}) custom-call(bf16[128,1024]{1,0:T(8,128)(2,1)} %tokens_ref.9, bf16[1024,8192]{1,0:T(8,128)(2,1)} %weight_ref.9, bf16[1032,128]{1,0:T(8,128)(2,1)S(1)} %encode.3.refs_0_), custom_call_target="tpu_custom_call" | custom-call | flops 402653184 | bytes 3145728 | tf_op jit(solution)/shard_map/products/pallas_call | solution.py:73
  7.4 0.4 collective-permute-start.1
  7.8 1.2 %collective-permute-done.1.theirs_ref = f32[128,512]{1,0:T(8,128)S(1)} collective-permute-done((f32[128,512]{1,0:T(8,128)S(1)}, f32[128,512]{1,0:T(8,128)S(1)}, u32[]{:S(2)}, u32[]{:S(2)}) %collective-permute-start.1) | collective-permute-done | bytes 262176 | tf_op jit(solution)/shard_map/ppermute | solution.py:474
  9.2 2.6 %products.8 = f32[128,2048]{1,0:T(8,128)S(1)} custom-call(bf16[128,1024]{1,0:T(8,128)(2,1)} %tokens_ref.9, bf16[1024,8192]{1,0:T(8,128)(2,1)} %weight_ref.9, bf16[520,128]{1,0:T(8,128)(2,1)S(1)} %encode.4.refs_0_), custom_call_target="tpu_custom_call" | custom-call | flops 536870912 | bytes 4194304 | tf_op jit(solution)/shard_map/products/pallas_call | solution.py:73
  11.9 0.4 collective-permute-start.2
  12.3 1.6 %products.9 = f32[128,512]{1,0:T(8,128)S(1)} custom-call(bf16[128,1024]{1,0:T(8,128)(2,1)} %tokens_ref.9, bf16[1024,8192]{1,0:T(8,128)(2,1)} %weight_ref.9), custom_call_target="tpu_custom_call" | custom-call | flops 134217728 | bytes 1048576 | tf_op jit(solution)/shard_map/products/pallas_call | solution.py:73
  14.2 2.8 %collective-permute-start.6 = (bf16[1032,128]{1,0:T(8,128)(2,1)S(1)}, bf16[1032,128]{1,0:T(8,128)(2,1)S(1)}, u32[]{:S(2)}, u32[]{:S(2)}) collective-permute-start(bf16[1032,128]{1,0:T(8,128)(2,1)S(1)} %encode.3.refs_0_), channel_id=1, source_target_pairs={{0,2},{1,3},{2,0},{3,1},{4,6},{5,7},{6,4},{7,5},{8,10},{9,11},{10,... | collective-permute-start | bytes 792584 | tf_op jit(solution)/shard_map/ppermute | solution.py:478
  17.2 1.2 %collective-permute-start.5 = (bf16[520,128]{1,0:T(8,128)(2,1)S(1)}, bf16[520,128]{1,0:T(8,128)(2,1)S(1)}, u32[]{:S(2)}, u32[]{:S(2)}) collective-permute-start(bf16[520,128]{1,0:T(8,128)(2,1)S(1)} %encode.5), channel_id=1, source_target_pairs={{0,2},{1,3},{2,0},{3,1},{4,6},{5,7},{6,4},{7,5},{8,10},{9,11},{10,... | collective-permute-start | bytes 399368 | tf_op jit(solution)/shard_map/ppermute | solution.py:478
  18.4 0.9 %collective-permute-start.3 = (bf16[520,128]{1,0:T(8,128)(2,1)S(1)}, bf16[520,128]{1,0:T(8,128)(2,1)S(1)}, u32[]{:S(2)}, u32[]{:S(2)}) collective-permute-start(bf16[520,128]{1,0:T(8,128)(2,1)S(1)} %encode.4.refs_0_), channel_id=1, source_target_pairs={{0,2},{1,3},{2,0},{3,1},{4,6},{5,7},{6,4},{7,5},{8,10},{9,11},{10,... | collective-permute-start | bytes 399368 | tf_op jit(solution)/shard_map/ppermute | solution.py:478
  19.3 2.6 %products.7.refs_0_ = f32[128,2048]{1,0:T(8,128)S(1)} custom-call(bf16[128,1024]{1,0:T(8,128)(2,1)} %tokens_ref.9, bf16[1024,8192]{1,0:T(8,128)(2,1)} %weight_ref.9, bf16[520,128]{1,0:T(8,128)(2,1)S(1)} %encode.4.refs_0_), custom_call_target="tpu_custom_call" | custom-call | flops 536870912 | bytes 4194304 | tf_op jit(solution)/shard_map/products/pallas_call | solution.py:73
  21.9 2.3 %collective-permute-done.6.refs_2_ = bf16[1032,128]{1,0:T(8,128)(2,1)S(1)} collective-permute-done((bf16[1032,128]{1,0:T(8,128)(2,1)S(1)}, bf16[1032,128]{1,0:T(8,128)(2,1)S(1)}, u32[]{:S(2)}, u32[]{:S(2)}) %collective-permute-start.6) | collective-permute-done | bytes 264224 | tf_op jit(solution)/shard_map/ppermute | solution.py:478
  24.2 0.5 %first.4 = (f32[1,3,128,128]{3,2,1,0:T(8,128)S(1)}, f32[1,5,128,128]{3,2,1,0:T(8,128)S(1)}, f32[1,5,8,128]{3,2,1,0:T(8,128)S(1)}, f32[8,128]{1,0:T(8,128)S(1)}) custom-call(f32[128,2048]{1,0:T(8,128)S(1)} %products.7.refs_0_, f32[128,2048]{1,0:T(8,128)S(1)} %collective-permute-done.2.refs_1_, bf16[1032,128]{1,0:T(8,128)(2,1)S(1)} %collective-permute-done.6.refs_2_, ...), custom_call_target="tpu_custom_call" | custom-call | flops 3932160 | bytes 1310720 | tf_op jit(solution)/shard_map/first/pallas_call | solution.py:260
  24.7 0.5 %first.5 = (f32[1,3,128,128]{3,2,1,0:T(8,128)S(1)}, f32[1,5,128,128]{3,2,1,0:T(8,128)S(1)}, f32[1,5,8,128]{3,2,1,0:T(8,128)S(1)}, f32[16,128]{1,0:T(8,128)S(1)}) custom-call(f32[128,2048]{1,0:T(8,128)S(1)} %products.7.refs_0_, f32[128,2048]{1,0:T(8,128)S(1)} %collective-permute-done.2.refs_1_, bf16[1032,128]{1,0:T(8,128)(2,1)S(1)} %collective-permute-done.6.refs_2_, ...), custom_call_target="tpu_custom_call" | custom-call | flops 3932160 | bytes 1310720 | tf_op jit(solution)/shard_map/first/pallas_call | solution.py:260
  25.3 1.8 %collective-permute-done.5.refs_2_ = bf16[520,128]{1,0:T(8,128)(2,1)S(1)} collective-permute-done((bf16[520,128]{1,0:T(8,128)(2,1)S(1)}, bf16[520,128]{1,0:T(8,128)(2,1)S(1)}, u32[]{:S(2)}, u32[]{:S(2)}) %collective-permute-start.5) | collective-permute-done | bytes 133152 | tf_op jit(solution)/shard_map/ppermute | solution.py:478
  27.1 0.5 %first.6 = (f32[1,3,128,128]{3,2,1,0:T(8,128)S(1)}, f32[1,5,128,128]{3,2,1,0:T(8,128)S(1)}, f32[1,5,8,128]{3,2,1,0:T(8,128)S(1)}, f32[24,128]{1,0:T(8,128)S(1)}) custom-call(f32[128,2048]{1,0:T(8,128)S(1)} %products.7.refs_0_, f32[128,2048]{1,0:T(8,128)S(1)} %collective-permute-done.2.refs_1_, bf16[520,128]{1,0:T(8,128)(2,1)S(1)} %collective-permute-done.5.refs_2_, ...), custom_call_target="tpu_custom_call" | custom-call | flops 3932160 | bytes 1310720 | tf_op jit(solution)/shard_map/first/pallas_call | solution.py:260
  27.6 1.8 %collective-permute-done.3.refs_2_ = bf16[520,128]{1,0:T(8,128)(2,1)S(1)} collective-permute-done((bf16[520,128]{1,0:T(8,128)(2,1)S(1)}, bf16[520,128]{1,0:T(8,128)(2,1)S(1)}, u32[]{:S(2)}, u32[]{:S(2)}) %collective-permute-start.3) | collective-permute-done | bytes 133152 | tf_op jit(solution)/shard_map/ppermute | solution.py:478
  29.4 0.5 %first.7 = (f32[1,3,128,128]{3,2,1,0:T(8,128)S(1)}, f32[1,5,128,128]{3,2,1,0:T(8,128)S(1)}, f32[1,5,8,128]{3,2,1,0:T(8,128)S(1)}, f32[32,128]{1,0:T(8,128)S(1)}) custom-call(f32[128,2048]{1,0:T(8,128)S(1)} %products.7.refs_0_, f32[128,2048]{1,0:T(8,128)S(1)} %collective-permute-done.2.refs_1_, bf16[520,128]{1,0:T(8,128)(2,1)S(1)} %collective-permute-done.3.refs_2_, ...), custom_call_target="tpu_custom_call" | custom-call | flops 3932160 | bytes 1310720 | tf_op jit(solution)/shard_map/first/pallas_call | solution.py:260
  29.9 3.9 %collective-permute-start.9 = (f32[32,128]{1,0:T(8,128)S(1)}, f32[32,128]{1,0:T(8,128)S(1)}, u32[]{:S(2)}, u32[]{:S(2)}) collective-permute-start(f32[32,128]{1,0:T(8,128)S(1)} %get-tuple-element.37), channel_id=1, source_target_pairs={{0,12},{4,8},{8,4},{12,0},{1,13},{5,9},{9,5},{13,1},{2,14},{6,10},... | collective-permute-start | bytes 49160 | tf_op jit(solution)/shard_map/ppermute | solution.py:484
  33.8 0.6 %collective-permute-start.7 = (f32[32,128]{1,0:T(8,128)S(1)}, f32[32,128]{1,0:T(8,128)S(1)}, u32[]{:S(2)}, u32[]{:S(2)}) collective-permute-start(f32[32,128]{1,0:T(8,128)S(1)} %get-tuple-element.37), channel_id=1, source_target_pairs={{0,4},{4,0},{8,12},{12,8},{1,5},{5,1},{9,13},{13,9},{2,6},{6,2},{1... | collective-permute-start | bytes 49160 | tf_op jit(solution)/shard_map/ppermute | solution.py:484
  34.6 1.2 %collective-permute-done.9.refs_2_ = f32[32,128]{1,0:T(8,128)S(1)} collective-permute-done((f32[32,128]{1,0:T(8,128)S(1)}, f32[32,128]{1,0:T(8,128)S(1)}, u32[]{:S(2)}, u32[]{:S(2)}) %collective-permute-start.9) | collective-permute-done | bytes 16416 | tf_op jit(solution)/shard_map/ppermute | solution.py:484
  35.7 2.7 %collective-permute-done.8.refs_1_ = f32[32,128]{1,0:T(8,128)S(1)} collective-permute-done((f32[32,128]{1,0:T(8,128)S(1)}, f32[32,128]{1,0:T(8,128)S(1)}, u32[]{:S(2)}, u32[]{:S(2)}) %collective-permute-start.8) | collective-permute-done | bytes 16416 | tf_op jit(solution)/shard_map/ppermute | solution.py:484
  38.4 0.6 %second.1 = (f32[4,3,128,128]{3,2,1,0:T(8,128)S(1)}, f32[4,6,8,128]{3,2,1,0:T(8,128)S(1)}, f32[32,128]{1,0:T(8,128)S(1)}) custom-call(f32[32,128]{1,0:T(8,128)S(1)} %collective-permute-done.7.refs_0_, f32[32,128]{1,0:T(8,128)S(1)} %collective-permute-done.8.refs_1_, f32[32,128]{1,0:T(8,128)S(1)} %collective-permute-done.9.refs_2_, ...), custom_call_target="tpu_custom_call" | custom-call | flops 5242880 | bytes 1572864 | tf_op jit(solution)/shard_map/second/pallas_call | solution.py:378
  39.1 1.5 %collective-permute-start.12 = (f32[32,128]{1,0:T(8,128)S(1)}, f32[32,128]{1,0:T(8,128)S(1)}, u32[]{:S(2)}, u32[]{:S(2)}) collective-permute-start(f32[32,128]{1,0:T(8,128)S(1)} %get-tuple-element.50), channel_id=1, source_target_pairs={{0,12},{4,8},{8,4},{12,0},{1,13},{5,9},{9,5},{13,1},{2,14},{6,10},... | collective-permute-start | bytes 49160 | tf_op jit(solution)/shard_map/ppermute | solution.py:484
  40.6 0.6 %collective-permute-start.11 = (f32[32,128]{1,0:T(8,128)S(1)}, f32[32,128]{1,0:T(8,128)S(1)}, u32[]{:S(2)}, u32[]{:S(2)}) collective-permute-start(f32[32,128]{1,0:T(8,128)S(1)} %get-tuple-element.50), channel_id=1, source_target_pairs={{0,8},{4,12},{8,0},{12,4},{1,9},{5,13},{9,1},{13,5},{2,10},{6,14},... | collective-permute-start | bytes 49160 | tf_op jit(solution)/shard_map/ppermute | solution.py:484
  41.3 2.3 %collective-permute-start.10 = (f32[32,128]{1,0:T(8,128)S(1)}, f32[32,128]{1,0:T(8,128)S(1)}, u32[]{:S(2)}, u32[]{:S(2)}) collective-permute-start(f32[32,128]{1,0:T(8,128)S(1)} %get-tuple-element.50), channel_id=1, source_target_pairs={{0,4},{4,0},{8,12},{12,8},{1,5},{5,1},{9,13},{13,9},{2,6},{6,2},{1... | collective-permute-start | bytes 49160 | tf_op jit(solution)/shard_map/ppermute | solution.py:484
  43.8 0.9 %collective-permute-done.12.refs_2_ = f32[32,128]{1,0:T(8,128)S(1)} collective-permute-done((f32[32,128]{1,0:T(8,128)S(1)}, f32[32,128]{1,0:T(8,128)S(1)}, u32[]{:S(2)}, u32[]{:S(2)}) %collective-permute-start.12) | collective-permute-done | bytes 16416 | tf_op jit(solution)/shard_map/ppermute | solution.py:484
  44.7 0.6 %collective-permute-done.11.refs_1_ = f32[32,128]{1,0:T(8,128)S(1)} collective-permute-done((f32[32,128]{1,0:T(8,128)S(1)}, f32[32,128]{1,0:T(8,128)S(1)}, u32[]{:S(2)}, u32[]{:S(2)}) %collective-permute-start.11) | collective-permute-done | bytes 16416 | tf_op jit(solution)/shard_map/ppermute | solution.py:484
  45.4 0.9 %last.1 = f32[512,128]{1,0:T(8,128)} custom-call(f32[32,128]{1,0:T(8,128)S(1)} %collective-permute-done.10.refs_0_, f32[32,128]{1,0:T(8,128)S(1)} %collective-permute-done.11.refs_1_, f32[32,128]{1,0:T(8,128)S(1)} %collective-permute-done.12.refs_2_, f32[12,128,128]{2,1,0:T(8,128)S(1)} %ordered.1.refs_3_), custom_call_target="tpu_custom_call" | custom-call | flops 655360 | bytes 1048576 | tf_op jit(solution)/shard_map/last/pallas_call | solution.py:438
  (16 shorter events, 1.1 us)
Async XLA Ops:
  2.6 2.1 %collective-permute-start = (f32[128,1024]{1,0:T(8,128)S(1)}, f32[128,1024]{1,0:T(8,128)S(1)}, u32[]{:S(2)}, u32[]{:S(2)}) collective-permute-start(f32[128,1024]{1,0:T(8,128)S(1)} %get-tuple-element.30), channel_id=1, source_target_pairs={{0,1},{1,0},{2,3},{3,2},{4,5},{5,4},{6,7},{7,6},{8,9},{9,8},{10,11... | collective-permute-start | bytes 1572872 | tf_op jit(solution)/shard_map/ppermute | solution.py:474
  7.4 1.6 %collective-permute-start.1 = (f32[128,512]{1,0:T(8,128)S(1)}, f32[128,512]{1,0:T(8,128)S(1)}, u32[]{:S(2)}, u32[]{:S(2)}) collective-permute-start(f32[128,512]{1,0:T(8,128)S(1)} %get-tuple-element.32), channel_id=1, source_target_pairs={{0,1},{1,0},{2,3},{3,2},{4,5},{5,4},{6,7},{7,6},{8,9},{9,8},{10,11... | collective-permute-start | bytes 786440 | tf_op jit(solution)/shard_map/ppermute | solution.py:474
  11.8 12.4 %copy-start = (f32[512,4]{0,1:T(4,128)S(1)}, f32[512,4]{0,1:T(4,128)}, u32[]{:S(2)}) copy-start(f32[512,4]{0,1:T(4,128)} %param.8) | copy-start | bytes 24580
  11.9 12.4 %copy-start.1 = (f32[512,2]{0,1:T(2,128)S(1)}, f32[512,2]{0,1:T(2,128)}, u32[]{:S(2)}) copy-start(f32[512,2]{0,1:T(2,128)} %param.7) | copy-start | bytes 12292
  11.9 12.4 %copy-start.2 = (f32[128]{0:T(128)S(1)}, f32[128]{0:T(128)}, u32[]{:S(2)}) copy-start(f32[128]{0:T(128)} %param.9) | copy-start | bytes 1540
  11.9 12.3 %collective-permute-start.2 = (f32[128,2048]{1,0:T(8,128)S(1)}, f32[128,2048]{1,0:T(8,128)S(1)}, u32[]{:S(2)}, u32[]{:S(2)}) collective-permute-start(f32[128,2048]{1,0:T(8,128)S(1)} %products.8), channel_id=1, source_target_pairs={{0,1},{1,0},{2,3},{3,2},{4,5},{5,4},{6,7},{7,6},{8,9},{9,8},{10,11... | collective-permute-start | bytes 3145736 | tf_op jit(solution)/shard_map/ppermute | solution.py:474
  14.0 3.1 %collective-permute-start.4 = (f32[128,512]{1,0:T(8,128)S(1)}, f32[128,512]{1,0:T(8,128)S(1)}, u32[]{:S(2)}, u32[]{:S(2)}) collective-permute-start(f32[128,512]{1,0:T(8,128)S(1)} %products.9), channel_id=1, source_target_pairs={{0,1},{1,0},{2,3},{3,2},{4,5},{5,4},{6,7},{7,6},{8,9},{9,8},{10,11... | collective-permute-start | bytes 786440 | tf_op jit(solution)/shard_map/ppermute | solution.py:474
  14.2 10.0 %collective-permute-start.6 = (bf16[1032,128]{1,0:T(8,128)(2,1)S(1)}, bf16[1032,128]{1,0:T(8,128)(2,1)S(1)}, u32[]{:S(2)}, u32[]{:S(2)}) collective-permute-start(bf16[1032,128]{1,0:T(8,128)(2,1)S(1)} %encode.3.refs_0_), channel_id=1, source_target_pairs={{0,2},{1,3},{2,0},{3,1},{4,6},{5,7},{6,4},{7,5},{8,10},{9,11},{10,... | collective-permute-start | bytes 792584 | tf_op jit(solution)/shard_map/ppermute | solution.py:478
  17.2 9.9 %collective-permute-start.5 = (bf16[520,128]{1,0:T(8,128)(2,1)S(1)}, bf16[520,128]{1,0:T(8,128)(2,1)S(1)}, u32[]{:S(2)}, u32[]{:S(2)}) collective-permute-start(bf16[520,128]{1,0:T(8,128)(2,1)S(1)} %encode.5), channel_id=1, source_target_pairs={{0,2},{1,3},{2,0},{3,1},{4,6},{5,7},{6,4},{7,5},{8,10},{9,11},{10,... | collective-permute-start | bytes 399368 | tf_op jit(solution)/shard_map/ppermute | solution.py:478
  18.4 10.9 %collective-permute-start.3 = (bf16[520,128]{1,0:T(8,128)(2,1)S(1)}, bf16[520,128]{1,0:T(8,128)(2,1)S(1)}, u32[]{:S(2)}, u32[]{:S(2)}) collective-permute-start(bf16[520,128]{1,0:T(8,128)(2,1)S(1)} %encode.4.refs_0_), channel_id=1, source_target_pairs={{0,2},{1,3},{2,0},{3,1},{4,6},{5,7},{6,4},{7,5},{8,10},{9,11},{10,... | collective-permute-start | bytes 399368 | tf_op jit(solution)/shard_map/ppermute | solution.py:478
  29.9 5.8 %collective-permute-start.9 = (f32[32,128]{1,0:T(8,128)S(1)}, f32[32,128]{1,0:T(8,128)S(1)}, u32[]{:S(2)}, u32[]{:S(2)}) collective-permute-start(f32[32,128]{1,0:T(8,128)S(1)} %get-tuple-element.37), channel_id=1, source_target_pairs={{0,12},{4,8},{8,4},{12,0},{1,13},{5,9},{9,5},{13,1},{2,14},{6,10},... | collective-permute-start | bytes 49160 | tf_op jit(solution)/shard_map/ppermute | solution.py:484
  33.8 4.6 %collective-permute-start.8 = (f32[32,128]{1,0:T(8,128)S(1)}, f32[32,128]{1,0:T(8,128)S(1)}, u32[]{:S(2)}, u32[]{:S(2)}) collective-permute-start(f32[32,128]{1,0:T(8,128)S(1)} %get-tuple-element.37), channel_id=1, source_target_pairs={{0,8},{4,12},{8,0},{12,4},{1,9},{5,13},{9,1},{13,5},{2,10},{6,14},... | collective-permute-start | bytes 49160 | tf_op jit(solution)/shard_map/ppermute | solution.py:484
  33.8 4.6 %collective-permute-start.7 = (f32[32,128]{1,0:T(8,128)S(1)}, f32[32,128]{1,0:T(8,128)S(1)}, u32[]{:S(2)}, u32[]{:S(2)}) collective-permute-start(f32[32,128]{1,0:T(8,128)S(1)} %get-tuple-element.37), channel_id=1, source_target_pairs={{0,4},{4,0},{8,12},{12,8},{1,5},{5,1},{9,13},{13,9},{2,6},{6,2},{1... | collective-permute-start | bytes 49160 | tf_op jit(solution)/shard_map/ppermute | solution.py:484
  39.1 5.6 %collective-permute-start.12 = (f32[32,128]{1,0:T(8,128)S(1)}, f32[32,128]{1,0:T(8,128)S(1)}, u32[]{:S(2)}, u32[]{:S(2)}) collective-permute-start(f32[32,128]{1,0:T(8,128)S(1)} %get-tuple-element.50), channel_id=1, source_target_pairs={{0,12},{4,8},{8,4},{12,0},{1,13},{5,9},{9,5},{13,1},{2,14},{6,10},... | collective-permute-start | bytes 49160 | tf_op jit(solution)/shard_map/ppermute | solution.py:484
  40.6 4.7 %collective-permute-start.11 = (f32[32,128]{1,0:T(8,128)S(1)}, f32[32,128]{1,0:T(8,128)S(1)}, u32[]{:S(2)}, u32[]{:S(2)}) collective-permute-start(f32[32,128]{1,0:T(8,128)S(1)} %get-tuple-element.50), channel_id=1, source_target_pairs={{0,8},{4,12},{8,0},{12,4},{1,9},{5,13},{9,1},{13,5},{2,10},{6,14},... | collective-permute-start | bytes 49160 | tf_op jit(solution)/shard_map/ppermute | solution.py:484
  41.3 4.2 %collective-permute-start.10 = (f32[32,128]{1,0:T(8,128)S(1)}, f32[32,128]{1,0:T(8,128)S(1)}, u32[]{:S(2)}, u32[]{:S(2)}) collective-permute-start(f32[32,128]{1,0:T(8,128)S(1)} %get-tuple-element.50), channel_id=1, source_target_pairs={{0,4},{4,0},{8,12},{12,8},{1,5},{5,1},{9,13},{13,9},{2,6},{6,2},{1... | collective-permute-start | bytes 49160 | tf_op jit(solution)/shard_map/ppermute | solution.py:484
